TPU v7x, 32 devices: a whole 2x2x4 slice. The times are simulated.
32 devices in a mesh: rep: 4 (over z), shard: 8 (over y, x, core).
Axes of the slice: x: 2, y: 2, z: 4, core: 2. Of those that a mesh axis runs over, the one named last changes fastest.
Arguments:
- tokens: bfloat16 [4096, 2048], P(('rep', 'shard')), may hold values from -6 to 6
- attn_gain: float32 [2048], replicated, may hold values from 0.5 to 1.5
- query_weight: bfloat16 [2048, 2048], P('shard'), may hold values from -0.5 to 0.5
- key_weight: bfloat16 [2048, 512], P('shard'), may hold values from -0.5 to 0.5
- value_weight: bfloat16 [2048, 512], P('shard'), may hold values from -0.5 to 0.5
- output_weight: bfloat16 [2048, 2048], P('shard'), may hold values from -1 to 1
- ffn_gain: float32 [2048], replicated, may hold values from 0.5 to 1.5
- gate_weight: bfloat16 [2048, 8192], P('shard'), may hold values from -0.125 to 0.125
- up_weight: bfloat16 [2048, 8192], P('shard'), may hold values from -0.125 to 0.125
- down_weight: bfloat16 [8192, 2048], P('shard'), may hold values from -0.25 to 0.25
- dealing: int32 [4, 1024], P('rep'), may hold values from 0 to 1023, each once within a row
- lengths: int32 [4, 3], P('rep'), may hold values from 1 to 768, 1024 in all within a row
- cotangent: bfloat16 [4096, 2048], P(('rep', 'shard')), may hold values from -6 to 6
Outputs:
- layer_output: bfloat16 [4096, 2048], P(('rep', 'shard'))
- tokens_grad: float32 [4096, 2048], P(('rep', 'shard'))
- attn_gain_grad: float32 [2048], replicated
- query_weight_grad: float32 [2048, 2048], P('shard')
- key_weight_grad: float32 [2048, 512], P('shard')
- value_weight_grad: float32 [2048, 512], P('shard')
- output_weight_grad: float32 [2048, 2048], P('shard')
- ffn_gain_grad: float32 [2048], replicated
- gate_weight_grad: float32 [2048, 8192], P('shard')
- up_weight_grad: float32 [2048, 8192], P('shard')
- down_weight_grad: float32 [8192, 2048], P('shard')
Inputs may be any that keep to these rules, and one draw needn't show every extreme that they name: Each row of dealing is a permutation of 0 to 1023. Each row of lengths sums to 1024 and holds one length of exactly 768.
All inputs are finite; a program needn't handle non-finite values.
Results may differ from a plain program's by a relative error of at most 0.023.
Values may be sent and summed in bfloat16 or wider, within the bound.
A program may use at most 640 MiB of HBM per device.

v0:
```python
import jax
import jax.numpy as jnp
from jax import lax
from jax.sharding import PartitionSpec as P

HEADS = 32
KV_HEADS = 8
HEAD = 64


EPSILON = 1e-05
RESIDUAL_SCALE = 0.22
SCORE_SCALE = 0.015625
ROPE_BASE = 10000000.0
MASKED = -1e30


def rms_scale(hidden, gain_vector):
    return (
        hidden
        * lax.rsqrt(jnp.mean(hidden * hidden, axis=-1, keepdims=True) + EPSILON)
        * gain_vector
    )


def places(packed_index, seq_lengths):
    seq_ends = jnp.cumsum(seq_lengths)
    starts = seq_ends - seq_lengths
    segment = jnp.sum((packed_index[:, None] >= seq_ends[None, :]).astype(jnp.int32), axis=1)
    chosen = segment[:, None] == jnp.arange(seq_lengths.shape[0], dtype=jnp.int32)[None, :]
    position = packed_index - jnp.sum(jnp.where(chosen, starts[None, :], 0), axis=1)
    return (segment, position)


def angles(position, half_width):
    frequency = ROPE_BASE ** (
        -(jnp.arange(half_width, dtype=jnp.float32) * 2.0) / (2.0 * half_width)
    )
    turned = position.astype(jnp.float32)[:, None] * frequency[None, :]
    return (jnp.cos(turned)[:, None, :], jnp.sin(turned)[:, None, :])


def rotate(values, cosine, sine_table):
    half_width = values.shape[-1] // 2
    first_half = values[..., :half_width]
    second = values[..., half_width:]
    return jnp.concatenate(
        [first_half * cosine - second * sine_table, second * cosine + first_half * sine_table],
        axis=-1,
    )


def unrotate(values, cosine, sine_table):
    half_width = values.shape[-1] // 2
    first_half = values[..., :half_width]
    second = values[..., half_width:]
    return jnp.concatenate(
        [first_half * cosine + second * sine_table, second * cosine - first_half * sine_table],
        axis=-1,
    )


def picker(wanted, running, shard_piece):
    inside = (wanted >= 0) & (wanted < shard_piece.shape[0])
    picked = jnp.take(shard_piece, jnp.clip(wanted, 0, shard_piece.shape[0] - 1), axis=0)
    return running + jnp.where(inside[:, None], picked, jnp.zeros_like(picked))


def add_rows(inputs, shard_piece):
    return jnp.dot(inputs, shard_piece, preferred_element_type=jnp.float32)


def times_transposed(gradient, shard_piece):
    return lax.dot_general(
        gradient, shard_piece, (((1,), (1,)), ((), ())), preferred_element_type=jnp.float32
    )


def single_rows(inputs, weight):
    return add_rows(inputs, lax.all_gather(weight, "shard", axis=0, tiled=True))


def single_cols(gradient, weight):
    return times_transposed(gradient, lax.all_gather(weight, "shard", axis=0, tiled=True))


def spread(inputs, gradient):
    return lax.psum_scatter(
        lax.dot_general(
            inputs, gradient, (((0,), (0,)), ((), ())), preferred_element_type=jnp.float32
        ).astype(jnp.bfloat16),
        "shard",
        scatter_dimension=0,
        tiled=True,
    ).astype(jnp.float32)


def block_scores(queries, key_block, query_segment, query_position, key_segment, key_position):
    raw_scores = jnp.einsum(
        "rkgd,ckd->kgrc", queries, key_block, preferred_element_type=jnp.float32
    )
    allowed = (key_segment[None, :] == query_segment[:, None]) & (
        key_position[None, :] <= query_position[:, None]
    )
    return (SCORE_SCALE * raw_scores, allowed)


def per_device(
    tokens,
    attn_gain,
    query_weight,
    key_weight,
    value_weight,
    output_weight,
    ffn_gain,
    gate_weight,
    up_weight,
    down_weight,
    dealing,
    lengths,
    cotangent,
):
    local_rows = tokens.shape[0]
    model_width = tokens.shape[1]
    group_rows = local_rows * lax.axis_size("shard")
    kv_count = KV_HEADS
    head_width = HEAD
    per_group = HEADS // KV_HEADS
    here_index = lax.axis_index("shard")
    order_row = dealing[0]
    key_segment, key_position = places(order_row, lengths[0])
    query_segment = lax.dynamic_slice_in_dim(key_segment, here_index * local_rows, local_rows)
    query_position = lax.dynamic_slice_in_dim(key_position, here_index * local_rows, local_rows)
    my_tokens = lax.dynamic_slice_in_dim(order_row, here_index * local_rows, local_rows)
    cosine, sine_table = angles(query_position, head_width // 2)
    placed = picker(
        my_tokens,
        jnp.zeros((local_rows, model_width), jnp.bfloat16),
        lax.all_gather(tokens, "shard", axis=0, tiled=True),
    )
    hidden = placed.astype(jnp.float32)
    normed = rms_scale(hidden, attn_gain).astype(jnp.bfloat16)
    shard_pieces = (
        lax.all_gather(query_weight, "shard", axis=0, tiled=True),
        lax.all_gather(key_weight, "shard", axis=0, tiled=True),
        lax.all_gather(value_weight, "shard", axis=0, tiled=True),
    )
    query_pre = add_rows(normed, shard_pieces[0])
    key_pre = add_rows(normed, shard_pieces[1])
    value_pre = add_rows(normed, shard_pieces[2])
    queries = (
        rotate(query_pre.reshape(local_rows, HEADS, head_width), cosine, sine_table)
        .astype(jnp.bfloat16)
        .reshape(local_rows, kv_count, per_group, head_width)
    )
    key_local = (
        rotate(key_pre.reshape(local_rows, kv_count, head_width), cosine, sine_table)
        .astype(jnp.bfloat16)
        .reshape(local_rows, kv_count * head_width)
    )
    value_local = value_pre.astype(jnp.bfloat16)
    key_all, value_all = (
        lax.all_gather(key_local, "shard", axis=0, tiled=True),
        lax.all_gather(value_local, "shard", axis=0, tiled=True),
    )
    block_rows = 4 * local_rows
    block_count = group_rows // block_rows
    key_blocks = key_all.reshape(block_count, block_rows, kv_count, head_width)
    value_blocks = value_all.reshape(block_count, block_rows, kv_count, head_width)
    segment_blocks = key_segment.reshape(block_count, block_rows)
    position_blocks = key_position.reshape(block_count, block_rows)

    def gather_stats(running, block_item):
        running_top, running_sum = running
        key_block, segment_block, position_block = block_item
        scaled, allowed = block_scores(
            queries, key_block, query_segment, query_position, segment_block, position_block
        )
        masked_scores = jnp.where(allowed, scaled, MASKED)
        new_top = jnp.maximum(running_top, jnp.max(masked_scores, axis=-1))
        exponent = jnp.where(allowed, jnp.exp(masked_scores - new_top[..., None]), 0.0)
        running_sum = running_sum * jnp.exp(running_top - new_top) + jnp.sum(exponent, axis=-1)
        return ((new_top, running_sum), None)

    start_top = jnp.full((kv_count, per_group, local_rows), MASKED, jnp.float32)
    start_sum = jnp.zeros((kv_count, per_group, local_rows), jnp.float32)
    (score_top, score_sum), unused_stats = lax.scan(
        gather_stats, (start_top, start_sum), (key_blocks, segment_blocks, position_blocks)
    )
    log_total = score_top + jnp.log(score_sum)

    def weigh_values(running, block_item):
        upper_part, lower_part = running
        key_block, value_block, segment_block, position_block = block_item
        scaled, allowed = block_scores(
            queries, key_block, query_segment, query_position, segment_block, position_block
        )
        probabilities = jnp.where(allowed, jnp.exp(scaled - log_total[..., None]), 0.0)
        probs_high = probabilities.astype(jnp.bfloat16)
        probs_rest = (probabilities - probs_high.astype(jnp.float32)).astype(jnp.bfloat16)
        upper_part = upper_part + jnp.einsum(
            "kgrc,ckd->rkgd", probs_high, value_block, preferred_element_type=jnp.float32
        )
        lower_part = lower_part + jnp.einsum(
            "kgrc,ckd->rkgd", probs_rest, value_block, preferred_element_type=jnp.float32
        )
        return ((upper_part, lower_part), None)

    empty_heads = jnp.zeros((local_rows, kv_count, per_group, head_width), jnp.float32)
    (upper_part, lower_part), unused_weigh = lax.scan(
        weigh_values,
        (empty_heads, empty_heads),
        (key_blocks, value_blocks, segment_blocks, position_blocks),
    )
    attention = upper_part.astype(jnp.bfloat16).reshape(local_rows, model_width)
    attn_branch = single_rows(attention, output_weight)
    middle = hidden + RESIDUAL_SCALE * attn_branch
    normed_ffn = rms_scale(middle, ffn_gain).astype(jnp.bfloat16)
    shard_pieces = (
        lax.all_gather(gate_weight, "shard", axis=0, tiled=True),
        lax.all_gather(up_weight, "shard", axis=0, tiled=True),
    )
    gate_pre = add_rows(normed_ffn, shard_pieces[0])
    up_pre = add_rows(normed_ffn, shard_pieces[1])
    activated = (jax.nn.silu(gate_pre) * up_pre).astype(jnp.bfloat16)
    down_out = single_rows(activated, down_weight)
    layer_output = (middle + RESIDUAL_SCALE * down_out).astype(jnp.bfloat16)
    out_grad = cotangent.astype(jnp.float32)
    down_grad = (RESIDUAL_SCALE * out_grad).astype(jnp.bfloat16)
    down_weight_part = spread(activated, down_grad)
    act_grad = single_cols(down_grad, down_weight)
    unused_value, silu_pull = jax.vjp(
        lambda gate_in, up_in: jax.nn.silu(gate_in) * up_in, gate_pre, up_pre
    )
    gate_grad, up_grad = silu_pull(act_grad)
    gate_grad = gate_grad.astype(jnp.bfloat16)
    up_grad = up_grad.astype(jnp.bfloat16)
    gate_weight_part = spread(normed_ffn, gate_grad)
    up_weight_part = spread(normed_ffn, up_grad)
    shard_pieces = lax.all_gather((gate_weight, up_weight), "shard", axis=0, tiled=True)
    normed_ffn_grad = times_transposed(gate_grad, shard_pieces[0]) + times_transposed(
        up_grad, shard_pieces[1]
    )
    unused_norm, ffn_pull = jax.vjp(rms_scale, middle, ffn_gain)
    middle_part, ffn_gain_part = ffn_pull(normed_ffn_grad)
    middle_grad = out_grad + middle_part
    branch_grad = (RESIDUAL_SCALE * middle_grad).astype(jnp.bfloat16)
    output_weight_part = spread(attention, branch_grad)
    attention_grad = single_cols(branch_grad, output_weight)
    attention_grad = attention_grad.astype(jnp.bfloat16).reshape(
        local_rows, kv_count, per_group, head_width
    )
    row_delta = jnp.einsum(
        "rkgd,rkgd->kgr", attention_grad.astype(jnp.float32), upper_part + lower_part
    )

    def backward_block(query_grad, block_item):
        key_block, value_block, segment_block, position_block = block_item
        scaled, allowed = block_scores(
            queries, key_block, query_segment, query_position, segment_block, position_block
        )
        probabilities = jnp.where(allowed, jnp.exp(scaled - log_total[..., None]), 0.0)
        probs_grad = jnp.einsum(
            "rkgd,ckd->kgrc", attention_grad, value_block, preferred_element_type=jnp.float32
        )
        score_grad = (probabilities * (probs_grad - row_delta[..., None])).astype(jnp.bfloat16)
        query_grad = query_grad + SCORE_SCALE * jnp.einsum(
            "kgrc,ckd->rkgd", score_grad, key_block, preferred_element_type=jnp.float32
        )
        key_part = SCORE_SCALE * jnp.einsum(
            "kgrc,rkgd->ckd", score_grad, queries, preferred_element_type=jnp.float32
        )
        value_part = jnp.einsum(
            "kgrc,rkgd->ckd",
            probabilities.astype(jnp.bfloat16),
            attention_grad,
            preferred_element_type=jnp.float32,
        )
        return (query_grad, (key_part, value_part))

    query_grad, (key_parts, value_parts) = lax.scan(
        backward_block, empty_heads, (key_blocks, value_blocks, segment_blocks, position_blocks)
    )
    key_sum, value_sum = (
        lax.psum_scatter(
            key_parts.reshape(group_rows, kv_count * head_width).astype(jnp.bfloat16),
            "shard",
            scatter_dimension=0,
            tiled=True,
        ).astype(jnp.float32),
        lax.psum_scatter(
            value_parts.reshape(group_rows, kv_count * head_width).astype(jnp.bfloat16),
            "shard",
            scatter_dimension=0,
            tiled=True,
        ).astype(jnp.float32),
    )
    query_pre_grad = (
        unrotate(query_grad.reshape(local_rows, HEADS, head_width), cosine, sine_table)
        .reshape(local_rows, model_width)
        .astype(jnp.bfloat16)
    )
    key_pre_grad = (
        unrotate(key_sum.reshape(local_rows, kv_count, head_width), cosine, sine_table)
        .reshape(local_rows, kv_count * head_width)
        .astype(jnp.bfloat16)
    )
    value_pre_grad = value_sum.astype(jnp.bfloat16)
    query_weight_part = spread(normed, query_pre_grad)
    key_weight_part = spread(normed, key_pre_grad)
    value_weight_part = spread(normed, value_pre_grad)
    shard_pieces = lax.all_gather(
        (query_weight, key_weight, value_weight), "shard", axis=0, tiled=True
    )
    normed_grad = (
        times_transposed(query_pre_grad, shard_pieces[0])
        + times_transposed(key_pre_grad, shard_pieces[1])
        + times_transposed(value_pre_grad, shard_pieces[2])
    )
    unused_first, attn_pull = jax.vjp(rms_scale, hidden, attn_gain)
    hidden_part, attn_gain_part = attn_pull(normed_grad)
    dealt_grad = middle_grad + hidden_part
    inverse = (
        jnp.zeros((group_rows,), jnp.int32)
        .at[order_row]
        .set(jnp.arange(group_rows, dtype=jnp.int32))
    )
    wanted_slots = lax.dynamic_slice_in_dim(inverse, here_index * local_rows, local_rows)
    tokens_grad = picker(
        wanted_slots,
        jnp.zeros((local_rows, model_width), jnp.float32),
        lax.all_gather(dealt_grad.astype(jnp.bfloat16), "shard", axis=0, tiled=True).astype(
            jnp.float32
        ),
    )
    summed = (
        lax.psum(query_weight_part.astype(jnp.bfloat16), "rep").astype(jnp.float32),
        lax.psum(key_weight_part.astype(jnp.bfloat16), "rep").astype(jnp.float32),
        lax.psum(value_weight_part.astype(jnp.bfloat16), "rep").astype(jnp.float32),
        lax.psum(output_weight_part.astype(jnp.bfloat16), "rep").astype(jnp.float32),
        lax.psum(gate_weight_part.astype(jnp.bfloat16), "rep").astype(jnp.float32),
        lax.psum(up_weight_part.astype(jnp.bfloat16), "rep").astype(jnp.float32),
        lax.psum(down_weight_part.astype(jnp.bfloat16), "rep").astype(jnp.float32),
    )
    attn_gain_grad, ffn_gain_grad = lax.psum((attn_gain_part, ffn_gain_part), ("rep", "shard"))
    return (
        layer_output,
        tokens_grad,
        attn_gain_grad,
        summed[0],
        summed[1],
        summed[2],
        summed[3],
        ffn_gain_grad,
        summed[4],
        summed[5],
        summed[6],
    )


def solution(mesh):
    return jax.shard_map(
        per_device,
        mesh=mesh,
        in_specs=(
            P(("rep", "shard"), None),
            P(),
            P("shard", None),
            P("shard", None),
            P("shard", None),
            P("shard", None),
            P(),
            P("shard", None),
            P("shard", None),
            P("shard", None),
            P("rep", None),
            P("rep", None),
            P(("rep", "shard"), None),
        ),
        out_specs=(
            P(("rep", "shard"), None),
            P(("rep", "shard"), None),
            P(),
            P("shard", None),
            P("shard", None),
            P("shard", None),
            P("shard", None),
            P(),
            P("shard", None),
            P("shard", None),
            P("shard", None),
        ),
        check_vma=False,
    )
```

profile of v0, /device:TPU:0, one launch (start us, length us, event | category | flops | bytes accessed | tf_op | source)
XLA Modules:
  0.0 2409.2 jit_solution(6717161342337709093)
XLA Ops:
  11.5 37.9 %all-gather.12.cloned.1.call-done = bf16[1024,2048]{1,0:T(8,128)(2,1)} async-done(((bf16[128,2048]{1,0:T(8,128)(2,1)}), bf16[1024,2048]{1,0:T(8,128)(2,1)}) %all-gather.12.cloned.1.call-update) | async-done | bytes 4194320 | tf_op jit(solution)/shard_map/all_gather | solution.py:139
  53.9 25.3 %all-gather.14.cloned.1.call-done = bf16[2048,512]{1,0:T(8,128)(2,1)} async-done(((bf16[256,512]{1,0:T(8,128)(2,1)}), bf16[2048,512]{1,0:T(8,128)(2,1)}) %all-gather.14.cloned.1.call-update) | async-done | bytes 2097168 | tf_op jit(solution)/shard_map/all_gather | solution.py:146
  82.7 26.3 %all-gather.18.cloned.1.call-done = bf16[2048,512]{1,0:T(8,128)(2,1)} async-done(((bf16[256,512]{1,0:T(8,128)(2,1)}), bf16[2048,512]{1,0:T(8,128)(2,1)}) %all-gather.18.cloned.1.call-update) | async-done | bytes 2097168 | tf_op jit(solution)/shard_map/all_gather | solution.py:145
  142.1 18.7 all-gather.20.cloned.1.call-done
  164.8 52.1 %all-gather.22.cloned.1.call-done = bf16[2048,2048]{1,0:T(8,128)(2,1)} async-done(((bf16[256,2048]{1,0:T(8,128)(2,1)}), bf16[2048,2048]{1,0:T(8,128)(2,1)}) %all-gather.22.cloned.1.call-update) | async-done | bytes 8388624 | tf_op jit(solution)/shard_map/all_gather | solution.py:144
  224.1 19.2 while.41
  243.3 30.6 %while.42 = (s32[]{:T(128)}, f32[128,8,4,64]{0,3,2,1:T(8,128)S(1)}, f32[128,8,4,64]{0,3,2,1:T(8,128)}, bf16[2,512,8,64]{1,3,2,0:T(8,128)(2,1)}, s32[2,512]{1,0:T...) while((s32[]{:T(128)}, f32[128,8,4,64]{0,3,2,1:T(8,128)S(1)}, ...), condition=%wide.region_9.10_spmd.clone, body=%wide.region_8.9_spmd.clone.sunk | while | flops 829620224 | bytes 77837592 | solution.py:210
  281.4 154.6 %all-gather.26.cloned.1.call-done = bf16[2048,8192]{1,0:T(8,128)(2,1)} async-done(((bf16[256,8192]{1,0:T(8,128)(2,1)}), bf16[2048,8192]{1,0:T(8,128)(2,1)}) %all-gather.26.cloned.1.call-update) | async-done | bytes 33554448 | tf_op jit(solution)/shard_map/all_gather | solution.py:220
  436.0 19.2 fusion.109
  455.2 143.5 %all-gather.28.cloned.1.call-done = bf16[2048,8192]{1,0:T(8,128)(2,1)} async-done(((bf16[256,8192]{1,0:T(8,128)(2,1)}), bf16[2048,8192]{1,0:T(8,128)(2,1)}) %all-gather.28.cloned.1.call-update) | async-done | bytes 33554448 | tf_op jit(solution)/shard_map/all_gather | solution.py:221
  598.7 19.3 fusion.110
  618.0 143.3 %all-gather.30.cloned.1.call-done = bf16[8192,2048]{1,0:T(8,128)(2,1)} async-done(((bf16[1024,2048]{1,0:T(8,128)(2,1)}), bf16[8192,2048]{1,0:T(8,128)(2,1)}) %all-gather.30.cloned.1.call-update) | async-done | bytes 33554448 | tf_op jit(solution)/shard_map/all_gather | solution.py:80
  761.3 21.4 multiply_convert_fusion
  798.9 18.2 multiply_reduce_fusion
  831.2 39.7 %while.43 = (s32[]{:T(128)}, f32[128,8,4,64]{0,3,2,1:T(8,128)S(1)}, bf16[2,512,8,64]{1,3,2,0:T(8,128)(2,1)}, bf16[2,512,8,64]{1,3,2,0:T(8,128)(2,1)}, bf16[2,512...) while((s32[]{:T(128)}, f32[128,8,4,64]{0,3,2,1:T(8,128)S(1)}, ...), condition=%wide.region_14.15_spmd.clone, body=%wide.region_13.14_spmd.clone.sunk | while | flops 1364393984 | bytes 129758592 | solution.py:281
  886.2 28.5 %reduce-scatter.28.cloned.1.call-done = bf16[128,512]{1,0:T(8,128)(2,1)} async-done(((bf16[1024,512]{1,0:T(8,128)(2,1)}), bf16[128,512]{1,0:T(8,128)(2,1)}) %reduce-scatter.28.cloned.1.call-update) | async-done | bytes 131088
  918.1 36.2 %reduce-scatter.30.cloned.1.call-done = bf16[128,512]{1,0:T(8,128)(2,1)} async-done(((bf16[1024,512]{1,0:T(8,128)(2,1)}), bf16[128,512]{1,0:T(8,128)(2,1)}) %reduce-scatter.30.cloned.1.call-update) | async-done | bytes 131088
  1043.6 75.2 %reduce-scatter.14.cloned.1.call-done = bf16[256,2048]{1,0:T(8,128)(2,1)} async-done(((bf16[2048,2048]{1,0:T(8,128)(2,1)}), bf16[256,2048]{1,0:T(8,128)(2,1)}) %reduce-scatter.14.cloned.1.call-update) | async-done | bytes 1048592 | tf_op jit(solution)/shard_map/reduce_scatter | solution.py:88
  1118.8 75.6 %reduce-scatter.20.cloned.1.call-done = bf16[256,2048]{1,0:T(8,128)(2,1)} async-done(((bf16[2048,2048]{1,0:T(8,128)(2,1)}), bf16[256,2048]{1,0:T(8,128)(2,1)}) %reduce-scatter.20.cloned.1.call-update) | async-done | bytes 1048592 | tf_op jit(solution)/shard_map/reduce_scatter | solution.py:88
  1194.4 208.7 %reduce-scatter.22.cloned.1.call-done = bf16[256,8192]{1,0:T(8,128)(2,1)} async-done(((bf16[2048,8192]{1,0:T(8,128)(2,1)}), bf16[256,8192]{1,0:T(8,128)(2,1)}) %reduce-scatter.22.cloned.1.call-update) | async-done | bytes 4194320 | tf_op jit(solution)/shard_map/reduce_scatter | solution.py:88
  1403.1 209.1 %reduce-scatter.24.cloned.1.call-done = bf16[256,8192]{1,0:T(8,128)(2,1)} async-done(((bf16[2048,8192]{1,0:T(8,128)(2,1)}), bf16[256,8192]{1,0:T(8,128)(2,1)}) %reduce-scatter.24.cloned.1.call-update) | async-done | bytes 4194320 | tf_op jit(solution)/shard_map/reduce_scatter | solution.py:88
  1612.3 208.8 %reduce-scatter.26.cloned.1.call-done = bf16[1024,2048]{1,0:T(8,128)(2,1)} async-done(((bf16[8192,2048]{1,0:T(8,128)(2,1)}), bf16[1024,2048]{1,0:T(8,128)(2,1)}) %reduce-scatter.26.cloned.1.call-update) | async-done | bytes 4194320 | tf_op jit(solution)/shard_map/reduce_scatter | solution.py:88
  1840.0 39.9 %all-reduce = (f32[2048]{0:T(1024)}, f32[2048]{0:T(1024)}) all-reduce(f32[2048]{0:T(1024)S(1)} %get-tuple-element.438, f32[2048]{0:T(1024)S(1)} %copy-done.37), channel_id=1, replica_groups=mesh['rep'=4,'shard'=8] {'rep','shard'}, use_global_device_ids=true, to_apply=%region_19.20 | all-reduce | flops 4096 | bytes 32768 | tf_op jit(solution)/shard_map/psum | solution.py:345
  1892.6 486.6 %all-reduce.4.cloned.1.call-done = (bf16[256,2048]{1,0:T(8,128)(2,1)}, bf16[256,512]{1,0:T(8,128)(2,1)}, bf16[256,512]{1,0:T(8,128)(2,1)}, bf16[256,2048]{1,0:T(...) async-done(((bf16[256,2048]{1,0:T(8,128)(2,1)}, bf16[256,512]{1,0:T(8,128)(2,1)}, bf16[256,512]{1,0:T(8,128)(2,1)}, ...) | async-done | bytes 15204368 | tf_op jit(solution)/shard_map/psum | solution.py:337
  (282 shorter events, 344.4 us)
Async XLA Ops:
  7.2 42.2 %all-gather.12.cloned.1.call-start = ((), (), s32[]{:S(2)}) async-start(), calls=%async_computation.9 | async-start | bytes 4718592 | tf_op jit(solution)/shard_map/all_gather | solution.py:139
  7.9 71.3 %all-gather.14.cloned.1.call-start = ((), (), s32[]{:S(2)}) async-start(), calls=%async_computation.10 | async-start | bytes 2359296 | tf_op jit(solution)/shard_map/all_gather | solution.py:146
  8.7 100.4 %all-gather.18.cloned.1.call-start = ((), (), s32[]{:S(2)}) async-start(), calls=%async_computation.12 | async-start | bytes 2359296 | tf_op jit(solution)/shard_map/all_gather | solution.py:145
  9.4 125.5 %all-gather.16.cloned.1.call-start = ((), (), s32[]{:S(2)}) async-start(), calls=%async_computation.11 | async-start | bytes 1179648 | tf_op jit(solution)/shard_map/all_gather | solution.py:164
  82.0 78.8 %all-gather.20.cloned.1.call-start = ((), (), s32[]{:S(2)}) async-start(), calls=%async_computation.13 | async-start | bytes 1179648 | tf_op jit(solution)/shard_map/all_gather | solution.py:163
  112.4 104.6 %all-gather.22.cloned.1.call-start = ((), (), s32[]{:S(2)}) async-start(), calls=%async_computation.14 | async-start | bytes 9437184 | tf_op jit(solution)/shard_map/all_gather | solution.py:144
  113.0 162.0 %all-gather.24.cloned.1.call-start = ((), (), s32[]{:S(2)}) async-start(), calls=%async_computation.15 | async-start | bytes 9437184 | tf_op jit(solution)/shard_map/all_gather | solution.py:80
  113.7 322.3 %all-gather.26.cloned.1.call-start = ((), (), s32[]{:S(2)}) async-start(), calls=%async_computation.16 | async-start | bytes 37748736 | tf_op jit(solution)/shard_map/all_gather | solution.py:220
  114.5 484.2 %all-gather.28.cloned.1.call-start = ((), (), s32[]{:S(2)}) async-start(), calls=%async_computation.17 | async-start | bytes 37748736 | tf_op jit(solution)/shard_map/all_gather | solution.py:221
  115.2 646.0 %all-gather.30.cloned.1.call-start = ((), (), s32[]{:S(2)}) async-start(), calls=%async_computation.18 | async-start | bytes 37748736 | tf_op jit(solution)/shard_map/all_gather | solution.py:80
  115.8 798.9 %reduce-scatter.28.cloned.1.call-start = ((), (), s32[]{:S(2)}) async-start(), calls=%async_computation.27 | async-start | bytes 1179648
  878.6 75.8 %reduce-scatter.30.cloned.1.call-start = ((), (), s32[]{:S(2)}) async-start(), calls=%async_computation.28 | async-start | bytes 1179648
  886.1 142.1 %reduce-scatter.16.cloned.1.call-start = ((), (), s32[]{:S(2)}) async-start(), calls=%async_computation.21 | async-start | bytes 2359296 | tf_op jit(solution)/shard_map/reduce_scatter | solution.py:88
  918.1 125.5 %reduce-scatter.18.cloned.1.call-start = ((), (), s32[]{:S(2)}) async-start(), calls=%async_computation.22 | async-start | bytes 2359296 | tf_op jit(solution)/shard_map/reduce_scatter | solution.py:88
  957.6 161.2 %reduce-scatter.14.cloned.1.call-start = ((), (), s32[]{:S(2)}) async-start(), calls=%async_computation.20 | async-start | bytes 9437184 | tf_op jit(solution)/shard_map/reduce_scatter | solution.py:88
  964.0 230.4 %reduce-scatter.20.cloned.1.call-start = ((), (), s32[]{:S(2)}) async-start(), calls=%async_computation.23 | async-start | bytes 9437184 | tf_op jit(solution)/shard_map/reduce_scatter | solution.py:88
  969.8 433.3 %reduce-scatter.22.cloned.1.call-start = ((), (), s32[]{:S(2)}) async-start(), calls=%async_computation.24 | async-start | bytes 37748736 | tf_op jit(solution)/shard_map/reduce_scatter | solution.py:88
  985.6 626.7 %reduce-scatter.24.cloned.1.call-start = ((), (), s32[]{:S(2)}) async-start(), calls=%async_computation.25 | async-start | bytes 37748736 | tf_op jit(solution)/shard_map/reduce_scatter | solution.py:88
  1001.4 819.7 %reduce-scatter.26.cloned.1.call-start = ((), (), s32[]{:S(2)}) async-start(), calls=%async_computation.26 | async-start | bytes 37748736 | tf_op jit(solution)/shard_map/reduce_scatter | solution.py:88
  1018.2 861.7 %all-gather.32.cloned.1.call-start = ((), (), s32[]{:S(2)}) async-start(), calls=%async_computation.19 | async-start | bytes 4718592 | tf_op jit(solution)/shard_map/all_gather | solution.py:332
  1028.2 793.0 %copy-start.36 = (s32[1,1024]{1,0:T(1,128)S(1)}, s32[1,1024]{1,0:T(1,128)}, u32[]{:S(2)}) copy-start(s32[1,1024]{1,0:T(1,128)} %param.29) | copy-start | bytes 12292
  1028.2 797.4 %copy-start.5 = (f32[128,2048]{1,0:T(8,128)S(1)}, f32[128,2048]{1,0:T(8,128)}, u32[]{:S(2)}) copy-start(f32[128,2048]{1,0:T(8,128)} %copy-done.4) | copy-start | bytes 3145732
  1028.2 797.5 %copy-start.9 = (bf16[128,8192]{1,0:T(8,128)(2,1)S(1)}, bf16[128,8192]{1,0:T(8,128)(2,1)}, u32[]{:S(2)}) copy-start(bf16[128,8192]{1,0:T(8,128)(2,1)} %get-tuple-element.531) | copy-start | bytes 6291460
  1028.2 1351.0 %all-reduce.4.cloned.1.call-start = ((), (), s32[]{:S(2)}) async-start(), calls=%async_computation.29 | async-start | bytes 30408704 | tf_op jit(solution)/shard_map/psum | solution.py:337
  (51 other events, 1667.4 us)
Sparse Core Ops, SparseCore 0:
  9.9 39.4 all-gather.11
  51.3 27.8 all-gather.13
  81.1 27.9 all-gather.17
  111.4 23.4 all-gather.15
  137.2 23.5 all-gather.19
  162.5 54.3 all-gather.21
  218.8 54.3 all-gather.23
  275.1 160.7 all-gather.25
  437.9 160.7 all-gather.27
  600.4 160.7 all-gather.29
  878.7 36.0 reduce-scatter.27
  918.3 35.9 reduce-scatter.29
  957.6 41.1 reduce-scatter.15
  1002.4 41.2 reduce-scatter.17
  1047.5 71.2 reduce-scatter.13
  1123.1 71.2 reduce-scatter.19
  1197.9 205.2 reduce-scatter.21
  1407.0 205.2 reduce-scatter.23
  1615.8 205.2 reduce-scatter.25
  1823.6 37.2 all-gather.31
  1864.7 514.4 all-reduce.3
where the time goes:
time: 2410 us
  waiting for transfers between devices  1970 us (82%)
  matrix products  272 us (11%)
  local copies, waits for them, and re-layouts  57.5 us (2%)
  other arithmetic  53.1 us (2%)
  blocking collectives  39.9 us (2%)
    reduce_scatter x7, waiting for transfers between devices, spread(): lax.psum_scatter(lax.dot_general(inputs, gradient, (((0,), (0,)), ((), ()...  793 us
    psum x1, waiting for transfers between devices, per_device(): lax.psum(query_weight_part.astype(jnp.bfloat16), 'rep').astype(jnp.float32)  487 us
    all_gather x1, waiting for transfers between devices, per_device(): lax.all_gather(gate_weight, 'shard', axis=0, tiled=True)  155 us
    all_gather x1, waiting for transfers between devices, per_device(): lax.all_gather(up_weight, 'shard', axis=0, tiled=True)  144 us
    all_gather x2, waiting for transfers between devices, single_rows(): return add_rows(inputs, lax.all_gather(weight, 'shard', axis=0, tiled=True))  143 us
    dot_general x7, matrix products, times_transposed(): lax.dot_general(gradient, shard_piece, (((1,), (1,)), ((), ())), preferre...  71.3 us
    unnamed x23, waiting for transfers between devices  70.2 us
    dot_general x7, matrix products, add_rows(): return jnp.dot(inputs, shard_piece, preferred_element_type=jnp.float32)  70.2 us
  transfers between devices with their start and end apart: 21, of which 18 were waited for; matrix products, arithmetic and copies ran while one was open for 10% of the time, Pallas kernels for 0%

commit v1 on v0

v1 whole, which is shorter than its diff:
```python
import functools

import jax
import jax.numpy as jnp
from jax import lax
from jax.experimental import pallas as pl
from jax.experimental.pallas import tpu as pltpu
from jax.sharding import PartitionSpec as P

HEADS = 32
KV_HEADS = 8
HEAD = 64
EPSILON = 1e-05
RESIDUAL_SCALE = 0.22
SCORE_SCALE = 0.015625
ROPE_BASE = 10000000.0
MASKED = -1e30
BF16 = jnp.bfloat16
F32 = jnp.float32


def mm(a, b):
    return jnp.dot(a, b, preferred_element_type=F32)


def mm_t(a, b):
    return lax.dot_general(a, b, (((1,), (1,)), ((), ())), preferred_element_type=F32)


def t_mm(a, b):
    return lax.dot_general(a, b, (((0,), (0,)), ((), ())), preferred_element_type=F32)


def rms_scale(hidden, gain_vector):
    return (
        hidden
        * lax.rsqrt(jnp.mean(hidden * hidden, axis=-1, keepdims=True) + EPSILON)
        * gain_vector
    )


def places(packed_index, seq_lengths):
    seq_ends = jnp.cumsum(seq_lengths)
    starts = seq_ends - seq_lengths
    segment = jnp.sum((packed_index[:, None] >= seq_ends[None, :]).astype(jnp.int32), axis=1)
    chosen = segment[:, None] == jnp.arange(seq_lengths.shape[0], dtype=jnp.int32)[None, :]
    position = packed_index - jnp.sum(jnp.where(chosen, starts[None, :], 0), axis=1)
    return segment, position


def rope_tables(position, width):
    half = HEAD // 2
    frequency = ROPE_BASE ** (-(jnp.arange(half, dtype=F32) * 2.0) / (2.0 * half))
    turned = position.astype(F32)[:, None] * frequency[None, :]
    cosine, sine = jnp.cos(turned), jnp.sin(turned)
    cos_full = jnp.concatenate([cosine, cosine], axis=-1)
    sin_full = jnp.concatenate([-sine, sine], axis=-1)
    return jnp.tile(cos_full, (1, width // HEAD)), jnp.tile(sin_full, (1, width // HEAD))


def swap_halves(x):
    rows, width = x.shape
    half = HEAD // 2
    y = x.reshape(rows, width // HEAD, 2, half)
    return jnp.concatenate([y[:, :, 1:], y[:, :, :1]], axis=2).reshape(rows, width)


def rotate(x, cos_full, sin_full):
    return x * cos_full + swap_halves(x) * sin_full


def unrotate(x, cos_full, sin_full):
    return x * cos_full - swap_halves(x) * sin_full


def softmax_block(q, k, allowed):
    scores = SCORE_SCALE * lax.dot_general(
        q, k, (((1,), (1,)), ((), ())), preferred_element_type=F32
    )
    scores = jnp.where(allowed, scores, MASKED)
    top = jnp.max(scores, axis=-1, keepdims=True)
    weight = jnp.exp(scores - top)
    return weight * (1.0 / jnp.sum(weight, axis=-1, keepdims=True))


def allowed_block(row0, rows, cols, seg_q, seg_k):
    q_index = row0 + lax.broadcasted_iota(jnp.int32, (rows, cols), 0)
    k_index = lax.broadcasted_iota(jnp.int32, (rows, cols), 1)
    return (seg_q == seg_k) & (k_index <= q_index)


def attention_kernel(heads, block, q_ref, k_ref, v_ref, segc_ref, segr_ref, o_ref):
    total = k_ref.shape[0]
    for i in range(total // block):
        cols = (i + 1) * block
        rows = pl.ds(i * block, block)
        allowed = allowed_block(i * block, block, cols, segc_ref[rows, :], segr_ref[:, :cols])
        k, v = k_ref[:cols, :], v_ref[:cols, :]
        for h in range(heads):
            lanes = slice(h * HEAD, (h + 1) * HEAD)
            probs = softmax_block(q_ref[rows, lanes], k, allowed)
            out = jnp.dot(probs.astype(BF16), v, preferred_element_type=F32)
            o_ref[rows, lanes] = out.astype(BF16)


def attention_forward(q, k, v, seg_col, seg_row):
    total, width = q.shape
    heads = width // HEAD
    return pl.pallas_call(
        functools.partial(attention_kernel, heads, 256),
        out_shape=jax.ShapeDtypeStruct((total, width), BF16),
        compiler_params=pltpu.CompilerParams(vmem_limit_bytes=40 << 20),
        cost_estimate=pl.CostEstimate(
            flops=2 * total * total * width, bytes_accessed=4 * total * width, transcendentals=heads * total * total // 2
        ),
        name="attention_forward",
    )(q, k, v, seg_col, seg_row)


def attention_backward_kernel(
    heads, block, q_ref, k_ref, v_ref, g_ref, segc_ref, segr_ref, dq_ref, dk_ref, dv_ref
):
    total = k_ref.shape[0]
    dk_ref[...] = jnp.zeros_like(dk_ref)
    dv_ref[...] = jnp.zeros_like(dv_ref)
    for i in range(total // block):
        cols = (i + 1) * block
        rows = pl.ds(i * block, block)
        allowed = allowed_block(i * block, block, cols, segc_ref[rows, :], segr_ref[:, :cols])
        k, v = k_ref[:cols, :], v_ref[:cols, :]
        for h in range(heads):
            lanes = slice(h * HEAD, (h + 1) * HEAD)
            q, g = q_ref[rows, lanes], g_ref[rows, lanes]
            probs = softmax_block(q, k, allowed)
            probs_grad = lax.dot_general(
                g, v, (((1,), (1,)), ((), ())), preferred_element_type=F32
            )
            delta = jnp.sum(probs * probs_grad, axis=-1, keepdims=True)
            score_grad = (probs * (probs_grad - delta)).astype(BF16)
            dq_ref[rows, lanes] = SCORE_SCALE * jnp.dot(
                score_grad, k, preferred_element_type=F32
            )
            dk_ref[:cols, :] += SCORE_SCALE * lax.dot_general(
                score_grad, q, (((0,), (0,)), ((), ())), preferred_element_type=F32
            )
            dv_ref[:cols, :] += lax.dot_general(
                probs.astype(BF16), g, (((0,), (0,)), ((), ())), preferred_element_type=F32
            )


def attention_backward(q, k, v, g, seg_col, seg_row):
    total, width = q.shape
    heads = width // HEAD
    return pl.pallas_call(
        functools.partial(attention_backward_kernel, heads, 256),
        out_shape=(
            jax.ShapeDtypeStruct((total, width), F32),
            jax.ShapeDtypeStruct((total, HEAD), F32),
            jax.ShapeDtypeStruct((total, HEAD), F32),
        ),
        compiler_params=pltpu.CompilerParams(vmem_limit_bytes=40 << 20),
        cost_estimate=pl.CostEstimate(
            flops=5 * total * total * width, bytes_accessed=10 * total * width, transcendentals=heads * total * total // 2
        ),
        name="attention_backward",
    )(q, k, v, g, seg_col, seg_row)


def gather_rows(x):
    return lax.all_gather(x, "shard", axis=0, tiled=True)


def scatter_rows(x):
    return lax.psum_scatter(x, "shard", scatter_dimension=0, tiled=True)


def exchange(blocks):
    return lax.all_to_all(blocks, "shard", split_axis=0, concat_axis=0, tiled=True)


def rep_sum(x):
    count = lax.axis_size("rep")
    where = lax.axis_index("rep")
    half = count // 2
    for hop in range(half - 1):
        moved = lax.ppermute(
            x, "rep", [(hop, hop + 1), (count - 1 - hop, count - 2 - hop)]
        )
        x = (x.astype(F32) + moved.astype(F32)).astype(BF16)
    moved = lax.ppermute(x, "rep", [(half - 1, half), (half, half - 1)])
    x = (x.astype(F32) + moved.astype(F32)).astype(BF16)
    for hop in range(half - 1):
        near, far = half - 1 - hop, half + hop
        moved = lax.ppermute(x, "rep", [(near, near - 1), (far, far + 1)])
        x = jnp.where((where == near - 1) | (where == far + 1), moved, x)
    return x


def per_device(
    tokens,
    attn_gain,
    query_weight,
    key_weight,
    value_weight,
    output_weight,
    ffn_gain,
    gate_weight,
    up_weight,
    down_weight,
    dealing,
    lengths,
    cotangent,
):
    n = lax.axis_size("shard")
    here = lax.axis_index("shard")
    local, width = tokens.shape
    total = local * n
    rows = query_weight.shape[0]
    ff_cols = gate_weight.shape[1] // n
    q_cols = query_weight.shape[1] // n
    copies = n // KV_HEADS
    own = here * local

    packed = jnp.arange(total, dtype=jnp.int32)
    segment, position = places(packed, lengths[0])
    seg_col, seg_row = segment[:, None], segment[None, :]
    cos_q, sin_q = rope_tables(position, q_cols)
    cos_k, sin_k = cos_q[:, :HEAD], sin_q[:, :HEAD]
    dealt = (dealing[0][:, None] == packed[None, :]).astype(BF16)

    def column_blocks(weight, cols):
        return weight.reshape(rows, n, cols).transpose(1, 0, 2)

    def head_blocks(weight):
        blocks = weight.reshape(rows, KV_HEADS, HEAD).transpose(1, 0, 2)
        return jnp.repeat(blocks, copies, axis=0)

    hidden = tokens.astype(F32)
    normed = gather_rows(rms_scale(hidden, attn_gain).astype(BF16))
    qkv = exchange(
        jnp.concatenate(
            [column_blocks(query_weight, q_cols), head_blocks(key_weight), head_blocks(value_weight)],
            axis=2,
        )
    ).reshape(width, q_cols + 2 * HEAD)
    gate_cols = exchange(column_blocks(gate_weight, ff_cols)).reshape(width, ff_cols)
    up_cols = exchange(column_blocks(up_weight, ff_cols)).reshape(width, ff_cols)
    spread_cotangent = gather_rows(cotangent)

    pre = mm(normed, qkv)
    queries = rotate(pre[:, :q_cols], cos_q, sin_q).astype(BF16)
    keys = rotate(pre[:, q_cols : q_cols + HEAD], cos_k, sin_k).astype(BF16)
    values = pre[:, q_cols + HEAD :].astype(BF16)
    attention = attention_forward(queries, keys, values, seg_col, seg_row)
    branch = scatter_rows(mm(attention, output_weight).astype(BF16))
    middle = hidden + RESIDUAL_SCALE * branch.astype(F32)
    normed_ffn = gather_rows(rms_scale(middle, ffn_gain).astype(BF16))

    out_grad_all = t_mm(dealt, spread_cotangent)
    down_grad = (RESIDUAL_SCALE * out_grad_all).astype(BF16)
    out_grad = lax.dynamic_slice_in_dim(out_grad_all, own, local)
    act_grad = mm_t(down_grad, down_weight)

    gate = mm(normed_ffn, gate_cols)
    up = mm(normed_ffn, up_cols)
    sigmoid = jax.nn.sigmoid(gate)
    activated = (gate * sigmoid * up).astype(BF16)
    gate_grad = (act_grad * up * sigmoid * (1.0 + gate * (1.0 - sigmoid))).astype(BF16)
    up_grad = (act_grad * gate * sigmoid).astype(BF16)

    down_part = rep_sum(t_mm(activated, down_grad).astype(BF16))
    gate_part = rep_sum(exchange(t_mm(normed_ffn, gate_grad).astype(BF16).reshape(n, rows, ff_cols)))
    up_part = rep_sum(exchange(t_mm(normed_ffn, up_grad).astype(BF16).reshape(n, rows, ff_cols)))

    own_columns = lax.dynamic_slice_in_dim(dealt, own, local, axis=1)
    layer_output = scatter_rows(
        (
            RESIDUAL_SCALE * mm(mm(dealt, activated).astype(BF16), down_weight)
            + mm(own_columns, middle.astype(BF16))
        ).astype(BF16)
    )

    normed_ffn_grad = scatter_rows(
        (mm_t(gate_grad, gate_cols) + mm_t(up_grad, up_cols)).astype(BF16)
    ).astype(F32)
    unused_norm, ffn_pull = jax.vjp(rms_scale, middle, ffn_gain)
    middle_part, ffn_gain_part = ffn_pull(normed_ffn_grad)
    middle_grad = out_grad + middle_part
    branch_grad = gather_rows((RESIDUAL_SCALE * middle_grad).astype(BF16))
    output_part = rep_sum(t_mm(attention, branch_grad).astype(BF16))
    attention_grad = mm_t(branch_grad, output_weight).astype(BF16)
    dq, dk, dv = attention_backward(queries, keys, values, attention_grad, seg_col, seg_row)
    pre_grad = jnp.concatenate(
        [
            unrotate(dq, cos_q, sin_q).astype(BF16),
            unrotate(dk, cos_k, sin_k).astype(BF16),
            dv.astype(BF16),
        ],
        axis=1,
    )
    qkv_part = rep_sum(exchange(t_mm(normed, pre_grad).astype(BF16).reshape(n, rows, q_cols + 2 * HEAD)))
    normed_grad = scatter_rows(mm_t(pre_grad, qkv).astype(BF16)).astype(F32)
    unused_first, attn_pull = jax.vjp(rms_scale, hidden, attn_gain)
    hidden_part, attn_gain_part = attn_pull(normed_grad)
    tokens_grad = middle_grad + hidden_part

    def join(blocks):
        return blocks.transpose(1, 0, 2).reshape(rows, -1).astype(F32)

    def join_heads(blocks):
        blocks = blocks.astype(F32).reshape(KV_HEADS, copies, rows, HEAD).sum(axis=1)
        return blocks.transpose(1, 0, 2).reshape(rows, KV_HEADS * HEAD)

    attn_gain_grad, ffn_gain_grad = lax.psum((attn_gain_part, ffn_gain_part), ("rep", "shard"))
    return (
        layer_output,
        tokens_grad,
        attn_gain_grad,
        join(qkv_part[:, :, :q_cols]),
        join_heads(qkv_part[:, :, q_cols : q_cols + HEAD]),
        join_heads(qkv_part[:, :, q_cols + HEAD :]),
        output_part.astype(F32),
        ffn_gain_grad,
        join(gate_part),
        join(up_part),
        down_part.astype(F32),
    )


def solution(mesh):
    both = P(("rep", "shard"), None)
    rowed = P("shard", None)
    return jax.shard_map(
        per_device,
        mesh=mesh,
        in_specs=(
            both, P(), rowed, rowed, rowed, rowed, P(), rowed, rowed, rowed,
            P("rep", None), P("rep", None), both,
        ),
        out_specs=(both, both, P(), rowed, rowed, rowed, rowed, P(), rowed, rowed, rowed),
        check_vma=False,
    )
```

time: 2410 us -> 1150 us (0.48)
  waiting for transfers between devices: 1970 us -> 681 us
  matrix products: 272 us -> 127 us
  starting transfers between devices: 1.48 us -> 92.4 us
  other arithmetic: 53.1 us -> 98.3 us
    reduce_scatter x7 -> x4, waiting for transfers between devices: 793 us -> 67 us  [scatter_rows(): return lax.psum_scatter(x, 'shard', scatter_dimension=0, tiled=True)]
    all_gather x11 -> x4, waiting for transfers between devices: 619 us -> 21.4 us  [gather_rows(): return lax.all_gather(x, 'shard', axis=0, tiled=True)]
    psum x1 -> x0, waiting for transfers between devices: 487 us -> none  [per_device(): lax.psum(query_weight_part.astype(jnp.bfloat16), 'rep').astype(jnp.float32)]
    ppermute x0 -> x15, waiting for transfers between devices: none -> 417 us  [the longest x5 235 us: rep_sum(): lax.ppermute(x, 'rep', [(hop, hop + 1), (count - 1 - hop, count - 2 - hop)])]
    all_to_all x0 -> x6, waiting for transfers between devices: none -> 175 us  [exchange(): lax.all_to_all(blocks, 'shard', split_axis=0, concat_axis=0, tiled=True)]
    dot_general x39 -> x17, matrix products: 272 us -> 127 us  [the longest x6 44 us: t_mm(): lax.dot_general(a, b, (((0,), (0,)), ((), ())), preferred_element_type=F32)]
    unnamed x23 -> x8, waiting for transfers between devices: 70.2 us -> 0.8 us
    ppermute x0 -> x15, starting transfers between devices: none -> 63.5 us  [the longest x5 44.7 us: rep_sum(): lax.ppermute(x, 'rep', [(hop, hop + 1), (count - 1 - hop, count - 2 - hop)])]
  transfers between devices with their start and end apart: 21 -> 29, of which waited for: 18 -> 16; matrix products, arithmetic and copies ran while one was open for 10% -> 19% of each run, Pallas kernels for 0% -> 1%
where the time goes in v1:
time: 1150 us
  waiting for transfers between devices  681 us (59%)
  matrix products  127 us (11%)
  other arithmetic  98.3 us (9%)
  starting transfers between devices  92.4 us (8%)
  local copies, waits for them, and re-layouts  74.2 us (6%)
  blocking collectives  38.4 us (3%)
  Pallas kernels  21.5 us (2%)
  between operations  15.1 us (1%)
    ppermute x5, waiting for transfers between devices, rep_sum(): lax.ppermute(x, 'rep', [(hop, hop + 1), (count - 1 - hop, count - 2 - hop)])  235 us
    ppermute x5, waiting for transfers between devices, rep_sum(): moved = lax.ppermute(x, 'rep', [(near, near - 1), (far, far + 1)])  182 us
    all_to_all x6, waiting for transfers between devices, exchange(): lax.all_to_all(blocks, 'shard', split_axis=0, concat_axis=0, tiled=True)  175 us
    reduce_scatter x4, waiting for transfers between devices, scatter_rows(): return lax.psum_scatter(x, 'shard', scatter_dimension=0, tiled=True)  67 us
    convert_element_type x10, other arithmetic, rep_sum(): x = (x.astype(F32) + moved.astype(F32)).astype(BF16)  54.5 us
    ppermute x5, starting transfers between devices, rep_sum(): lax.ppermute(x, 'rep', [(hop, hop + 1), (count - 1 - hop, count - 2 - hop)])  44.7 us
    dot_general x6, matrix products, t_mm(): lax.dot_general(a, b, (((0,), (0,)), ((), ())), preferred_element_type=F32)  44 us
    dot_general x6, matrix products, mm(): return jnp.dot(a, b, preferred_element_type=F32)  42 us
  transfers between devices with their start and end apart: 29, of which 16 were waited for; matrix products, arithmetic and copies ran while one was open for 19% of the time, Pallas kernels for 1%

profile of v1, /device:TPU:0, one launch (start us, length us, event | category | flops | bytes accessed | tf_op | source)
XLA Modules:
  0.0 1147.6 jit_solution(10334988998676402477)
XLA Ops:
  25.4 22.3 %all-to-all-done = bf16[8,256,384]{1,2,0:T(8,128)(2,1)} async-done(((bf16[8,256,384]{1,2,0:T(8,128)(2,1)}), bf16[8,256,384]{1,2,0:T(8,128)(2,1)}, u32[]{:S(2)}, u32[]{:S(2)}) %all-to-all-start) | async-done | bytes 1572896 | tf_op jit(solution)/shard_map/all_to_all | solution.py:178
  50.4 14.2 %all-gather.5.cloned.1.call-done = bf16[1024,2048]{1,0:T(8,128)(2,1)} async-done(((bf16[128,2048]{1,0:T(8,128)(2,1)}), bf16[1024,2048]{1,0:T(8,128)(2,1)}) %all-gather.5.cloned.1.call-update) | async-done | bytes 4194320 | tf_op jit(solution)/shard_map/all_gather | solution.py:170
  107.3 67.0 %reduce-scatter.5.cloned.1.call-done = bf16[128,2048]{1,0:T(8,128)(2,1)} async-done(((bf16[1024,2048]{1,0:T(8,128)(2,1)}), bf16[128,2048]{1,0:T(8,128)(2,1)}) %reduce-scatter.5.cloned.1.call-update) | async-done | bytes 524304 | tf_op jit(solution)/shard_map/reduce_scatter | solution.py:174
  195.5 55.9 %all-to-all-done.2 = bf16[8,256,1024]{1,2,0:T(8,128)(2,1)} async-done(((bf16[8,256,1024]{1,2,0:T(8,128)(2,1)}), bf16[8,256,1024]{1,2,0:T(8,128)(2,1)}, u32[]{:S(2)}, u32[]{:S(2)}) %all-to-all-start.2) | async-done | bytes 4194336 | tf_op jit(solution)/shard_map/all_to_all | solution.py:178
  257.8 9.6 fusion
  274.5 10.1 fusion.36
  291.1 16.0 %multiply_convert_fusion.1 = (bf16[1024,1024]{1,0:T(8,128)(2,1)}, bf16[1024,1024]{1,0:T(8,128)(2,1)}, bf16[1024,1024]{1,0:T(8,128)(2,1)}) fusion(f32[1024,1024]{1,0:T(8,128)} %fusion.36, f32[1024,1024]{1,0:T(8,128)} %fusion.37, bf16[1024,2048]{1,0:T(8,128)(2,1)} %param.22, f32[1024,2048]{1,0:T(8,128)} %fusion), kind=kOutput, calls=%fused_computation.12 | convolution fusion | flops 4315938816 | bytes 27262976 | tf_op jit(solution)/shard_map/dot_general | solution.py:27
  324.1 9.5 convolution_convert_fusion.4
  338.2 9.5 convolution_convert_fusion.3
  347.7 56.4 %all-to-all-done.4 = bf16[8,256,1024]{2,1,0:T(8,128)(2,1)} async-done(((bf16[8,256,1024]{2,1,0:T(8,128)(2,1)}), bf16[8,256,1024]{2,1,0:T(8,128)(2,1)}, u32[]{:S(2)}, u32[]{:S(2)}) %all-to-all-start.4) | async-done | bytes 4194336 | tf_op jit(solution)/shard_map/all_to_all | solution.py:178
  413.4 10.6 convolution_convert_fusion.2
  432.6 40.4 %all-to-all-done.5 = bf16[8,256,1024]{2,1,0:T(8,128)(2,1)} async-done(((bf16[8,256,1024]{2,1,0:T(8,128)(2,1)}), bf16[8,256,1024]{2,1,0:T(8,128)(2,1)}, u32[]{:S(2)}, u32[]{:S(2)}) %all-to-all-start.5) | async-done | bytes 4194336 | tf_op jit(solution)/shard_map/all_to_all | solution.py:178
  476.5 42.0 %collective-permute-done.12 = bf16[1024,2048]{1,0:T(8,128)(2,1)} collective-permute-done((bf16[1024,2048]{1,0:T(8,128)(2,1)}, bf16[1024,2048]{1,0:T(8,128)(2,1)}, u32[]{:S(2)}, u32[]{:S(2)}) %collective-permute-start.12) | collective-permute-done | bytes 4194336 | tf_op jit(solution)/shard_map/ppermute | solution.py:186
  528.9 79.6 %collective-permute-done.6 = bf16[8,256,1024]{2,1,0:T(8,128)(2,1)} collective-permute-done((bf16[8,256,1024]{2,1,0:T(8,128)(2,1)}, bf16[8,256,1024]{2,1,0:T(8,128)(2,1)}, u32[]{:S(2)}, u32[]{:S(2)}) %collective-permute-start.6) | collective-permute-done | bytes 4194336 | tf_op jit(solution)/shard_map/ppermute | solution.py:186
  618.9 78.8 %collective-permute-done.9 = bf16[8,256,1024]{2,1,0:T(8,128)(2,1)S(1)} collective-permute-done((bf16[8,256,1024]{2,1,0:T(8,128)(2,1)}, bf16[8,256,1024]{2,1,0:T(8,128)(2,1)S(1)}, u32[]{:S(2)}, u32[]{:S(2)}) %collective-permute-start.9) | collective-permute-done | bytes 4194336 | tf_op jit(solution)/shard_map/ppermute | solution.py:186
  711.9 13.6 %attention_backward.1 = (f32[1024,256]{1,0:T(8,128)S(1)}, f32[1024,64]{1,0:T(8,128)S(1)}, f32[1024,64]{1,0:T(8,128)S(1)}) custom-call(bf16[1024,256]{1,0:T(8,128)(2,1)S(1)} %add_convert_fusion.12.q_ref, bf16[1024,64]{1,0:T(8,128)(2,1)S(1)} %add_convert_fusion.13.k_ref, bf16[1024,64]{1,0:T(8,128)(2,1)S(1)} %copy-done.8, ...), custom_call_target="tpu_custom_call" | custom-call | flops 1342177280 | bytes 2621440 | tf_op jit(solution)/shard_map/attention_backward/pallas_call | solution.py:154
  787.6 30.1 %collective-permute-start.3 = (bf16[256,2048]{1,0:T(8,128)(2,1)S(1)}, bf16[256,2048]{1,0:T(8,128)(2,1)}, u32[]{:S(2)}, u32[]{:S(2)}) collective-permute-start(bf16[256,2048]{1,0:T(8,128)(2,1)S(1)} %convolution_convert_fusion.6), channel_id=1, source_target_pairs={{0,8},{24,16},{1,9},{25,17},{2,10},{26,18},{3,11},{27,19},{4,12},{... | collective-permute-start | bytes 3145736 | tf_op jit(solution)/shard_map/ppermute | solution.py:186
  820.2 12.6 %add_convert_fusion.7 = bf16[1024,2048]{1,0:T(8,128)(2,1)} fusion(f32[1024,2048]{1,0:T(8,128)} %fusion.18, bf16[1024,2048]{1,0:T(8,128)(2,1)} %param.22, bf16[1024,1024]{1,0:T(8,128)(2,1)} %get-tuple-element.58, s32[1024]{0:T(1024)S(1)} %bitcast.120), kind=kOutput, calls=%fused_computation.10 | convolution fusion | flops 6450839552 | bytes 18878464 | tf_op jit(solution)/shard_map/dot_general | solution.py:23
  844.1 26.7 %collective-permute-done = bf16[8,256,384]{1,2,0:T(8,128)(2,1)} collective-permute-done((bf16[8,256,384]{1,2,0:T(8,128)(2,1)}, bf16[8,256,384]{1,2,0:T(8,128)(2,1)}, u32[]{:S(2)}, u32[]{:S(2)}) %collective-permute-start) | collective-permute-done | bytes 1572896 | tf_op jit(solution)/shard_map/ppermute | solution.py:186
  889.0 53.3 %collective-permute-done.8 = bf16[8,256,1024]{2,1,0:T(8,128)(2,1)} collective-permute-done((bf16[8,256,1024]{2,1,0:T(8,128)(2,1)}, bf16[8,256,1024]{2,1,0:T(8,128)(2,1)}, u32[]{:S(2)}, u32[]{:S(2)}) %collective-permute-start.8) | collective-permute-done | bytes 4194336 | tf_op jit(solution)/shard_map/ppermute | solution.py:194
  949.3 82.9 %collective-permute-done.11 = bf16[8,256,1024]{2,1,0:T(8,128)(2,1)} collective-permute-done((bf16[8,256,1024]{2,1,0:T(8,128)(2,1)}, bf16[8,256,1024]{2,1,0:T(8,128)(2,1)}, u32[]{:S(2)}, u32[]{:S(2)}) %collective-permute-start.11) | collective-permute-done | bytes 4194336 | tf_op jit(solution)/shard_map/ppermute | solution.py:194
  1039.2 15.4 %collective-permute-done.5 = bf16[256,2048]{1,0:T(8,128)(2,1)S(1)} collective-permute-done((bf16[256,2048]{1,0:T(8,128)(2,1)S(1)}, bf16[256,2048]{1,0:T(8,128)(2,1)S(1)}, u32[]{:S(2)}, u32[]{:S(2)}) %collective-permute-start.5) | collective-permute-done | bytes 1048608 | tf_op jit(solution)/shard_map/ppermute | solution.py:194
  1056.0 30.6 %collective-permute-done.2 = bf16[8,256,384]{1,2,0:T(8,128)(2,1)S(1)} collective-permute-done((bf16[8,256,384]{1,2,0:T(8,128)(2,1)S(1)}, bf16[8,256,384]{1,2,0:T(8,128)(2,1)S(1)}, u32[]{:S(2)}, u32[]{:S(2)}) %collective-permute-start.2) | collective-permute-done | bytes 1572896 | tf_op jit(solution)/shard_map/ppermute | solution.py:194
  1098.9 38.4 %all-reduce = (f32[2048]{0:T(1024)}, f32[2048]{0:T(1024)}) all-reduce(f32[2048]{0:T(1024)S(1)} %get-tuple-element.52, f32[2048]{0:T(1024)S(1)} %get-tuple-element.50), channel_id=1, replica_groups=mesh['rep'=4,'shard'=8] {'rep','shard'}, use_global_device_ids=true, to_apply=%region_12.13 | all-reduce | flops 4096 | bytes 32768 | tf_op jit(solution)/shard_map/psum | solution.py:314
  (221 shorter events, 307.2 us)
Async XLA Ops:
  7.2 57.4 %all-gather.5.cloned.1.call-start = ((), (), s32[]{:S(2)}) async-start(), calls=%async_computation.10 | async-start | bytes 4718592 | tf_op jit(solution)/shard_map/all_gather | solution.py:170
  21.2 153.0 %reduce-scatter.5.cloned.1.call-start = ((), (), s32[]{:S(2)}) async-start(), calls=%async_computation.11 | async-start | bytes 4718592 | tf_op jit(solution)/shard_map/reduce_scatter | solution.py:174
  95.3 162.5 %all-gather.9.cloned.1.call-start = ((), (), s32[]{:S(2)}) async-start(), calls=%async_computation.14 | async-start | bytes 4718592 | tf_op jit(solution)/shard_map/all_gather | solution.py:170
  102.5 81.9 %all-to-all-start.1 = ((bf16[8,256,1024]{1,2,0:T(8,128)(2,1)}), bf16[8,256,1024]{1,2,0:T(8,128)(2,1)}, u32[]{:S(2)}, u32[]{:S(2)}) async-start(bf16[8,256,1024]{1,2,0:T(8,128)(2,1)} %bitcast.89), calls=%async_computation.2 | async-start | bytes 8388608 | tf_op jit(solution)/shard_map/all_to_all | solution.py:178
  107.3 167.3 %all-gather.7.cloned.1.call-start = ((), (), s32[]{:S(2)}) async-start(), calls=%async_computation.12 | async-start | bytes 4718592 | tf_op jit(solution)/shard_map/all_gather | solution.py:170
  184.4 67.0 %all-to-all-start.2 = ((bf16[8,256,1024]{1,2,0:T(8,128)(2,1)}), bf16[8,256,1024]{1,2,0:T(8,128)(2,1)}, u32[]{:S(2)}, u32[]{:S(2)}) async-start(bf16[8,256,1024]{1,2,0:T(8,128)(2,1)} %bitcast.90), calls=%async_computation.3 | async-start | bytes 8388608 | tf_op jit(solution)/shard_map/all_to_all | solution.py:178
  189.0 219.9 %reduce-scatter.9.cloned.1.call-start = ((), (), s32[]{:S(2)}) async-start(), calls=%async_computation.15 | async-start | bytes 4718592 | tf_op jit(solution)/shard_map/reduce_scatter | solution.py:174
  333.5 70.6 %all-to-all-start.4 = ((bf16[8,256,1024]{2,1,0:T(8,128)(2,1)}), bf16[8,256,1024]{2,1,0:T(8,128)(2,1)}, u32[]{:S(2)}, u32[]{:S(2)}) async-start(bf16[8,256,1024]{2,1,0:T(8,128)(2,1)} %bitcast.102), calls=%async_computation.8 | async-start | bytes 8388608 | tf_op jit(solution)/shard_map/all_to_all | solution.py:178
  404.1 68.8 %all-to-all-start.5 = ((bf16[8,256,1024]{2,1,0:T(8,128)(2,1)}), bf16[8,256,1024]{2,1,0:T(8,128)(2,1)}, u32[]{:S(2)}, u32[]{:S(2)}) async-start(bf16[8,256,1024]{2,1,0:T(8,128)(2,1)} %bitcast.97), calls=%async_computation.9 | async-start | bytes 8388608 | tf_op jit(solution)/shard_map/all_to_all | solution.py:178
  408.8 297.6 %all-gather.11.cloned.1.call-start = ((), (), s32[]{:S(2)}) async-start(), calls=%async_computation.16 | async-start | bytes 4718592 | tf_op jit(solution)/shard_map/all_gather | solution.py:170
  413.1 684.2 %reduce-scatter.11.cloned.1.call-start = ((), (), s32[]{:S(2)}) async-start(), calls=%async_computation.17 | async-start | bytes 4718592 | tf_op jit(solution)/shard_map/reduce_scatter | solution.py:174
  424.0 94.5 %collective-permute-start.12 = (bf16[1024,2048]{1,0:T(8,128)(2,1)}, bf16[1024,2048]{1,0:T(8,128)(2,1)}, u32[]{:S(2)}, u32[]{:S(2)}) collective-permute-start(bf16[1024,2048]{1,0:T(8,128)(2,1)} %convolution_convert_fusion.2), channel_id=1, source_target_pairs={{0,8},{24,16},{1,9},{25,17},{2,10},{26,18},{3,11},{27,19},{4,12},{... | collective-permute-start | bytes 12582920 | tf_op jit(solution)/shard_map/ppermute | solution.py:186
  429.3 179.1 %collective-permute-start.6 = (bf16[8,256,1024]{2,1,0:T(8,128)(2,1)}, bf16[8,256,1024]{2,1,0:T(8,128)(2,1)}, u32[]{:S(2)}, u32[]{:S(2)}) collective-permute-start(bf16[8,256,1024]{2,1,0:T(8,128)(2,1)} %all-to-all-done.4), channel_id=1, source_target_pairs={{0,8},{24,16},{1,9},{25,17},{2,10},{26,18},{3,11},{27,19},{4,12},{... | collective-permute-start | bytes 12582920 | tf_op jit(solution)/shard_map/ppermute | solution.py:186
  473.0 224.7 %collective-permute-start.9 = (bf16[8,256,1024]{2,1,0:T(8,128)(2,1)}, bf16[8,256,1024]{2,1,0:T(8,128)(2,1)S(1)}, u32[]{:S(2)}, u32[]{:S(2)}) collective-permute-start(bf16[8,256,1024]{2,1,0:T(8,128)(2,1)} %all-to-all-done.5), channel_id=1, source_target_pairs={{0,8},{24,16},{1,9},{25,17},{2,10},{26,18},{3,11},{27,19},{4,12},{... | collective-permute-start | bytes 12582920 | tf_op jit(solution)/shard_map/ppermute | solution.py:186
  526.3 221.3 %collective-permute-start.13 = (bf16[1024,2048]{1,0:T(8,128)(2,1)}, bf16[1024,2048]{1,0:T(8,128)(2,1)}, u32[]{:S(2)}, u32[]{:S(2)}) collective-permute-start(bf16[1024,2048]{1,0:T(8,128)(2,1)} %add_convert_fusion.1), channel_id=1, source_target_pairs={{8,16},{16,8},{9,17},{17,9},{10,18},{18,10},{11,19},{19,11},{12,20... | collective-permute-start | bytes 12582920 | tf_op jit(solution)/shard_map/ppermute | solution.py:190
  616.2 151.7 %collective-permute-start.7 = (bf16[8,256,1024]{2,1,0:T(8,128)(2,1)}, bf16[8,256,1024]{2,1,0:T(8,128)(2,1)}, u32[]{:S(2)}, u32[]{:S(2)}) collective-permute-start(bf16[8,256,1024]{2,1,0:T(8,128)(2,1)} %add_convert_fusion.5), channel_id=1, source_target_pairs={{8,16},{16,8},{9,17},{17,9},{10,18},{18,10},{11,19},{19,11},{12,20... | collective-permute-start | bytes 12582920 | tf_op jit(solution)/shard_map/ppermute | solution.py:190
  703.4 73.8 %collective-permute-start.10 = (bf16[8,256,1024]{2,1,0:T(8,128)(2,1)}, bf16[8,256,1024]{2,1,0:T(8,128)(2,1)}, u32[]{:S(2)}, u32[]{:S(2)}) collective-permute-start(bf16[8,256,1024]{2,1,0:T(8,128)(2,1)} %add_convert_fusion.3), channel_id=1, source_target_pairs={{8,16},{16,8},{9,17},{17,9},{10,18},{18,10},{11,19},{19,11},{12,20... | collective-permute-start | bytes 12582920 | tf_op jit(solution)/shard_map/ppermute | solution.py:190
  755.8 120.3 %collective-permute-start.14 = (bf16[1024,2048]{1,0:T(8,128)(2,1)}, bf16[1024,2048]{1,0:T(8,128)(2,1)}, u32[]{:S(2)}, u32[]{:S(2)}) collective-permute-start(bf16[1024,2048]{1,0:T(8,128)(2,1)} %add_convert_fusion), channel_id=1, source_target_pairs={{8,0},{16,24},{9,1},{17,25},{10,2},{18,26},{11,3},{19,27},{12,4},{... | collective-permute-start | bytes 12582920 | tf_op jit(solution)/shard_map/ppermute | solution.py:194
  763.3 54.4 %all-to-all-start.3 = ((bf16[8,256,384]{1,2,0:T(8,128)(2,1)}), bf16[8,256,384]{1,2,0:T(8,128)(2,1)}, u32[]{:S(2)}, u32[]{:S(2)}) async-start(bf16[8,256,384]{1,2,0:T(8,128)(2,1)} %copy.121), calls=%async_computation.7 | async-start | bytes 3145728 | tf_op jit(solution)/shard_map/all_to_all | solution.py:178
  767.6 372.8 %reduce-scatter.7.cloned.1.call-start = ((), (), s32[]{:S(2)}) async-start(), calls=%async_computation.13 | async-start | bytes 4718592 | tf_op jit(solution)/shard_map/reduce_scatter | solution.py:174
  775.7 166.6 %collective-permute-start.8 = (bf16[8,256,1024]{2,1,0:T(8,128)(2,1)}, bf16[8,256,1024]{2,1,0:T(8,128)(2,1)}, u32[]{:S(2)}, u32[]{:S(2)}) collective-permute-start(bf16[8,256,1024]{2,1,0:T(8,128)(2,1)} %add_convert_fusion.4), channel_id=1, source_target_pairs={{8,0},{16,24},{9,1},{17,25},{10,2},{18,26},{11,3},{19,27},{12,4},{... | collective-permute-start | bytes 12582920 | tf_op jit(solution)/shard_map/ppermute | solution.py:194
  785.0 247.2 %collective-permute-start.11 = (bf16[8,256,1024]{2,1,0:T(8,128)(2,1)}, bf16[8,256,1024]{2,1,0:T(8,128)(2,1)}, u32[]{:S(2)}, u32[]{:S(2)}) collective-permute-start(bf16[8,256,1024]{2,1,0:T(8,128)(2,1)} %add_convert_fusion.2), channel_id=1, source_target_pairs={{8,0},{16,24},{9,1},{17,25},{10,2},{18,26},{11,3},{19,27},{12,4},{... | collective-permute-start | bytes 12582920 | tf_op jit(solution)/shard_map/ppermute | solution.py:194
  883.9 170.6 %collective-permute-start.5 = (bf16[256,2048]{1,0:T(8,128)(2,1)S(1)}, bf16[256,2048]{1,0:T(8,128)(2,1)S(1)}, u32[]{:S(2)}, u32[]{:S(2)}) collective-permute-start(bf16[256,2048]{1,0:T(8,128)(2,1)S(1)} %add_convert_fusion.10), channel_id=1, source_target_pairs={{8,0},{16,24},{9,1},{17,25},{10,2},{18,26},{11,3},{19,27},{12,4},{... | collective-permute-start | bytes 3145736 | tf_op jit(solution)/shard_map/ppermute | solution.py:194
  887.5 199.1 %collective-permute-start.2 = (bf16[8,256,384]{1,2,0:T(8,128)(2,1)S(1)}, bf16[8,256,384]{1,2,0:T(8,128)(2,1)S(1)}, u32[]{:S(2)}, u32[]{:S(2)}) collective-permute-start(bf16[8,256,384]{1,2,0:T(8,128)(2,1)S(1)} %add_convert_fusion.8), channel_id=1, source_target_pairs={{8,0},{16,24},{9,1},{17,25},{10,2},{18,26},{11,3},{19,27},{12,4},{... | collective-permute-start | bytes 4718600 | tf_op jit(solution)/shard_map/ppermute | solution.py:194
  (44 other events, 848.4 us)
Sparse Core Ops, SparseCore 0:
  11.2 53.3 all-gather.4
  95.4 78.8 reduce-scatter.4
  176.3 58.3 all-gather.8
  237.2 37.2 all-gather.6
  324.2 79.5 reduce-scatter.8
  413.3 63.1 all-gather.10
  741.8 69.0 reduce-scatter.10
  833.0 51.2 reduce-scatter.6

commit v2 on v1

--- a/solution.py
+++ b/solution.py
@@ -196,6 +196,295 @@
     return x
 
 
+MESH = pl.DeviceIdType.MESH
+
+
+def flip(index, bits):
+    for weight in (1, 2, 4):
+        if bits & weight:
+            index = index + weight - 2 * weight * lax.rem(lax.div(index, weight), 2)
+    return index
+
+
+def send(src, dst, sems, k, target):
+    return pltpu.make_async_remote_copy(
+        src_ref=src,
+        dst_ref=dst,
+        send_sem=sems.at[0, k],
+        recv_sem=sems.at[1, k],
+        device_id={"shard": target},
+        device_id_type=MESH,
+    )
+
+
+def greet(me, masks):
+    barrier = pltpu.get_barrier_semaphore()
+    for mask in masks:
+        pl.semaphore_signal(
+            barrier, inc=1, device_id={"shard": flip(me, mask)}, device_id_type=MESH
+        )
+    pl.semaphore_wait(barrier, len(masks))
+
+
+GATHER_SEMS = 13
+
+
+def gather_blocks(me, out, sems):
+    core, px, py, diag = (flip(me, mask) for mask in (1, 2, 4, 6))
+    half = out.shape[1] // 2
+    low, high, whole = pl.ds(0, half), pl.ds(half, half), pl.ds(0, 2 * half)
+
+    def move(k, block, rows, target):
+        ref = out.at[block, rows]
+        copy = send(ref, ref, sems, k, target)
+        copy.start()
+        return copy
+
+    x_low, y_high = move(0, me, low, px), move(1, me, high, py)
+    own = move(2, me, whole, core)
+    x_high, y_low = move(3, me, high, px), move(4, me, low, py)
+    x_low.wait_recv()
+    diag_low = move(5, px, low, py)
+    pieces = [own, move(6, px, low, core)]
+    y_high.wait_recv()
+    diag_high = move(7, py, high, px)
+    pieces.append(move(8, py, high, core))
+    x_high.wait_recv()
+    pieces.append(move(9, px, high, core))
+    y_low.wait_recv()
+    pieces.append(move(10, py, low, core))
+    diag_low.wait_recv()
+    pieces.append(move(11, diag, low, core))
+    diag_high.wait_recv()
+    pieces.append(move(12, diag, high, core))
+    for copy in pieces:
+        copy.wait_recv()
+    for copy in [x_low, y_high, x_high, y_low, diag_low, diag_high] + pieces:
+        copy.wait_send()
+
+
+SCATTER_SEMS = 10
+
+
+def scatter_blocks(me, partial, sib_out, sib_in, acc, x_out, x_in, y_out, y_in, sems):
+    core, px, py = (flip(me, mask) for mask in (1, 2, 4))
+    half = acc.shape[1] // 2
+    masks = (6, 2, 4, 0)
+    low, high = pl.ds(0, half), pl.ds(half, half)
+    copies = []
+
+    def move(src, dst, k, target):
+        copy = send(src, dst, sems, k, target)
+        copy.start()
+        copies.append(copy)
+        return copy
+
+    inside = []
+    for i, mask in enumerate(masks):
+        sib_out[i] = partial(flip(core, mask)).astype(BF16)
+        inside.append(move(sib_out.at[i], sib_in.at[i], i, core))
+    for i, mask in enumerate(masks):
+        term = partial(flip(me, mask))
+        inside[i].wait_recv()
+        acc[i] = term + sib_in[i].astype(F32)
+        if mask == 6:
+            x_out[0] = acc[i, low].astype(BF16)
+            x_diag = move(x_out.at[0], x_in.at[0], 4, px)
+            y_out[0] = acc[i, high].astype(BF16)
+            y_diag = move(y_out.at[0], y_in.at[0], 5, py)
+        if mask == 2:
+            x_out[1] = acc[i, low].astype(BF16)
+            x_near = move(x_out.at[1], x_in.at[1], 6, px)
+        if mask == 4:
+            y_out[1] = acc[i, high].astype(BF16)
+            y_near = move(y_out.at[1], y_in.at[1], 7, py)
+    x_diag.wait_recv()
+    y_out[2] = (acc[2, low] + x_in[0].astype(F32)).astype(BF16)
+    y_last = move(y_out.at[2], y_in.at[2], 8, py)
+    y_diag.wait_recv()
+    x_out[2] = (acc[1, high] + y_in[0].astype(F32)).astype(BF16)
+    x_last = move(x_out.at[2], x_in.at[2], 9, px)
+    x_near.wait_recv()
+    y_near.wait_recv()
+    y_last.wait_recv()
+    acc[3, low] = acc[3, low] + x_in[1].astype(F32) + y_in[2].astype(F32)
+    x_last.wait_recv()
+    acc[3, high] = acc[3, high] + y_in[1].astype(F32) + x_in[2].astype(F32)
+    for copy in copies:
+        copy.wait_send()
+    return acc[3]
+
+
+def scatter_scratch(rows, width):
+    half = rows // 2
+    return [
+        pltpu.VMEM((4, rows, width), BF16),
+        pltpu.VMEM((4, rows, width), BF16),
+        pltpu.VMEM((4, rows, width), F32),
+        pltpu.VMEM((3, half, width), BF16),
+        pltpu.VMEM((3, half, width), BF16),
+        pltpu.VMEM((3, half, width), BF16),
+        pltpu.VMEM((3, half, width), BF16),
+        pltpu.SemaphoreType.DMA((2, SCATTER_SEMS)),
+    ]
+
+
+VMEM = pl.BlockSpec(memory_space=pltpu.VMEM)
+
+
+def comm_params(collective_id, mebibytes):
+    return pltpu.CompilerParams(
+        collective_id=collective_id, has_side_effects=True, vmem_limit_bytes=mebibytes << 20
+    )
+
+
+def norm_gather(x, gain, normalise, collective_id):
+    rows, width = x.shape
+
+    def kernel(x_ref, gain_ref, out, sems):
+        me = lax.axis_index("shard")
+        block = x_ref[...]
+        if normalise:
+            block = rms_scale(block.astype(F32), gain_ref[...]).astype(BF16)
+        out[me] = block
+        greet(me, (1, 2, 4))
+        gather_blocks(me, out, sems)
+
+    return pl.pallas_call(
+        kernel,
+        out_shape=jax.ShapeDtypeStruct((8, rows, width), BF16),
+        in_specs=[VMEM, VMEM],
+        out_specs=VMEM,
+        scratch_shapes=[pltpu.SemaphoreType.DMA((2, GATHER_SEMS))],
+        compiler_params=comm_params(collective_id, 20),
+        cost_estimate=pl.CostEstimate(
+            flops=8 * rows * width, bytes_accessed=18 * rows * width, transcendentals=rows
+        ),
+        name="gather_kernel",
+    )(x, gain[None, :]).reshape(8 * rows, width)
+
+
+def branch_middle_gather(attention, weight, hidden, gain, collective_id):
+    rows, width = hidden.shape
+
+    def kernel(a_ref, w_ref, h_ref, gain_ref, mid, out, *scratch):
+        me = lax.axis_index("shard")
+        *buffers, scatter_sems, sems = scratch
+        greet(me, (1, 2, 4))
+
+        def partial(d):
+            return jnp.dot(
+                a_ref[pl.ds(pl.multiple_of(d * rows, rows), rows), :],
+                w_ref[...],
+                preferred_element_type=F32,
+            )
+
+        branch = scatter_blocks(me, partial, *buffers, scatter_sems)
+        middle = h_ref[...].astype(F32) + RESIDUAL_SCALE * branch
+        mid[...] = middle
+        out[me] = rms_scale(middle, gain_ref[...]).astype(BF16)
+        gather_blocks(me, out, sems)
+
+    return pl.pallas_call(
+        kernel,
+        out_shape=(
+            jax.ShapeDtypeStruct((rows, width), F32),
+            jax.ShapeDtypeStruct((8, rows, width), BF16),
+        ),
+        in_specs=[VMEM] * 4,
+        out_specs=[VMEM] * 2,
+        scratch_shapes=scatter_scratch(rows, width)
+        + [pltpu.SemaphoreType.DMA((2, GATHER_SEMS))],
+        compiler_params=comm_params(collective_id, 40),
+        cost_estimate=pl.CostEstimate(
+            flops=2 * 8 * rows * width * weight.shape[0], bytes_accessed=40 * rows * width, transcendentals=rows
+        ),
+        name="branch_middle_gather",
+    )(attention, weight, hidden, gain[None, :])
+
+
+def norm_pull(x, gain, grad):
+    scale = lax.rsqrt(jnp.mean(x * x, axis=-1, keepdims=True) + EPSILON)
+    pulled = gain * grad
+    rows_part = scale * pulled - x * (
+        scale * scale * scale * jnp.mean(pulled * x, axis=-1, keepdims=True)
+    )
+    return rows_part, jnp.sum(grad * x * scale, axis=0, keepdims=True)
+
+
+def pull_gather(part, middle, gain, out_grad, collective_id):
+    rows, width = middle.shape
+
+    def kernel(p_ref, m_ref, gain_ref, g_ref, mg_ref, gain_part, out, *scratch):
+        me = lax.axis_index("shard")
+        *buffers, scatter_sems, sems = scratch
+        greet(me, (1, 2, 4))
+        grad = scatter_blocks(
+            me,
+            lambda d: p_ref[pl.ds(pl.multiple_of(d * rows, rows), rows), :].astype(F32),
+            *buffers,
+            scatter_sems,
+        )
+        rows_part, gain_row = norm_pull(m_ref[...], gain_ref[...], grad)
+        gain_part[...] = gain_row
+        middle_grad = g_ref[...] + rows_part
+        mg_ref[...] = middle_grad
+        out[me] = (RESIDUAL_SCALE * middle_grad).astype(BF16)
+        gather_blocks(me, out, sems)
+
+    return pl.pallas_call(
+        kernel,
+        out_shape=(
+            jax.ShapeDtypeStruct((rows, width), F32),
+            jax.ShapeDtypeStruct((1, width), F32),
+            jax.ShapeDtypeStruct((8, rows, width), BF16),
+        ),
+        in_specs=[VMEM] * 4,
+        out_specs=[VMEM] * 3,
+        scratch_shapes=scatter_scratch(rows, width)
+        + [pltpu.SemaphoreType.DMA((2, GATHER_SEMS))],
+        compiler_params=comm_params(collective_id, 44),
+        cost_estimate=pl.CostEstimate(
+            flops=40 * rows * width, bytes_accessed=50 * rows * width, transcendentals=rows
+        ),
+        name="pull_gather",
+    )(part, middle, gain[None, :], out_grad)
+
+
+def pull_tokens(part, hidden, gain, middle_grad, collective_id):
+    rows, width = middle_grad.shape
+
+    def kernel(p_ref, h_ref, gain_ref, mg_ref, out, gain_part, *scratch):
+        me = lax.axis_index("shard")
+        *buffers, scatter_sems = scratch
+        greet(me, (1, 2, 4))
+        grad = scatter_blocks(
+            me,
+            lambda d: p_ref[pl.ds(pl.multiple_of(d * rows, rows), rows), :].astype(F32),
+            *buffers,
+            scatter_sems,
+        )
+        rows_part, gain_row = norm_pull(h_ref[...].astype(F32), gain_ref[...], grad)
+        gain_part[...] = gain_row
+        out[...] = mg_ref[...] + rows_part
+
+    return pl.pallas_call(
+        kernel,
+        out_shape=(
+            jax.ShapeDtypeStruct((rows, width), F32),
+            jax.ShapeDtypeStruct((1, width), F32),
+        ),
+        in_specs=[VMEM] * 4,
+        out_specs=[VMEM] * 2,
+        scratch_shapes=scatter_scratch(rows, width),
+        compiler_params=comm_params(collective_id, 40),
+        cost_estimate=pl.CostEstimate(
+            flops=40 * rows * width, bytes_accessed=50 * rows * width, transcendentals=rows
+        ),
+        name="pull_tokens",
+    )(part, hidden, gain[None, :], middle_grad)
+
+
 def per_device(
     tokens,
     attn_gain,
@@ -235,8 +524,10 @@
         blocks = weight.reshape(rows, KV_HEADS, HEAD).transpose(1, 0, 2)
         return jnp.repeat(blocks, copies, axis=0)
 
-    hidden = tokens.astype(F32)
-    normed = gather_rows(rms_scale(hidden, attn_gain).astype(BF16))
+    fast = n == 8
+
+    spread_cotangent = lax.all_gather(cotangent, ("rep", "shard"), axis=0, tiled=True)
+    all_dealing = lax.all_gather(dealing, "rep", axis=0, tiled=True)
     qkv = exchange(
         jnp.concatenate(
             [column_blocks(query_weight, q_cols), head_blocks(key_weight), head_blocks(value_weight)],
@@ -245,32 +536,63 @@
     ).reshape(width, q_cols + 2 * HEAD)
     gate_cols = exchange(column_blocks(gate_weight, ff_cols)).reshape(width, ff_cols)
     up_cols = exchange(column_blocks(up_weight, ff_cols)).reshape(width, ff_cols)
-    spread_cotangent = gather_rows(cotangent)
-
+
+    if fast:
+        normed = norm_gather(tokens, attn_gain, True, 0)
+    else:
+        normed = gather_rows(rms_scale(tokens.astype(F32), attn_gain).astype(BF16))
     pre = mm(normed, qkv)
     queries = rotate(pre[:, :q_cols], cos_q, sin_q).astype(BF16)
     keys = rotate(pre[:, q_cols : q_cols + HEAD], cos_k, sin_k).astype(BF16)
     values = pre[:, q_cols + HEAD :].astype(BF16)
     attention = attention_forward(queries, keys, values, seg_col, seg_row)
-    branch = scatter_rows(mm(attention, output_weight).astype(BF16))
-    middle = hidden + RESIDUAL_SCALE * branch.astype(F32)
-    normed_ffn = gather_rows(rms_scale(middle, ffn_gain).astype(BF16))
-
-    out_grad_all = t_mm(dealt, spread_cotangent)
-    down_grad = (RESIDUAL_SCALE * out_grad_all).astype(BF16)
-    out_grad = lax.dynamic_slice_in_dim(out_grad_all, own, local)
-    act_grad = mm_t(down_grad, down_weight)
-
-    gate = mm(normed_ffn, gate_cols)
-    up = mm(normed_ffn, up_cols)
-    sigmoid = jax.nn.sigmoid(gate)
-    activated = (gate * sigmoid * up).astype(BF16)
-    gate_grad = (act_grad * up * sigmoid * (1.0 + gate * (1.0 - sigmoid))).astype(BF16)
-    up_grad = (act_grad * gate * sigmoid).astype(BF16)
-
-    down_part = rep_sum(t_mm(activated, down_grad).astype(BF16))
-    gate_part = rep_sum(exchange(t_mm(normed_ffn, gate_grad).astype(BF16).reshape(n, rows, ff_cols)))
-    up_part = rep_sum(exchange(t_mm(normed_ffn, up_grad).astype(BF16).reshape(n, rows, ff_cols)))
+    if fast:
+        middle, normed_ffn = branch_middle_gather(attention, output_weight, tokens, ffn_gain, 1)
+        normed_ffn = normed_ffn.reshape(total, width)
+    else:
+        branch = scatter_rows(mm(attention, output_weight).astype(BF16))
+        middle = tokens.astype(F32) + RESIDUAL_SCALE * branch.astype(F32)
+        normed_ffn = gather_rows(rms_scale(middle, ffn_gain).astype(BF16))
+    own_normed = lax.dynamic_slice_in_dim(normed_ffn, own, local)
+    all_normed = lax.all_gather(own_normed, ("rep", "shard"), axis=0, tiled=True)
+
+    reps = lax.axis_size("rep")
+    group = lax.axis_index("rep")
+    deals = (all_dealing[:, :, None] == packed[None, None, :]).astype(BF16)
+    out_grad_all = lax.dot_general(
+        deals,
+        spread_cotangent.reshape(reps, total, width),
+        (((1,), (1,)), ((0,), (0,))),
+        preferred_element_type=F32,
+    ).reshape(reps * total, width)
+    down_grad_all = (RESIDUAL_SCALE * out_grad_all).astype(BF16)
+    out_grad = lax.dynamic_slice_in_dim(out_grad_all, group * total + own, local)
+    act_grad_all = mm_t(down_grad_all, down_weight)
+
+    def ffn(rows_in, act_grad):
+        gate = mm(rows_in, gate_cols)
+        up = mm(rows_in, up_cols)
+        sigmoid = jax.nn.sigmoid(gate)
+        activated = (gate * sigmoid * up).astype(BF16)
+        gate_grad = (act_grad * up * sigmoid * (1.0 + gate * (1.0 - sigmoid))).astype(BF16)
+        up_grad = (act_grad * gate * sigmoid).astype(BF16)
+        return activated, gate_grad, up_grad
+
+    activated, gate_grad, up_grad = ffn(
+        normed_ffn, lax.dynamic_slice_in_dim(act_grad_all, group * total, total)
+    )
+    normed_ffn_part = (mm_t(gate_grad, gate_cols) + mm_t(up_grad, up_cols)).astype(BF16)
+    if fast:
+        middle_grad, ffn_gain_part, branch_grad = pull_gather(
+            normed_ffn_part, middle, ffn_gain, out_grad, 2
+        )
+        branch_grad = branch_grad.reshape(total, width)
+    else:
+        middle_part, ffn_gain_part = norm_pull(
+            middle, ffn_gain, scatter_rows(normed_ffn_part).astype(F32)
+        )
+        middle_grad = out_grad + middle_part
+        branch_grad = gather_rows((RESIDUAL_SCALE * middle_grad).astype(BF16))
 
     own_columns = lax.dynamic_slice_in_dim(dealt, own, local, axis=1)
     layer_output = scatter_rows(
@@ -280,14 +602,6 @@
         ).astype(BF16)
     )
 
-    normed_ffn_grad = scatter_rows(
-        (mm_t(gate_grad, gate_cols) + mm_t(up_grad, up_cols)).astype(BF16)
-    ).astype(F32)
-    unused_norm, ffn_pull = jax.vjp(rms_scale, middle, ffn_gain)
-    middle_part, ffn_gain_part = ffn_pull(normed_ffn_grad)
-    middle_grad = out_grad + middle_part
-    branch_grad = gather_rows((RESIDUAL_SCALE * middle_grad).astype(BF16))
-    output_part = rep_sum(t_mm(attention, branch_grad).astype(BF16))
     attention_grad = mm_t(branch_grad, output_weight).astype(BF16)
     dq, dk, dv = attention_backward(queries, keys, values, attention_grad, seg_col, seg_row)
     pre_grad = jnp.concatenate(
@@ -298,11 +612,21 @@
         ],
         axis=1,
     )
+    normed_part = mm_t(pre_grad, qkv).astype(BF16)
+    if fast:
+        tokens_grad, attn_gain_part = pull_tokens(normed_part, tokens, attn_gain, middle_grad, 3)
+    else:
+        hidden_part, attn_gain_part = norm_pull(
+            tokens.astype(F32), attn_gain, scatter_rows(normed_part).astype(F32)
+        )
+        tokens_grad = middle_grad + hidden_part
+
+    activated, gate_grad, up_grad = ffn(all_normed, act_grad_all)
+    gate_part = exchange(t_mm(all_normed, gate_grad).astype(BF16).reshape(n, rows, ff_cols))
+    up_part = exchange(t_mm(all_normed, up_grad).astype(BF16).reshape(n, rows, ff_cols))
+    down_part = t_mm(activated, down_grad_all)
+    output_part = rep_sum(t_mm(attention, branch_grad).astype(BF16))
     qkv_part = rep_sum(exchange(t_mm(normed, pre_grad).astype(BF16).reshape(n, rows, q_cols + 2 * HEAD)))
-    normed_grad = scatter_rows(mm_t(pre_grad, qkv).astype(BF16)).astype(F32)
-    unused_first, attn_pull = jax.vjp(rms_scale, hidden, attn_gain)
-    hidden_part, attn_gain_part = attn_pull(normed_grad)
-    tokens_grad = middle_grad + hidden_part
 
     def join(blocks):
         return blocks.transpose(1, 0, 2).reshape(rows, -1).astype(F32)
@@ -311,19 +635,19 @@
         blocks = blocks.astype(F32).reshape(KV_HEADS, copies, rows, HEAD).sum(axis=1)
         return blocks.transpose(1, 0, 2).reshape(rows, KV_HEADS * HEAD)
 
-    attn_gain_grad, ffn_gain_grad = lax.psum((attn_gain_part, ffn_gain_part), ("rep", "shard"))
+    gain_grads = lax.psum(jnp.concatenate([attn_gain_part, ffn_gain_part]), ("rep", "shard"))
     return (
         layer_output,
         tokens_grad,
-        attn_gain_grad,
+        gain_grads[0],
         join(qkv_part[:, :, :q_cols]),
         join_heads(qkv_part[:, :, q_cols : q_cols + HEAD]),
         join_heads(qkv_part[:, :, q_cols + HEAD :]),
         output_part.astype(F32),
-        ffn_gain_grad,
+        gain_grads[1],
         join(gate_part),
         join(up_part),
-        down_part.astype(F32),
+        down_part,
     )
 
 

time: 1150 us -> 840 us (0.73)
  waiting for transfers between devices: 681 us -> 135 us
  Pallas kernels: 21.5 us -> 198 us
  matrix products: 127 us -> 271 us
  other arithmetic: 98.3 us -> 36.5 us
  starting transfers between devices: 92.4 us -> 45.5 us
  blocking collectives: 38.4 us -> 52.9 us
    ppermute x5 -> x2, waiting for transfers between devices: 235 us -> 0.01 us  [rep_sum(): lax.ppermute(x, 'rep', [(hop, hop + 1), (count - 1 - hop, count - 2 - hop)])]
    pallas_call x0 -> x4, Pallas kernels: none -> 177 us  [the longest x1 60.3 us: branch_middle_gather(): pl.pallas_call(kernel, out_shape=(jax.ShapeDtypeStruct((rows, width), F32...]
    ppermute x5 -> x2, waiting for transfers between devices: 182 us -> 17.8 us  [rep_sum(): moved = lax.ppermute(x, 'rep', [(near, near - 1), (far, far + 1)])]
    reduce_scatter x4 -> x1, waiting for transfers between devices: 67 us -> 0.01 us  [scatter_rows(): return lax.psum_scatter(x, 'shard', scatter_dimension=0, tiled=True)]
    all_to_all x6, waiting for transfers between devices: 175 us -> 117 us  [exchange(): lax.all_to_all(blocks, 'shard', split_axis=0, concat_axis=0, tiled=True)]
    dot_general x6 -> x5, matrix products: 44 us -> 102 us  [t_mm(): lax.dot_general(a, b, (((0,), (0,)), ((), ())), preferred_element_type=F32)]
    dot_general x6 -> x7, matrix products: 42 us -> 87.5 us  [mm(): return jnp.dot(a, b, preferred_element_type=F32)]
    convert_element_type x10 -> x4, other arithmetic: 54.5 us -> 10 us  [rep_sum(): x = (x.astype(F32) + moved.astype(F32)).astype(BF16)]
  transfers between devices with their start and end apart: 29 -> 15, of which waited for: 16 -> 5; matrix products, arithmetic and copies ran while one was open for 19% -> 45% of each run, Pallas kernels for 1% -> 24%
where the time goes in v2:
time: 840 us; the launch traced here: 835 us
  matrix products  271 us (32%)
  Pallas kernels  198 us (24%)
  waiting for transfers between devices  135 us (16%)
  local copies, waits for them, and re-layouts  78.3 us (9%)
  blocking collectives  52.9 us (6%)
  starting transfers between devices  45.5 us (5%)
  other arithmetic  36.5 us (4%)
  between operations  16.6 us (2%)
    all_to_all x6, waiting for transfers between devices, exchange(): lax.all_to_all(blocks, 'shard', split_axis=0, concat_axis=0, tiled=True)  117 us
    dot_general x5, matrix products, t_mm(): lax.dot_general(a, b, (((0,), (0,)), ((), ())), preferred_element_type=F32)  102 us
    dot_general x7, matrix products, mm(): return jnp.dot(a, b, preferred_element_type=F32)  87.5 us
    pallas_call x1, Pallas kernels, branch_middle_gather(): pl.pallas_call(kernel, out_shape=(jax.ShapeDtypeStruct((rows, width), F32...  60.3 us
    dot_general x5, matrix products, mm_t(): lax.dot_general(a, b, (((1,), (1,)), ((), ())), preferred_element_type=F32)  56.9 us
    pallas_call x1, Pallas kernels, pull_gather(): pl.pallas_call(kernel, out_shape=(jax.ShapeDtypeStruct((rows, width), F32...  45 us
    pallas_call x1, Pallas kernels, norm_gather(): pl.pallas_call(kernel, out_shape=jax.ShapeDtypeStruct((8, rows, width), B...  42.1 us
    psum x1, blocking collectives, per_device(): lax.psum(jnp.concatenate([attn_gain_part, ffn_gain_part]), ('rep', 'shard'))  39.7 us
  transfers between devices with their start and end apart: 15, of which 5 were waited for; matrix products, arithmetic and copies ran while one was open for 45% of the time, Pallas kernels for 24%

profile of v2, /device:TPU:0, one launch (start us, length us, event | category | flops | bytes accessed | tf_op | source)
XLA Modules:
  0.0 834.7 jit_solution(5964099554111486627)
XLA Ops:
  26.7 42.1 %gather_kernel.1 = bf16[8,128,2048]{2,1,0:T(8,128)(2,1)S(1)} custom-call(bf16[128,2048]{1,0:T(8,128)(2,1)S(1)} %copy-done.2, f32[1,2048]{1,0:T(1,128)S(1)} %bitcast.103), custom_call_target="tpu_custom_call" | custom-call | flops 2097152 | bytes 4718592 | tf_op jit(solution)/shard_map/gather_kernel/pallas_call | solution.py:353
  93.2 7.9 attention_forward.1.a_ref
  101.1 60.3 %branch_middle_gather.1 = (f32[128,2048]{1,0:T(8,128)S(1)}, bf16[8,128,2048]{2,1,0:T(8,128)(2,1)S(1)}) custom-call(bf16[1024,256]{1,0:T(8,128)(2,1)S(1)} %attention_forward.1.a_ref, bf16[256,2048]{1,0:T(8,128)(2,1)S(1)} %copy-done.20, bf16[128,2048]{1,0:T(8,128)(2,1)S(1)} %copy-done.2, f32[1,2048]{1,0:T(1,128)S(1)} %bitcast.105), custom_call_target="tpu_custom_call" | custom-call | flops 1073741824 | bytes 10485760 | tf_op jit(solution)/shard_map/branch_middle_gather/pallas_call | solution.py:388
  175.3 6.5 copy.145
  181.8 58.9 %all-to-all-done.1 = bf16[8,256,1024]{1,2,0:T(8,128)(2,1)} async-done(((bf16[8,256,1024]{1,2,0:T(8,128)(2,1)}), bf16[8,256,1024]{1,2,0:T(8,128)(2,1)}, u32[]{:S(2)}, u32[]{:S(2)}) %all-to-all-start.1) | async-done | bytes 4194336 | tf_op jit(solution)/shard_map/all_to_all | solution.py:178
  245.4 13.2 %all-gather = s32[4,1,1024]{2,1,0:T(1,128)S(1)} all-gather(s32[1,1,1024]{2,1,0:T(1,128)S(1)} %bitcast.143), channel_id=1, replica_groups=mesh['rep'=4,'shard'=8] {'rep'}, dimensions={0}, use_global_device_ids=true | all-gather | bytes 20480 | tf_op jit(solution)/shard_map/all_gather | solution.py:530
  270.4 54.0 %all-to-all-done.2 = bf16[8,256,1024]{1,2,0:T(8,128)(2,1)} async-done(((bf16[8,256,1024]{1,2,0:T(8,128)(2,1)}), bf16[8,256,1024]{1,2,0:T(8,128)(2,1)}, u32[]{:S(2)}, u32[]{:S(2)}) %all-to-all-start.2) | async-done | bytes 4194336 | tf_op jit(solution)/shard_map/all_to_all | solution.py:178
  324.5 6.5 copy.146
  331.0 10.5 %fusion.37 = f32[1024,1024]{1,0:T(8,128)} fusion(bf16[1024,2048]{1,0:T(8,128)(2,1)} %bitcast.98, bf16[2048,1024]{1,0:T(8,128)(2,1)} %bitcast.117), kind=kOutput, calls=%fused_computation.90 | convolution fusion | flops 4294967296 | bytes 12582912 | tf_op jit(solution)/shard_map/dot_general | solution.py:23
  347.5 15.9 %add_convert_fusion.1 = bf16[1024,2048]{1,0:T(8,128)(2,1)} fusion(f32[1024,2048]{1,0:T(8,128)} %fusion.12, bf16[1024,2048]{1,0:T(8,128)(2,1)} %param.22, f32[1024,1024]{1,0:T(8,128)} %fusion.38, f32[1024,1024]{1,0:T(8,128)} %fusion.37, s32[1024]{0:T(1024)S(1)} %bitcast.145), kind=kOutput, calls=%fused_computation.11 | convolution fusion | flops 6457131008 | bytes 25169920 | tf_op jit(solution)/shard_map/dot_general | solution.py:23
  363.4 25.0 %fusion = f32[4,1024,2048]{2,1,0:T(8,128)} fusion(bf16[4,1024,2048]{2,1,0:T(8,128)(2,1)} %bitcast.150, s32[4,1024]{1,0:T(4,128)S(1)} %bitcast.146), kind=kOutput, calls=%fused_computation.6 | convolution fusion | flops 17184063488 | bytes 50348032 | tf_op jit(solution)/shard_map/dot_general | solution.py:562
  388.4 26.5 %fusion.5 = f32[4096,1024]{1,0:T(8,128)} fusion(bf16[1024,2048]{1,0:T(8,128)(2,1)} %param.22, f32[4096,2048]{1,0:T(8,128)} %bitcast.140), kind=kOutput, calls=%fused_computation.15 | convolution fusion | flops 17196646400 | bytes 54525952 | tf_op jit(solution)/shard_map/dot_general | solution.py:27
  416.2 15.0 %fusion.10 = f32[1024,2048]{1,0:T(8,128)} fusion(bf16[2048,1024]{1,0:T(8,128)(2,1)} %bitcast.118, f32[1024,1024]{1,0:T(8,128)} %fusion.37, f32[1024,1024]{1,0:T(8,128)} %fusion.38, f32[4096,1024]{1,0:T(8,128)} %fusion.5, s32[]{:T(128)S(6)} %select_n.32), kind=kOutput, calls=%fused_computation.32 | convolution fusion | flops 4305453056 | bytes 25165828 | tf_op jit(solution)/shard_map/dot_general | solution.py:27
  431.2 10.3 %add_convert_fusion.p_ref = bf16[1024,2048]{1,0:T(8,128)(2,1)} fusion(f32[1024,2048]{1,0:T(8,128)} %fusion.10, bf16[2048,1024]{1,0:T(8,128)(2,1)S(1)} %bitcast.121, f32[1024,1024]{1,0:T(8,128)S(1)} %copy-done.40, f32[4096,1024]{1,0:T(8,128)} %fusion.5, s32[]{:T(128)S(6)} %select_n.32), kind=kOutput, calls=%fused_computation.9 | convolution fusion | flops 4305453056 | bytes 25165828 | tf_op jit(solution)/shard_map/dot_general | solution.py:27
  441.6 45.0 %pull_gather.1 = (f32[128,2048]{1,0:T(8,128)S(1)}, f32[1,2048]{1,0:T(1,128)S(1)}, bf16[8,128,2048]{2,1,0:T(8,128)(2,1)S(1)}) custom-call(bf16[1024,2048]{1,0:T(8,128)(2,1)} %add_convert_fusion.p_ref, f32[128,2048]{1,0:T(8,128)S(1)} %get-tuple-element.22.m_ref, f32[1,2048]{1,0:T(1,128)S(1)} %bitcast.106, f32[128,2048]{1,0:T(8,128)S(1)} %constant_dynamic-slice_fusion.1.g_ref), custom_call_target="tpu_custom_call" | custom-call | flops 10485760 | bytes 13107200 | tf_op jit(solution)/shard_map/pull_gather/pallas_call | solution.py:435
  490.2 13.6 %attention_backward.1 = (f32[1024,256]{1,0:T(8,128)S(1)}, f32[1024,64]{1,0:T(8,128)S(1)}, f32[1024,64]{1,0:T(8,128)S(1)}) custom-call(bf16[1024,256]{1,0:T(8,128)(2,1)S(1)} %copy-done.5, bf16[1024,64]{1,0:T(8,128)(2,1)S(1)} %copy-done.9, bf16[1024,64]{1,0:T(8,128)(2,1)S(1)} %copy-done.11, bf16[1024,256]{1,0:T(8,128)(2,1)S(1)} %convolution_convert_fusion.3.g_ref, ...), custom_call_target="tpu_custom_call" | custom-call | flops 1342177280 | bytes 2621440 | tf_op jit(solution)/shard_map/attention_backward/pallas_call | solution.py:154
  535.2 29.5 %pull_tokens.1 = (f32[128,2048]{1,0:T(8,128)S(1)}, f32[1,2048]{1,0:T(1,128)S(1)}) custom-call(bf16[1024,2048]{1,0:T(8,128)(2,1)S(1)} %convolution_convert_fusion.p_ref, bf16[128,2048]{1,0:T(8,128)(2,1)S(1)} %copy-done.3, f32[1,2048]{1,0:T(1,128)S(1)} %bitcast.104, f32[128,2048]{1,0:T(8,128)S(1)} %get-tuple-element.27.mg_ref), custom_call_target="tpu_custom_call" | custom-call | flops 10485760 | bytes 13107200 | tf_op jit(solution)/shard_map/pull_tokens/pallas_call | solution.py:471
  564.8 39.7 %psum.7 = f32[2,2048]{1,0:T(2,128)S(1)} all-reduce(f32[2,2048]{1,0:T(2,128)S(1)} %pad_maximum_fusion.10), channel_id=1, replica_groups=mesh['rep'=4,'shard'=8] {'rep','shard'}, use_global_device_ids=true, to_apply=%region_4.5 | all-reduce | flops 4096 | bytes 32768 | tf_op jit(solution)/shard_map/psum | solution.py:638
  609.5 23.4 %fusion.40 = f32[4096,1024]{1,0:T(8,128)} fusion(bf16[4096,2048]{1,0:T(8,128)(2,1)} %all-gather.6.cloned.1.call-done, bf16[2048,1024]{1,0:T(8,128)(2,1)} %bitcast.119), kind=kOutput, calls=%fused_computation.93 | convolution fusion | flops 17179869184 | bytes 37748736 | tf_op jit(solution)/shard_map/dot_general | solution.py:23
  632.9 30.2 %fusion.7 = bf16[2048,1024]{1,0:T(8,128)(2,1)} fusion(bf16[4096,2048]{1,0:T(8,128)(2,1)} %all-gather.6.cloned.1.call-done, f32[4096,1024]{1,0:T(8,128)} %fusion.5, f32[4096,1024]{1,0:T(8,128)} %fusion.40), kind=kOutput, calls=%fused_computation.22 | convolution fusion | flops 17207132160 | bytes 54525952 | tf_op jit(solution)/shard_map/dot_general | solution.py:31
  663.1 22.1 %fusion.39 = f32[4096,1024]{1,0:T(8,128)} fusion(bf16[4096,2048]{1,0:T(8,128)(2,1)} %all-gather.6.cloned.1.call-done, bf16[2048,1024]{1,0:T(8,128)(2,1)S(1)} %bitcast.122), kind=kOutput, calls=%fused_computation.92 | convolution fusion | flops 17179869184 | bytes 37748736 | tf_op jit(solution)/shard_map/dot_general | solution.py:23
  696.0 32.9 %fusion.6 = bf16[2048,1024]{1,0:T(8,128)(2,1)} fusion(bf16[4096,2048]{1,0:T(8,128)(2,1)} %all-gather.6.cloned.1.call-done, f32[4096,1024]{1,0:T(8,128)} %fusion.40, f32[4096,1024]{1,0:T(8,128)} %fusion.5, f32[4096,1024]{1,0:T(8,128)} %fusion.39), kind=kOutput, calls=%fused_computation.21 | convolution fusion | flops 17223909376 | bytes 71303168 | tf_op jit(solution)/shard_map/dot_general | solution.py:31
  743.7 32.9 %fusion.3 = f32[1024,2048]{1,0:T(8,128)} fusion(f32[4096,1024]{1,0:T(8,128)} %fusion.39, f32[4096,1024]{1,0:T(8,128)} %fusion.40, f32[4096,2048]{1,0:T(8,128)} %bitcast.142), kind=kOutput, calls=%fused_computation.13 | convolution fusion | flops 17221812224 | bytes 75497472 | tf_op jit(solution)/shard_map/dot_general | solution.py:31
  800.3 17.8 %collective-permute-done.2 = bf16[8,256,384]{1,2,0:T(8,128)(2,1)} collective-permute-done((bf16[8,256,384]{1,2,0:T(8,128)(2,1)S(1)}, bf16[8,256,384]{1,2,0:T(8,128)(2,1)}, u32[]{:S(2)}, u32[]{:S(2)}) %collective-permute-start.2) | collective-permute-done | bytes 1572896 | tf_op jit(solution)/shard_map/ppermute | solution.py:194
  (186 shorter events, 178.6 us)
Async XLA Ops:
  8.0 355.4 %all-gather.4.cloned.1.call-start = ((), (), s32[]{:S(2)}) async-start(), calls=%async_computation.8 | async-start | bytes 17301504 | tf_op jit(solution)/shard_map/all_gather | solution.py:529
  13.7 57.1 %all-to-all-start = ((bf16[8,256,384]{1,2,0:T(8,128)(2,1)}), bf16[8,256,384]{1,2,0:T(8,128)(2,1)}, u32[]{:S(2)}, u32[]{:S(2)}) async-start(bf16[8,256,384]{1,2,0:T(8,128)(2,1)} %pad_maximum_fusion), calls=%async_computation | async-start | bytes 3145728 | tf_op jit(solution)/shard_map/all_to_all | solution.py:178
  18.8 590.7 %all-gather.6.cloned.1.call-start = ((), (), s32[]{:S(2)}) async-start(), calls=%async_computation.9 | async-start | bytes 17301504 | tf_op jit(solution)/shard_map/all_gather | solution.py:557
  19.2 74.0 %copy-start.14 = (s32[1024]{0:T(1024)}, s32[1024]{0:T(1024)S(1)}, u32[]{:S(2)}) copy-start(s32[1024]{0:T(1024)S(1)} %convert_reduce_fusion) | copy-start | bytes 12292
  19.4 73.7 %copy-start.6 = (s32[1024,1]{1,0:T(8,128)}, s32[1024,1]{1,0:T(8,128)S(1)}, u32[]{:S(2)}) copy-start(s32[1024,1]{1,0:T(8,128)S(1)} %copy.142.segc_ref) | copy-start | bytes 12292
  22.8 67.1 %copy-start.24 = (f32[1024,256]{1,0:T(8,128)}, f32[1024,256]{1,0:T(8,128)S(1)}, u32[]{:S(2)}) copy-start(f32[1024,256]{1,0:T(8,128)S(1)} %copy.132) | copy-start | bytes 3145732
  78.7 14.5 %copy-start.10 = (bf16[1024,64]{1,0:T(8,128)(2,1)}, bf16[1024,64]{1,0:T(8,128)(2,1)S(1)}, u32[]{:S(2)}) copy-start(bf16[1024,64]{1,0:T(8,128)(2,1)S(1)} %slice.101.v_ref) | copy-start | bytes 393220
  101.0 60.3 %copy-start.22 = (bf16[1024,256]{1,0:T(8,128)(2,1)}, bf16[1024,256]{1,0:T(8,128)(2,1)S(1)}, u32[]{:S(2)}) copy-start(bf16[1024,256]{1,0:T(8,128)(2,1)S(1)} %attention_forward.1.a_ref) | copy-start | bytes 1572868
  170.6 70.0 %all-to-all-start.1 = ((bf16[8,256,1024]{1,2,0:T(8,128)(2,1)}), bf16[8,256,1024]{1,2,0:T(8,128)(2,1)}, u32[]{:S(2)}, u32[]{:S(2)}) async-start(bf16[8,256,1024]{1,2,0:T(8,128)(2,1)} %bitcast.110), calls=%async_computation.1 | async-start | bytes 8388608 | tf_op jit(solution)/shard_map/all_to_all | solution.py:178
  240.7 83.8 %all-to-all-start.2 = ((bf16[8,256,1024]{1,2,0:T(8,128)(2,1)}), bf16[8,256,1024]{1,2,0:T(8,128)(2,1)}, u32[]{:S(2)}, u32[]{:S(2)}) async-start(bf16[8,256,1024]{1,2,0:T(8,128)(2,1)} %bitcast.109), calls=%async_computation.2 | async-start | bytes 8388608 | tf_op jit(solution)/shard_map/all_to_all | solution.py:178
  245.4 580.7 %reduce-scatter.2.cloned.1.call-start = ((), (), s32[]{:S(2)}) async-start(), calls=%async_computation.7 | async-start | bytes 4718592 | tf_op jit(solution)/shard_map/reduce_scatter | solution.py:174
  416.2 15.1 %copy-start.30 = (bf16[8,256,1024]{2,1,0:T(8,128)(2,1)S(1)}, bf16[8,256,1024]{2,1,0:T(8,128)(2,1)}, u32[]{:S(2)}) copy-start(bf16[8,256,1024]{2,1,0:T(8,128)(2,1)} %copy.146) | copy-start | bytes 12582916
  416.2 15.1 %copy-start.40 = (f32[1024,1024]{1,0:T(8,128)S(1)}, f32[1024,1024]{1,0:T(8,128)}, u32[]{:S(2)}) copy-start(f32[1024,1024]{1,0:T(8,128)} %fusion.37) | copy-start | bytes 12582916
  441.5 45.0 %copy-start.23 = (bf16[1024,256]{1,0:T(8,128)(2,1)S(1)}, bf16[1024,256]{1,0:T(8,128)(2,1)}, u32[]{:S(2)}) copy-start(bf16[1024,256]{1,0:T(8,128)(2,1)} %copy-done.22) | copy-start | bytes 1572868
  522.4 162.8 %all-to-all-start.3 = ((bf16[8,256,384]{1,2,0:T(8,128)(2,1)}), bf16[8,256,384]{1,2,0:T(8,128)(2,1)}, u32[]{:S(2)}, u32[]{:S(2)}) async-start(bf16[8,256,384]{1,2,0:T(8,128)(2,1)} %copy.154), calls=%async_computation.4 | async-start | bytes 3145728 | tf_op jit(solution)/shard_map/all_to_all | solution.py:178
  526.7 78.3 %collective-permute-start.3 = (bf16[256,2048]{1,0:T(8,128)(2,1)S(1)}, bf16[256,2048]{1,0:T(8,128)(2,1)}, u32[]{:S(2)}, u32[]{:S(2)}) collective-permute-start(bf16[256,2048]{1,0:T(8,128)(2,1)S(1)} %copy-done.32), channel_id=1, source_target_pairs={{0,8},{24,16},{1,9},{25,17},{2,10},{26,18},{3,11},{27,19},{4,12},{... | collective-permute-start | bytes 3145736 | tf_op jit(solution)/shard_map/ppermute | solution.py:186
  607.7 121.3 %collective-permute-start.4 = (bf16[256,2048]{1,0:T(8,128)(2,1)}, bf16[256,2048]{1,0:T(8,128)(2,1)}, u32[]{:S(2)}, u32[]{:S(2)}) collective-permute-start(bf16[256,2048]{1,0:T(8,128)(2,1)} %add_convert_fusion.5), channel_id=1, source_target_pairs={{8,16},{16,8},{9,17},{17,9},{10,18},{18,10},{11,19},{19,11},{12,20... | collective-permute-start | bytes 3145736 | tf_op jit(solution)/shard_map/ppermute | solution.py:190
  632.9 30.2 %copy-start.31 = (bf16[8,256,1024]{2,1,0:T(8,128)(2,1)S(1)}, bf16[8,256,1024]{2,1,0:T(8,128)(2,1)}, u32[]{:S(2)}) copy-start(bf16[8,256,1024]{2,1,0:T(8,128)(2,1)} %copy.146) | copy-start | bytes 12582916
  685.2 53.7 %all-to-all-start.5 = ((bf16[8,256,1024]{2,1,0:T(8,128)(2,1)}), bf16[8,256,1024]{2,1,0:T(8,128)(2,1)}, u32[]{:S(2)}, u32[]{:S(2)}) async-start(bf16[8,256,1024]{2,1,0:T(8,128)(2,1)} %bitcast.124), calls=%async_computation.6 | async-start | bytes 8388608 | tf_op jit(solution)/shard_map/all_to_all | solution.py:178
  689.8 43.3 %collective-permute-start = (bf16[8,256,384]{1,2,0:T(8,128)(2,1)}, bf16[8,256,384]{1,2,0:T(8,128)(2,1)}, u32[]{:S(2)}, u32[]{:S(2)}) collective-permute-start(bf16[8,256,384]{1,2,0:T(8,128)(2,1)} %all-to-all-done.3), channel_id=1, source_target_pairs={{0,8},{24,16},{1,9},{25,17},{2,10},{26,18},{3,11},{27,19},{4,12},{... | collective-permute-start | bytes 4718600 | tf_op jit(solution)/shard_map/ppermute | solution.py:186
  731.8 48.5 %collective-permute-start.5 = (bf16[256,2048]{1,0:T(8,128)(2,1)}, bf16[256,2048]{1,0:T(8,128)(2,1)}, u32[]{:S(2)}, u32[]{:S(2)}) collective-permute-start(bf16[256,2048]{1,0:T(8,128)(2,1)} %add_convert_fusion.4), channel_id=1, source_target_pairs={{8,0},{16,24},{9,1},{17,25},{10,2},{18,26},{11,3},{19,27},{12,4},{... | collective-permute-start | bytes 3145736 | tf_op jit(solution)/shard_map/ppermute | solution.py:194
  735.4 41.1 %collective-permute-start.1 = (bf16[8,256,384]{1,2,0:T(8,128)(2,1)S(1)}, bf16[8,256,384]{1,2,0:T(8,128)(2,1)}, u32[]{:S(2)}, u32[]{:S(2)}) collective-permute-start(bf16[8,256,384]{1,2,0:T(8,128)(2,1)S(1)} %add_convert_fusion.3), channel_id=1, source_target_pairs={{8,16},{16,8},{9,17},{17,9},{10,18},{18,10},{11,19},{19,11},{12,20... | collective-permute-start | bytes 4718600 | tf_op jit(solution)/shard_map/ppermute | solution.py:190
  738.9 53.9 %all-to-all-start.4 = ((bf16[8,256,1024]{2,1,0:T(8,128)(2,1)}), bf16[8,256,1024]{2,1,0:T(8,128)(2,1)}, u32[]{:S(2)}, u32[]{:S(2)}) async-start(bf16[8,256,1024]{2,1,0:T(8,128)(2,1)} %bitcast.123), calls=%async_computation.5 | async-start | bytes 8388608 | tf_op jit(solution)/shard_map/all_to_all | solution.py:178
  778.8 39.2 %collective-permute-start.2 = (bf16[8,256,384]{1,2,0:T(8,128)(2,1)S(1)}, bf16[8,256,384]{1,2,0:T(8,128)(2,1)}, u32[]{:S(2)}, u32[]{:S(2)}) collective-permute-start(bf16[8,256,384]{1,2,0:T(8,128)(2,1)S(1)} %add_convert_fusion.2), channel_id=1, source_target_pairs={{8,0},{16,24},{9,1},{17,25},{10,2},{18,26},{11,3},{19,27},{12,4},{... | collective-permute-start | bytes 4718600 | tf_op jit(solution)/shard_map/ppermute | solution.py:194
  (32 other events, 187.2 us)
Sparse Core Ops, SparseCore 0:
  12.1 146.7 all-gather.3
  164.4 172.8 all-gather.5
Sparse Core Ops, SparseCore 1:
  363.4 50.2 reduce-scatter.1

commit v3 on v2

--- a/solution.py
+++ b/solution.py
@@ -71,99 +71,6 @@
 
 def unrotate(x, cos_full, sin_full):
     return x * cos_full - swap_halves(x) * sin_full
-
-
-def softmax_block(q, k, allowed):
-    scores = SCORE_SCALE * lax.dot_general(
-        q, k, (((1,), (1,)), ((), ())), preferred_element_type=F32
-    )
-    scores = jnp.where(allowed, scores, MASKED)
-    top = jnp.max(scores, axis=-1, keepdims=True)
-    weight = jnp.exp(scores - top)
-    return weight * (1.0 / jnp.sum(weight, axis=-1, keepdims=True))
-
-
-def allowed_block(row0, rows, cols, seg_q, seg_k):
-    q_index = row0 + lax.broadcasted_iota(jnp.int32, (rows, cols), 0)
-    k_index = lax.broadcasted_iota(jnp.int32, (rows, cols), 1)
-    return (seg_q == seg_k) & (k_index <= q_index)
-
-
-def attention_kernel(heads, block, q_ref, k_ref, v_ref, segc_ref, segr_ref, o_ref):
-    total = k_ref.shape[0]
-    for i in range(total // block):
-        cols = (i + 1) * block
-        rows = pl.ds(i * block, block)
-        allowed = allowed_block(i * block, block, cols, segc_ref[rows, :], segr_ref[:, :cols])
-        k, v = k_ref[:cols, :], v_ref[:cols, :]
-        for h in range(heads):
-            lanes = slice(h * HEAD, (h + 1) * HEAD)
-            probs = softmax_block(q_ref[rows, lanes], k, allowed)
-            out = jnp.dot(probs.astype(BF16), v, preferred_element_type=F32)
-            o_ref[rows, lanes] = out.astype(BF16)
-
-
-def attention_forward(q, k, v, seg_col, seg_row):
-    total, width = q.shape
-    heads = width // HEAD
-    return pl.pallas_call(
-        functools.partial(attention_kernel, heads, 256),
-        out_shape=jax.ShapeDtypeStruct((total, width), BF16),
-        compiler_params=pltpu.CompilerParams(vmem_limit_bytes=40 << 20),
-        cost_estimate=pl.CostEstimate(
-            flops=2 * total * total * width, bytes_accessed=4 * total * width, transcendentals=heads * total * total // 2
-        ),
-        name="attention_forward",
-    )(q, k, v, seg_col, seg_row)
-
-
-def attention_backward_kernel(
-    heads, block, q_ref, k_ref, v_ref, g_ref, segc_ref, segr_ref, dq_ref, dk_ref, dv_ref
-):
-    total = k_ref.shape[0]
-    dk_ref[...] = jnp.zeros_like(dk_ref)
-    dv_ref[...] = jnp.zeros_like(dv_ref)
-    for i in range(total // block):
-        cols = (i + 1) * block
-        rows = pl.ds(i * block, block)
-        allowed = allowed_block(i * block, block, cols, segc_ref[rows, :], segr_ref[:, :cols])
-        k, v = k_ref[:cols, :], v_ref[:cols, :]
-        for h in range(heads):
-            lanes = slice(h * HEAD, (h + 1) * HEAD)
-            q, g = q_ref[rows, lanes], g_ref[rows, lanes]
-            probs = softmax_block(q, k, allowed)
-            probs_grad = lax.dot_general(
-                g, v, (((1,), (1,)), ((), ())), preferred_element_type=F32
-            )
-            delta = jnp.sum(probs * probs_grad, axis=-1, keepdims=True)
-            score_grad = (probs * (probs_grad - delta)).astype(BF16)
-            dq_ref[rows, lanes] = SCORE_SCALE * jnp.dot(
-                score_grad, k, preferred_element_type=F32
-            )
-            dk_ref[:cols, :] += SCORE_SCALE * lax.dot_general(
-                score_grad, q, (((0,), (0,)), ((), ())), preferred_element_type=F32
-            )
-            dv_ref[:cols, :] += lax.dot_general(
-                probs.astype(BF16), g, (((0,), (0,)), ((), ())), preferred_element_type=F32
-            )
-
-
-def attention_backward(q, k, v, g, seg_col, seg_row):
-    total, width = q.shape
-    heads = width // HEAD
-    return pl.pallas_call(
-        functools.partial(attention_backward_kernel, heads, 256),
-        out_shape=(
-            jax.ShapeDtypeStruct((total, width), F32),
-            jax.ShapeDtypeStruct((total, HEAD), F32),
-            jax.ShapeDtypeStruct((total, HEAD), F32),
-        ),
-        compiler_params=pltpu.CompilerParams(vmem_limit_bytes=40 << 20),
-        cost_estimate=pl.CostEstimate(
-            flops=5 * total * total * width, bytes_accessed=10 * total * width, transcendentals=heads * total * total // 2
-        ),
-        name="attention_backward",
-    )(q, k, v, g, seg_col, seg_row)
 
 
 def gather_rows(x):
@@ -229,7 +136,7 @@
 GATHER_SEMS = 13
 
 
-def gather_blocks(me, out, sems):
+def gather_steps(me, out, sems):
     core, px, py, diag = (flip(me, mask) for mask in (1, 2, 4, 6))
     half = out.shape[1] // 2
     low, high, whole = pl.ds(0, half), pl.ds(half, half), pl.ds(0, 2 * half)
@@ -243,30 +150,43 @@
     x_low, y_high = move(0, me, low, px), move(1, me, high, py)
     own = move(2, me, whole, core)
     x_high, y_low = move(3, me, high, px), move(4, me, low, py)
+    yield
     x_low.wait_recv()
     diag_low = move(5, px, low, py)
     pieces = [own, move(6, px, low, core)]
+    yield
     y_high.wait_recv()
     diag_high = move(7, py, high, px)
     pieces.append(move(8, py, high, core))
+    yield
     x_high.wait_recv()
     pieces.append(move(9, px, high, core))
+    yield
     y_low.wait_recv()
     pieces.append(move(10, py, low, core))
+    yield
     diag_low.wait_recv()
     pieces.append(move(11, diag, low, core))
     diag_high.wait_recv()
     pieces.append(move(12, diag, high, core))
+    yield
     for copy in pieces:
         copy.wait_recv()
     for copy in [x_low, y_high, x_high, y_low, diag_low, diag_high] + pieces:
         copy.wait_send()
 
 
+def gather_blocks(me, out, sems):
+    for unused_step in gather_steps(me, out, sems):
+        pass
+
+
 SCATTER_SEMS = 10
 
 
-def scatter_blocks(me, partial, sib_out, sib_in, acc, x_out, x_in, y_out, y_in, sems):
+def scatter_blocks(
+    me, partial, sib_out, sib_in, acc, x_out, x_in, y_out, y_in, sems, meanwhile=None
+):
     core, px, py = (flip(me, mask) for mask in (1, 2, 4))
     half = acc.shape[1] // 2
     masks = (6, 2, 4, 0)
@@ -304,6 +224,8 @@
     y_diag.wait_recv()
     x_out[2] = (acc[1, high] + y_in[0].astype(F32)).astype(BF16)
     x_last = move(x_out.at[2], x_in.at[2], 9, px)
+    if meanwhile is not None:
+        meanwhile()
     x_near.wait_recv()
     y_near.wait_recv()
     y_last.wait_recv()
@@ -330,6 +252,8 @@
 
 
 VMEM = pl.BlockSpec(memory_space=pltpu.VMEM)
+SMEM = pl.BlockSpec(memory_space=pltpu.SMEM)
+ANY = pl.BlockSpec(memory_space=pl.ANY)
 
 
 def comm_params(collective_id, mebibytes):
@@ -338,69 +262,220 @@
     )
 
 
-def norm_gather(x, gain, normalise, collective_id):
-    rows, width = x.shape
-
-    def kernel(x_ref, gain_ref, out, sems):
+def front(
+    tokens, attn_gain, query_weight, key_weight, value_weight, output_weight, ffn_gain,
+    gate_weight, up_weight, dealing, lengths, cotangent, freq, replicas,
+):
+    local, width = tokens.shape
+    total = 8 * local
+    shard_rows = query_weight.shape[0]
+    q_cols = query_weight.shape[1] // 8
+    ff_cols = gate_weight.shape[1] // 8
+    block = 256
+    others = (1, 2, 3, 4, 5, 6, 7)
+
+    def kernel(
+        tok_ref, gain_ref, wq_hbm, wk_ref, wv_ref, wo_ref, fgain_ref, wg_hbm, wu_hbm,
+        deal_ref, len_ref, cot_ref, freq_ref,
+        n_ref, q_ref, kv_ref, att_ref, qw_ref, kvw_ref, wg_out, wu_out, mid_ref, nf_ref, dg_out, cot_out,
+        kv_stage, c_all, dg_own,
+        sib_out, sib_in, acc, x_out, x_in, y_out, y_in, scatter_sems,
+        n_sems, c_sems, nf_sems, qkv_sems, bulk_sems, ring_sems, pair_sems, local_sems,
+    ):
         me = lax.axis_index("shard")
-        block = x_ref[...]
-        if normalise:
-            block = rms_scale(block.astype(F32), gain_ref[...]).astype(BF16)
-        out[me] = block
-        greet(me, (1, 2, 4))
-        gather_blocks(me, out, sems)
-
-    return pl.pallas_call(
-        kernel,
-        out_shape=jax.ShapeDtypeStruct((8, rows, width), BF16),
-        in_specs=[VMEM, VMEM],
-        out_specs=VMEM,
-        scratch_shapes=[pltpu.SemaphoreType.DMA((2, GATHER_SEMS))],
-        compiler_params=comm_params(collective_id, 20),
-        cost_estimate=pl.CostEstimate(
-            flops=8 * rows * width, bytes_accessed=18 * rows * width, transcendentals=rows
-        ),
-        name="gather_kernel",
-    )(x, gain[None, :]).reshape(8 * rows, width)
-
-
-def branch_middle_gather(attention, weight, hidden, gain, collective_id):
-    rows, width = hidden.shape
-
-    def kernel(a_ref, w_ref, h_ref, gain_ref, mid, out, *scratch):
-        me = lax.axis_index("shard")
-        *buffers, scatter_sems, sems = scratch
-        greet(me, (1, 2, 4))
+        group = lax.axis_index("rep")
+        core = lax.rem(me, 2)
+        after = lax.rem(group + 1, replicas)
+        before = lax.rem(group + replicas - 1, replicas)
+
+        barrier = pltpu.get_barrier_semaphore()
+        for mask in others:
+            pl.semaphore_signal(
+                barrier, inc=1, device_id={"shard": flip(me, mask)}, device_id_type=MESH
+            )
+        for neighbour in (after, before):
+            pl.semaphore_signal(
+                barrier, inc=1, device_id={"rep": neighbour}, device_id_type=MESH
+            )
+        n_ref[me] = rms_scale(tok_ref[...].astype(F32), gain_ref[...]).astype(BF16)
+        c_all[me] = cot_ref[...]
+        for d in range(8):
+            lanes = slice(d * HEAD, (d + 1) * HEAD)
+            kv_stage[d] = jnp.concatenate([wk_ref[:, lanes], wv_ref[:, lanes]], axis=1)
+        pl.semaphore_wait(barrier, len(others) + 2)
+
+        gather_n = gather_steps(me, n_ref, n_sems)
+        next(gather_n)
+        weights = []
+        for mask in others:
+            peer = flip(me, mask)
+            columns = pl.ds(pl.multiple_of(peer * q_cols, q_cols), q_cols)
+            weights.append(send(wq_hbm.at[:, columns], qw_ref.at[me], qkv_sems, 2 * mask - 2, peer))
+            weights.append(send(kv_stage.at[peer], kvw_ref.at[me], qkv_sems, 2 * mask - 1, peer))
+        gather_c = gather_steps(me, c_all, c_sems)
+        for copy in weights:
+            copy.start()
+        next(gather_c)
+        bulk = []
+        for i, (source, target) in enumerate(((wg_hbm, wg_out), (wu_hbm, wu_out))):
+            for mask in others:
+                peer = flip(me, mask)
+                columns = pl.ds(pl.multiple_of(peer * ff_cols, ff_cols), ff_cols)
+                bulk.append(
+                    send(source.at[:, columns], target.at[me], bulk_sems, 7 * i + mask - 1, peer)
+                )
+        for copy in bulk:
+            copy.start()
+        own_columns = pl.ds(pl.multiple_of(me * ff_cols, ff_cols), ff_cols)
+        own_q = pl.ds(pl.multiple_of(me * q_cols, q_cols), q_cols)
+        kept = [
+            pltpu.make_async_copy(wg_hbm.at[:, own_columns], wg_out.at[me], local_sems.at[0]),
+            pltpu.make_async_copy(wu_hbm.at[:, own_columns], wu_out.at[me], local_sems.at[1]),
+            pltpu.make_async_copy(wq_hbm.at[:, own_q], qw_ref.at[me], local_sems.at[2]),
+        ]
+        for copy in kept:
+            copy.start()
+        kvw_ref[me] = kv_stage[me]
+        for unused in range(5):
+            next(gather_n)
+            next(gather_c)
+        for unused in gather_n:
+            pass
+        for unused in gather_c:
+            pass
+
+        for i in range(total // block):
+            rows = pl.ds(i * block, block)
+            packed = i * block + lax.broadcasted_iota(jnp.int32, (block, total), 0)
+            chosen = (deal_ref[...] == packed).astype(BF16)
+            dealt = mm(chosen, c_all[...].reshape(total, width))
+            dg_own[rows, :] = (RESIDUAL_SCALE * dealt).astype(BF16)
+        packed = me * local + lax.broadcasted_iota(jnp.int32, (local, total), 0)
+        chosen = (deal_ref[...] == packed).astype(BF16)
+        cot_out[...] = mm(chosen, c_all[...].reshape(total, width)).astype(BF16)
+        half = pl.ds(pl.multiple_of(core * (total // 2), total // 2), total // 2)
+        store = pltpu.make_async_copy(dg_own, dg_out.at[group], local_sems.at[3])
+        store.start()
+
+        def ring(hop):
+            held = lax.rem(group + replicas - hop, replicas)
+            ref = dg_out.at[held, half]
+            copy = pltpu.make_async_remote_copy(
+                src_ref=dg_own.at[half] if hop == 0 else ref,
+                dst_ref=ref,
+                send_sem=ring_sems.at[0, hop],
+                recv_sem=ring_sems.at[1, hop],
+                device_id={"rep": after},
+                device_id_type=MESH,
+            )
+            copy.start()
+            return copy
+
+        def share(hop):
+            held = lax.rem(group + replicas - hop, replicas)
+            ref = dg_out.at[held, half]
+            copy = send(ref, ref, pair_sems, hop - 1, flip(me, 1))
+            copy.start()
+            return copy
+
+        hops, shares = [ring(0)], []
+
+        for copy in kept[2:]:
+            copy.wait()
+        for copy in weights:
+            copy.wait_recv()
+        for i in range(total // block):
+            rows = pl.ds(i * block, block)
+            x = n_ref[pl.ds(i * block // local, block // local)].reshape(block, width)
+            cosine, sine = lane_rope(i * block, block, freq_ref[...], len_ref)
+            pre = mm(x, qw_ref[...].reshape(width, q_cols))
+            for j in range(q_cols // (2 * HEAD)):
+                lanes = slice(j * 2 * HEAD, (j + 1) * 2 * HEAD)
+                y = pre[:, lanes]
+                q_ref[rows, lanes] = (y * cosine + lane_swap(y) * sine).astype(BF16)
+            cosine, sine = keys_only(cosine, sine)
+            y = mm(x, kvw_ref[...].reshape(width, 2 * HEAD))
+            kv_ref[rows, :] = (y * cosine + lane_swap(y) * sine).astype(BF16)
+        attend(q_cols // HEAD, block, q_ref, kv_ref, len_ref, att_ref)
 
         def partial(d):
-            return jnp.dot(
-                a_ref[pl.ds(pl.multiple_of(d * rows, rows), rows), :],
-                w_ref[...],
-                preferred_element_type=F32,
-            )
-
-        branch = scatter_blocks(me, partial, *buffers, scatter_sems)
-        middle = h_ref[...].astype(F32) + RESIDUAL_SCALE * branch
-        mid[...] = middle
-        out[me] = rms_scale(middle, gain_ref[...]).astype(BF16)
-        gather_blocks(me, out, sems)
-
-    return pl.pallas_call(
+            return mm(att_ref[pl.ds(pl.multiple_of(d * local, local), local), :], wo_ref[...])
+
+        def next_hop():
+            hop = len(hops)
+            hops[-1].wait_recv()
+            if hop < replicas - 1:
+                hops.append(ring(hop))
+            shares.append(share(hop))
+
+        branch = scatter_blocks(
+            me, partial, sib_out, sib_in, acc, x_out, x_in, y_out, y_in, scatter_sems, next_hop
+        )
+        middle = tok_ref[...].astype(F32) + RESIDUAL_SCALE * branch
+        mid_ref[...] = middle
+        nf_ref[me] = rms_scale(middle, fgain_ref[...]).astype(BF16)
+        gather_blocks(me, nf_ref, nf_sems)
+        while len(shares) < replicas - 1:
+            next_hop()
+        for copy in kept[:2] + [store]:
+            copy.wait()
+        for copy in bulk + shares:
+            copy.wait_recv()
+        for copy in weights + bulk + hops + shares:
+            copy.wait_send()
+
+    rows8 = jax.ShapeDtypeStruct((8, local, width), BF16)
+    half_sems = pltpu.SemaphoreType.DMA
+    outs = pl.pallas_call(
         kernel,
         out_shape=(
-            jax.ShapeDtypeStruct((rows, width), F32),
-            jax.ShapeDtypeStruct((8, rows, width), BF16),
-        ),
-        in_specs=[VMEM] * 4,
-        out_specs=[VMEM] * 2,
-        scratch_shapes=scatter_scratch(rows, width)
-        + [pltpu.SemaphoreType.DMA((2, GATHER_SEMS))],
-        compiler_params=comm_params(collective_id, 40),
+            rows8,
+            jax.ShapeDtypeStruct((total, q_cols), BF16),
+            jax.ShapeDtypeStruct((total, 2 * HEAD), BF16),
+            jax.ShapeDtypeStruct((total, q_cols), BF16),
+            jax.ShapeDtypeStruct((8, shard_rows, q_cols), BF16),
+            jax.ShapeDtypeStruct((8, shard_rows, 2 * HEAD), BF16),
+            jax.ShapeDtypeStruct((8, shard_rows, ff_cols), BF16),
+            jax.ShapeDtypeStruct((8, shard_rows, ff_cols), BF16),
+            jax.ShapeDtypeStruct((local, width), F32),
+            rows8,
+            jax.ShapeDtypeStruct((replicas, total, width), BF16),
+            jax.ShapeDtypeStruct((local, width), BF16),
+        ),
+        in_specs=[VMEM, VMEM, ANY, VMEM, VMEM, VMEM, VMEM, ANY, ANY, VMEM, SMEM, VMEM, VMEM],
+        out_specs=[VMEM] * 6 + [ANY, ANY, VMEM, VMEM, ANY, VMEM],
+        scratch_shapes=[
+            pltpu.VMEM((8, shard_rows, 2 * HEAD), BF16),
+            pltpu.VMEM((8, local, width), BF16),
+            pltpu.VMEM((total, width), BF16),
+        ]
+        + scatter_scratch(local, width)
+        + [
+            half_sems((2, GATHER_SEMS)),
+            half_sems((2, GATHER_SEMS)),
+            half_sems((2, GATHER_SEMS)),
+            half_sems((2, 14)),
+            half_sems((2, 14)),
+            half_sems((2, replicas)),
+            half_sems((2, replicas)),
+            half_sems((4,)),
+        ],
+        compiler_params=comm_params(0, 56),
         cost_estimate=pl.CostEstimate(
-            flops=2 * 8 * rows * width * weight.shape[0], bytes_accessed=40 * rows * width, transcendentals=rows
-        ),
-        name="branch_middle_gather",
-    )(attention, weight, hidden, gain[None, :])
+            flops=150_000_000_000, bytes_accessed=50 << 20, transcendentals=total * total
+        ),
+        name="front",
+    )(
+        tokens, attn_gain[None, :], query_weight, key_weight, value_weight, output_weight,
+        ffn_gain[None, :], gate_weight, up_weight, dealing, lengths, cotangent, freq,
+    )
+    normed, q, kv, attention, qw, kvw, wg, wu, middle, nf, dg, cot = outs
+    return (
+        normed.reshape(total, width), q, kv, attention,
+        qw.reshape(width, q_cols), kvw.reshape(width, 2 * HEAD),
+        wg.reshape(width, ff_cols), wu.reshape(width, ff_cols),
+        middle, nf.reshape(total, width), dg, cot,
+    )
 
 
 def norm_pull(x, gain, grad):
@@ -427,7 +502,7 @@
         )
         rows_part, gain_row = norm_pull(m_ref[...], gain_ref[...], grad)
         gain_part[...] = gain_row
-        middle_grad = g_ref[...] + rows_part
+        middle_grad = g_ref[...].astype(F32) + rows_part
         mg_ref[...] = middle_grad
         out[me] = (RESIDUAL_SCALE * middle_grad).astype(BF16)
         gather_blocks(me, out, sems)
@@ -483,6 +558,432 @@
         ),
         name="pull_tokens",
     )(part, hidden, gain[None, :], middle_grad)
+
+
+def softmax_block(q, k, allowed):
+    scores = SCORE_SCALE * mm_t(q, k)
+    scores = jnp.where(allowed, scores, MASKED)
+    top = jnp.max(scores, axis=-1, keepdims=True)
+    weight = jnp.exp(scores - top)
+    return weight * (1.0 / jnp.sum(weight, axis=-1, keepdims=True))
+
+
+def allowed_block(row0, cols, start):
+    shape = (start.shape[0], cols)
+    query = row0 + lax.broadcasted_iota(jnp.int32, shape, 0)
+    key = lax.broadcasted_iota(jnp.int32, shape, 1)
+    return (key >= start) & (key <= query)
+
+
+def sequence_starts(row0, shape, lengths_ref):
+    row = row0 + lax.broadcasted_iota(jnp.int32, shape, 0)
+    start = jnp.zeros(shape, jnp.int32)
+    end = 0
+    for i in range(lengths_ref.shape[1]):
+        length = lengths_ref[0, i]
+        end = end + length
+        start = start + jnp.where(row >= end, length, 0)
+    return start
+
+
+def attend(heads, block, q_ref, kv_ref, lengths_ref, o_ref):
+    total = kv_ref.shape[0]
+    for i in range(total // block):
+        cols = (i + 1) * block
+        rows = pl.ds(i * block, block)
+        allowed = allowed_block(
+            i * block, cols, sequence_starts(i * block, (block, 1), lengths_ref)
+        )
+        kv = kv_ref[:cols, :]
+        k, v = kv[:, :HEAD], kv[:, HEAD:]
+        for h in range(heads):
+            lanes = slice(h * HEAD, (h + 1) * HEAD)
+            probs = softmax_block(q_ref[rows, lanes], k, allowed)
+            o_ref[rows, lanes] = mm(probs.astype(BF16), v).astype(BF16)
+
+
+def attend_back(heads, block, q_ref, kv_ref, g_ref, lengths_ref, dq_ref, dk_ref, dv_ref):
+    total = kv_ref.shape[0]
+    dk_ref[...] = jnp.zeros_like(dk_ref)
+    dv_ref[...] = jnp.zeros_like(dv_ref)
+    for i in range(total // block):
+        cols = (i + 1) * block
+        rows = pl.ds(i * block, block)
+        allowed = allowed_block(
+            i * block, cols, sequence_starts(i * block, (block, 1), lengths_ref)
+        )
+        kv = kv_ref[:cols, :]
+        k, v = kv[:, :HEAD], kv[:, HEAD:]
+        for h in range(heads):
+            lanes = slice(h * HEAD, (h + 1) * HEAD)
+            q, g = q_ref[rows, lanes], g_ref[rows, lanes]
+            probs = softmax_block(q, k, allowed)
+            probs_grad = mm_t(g, v)
+            delta = jnp.sum(probs * probs_grad, axis=-1, keepdims=True)
+            score_grad = (probs * (probs_grad - delta)).astype(BF16)
+            dq_ref[rows, lanes] = SCORE_SCALE * mm(score_grad, k)
+            dk_ref[:cols, :] += SCORE_SCALE * t_mm(score_grad, q)
+            dv_ref[:cols, :] += t_mm(probs.astype(BF16), g)
+
+
+def attention_forward(q, kv, lengths):
+    total, width = q.shape
+
+    def kernel(q_ref, kv_ref, lengths_ref, o_ref):
+        attend(width // HEAD, 256, q_ref, kv_ref, lengths_ref, o_ref)
+
+    return pl.pallas_call(
+        kernel,
+        out_shape=jax.ShapeDtypeStruct((total, width), BF16),
+        in_specs=[VMEM, VMEM, SMEM],
+        out_specs=VMEM,
+        compiler_params=pltpu.CompilerParams(vmem_limit_bytes=40 << 20),
+        name="attention_forward",
+    )(q, kv, lengths)
+
+
+def attention_gradients(q, kv, grad, lengths):
+    total, width = q.shape
+
+    def kernel(q_ref, kv_ref, g_ref, lengths_ref, dq_ref, dk_ref, dv_ref):
+        attend_back(width // HEAD, 256, q_ref, kv_ref, g_ref, lengths_ref, dq_ref, dk_ref, dv_ref)
+
+    return pl.pallas_call(
+        kernel,
+        out_shape=(
+            jax.ShapeDtypeStruct((total, width), F32),
+            jax.ShapeDtypeStruct((total, HEAD), F32),
+            jax.ShapeDtypeStruct((total, HEAD), F32),
+        ),
+        in_specs=[VMEM, VMEM, VMEM, SMEM],
+        out_specs=[VMEM] * 3,
+        compiler_params=pltpu.CompilerParams(vmem_limit_bytes=40 << 20),
+        name="attention_gradients",
+    )(q, kv, grad, lengths)
+
+
+def lane_rope(row0, rows, freq, lengths_ref):
+    shape = (rows, 2 * HEAD)
+    row = row0 + lax.broadcasted_iota(jnp.int32, shape, 0)
+    position = row - sequence_starts(row0, shape, lengths_ref)
+    turned = position.astype(F32) * freq
+    lane = lax.broadcasted_iota(jnp.int32, shape, 1)
+    first = lax.rem(lane, HEAD) < HEAD // 2
+    sine = jnp.sin(turned)
+    return jnp.cos(turned), jnp.where(first, -sine, sine)
+
+
+def lane_swap(x):
+    half = HEAD // 2
+    lane = lax.broadcasted_iota(jnp.int32, x.shape, 1)
+    first = lax.rem(lane, HEAD) < half
+    return jnp.where(first, pltpu.roll(x, 2 * HEAD - half, 1), pltpu.roll(x, half, 1))
+
+
+def keys_only(cosine, sine):
+    lane = lax.broadcasted_iota(jnp.int32, cosine.shape, 1)
+    return jnp.where(lane < HEAD, cosine, 1.0), jnp.where(lane < HEAD, sine, 0.0)
+
+
+def attention_backward(
+    branch_grad, output_weight, attention, q, kv, normed, q_weight, kv_weight, lengths, freq
+):
+    total, q_cols = q.shape
+    width = normed.shape[1]
+    block = 256
+
+    def kernel(
+        bg_ref, wo_ref, a_ref, q_ref, kv_ref, n_ref, qw_ref, kvw_ref, len_ref, freq_ref,
+        dn_ref, dqw_ref, dkvw_ref, dwo_ref, g_ref, dq_ref, dk_ref, dv_ref, pq_ref, pkv_ref,
+    ):
+        for i in range(total // block):
+            rows = pl.ds(i * block, block)
+            g_ref[rows, :] = mm_t(bg_ref[rows, :], wo_ref[...]).astype(BF16)
+        attend_back(
+            q_cols // HEAD, block, q_ref, kv_ref, g_ref, len_ref, dq_ref, dk_ref, dv_ref
+        )
+        for i in range(total // block):
+            rows = pl.ds(i * block, block)
+            cosine, sine = lane_rope(i * block, block, freq_ref[...], len_ref)
+            for j in range(q_cols // (2 * HEAD)):
+                lanes = slice(j * 2 * HEAD, (j + 1) * 2 * HEAD)
+                x = dq_ref[rows, lanes]
+                pq_ref[rows, lanes] = (x * cosine - lane_swap(x) * sine).astype(BF16)
+            cosine, sine = keys_only(cosine, sine)
+            x = jnp.concatenate([dk_ref[rows, :], dv_ref[rows, :]], axis=1)
+            pkv_ref[rows, :] = (x * cosine - lane_swap(x) * sine).astype(BF16)
+            dn_ref[rows, :] = (
+                mm_t(pq_ref[rows, :], qw_ref[...]) + mm_t(pkv_ref[rows, :], kvw_ref[...])
+            ).astype(BF16)
+        for i in range(width // 512):
+            cols = slice(i * 512, (i + 1) * 512)
+            dqw_ref[cols, :] = t_mm(n_ref[:, cols], pq_ref[...]).astype(BF16)
+            dkvw_ref[cols, :] = t_mm(n_ref[:, cols], pkv_ref[...]).astype(BF16)
+            dwo_ref[:, cols] = t_mm(a_ref[...], bg_ref[:, cols]).astype(BF16)
+
+    return pl.pallas_call(
+        kernel,
+        out_shape=(
+            jax.ShapeDtypeStruct((total, width), BF16),
+            jax.ShapeDtypeStruct((width, q_cols), BF16),
+            jax.ShapeDtypeStruct((width, 2 * HEAD), BF16),
+            jax.ShapeDtypeStruct((q_cols, width), BF16),
+        ),
+        in_specs=[VMEM] * 8 + [SMEM, VMEM],
+        out_specs=[VMEM] * 4,
+        scratch_shapes=[
+            pltpu.VMEM((total, q_cols), BF16),
+            pltpu.VMEM((total, q_cols), F32),
+            pltpu.VMEM((total, HEAD), F32),
+            pltpu.VMEM((total, HEAD), F32),
+            pltpu.VMEM((total, q_cols), BF16),
+            pltpu.VMEM((total, 2 * HEAD), BF16),
+        ],
+        compiler_params=pltpu.CompilerParams(vmem_limit_bytes=56 << 20),
+        cost_estimate=pl.CostEstimate(flops=30_000_000_000, bytes_accessed=30 << 20, transcendentals=total * total),
+        name="attention_backward",
+    )(branch_grad, output_weight, attention, q, kv, normed, q_weight, kv_weight, lengths, freq)
+
+
+def ffn_rows(nf, dg, wg, wu, wd):
+    gate, up, act_grad = mm(nf, wg), mm(nf, wu), mm_t(dg, wd)
+    sigmoid = 1.0 / (1.0 + jnp.exp(-gate))
+    silu = gate * sigmoid
+    activated = (silu * up).astype(BF16)
+    gate_grad = (act_grad * up * sigmoid * (1.0 + gate * (1.0 - sigmoid))).astype(BF16)
+    return activated, gate_grad, (act_grad * silu).astype(BF16)
+
+
+def ffn_own(group, nf, dg_all, wg, wu, wd, groups):
+    total, width = nf.shape
+    cols = wg.shape[1]
+    block = 256
+
+    def kernel(g_ref, nf_ref, dg_ref, wg_ref, wu_ref, wd_ref, na_ref, act_ref, gg_ref, ug_ref, dn_ref):
+        nf = nf_ref[...]
+        act, gg, ug = ffn_rows(nf, dg_ref[0], wg_ref[...], wu_ref[...], wd_ref[...])
+        na_ref[0], act_ref[0], gg_ref[0], ug_ref[0] = nf, act, gg, ug
+        dn_ref[...] = (mm_t(gg, wg_ref[...]) + mm_t(ug, wu_ref[...])).astype(BF16)
+
+    mine = pl.BlockSpec((1, block, width), lambda i, g: (g[0], i, 0))
+    hid = pl.BlockSpec((1, block, cols), lambda i, g: (g[0], i, 0))
+    plain = pl.BlockSpec((block, width), lambda i, g: (i, 0))
+    whole = [
+        pl.BlockSpec(w.shape, lambda i, g: (0, 0), pipeline_mode=pl.Buffered(1)) for w in (wg, wu, wd)
+    ]
+    hidden = jax.ShapeDtypeStruct((groups, total, cols), BF16)
+    return pl.pallas_call(
+        kernel,
+        grid_spec=pltpu.PrefetchScalarGridSpec(
+            num_scalar_prefetch=1,
+            grid=(total // block,),
+            in_specs=[plain, mine] + whole,
+            out_specs=[mine, hid, hid, hid, plain],
+        ),
+        out_shape=(
+            jax.ShapeDtypeStruct((groups, total, width), BF16),
+            hidden,
+            hidden,
+            hidden,
+            jax.ShapeDtypeStruct((total, width), BF16),
+        ),
+        compiler_params=pltpu.CompilerParams(vmem_limit_bytes=56 << 20),
+        cost_estimate=pl.CostEstimate(
+            flops=10 * total * width * cols, bytes_accessed=40 << 20, transcendentals=total * cols
+        ),
+        name="ffn_own",
+    )(group, nf, dg_all, wg, wu, wd)
+
+
+def ffn_other(where, held, fetched, dg_all, wg, wu, wd, filled):
+    groups, total, width = dg_all.shape
+    cols = wg.shape[1]
+    block = 256
+    per_half = total // 2 // block
+
+    def kernel(
+        w_ref, held_ref, fetched_ref, dg_ref, wg_ref, wu_ref, wd_ref, *rest
+    ):
+        na_ref, act_ref, gg_ref, ug_ref, nf_ref = rest[4:]
+        i = pl.program_id(0)
+
+        @pl.when(i < per_half)
+        def _():
+            nf_ref[...] = held_ref[...]
+
+        @pl.when(i >= per_half)
+        def _():
+            nf_ref[...] = fetched_ref[...]
+
+        nf = nf_ref[...]
+        act, gg, ug = ffn_rows(nf, dg_ref[0], wg_ref[...], wu_ref[...], wd_ref[...])
+        na_ref[0], act_ref[0], gg_ref[0], ug_ref[0] = nf, act, gg, ug
+
+    def row(i, w):
+        half = jnp.where(i < per_half, w[1], 1 - w[1])
+        return half * per_half + lax.rem(i, per_half)
+
+    mine = pl.BlockSpec((1, block, width), lambda i, w: (w[0], row(i, w), 0))
+    hid = pl.BlockSpec((1, block, cols), lambda i, w: (w[0], row(i, w), 0))
+    first = pl.BlockSpec((block, width), lambda i, w: (jnp.minimum(i, per_half - 1), 0))
+    last = pl.BlockSpec((block, width), lambda i, w: (jnp.maximum(i - per_half, 0), 0))
+    whole = [
+        pl.BlockSpec(w.shape, lambda i, g: (0, 0), pipeline_mode=pl.Buffered(1)) for w in (wg, wu, wd)
+    ]
+    hidden = jax.ShapeDtypeStruct((groups, total, cols), BF16)
+    return pl.pallas_call(
+        kernel,
+        grid_spec=pltpu.PrefetchScalarGridSpec(
+            num_scalar_prefetch=1,
+            grid=(2 * per_half,),
+            in_specs=[first, last, mine] + whole + [pl.BlockSpec(memory_space=pl.ANY)] * 4,
+            out_specs=[mine, hid, hid, hid],
+            scratch_shapes=[pltpu.VMEM((block, width), BF16)],
+        ),
+        out_shape=(jax.ShapeDtypeStruct((groups, total, width), BF16), hidden, hidden, hidden),
+        input_output_aliases={7: 0, 8: 1, 9: 2, 10: 3},
+        compiler_params=pltpu.CompilerParams(vmem_limit_bytes=56 << 20),
+        cost_estimate=pl.CostEstimate(
+            flops=6 * total * width * cols, bytes_accessed=40 << 20, transcendentals=total * cols
+        ),
+        name="ffn_other",
+    )(where, held, fetched, dg_all, wg, wu, wd, *filled)
+
+
+def weight_grad(left, right):
+    groups, total, m = left.shape
+    n = right.shape[2]
+    block = 512
+    steps = groups * total // block
+
+    def kernel(l_ref, r_ref, o_ref, acc):
+        k = pl.program_id(0)
+        term = t_mm(l_ref[...], r_ref[...])
+
+        @pl.when(k == 0)
+        def _():
+            acc[...] = term
+
+        @pl.when(k > 0)
+        def _():
+            acc[...] += term
+
+        @pl.when(k == steps - 1)
+        def _():
+            o_ref[...] = acc[...].astype(o_ref.dtype)
+
+    return pl.pallas_call(
+        kernel,
+        grid=(steps,),
+        in_specs=[
+            pl.BlockSpec((block, m), lambda k: (k, 0)),
+            pl.BlockSpec((block, n), lambda k: (k, 0)),
+        ],
+        out_specs=pl.BlockSpec((m, n), lambda k: (0, 0), pipeline_mode=pl.Buffered(1)),
+        out_shape=jax.ShapeDtypeStruct((m, n), BF16),
+        scratch_shapes=[pltpu.VMEM((m, n), F32)],
+        compiler_params=pltpu.CompilerParams(vmem_limit_bytes=56 << 20),
+        cost_estimate=pl.CostEstimate(
+            flops=2 * groups * total * m * n, bytes_accessed=2 * groups * total * (m + n), transcendentals=0
+        ),
+        name="weight_grad",
+    )(left.reshape(groups * total, m), right.reshape(groups * total, n))
+
+
+def per_device_plane(
+    tokens, attn_gain, query_weight, key_weight, value_weight, output_weight, ffn_gain,
+    gate_weight, up_weight, down_weight, dealing, lengths, cotangent,
+):
+    n = 8
+    here = lax.axis_index("shard")
+    group = lax.axis_index("rep")
+    replicas = lax.axis_size("rep")
+    local, width = tokens.shape
+    total = local * n
+    rows = query_weight.shape[0]
+    q_cols = query_weight.shape[1] // n
+    ff_cols = gate_weight.shape[1] // n
+    core = lax.rem(here, 2)
+    half = HEAD // 2
+    freq = ROPE_BASE ** (-(jnp.arange(half, dtype=F32) * 2.0) / (2.0 * half))
+    freq = jnp.tile(freq, 4)[None, :]
+
+    (
+        normed, q, kv, attention, q_weight, kv_weight, gate_cols, up_cols,
+        middle, normed_ffn, down_grads, cot_own,
+    ) = front(
+        tokens, attn_gain, query_weight, key_weight, value_weight, output_weight, ffn_gain,
+        gate_weight, up_weight, dealing, lengths, cotangent, freq, replicas,
+    )
+
+    held = lax.dynamic_slice_in_dim(normed_ffn, core * (total // 2), total // 2)
+    onward = [(i, (i + 1) % replicas) for i in range(replicas)]
+    beside = [(i, i ^ 1) for i in range(n)]
+    arrivals = []
+    for hop in range(1, replicas):
+        held = lax.ppermute(held, "rep", onward)
+        where = jnp.stack([lax.rem(group + replicas - hop, replicas), core]).astype(jnp.int32)
+        arrivals.append((where, held, lax.ppermute(held, "shard", beside)))
+
+    *filled, normed_ffn_part = ffn_own(
+        group.astype(jnp.int32)[None], normed_ffn, down_grads, gate_cols, up_cols, down_weight, replicas
+    )
+    activated = lax.dynamic_index_in_dim(filled[1], group, keepdims=False)
+    middle_grad, ffn_gain_part, branch_grad = pull_gather(
+        normed_ffn_part, middle, ffn_gain, cot_own, 2
+    )
+    branch_grad = branch_grad.reshape(total, width)
+    for where, from_ring, from_core in arrivals:
+        filled = ffn_other(
+            where, from_ring, from_core, down_grads, gate_cols, up_cols, down_weight, filled
+        )
+    all_normed, all_activated, all_gate_grad, all_up_grad = filled
+
+    normed_part, q_grad, kv_grad, output_grad = attention_backward(
+        branch_grad, output_weight, attention, q, kv, normed, q_weight, kv_weight, lengths, freq
+    )
+    tokens_grad, attn_gain_part = pull_tokens(normed_part, tokens, attn_gain, middle_grad, 3)
+
+    packed = jnp.arange(total, dtype=jnp.int32)
+    dealt = (dealing[0][:, None] == packed[None, :]).astype(BF16)
+    own_rows = (packed[:, None] - here * local == jnp.arange(local, dtype=jnp.int32)[None, :]).astype(BF16)
+    layer_output = scatter_rows(
+        mm(
+            dealt,
+            (
+                RESIDUAL_SCALE * mm(activated, down_weight)
+                + mm(own_rows, middle.astype(BF16))
+            ).astype(BF16),
+        ).astype(BF16)
+    )
+
+    gate_part = exchange(weight_grad(all_normed, all_gate_grad).reshape(n, rows, ff_cols))
+    up_part = exchange(weight_grad(all_normed, all_up_grad).reshape(n, rows, ff_cols))
+    down_part = weight_grad(all_activated, down_grads)
+    output_part = rep_sum(output_grad)
+    qkv_part = rep_sum(
+        exchange(jnp.concatenate([q_grad, kv_grad], axis=1).reshape(n, rows, q_cols + 2 * HEAD))
+    )
+
+    def join(blocks):
+        return blocks.transpose(1, 0, 2).reshape(rows, -1).astype(F32)
+
+    gains = lax.all_gather(
+        jnp.concatenate([attn_gain_part, ffn_gain_part]), ("rep", "shard"), axis=0
+    ).sum(axis=0)
+    return (
+        layer_output,
+        tokens_grad,
+        gains[0],
+        join(qkv_part[:, :, :q_cols]),
+        join(qkv_part[:, :, q_cols : q_cols + HEAD]),
+        join(qkv_part[:, :, q_cols + HEAD :]),
+        output_part.astype(F32),
+        gains[1],
+        join(gate_part),
+        join(up_part),
+        down_part.astype(F32),
+    )
 
 
 def per_device(
@@ -512,7 +1013,6 @@
 
     packed = jnp.arange(total, dtype=jnp.int32)
     segment, position = places(packed, lengths[0])
-    seg_col, seg_row = segment[:, None], segment[None, :]
     cos_q, sin_q = rope_tables(position, q_cols)
     cos_k, sin_k = cos_q[:, :HEAD], sin_q[:, :HEAD]
     dealt = (dealing[0][:, None] == packed[None, :]).astype(BF16)
@@ -523,8 +1023,6 @@
     def head_blocks(weight):
         blocks = weight.reshape(rows, KV_HEADS, HEAD).transpose(1, 0, 2)
         return jnp.repeat(blocks, copies, axis=0)
-
-    fast = n == 8
 
     spread_cotangent = lax.all_gather(cotangent, ("rep", "shard"), axis=0, tiled=True)
     all_dealing = lax.all_gather(dealing, "rep", axis=0, tiled=True)
@@ -537,22 +1035,15 @@
     gate_cols = exchange(column_blocks(gate_weight, ff_cols)).reshape(width, ff_cols)
     up_cols = exchange(column_blocks(up_weight, ff_cols)).reshape(width, ff_cols)
 
-    if fast:
-        normed = norm_gather(tokens, attn_gain, True, 0)
-    else:
-        normed = gather_rows(rms_scale(tokens.astype(F32), attn_gain).astype(BF16))
+    normed = gather_rows(rms_scale(tokens.astype(F32), attn_gain).astype(BF16))
     pre = mm(normed, qkv)
     queries = rotate(pre[:, :q_cols], cos_q, sin_q).astype(BF16)
     keys = rotate(pre[:, q_cols : q_cols + HEAD], cos_k, sin_k).astype(BF16)
     values = pre[:, q_cols + HEAD :].astype(BF16)
-    attention = attention_forward(queries, keys, values, seg_col, seg_row)
-    if fast:
-        middle, normed_ffn = branch_middle_gather(attention, output_weight, tokens, ffn_gain, 1)
-        normed_ffn = normed_ffn.reshape(total, width)
-    else:
-        branch = scatter_rows(mm(attention, output_weight).astype(BF16))
-        middle = tokens.astype(F32) + RESIDUAL_SCALE * branch.astype(F32)
-        normed_ffn = gather_rows(rms_scale(middle, ffn_gain).astype(BF16))
+    attention = attention_forward(queries, jnp.concatenate([keys, values], axis=1), lengths)
+    branch = scatter_rows(mm(attention, output_weight).astype(BF16))
+    middle = tokens.astype(F32) + RESIDUAL_SCALE * branch.astype(F32)
+    normed_ffn = gather_rows(rms_scale(middle, ffn_gain).astype(BF16))
     own_normed = lax.dynamic_slice_in_dim(normed_ffn, own, local)
     all_normed = lax.all_gather(own_normed, ("rep", "shard"), axis=0, tiled=True)
 
@@ -582,17 +1073,11 @@
         normed_ffn, lax.dynamic_slice_in_dim(act_grad_all, group * total, total)
     )
     normed_ffn_part = (mm_t(gate_grad, gate_cols) + mm_t(up_grad, up_cols)).astype(BF16)
-    if fast:
-        middle_grad, ffn_gain_part, branch_grad = pull_gather(
-            normed_ffn_part, middle, ffn_gain, out_grad, 2
-        )
-        branch_grad = branch_grad.reshape(total, width)
-    else:
-        middle_part, ffn_gain_part = norm_pull(
-            middle, ffn_gain, scatter_rows(normed_ffn_part).astype(F32)
-        )
-        middle_grad = out_grad + middle_part
-        branch_grad = gather_rows((RESIDUAL_SCALE * middle_grad).astype(BF16))
+    middle_part, ffn_gain_part = norm_pull(
+        middle, ffn_gain, scatter_rows(normed_ffn_part).astype(F32)
+    )
+    middle_grad = out_grad + middle_part
+    branch_grad = gather_rows((RESIDUAL_SCALE * middle_grad).astype(BF16))
 
     own_columns = lax.dynamic_slice_in_dim(dealt, own, local, axis=1)
     layer_output = scatter_rows(
@@ -603,7 +1088,9 @@
     )
 
     attention_grad = mm_t(branch_grad, output_weight).astype(BF16)
-    dq, dk, dv = attention_backward(queries, keys, values, attention_grad, seg_col, seg_row)
+    dq, dk, dv = attention_gradients(
+        queries, jnp.concatenate([keys, values], axis=1), attention_grad, lengths
+    )
     pre_grad = jnp.concatenate(
         [
             unrotate(dq, cos_q, sin_q).astype(BF16),
@@ -613,13 +1100,10 @@
         axis=1,
     )
     normed_part = mm_t(pre_grad, qkv).astype(BF16)
-    if fast:
-        tokens_grad, attn_gain_part = pull_tokens(normed_part, tokens, attn_gain, middle_grad, 3)
-    else:
-        hidden_part, attn_gain_part = norm_pull(
-            tokens.astype(F32), attn_gain, scatter_rows(normed_part).astype(F32)
-        )
-        tokens_grad = middle_grad + hidden_part
+    hidden_part, attn_gain_part = norm_pull(
+        tokens.astype(F32), attn_gain, scatter_rows(normed_part).astype(F32)
+    )
+    tokens_grad = middle_grad + hidden_part
 
     activated, gate_grad, up_grad = ffn(all_normed, act_grad_all)
     gate_part = exchange(t_mm(all_normed, gate_grad).astype(BF16).reshape(n, rows, ff_cols))
@@ -655,7 +1139,7 @@
     both = P(("rep", "shard"), None)
     rowed = P("shard", None)
     return jax.shard_map(
-        per_device,
+        per_device_plane if mesh.shape["shard"] == 8 else per_device,
         mesh=mesh,
         in_specs=(
             both, P(), rowed, rowed, rowed, rowed, P(), rowed, rowed, rowed,

time: 840 us -> 883 us (1.051)
  Pallas kernels: 198 us -> 642 us
  matrix products: 271 us -> 21.1 us
  waiting for transfers between devices: 135 us -> 59.4 us
  local copies, waits for them, and re-layouts: 78.3 us -> 28 us
  blocking collectives: 52.9 us -> 38.9 us
  starting transfers between devices: 45.5 us -> 34 us
    pallas_call x4 -> x9, Pallas kernels: 124 us -> 520 us  [the longest x1 307 us: front(): pl.pallas_call(kernel, out_shape=(rows8, jax.ShapeDtypeStruct((total, q_c...]
    dot_general x11 -> x0, matrix products: 184 us -> none  [the longest x5 102 us: t_mm(): lax.dot_general(a, b, (((0,), (0,)), ((), ())), preferred_element_type=F32)]
    all_to_all x6 -> x3, waiting for transfers between devices: 117 us -> 0.01 us  [exchange(): lax.all_to_all(blocks, 'shard', split_axis=0, concat_axis=0, tiled=True)]
    dot_general x7 -> x2, matrix products: 87.5 us -> 21.1 us  [mm(): return jnp.dot(a, b, preferred_element_type=F32)]
    pallas_call x1, Pallas kernels: 29.5 us -> 75.4 us  [pull_tokens(): pl.pallas_call(kernel, out_shape=(jax.ShapeDtypeStruct((rows, width), F32...]
    psum x1 -> x0, blocking collectives: 39.7 us -> none  [per_device(): lax.psum(jnp.concatenate([attn_gain_part, ffn_gain_part]), ('rep', 'shard'))]
    ppermute x0 -> x6, waiting for transfers between devices: none -> 39.6 us  [the longest x3 39.6 us: per_device_plane(): held = lax.ppermute(held, 'rep', onward)]
    all_gather x1, blocking collectives: 13.2 us -> 38.9 us  [per_device_plane(): lax.all_gather(jnp.concatenate([attn_gain_part, ffn_gain_part]), ('rep',...]
  transfers between devices with their start and end apart: 15 -> 16, of which waited for: 5 -> 4; matrix products, arithmetic and copies ran while one was open for 45% -> 8% of each run, Pallas kernels for 24% -> 38%
where the time goes in v3:
time: 883 us; the launch traced here: 873 us
  Pallas kernels  642 us (73%)
  waiting for transfers between devices  59.4 us (7%)
  blocking collectives  38.9 us (4%)
  other arithmetic  35.3 us (4%)
  starting transfers between devices  34 us (4%)
  local copies, waits for them, and re-layouts  28 us (3%)
  matrix products  21.1 us (2%)
  between operations  14.8 us (2%)
    pallas_call x1, Pallas kernels, front(): pl.pallas_call(kernel, out_shape=(rows8, jax.ShapeDtypeStruct((total, q_c...  307 us
    pallas_call x3, Pallas kernels, weight_grad(): pl.pallas_call(kernel, grid=(steps,), in_specs=[pl.BlockSpec((block, m),...  89.2 us
    pallas_call x1, Pallas kernels, pull_tokens(): pl.pallas_call(kernel, out_shape=(jax.ShapeDtypeStruct((rows, width), F32...  75.4 us
    pallas_call x3, Pallas kernels, ffn_other(): pl.pallas_call(kernel, grid_spec=pltpu.PrefetchScalarGridSpec(num_scalar_...  66.9 us
    pallas_call x1, Pallas kernels, pull_gather(): pl.pallas_call(kernel, out_shape=(jax.ShapeDtypeStruct((rows, width), F32...  46.4 us
    ppermute x3, waiting for transfers between devices, per_device_plane(): held = lax.ppermute(held, 'rep', onward)  39.6 us
    all_gather x1, blocking collectives, per_device_plane(): lax.all_gather(jnp.concatenate([attn_gain_part, ffn_gain_part]), ('rep',...  38.9 us
    pallas_call x1, Pallas kernels, ffn_own(): pl.pallas_call(kernel, grid_spec=pltpu.PrefetchScalarGridSpec(num_scalar_...  29.8 us
  transfers between devices with their start and end apart: 16, of which 4 were waited for; matrix products, arithmetic and copies ran while one was open for 8% of the time, Pallas kernels for 38%

profile of v3, /device:TPU:0, one launch (start us, length us, event | category | flops | bytes accessed | tf_op | source)
XLA Modules:
  0.0 873.4 jit_solution(13590722428661280237)
XLA Ops:
  7.8 306.6 %front.1 = (bf16[8,128,2048]{2,1,0:T(8,128)(2,1)}, bf16[1024,256]{1,0:T(8,128)(2,1)}, bf16[1024,128]{1,0:T(8,128)(2,1)}, bf16[1024,256]{1,0:T(8,128)(2,1)}, bf16...) custom-call(bf16[128,2048]{1,0:T(8,128)(2,1)} %h_ref.1, ...), custom_call_target="tpu_custom_call" | custom-call | flops 149999992832 | bytes 52428800 | tf_op jit(solution)/shard_map/front/pallas_call | solution.py:429
  319.2 29.8 %ffn_own.1 = (bf16[4,1024,2048]{2,1,0:T(8,128)(2,1)}, bf16[4,1024,1024]{2,1,0:T(8,128)(2,1)}, bf16[4,1024,1024]{2,1,0:T(8,128)(2,1)}, bf16[4,1024,1024]{2,1,0:T(8,128)(2,1)}, bf16[1024,2048]{1,0:T(8,128)(2,1)}) custom-call(s32[1]{0:T(128)} %bitcast.1.g_ref, bf16[1024,2048]{1,0:T(8,128)(2,1)} %bitcast.78, bf16[4,1024,2048]{2,1,0:T(8,128)(2,1)} %get-tuple-element.50.dg_ref, ...), custom_call_target="tpu_custom_call" | custom-call | flops 21474836480 | bytes 41943040 | tf_op jit(solution)/shard_map/ffn_own/pallas_call | solution.py:775
  349.0 46.4 %pull_gather.1 = (f32[128,2048]{1,0:T(8,128)S(1)}, f32[1,2048]{1,0:T(1,128)S(1)}, bf16[8,128,2048]{2,1,0:T(8,128)(2,1)S(1)}) custom-call(bf16[1024,2048]{1,0:T(8,128)(2,1)} %get-tuple-element.55.p_ref, f32[128,2048]{1,0:T(8,128)S(1)} %copy-done.1, f32[1,2048]{1,0:T(1,128)S(1)} %bitcast.51, bf16[128,2048]{1,0:T(8,128)(2,1)S(1)} %copy-done.3), custom_call_target="tpu_custom_call" | custom-call | flops 10485760 | bytes 13107200 | tf_op jit(solution)/shard_map/pull_gather/pallas_call | solution.py:510
  399.2 27.6 %attention_backward.1 = (bf16[1024,2048]{1,0:T(8,128)(2,1)}, bf16[2048,256]{1,0:T(8,128)(2,1)}, bf16[2048,128]{1,0:T(8,128)(2,1)}, bf16[256,2048]{1,0:T(8,128)(2,1)}) custom-call(bf16[1024,2048]{1,0:T(8,128)(2,1)} %bitcast.54, bf16[256,2048]{1,0:T(8,128)(2,1)} %wo_ref.3, bf16[1024,256]{1,0:T(8,128)(2,1)} %get-tuple-element.58.a_ref, ...), custom_call_target="tpu_custom_call" | custom-call | flops 30000001024 | bytes 31457280 | tf_op jit(solution)/shard_map/attention_backward/pallas_call | solution.py:724
  434.9 4.3 all-to-all-start
  439.3 4.7 fusion.5
  444.3 3.9 collective-permute-done.7.held_ref
  448.6 16.4 %fusion.1 = bf16[1024,2048]{1,0:T(8,128)(2,1)} fusion(s32[1024]{0:T(1024)S(1)} %bitcast.81, f32[1024,2048]{1,0:T(8,128)} %fusion.5, bf16[1024,2048]{1,0:T(8,128)(2,1)} %wd_ref.7, bf16[4,1024,1024]{2,1,0:T(8,128)(2,1)} %get-tuple-element.53.rest_1_, s32[]{:T(128)S(6)} %select_n.23), kind=kOutput, calls=%fused_computation.5 | convolution fusion | flops 8599371776 | bytes 18878468 | tf_op jit(solution)/shard_map/dot_general | solution.py:23
  472.5 7.3 collective-permute-start
  479.8 35.7 %collective-permute-done.8.held_ref = bf16[512,2048]{1,0:T(8,128)(2,1)S(1)} collective-permute-done((bf16[512,2048]{1,0:T(8,128)(2,1)}, bf16[512,2048]{1,0:T(8,128)(2,1)S(1)}, u32[]{:S(2)}, u32[]{:S(2)}) %collective-permute-start.8) | collective-permute-done | bytes 2097184 | tf_op jit(solution)/shard_map/ppermute | solution.py:924
  515.5 22.3 %ffn_other.3 = (bf16[4,1024,2048]{2,1,0:T(8,128)(2,1)}, bf16[4,1024,1024]{2,1,0:T(8,128)(2,1)}, bf16[4,1024,1024]{2,1,0:T(8,128)(2,1)}, bf16[4,1024,1024]{2,1,0:T(8,128)(2,1)}) custom-call(s32[2]{0:T(128)} %pad_add_fusion.2.w_ref, ...), custom_call_target="tpu_custom_call", output_to_operand_aliasing={{0}: (7, {}), {1}: (8, {}), {2}: (9, {}), {3}: (10, {})} | custom-call | flops 12884901888 | bytes 41943040 | tf_op jit(solution)/shard_map/ffn_other/pallas_call | solution.py:834
  537.8 22.3 %ffn_other.4 = (bf16[4,1024,2048]{2,1,0:T(8,128)(2,1)}, bf16[4,1024,1024]{2,1,0:T(8,128)(2,1)}, bf16[4,1024,1024]{2,1,0:T(8,128)(2,1)}, bf16[4,1024,1024]{2,1,0:T(8,128)(2,1)}) custom-call(s32[2]{0:T(128)} %pad_add_fusion.1.w_ref, ...), custom_call_target="tpu_custom_call", output_to_operand_aliasing={{0}: (7, {}), {1}: (8, {}), {2}: (9, {}), {3}: (10, {})} | custom-call | flops 12884901888 | bytes 41943040 | tf_op jit(solution)/shard_map/ffn_other/pallas_call | solution.py:834
  561.5 22.3 %ffn_other.5 = (bf16[4,1024,2048]{2,1,0:T(8,128)(2,1)}, bf16[4,1024,1024]{2,1,0:T(8,128)(2,1)}, bf16[4,1024,1024]{2,1,0:T(8,128)(2,1)}, bf16[4,1024,1024]{2,1,0:T(8,128)(2,1)}) custom-call(s32[2]{0:T(128)} %pad_add_fusion.w_ref, bf16[512,2048]{1,0:T(8,128)(2,1)} %copy-done.8, ...), custom_call_target="tpu_custom_call", output_to_operand_aliasing={{0}: (7, {}), {1}: (8, {}), {2}: (9, {}), {3}: (10, {})} | custom-call | flops 12884901888 | bytes 41943040 | tf_op jit(solution)/shard_map/ffn_other/pallas_call | solution.py:834
  583.8 29.9 %weight_grad.4 = bf16[2048,1024]{1,0:T(8,128)(2,1)} custom-call(bf16[4096,2048]{1,0:T(8,128)(2,1)} %bitcast.56, bf16[4096,1024]{1,0:T(8,128)(2,1)} %bitcast.60), custom_call_target="tpu_custom_call" | custom-call | flops 17179869184 | bytes 25165824 | tf_op jit(solution)/shard_map/weight_grad/pallas_call | solution.py:875
  613.7 4.6 all-to-all-start.2
  625.8 75.4 %pull_tokens.1 = (f32[128,2048]{1,0:T(8,128)S(1)}, f32[1,2048]{1,0:T(1,128)S(1)}) custom-call(bf16[1024,2048]{1,0:T(8,128)(2,1)S(1)} %copy-done, bf16[128,2048]{1,0:T(8,128)(2,1)S(1)} %copy-done.2, f32[1,2048]{1,0:T(1,128)S(1)} %bitcast.53, f32[128,2048]{1,0:T(8,128)S(1)} %get-tuple-element.65.mg_ref), custom_call_target="tpu_custom_call" | custom-call | flops 10485760 | bytes 13107200 | tf_op jit(solution)/shard_map/pull_tokens/pallas_call | solution.py:546
  701.2 38.9 %all-gather.1 = f32[32,2,2048]{2,1,0:T(2,128)S(1)} all-gather(f32[1,2,2048]{2,1,0:T(2,128)S(1)} %maximum_bitcast_fusion), channel_id=2, replica_groups=mesh['rep'=4,'shard'=8] {'rep','shard'}, dimensions={0}, use_global_device_ids=true | all-gather | bytes 540672 | tf_op jit(solution)/shard_map/all_gather | solution.py:971
  748.3 29.7 %weight_grad.3 = bf16[2048,1024]{1,0:T(8,128)(2,1)} custom-call(bf16[4096,2048]{1,0:T(8,128)(2,1)} %bitcast.57, bf16[4096,1024]{1,0:T(8,128)(2,1)} %bitcast.59), custom_call_target="tpu_custom_call" | custom-call | flops 17179869184 | bytes 25165824 | tf_op jit(solution)/shard_map/weight_grad/pallas_call | solution.py:875
  777.9 4.8 all-to-all-start.1
  784.8 18.6 %collective-permute-done.2 = bf16[8,256,384]{1,2,0:T(8,128)(2,1)} collective-permute-done((bf16[8,256,384]{1,2,0:T(8,128)(2,1)}, bf16[8,256,384]{1,2,0:T(8,128)(2,1)}, u32[]{:S(2)}, u32[]{:S(2)}) %collective-permute-start.2) | collective-permute-done | bytes 1572896 | tf_op jit(solution)/shard_map/ppermute | solution.py:101
  813.8 29.7 %weight_grad.5 = bf16[1024,2048]{1,0:T(8,128)(2,1)} custom-call(bf16[4096,1024]{1,0:T(8,128)(2,1)} %bitcast.58, bf16[4096,2048]{1,0:T(8,128)(2,1)} %bitcast.55), custom_call_target="tpu_custom_call" | custom-call | flops 17179869184 | bytes 25165824 | tf_op jit(solution)/shard_map/weight_grad/pallas_call | solution.py:875
  843.5 6.7 convert_element_type.129
  853.4 4.2 copy.54
  860.9 4.2 copy.53
  (75 shorter events, 62.4 us)
Async XLA Ops:
  317.6 79.8 %collective-permute-start.6 = (bf16[512,2048]{1,0:T(8,128)(2,1)}, bf16[512,2048]{1,0:T(8,128)(2,1)}, u32[]{:S(2)}, u32[]{:S(2)}) collective-permute-start(bf16[512,2048]{1,0:T(8,128)(2,1)} %constant_dynamic-slice_fusion), channel_id=1, source_target_pairs={{0,8},{8,16},{16,24},{24,0},{1,9},{9,17},{17,25},{25,1},{2,10},{10... | collective-permute-start | bytes 6291464 | tf_op jit(solution)/shard_map/ppermute | solution.py:924
  319.2 29.8 %copy-start.1 = (f32[128,2048]{1,0:T(8,128)S(1)}, f32[128,2048]{1,0:T(8,128)}, u32[]{:S(2)}) copy-start(f32[128,2048]{1,0:T(8,128)} %get-tuple-element.54.m_ref) | copy-start | bytes 3145732
  319.2 29.8 %copy-start.3 = (bf16[128,2048]{1,0:T(8,128)(2,1)S(1)}, bf16[128,2048]{1,0:T(8,128)(2,1)}, u32[]{:S(2)}) copy-start(bf16[128,2048]{1,0:T(8,128)(2,1)} %get-tuple-element.56.g_ref) | copy-start | bytes 1572868
  319.2 29.8 %copy-start.4 = (f32[2048]{0:T(1024)S(1)}, f32[2048]{0:T(1024)}, u32[]{:S(2)}) copy-start(f32[2048]{0:T(1024)} %param.19) | copy-start | bytes 24580
  397.4 50.7 %collective-permute-start.7 = (bf16[512,2048]{1,0:T(8,128)(2,1)}, bf16[512,2048]{1,0:T(8,128)(2,1)}, u32[]{:S(2)}, u32[]{:S(2)}) collective-permute-start(bf16[512,2048]{1,0:T(8,128)(2,1)} %collective-permute-done.6.held_ref), channel_id=1, source_target_pairs={{0,8},{8,16},{16,24},{24,0},{1,9},{9,17},{17,25},{25,1},{2,10},{10... | collective-permute-start | bytes 6291464 | tf_op jit(solution)/shard_map/ppermute | solution.py:924
  426.8 41.2 %collective-permute-start.3 = (bf16[256,2048]{1,0:T(8,128)(2,1)}, bf16[256,2048]{1,0:T(8,128)(2,1)}, u32[]{:S(2)}, u32[]{:S(2)}) collective-permute-start(bf16[256,2048]{1,0:T(8,128)(2,1)} %get-tuple-element.71), channel_id=1, source_target_pairs={{0,8},{24,16},{1,9},{25,17},{2,10},{26,18},{3,11},{27,19},{4,12},{... | collective-permute-start | bytes 3145736 | tf_op jit(solution)/shard_map/ppermute | solution.py:93
  434.9 37.5 %all-to-all-start = ((bf16[8,256,384]{1,2,0:T(8,128)(2,1)}), bf16[8,256,384]{1,2,0:T(8,128)(2,1)}, u32[]{:S(2)}, u32[]{:S(2)}) async-start(bf16[8,256,384]{1,2,0:T(8,128)(2,1)} %copy.47), calls=%async_computation.1 | async-start | bytes 3145728 | tf_op jit(solution)/shard_map/all_to_all | solution.py:85
  439.3 9.3 %copy-start.10 = (s32[1,1024]{1,0:T(1,128)S(1)}, s32[1,1024]{1,0:T(1,128)}, u32[]{:S(2)}) copy-start(s32[1,1024]{1,0:T(1,128)} %deal_ref.1) | copy-start | bytes 12292
  444.0 71.6 %collective-permute-start.11 = (bf16[512,2048]{1,0:T(8,128)(2,1)}, bf16[512,2048]{1,0:T(8,128)(2,1)}, u32[]{:S(2)}, u32[]{:S(2)}) collective-permute-start(bf16[512,2048]{1,0:T(8,128)(2,1)} %collective-permute-done.6.held_ref), channel_id=1, source_target_pairs={{0,1},{1,0},{2,3},{3,2},{4,5},{5,4},{6,7},{7,6},{8,9},{9,8},{10,11... | collective-permute-start | bytes 6291464 | tf_op jit(solution)/shard_map/ppermute | solution.py:926
  448.2 89.7 %collective-permute-start.10 = (bf16[512,2048]{1,0:T(8,128)(2,1)}, bf16[512,2048]{1,0:T(8,128)(2,1)}, u32[]{:S(2)}, u32[]{:S(2)}) collective-permute-start(bf16[512,2048]{1,0:T(8,128)(2,1)} %collective-permute-done.7.held_ref), channel_id=1, source_target_pairs={{0,1},{1,0},{2,3},{3,2},{4,5},{5,4},{6,7},{7,6},{8,9},{9,8},{10,11... | collective-permute-start | bytes 6291464 | tf_op jit(solution)/shard_map/ppermute | solution.py:926
  448.2 67.3 %collective-permute-start.8 = (bf16[512,2048]{1,0:T(8,128)(2,1)}, bf16[512,2048]{1,0:T(8,128)(2,1)S(1)}, u32[]{:S(2)}, u32[]{:S(2)}) collective-permute-start(bf16[512,2048]{1,0:T(8,128)(2,1)} %collective-permute-done.7.held_ref), channel_id=1, source_target_pairs={{0,8},{8,16},{16,24},{24,0},{1,9},{9,17},{17,25},{25,1},{2,10},{10... | collective-permute-start | bytes 6291464 | tf_op jit(solution)/shard_map/ppermute | solution.py:924
  470.8 269.5 %collective-permute-start.4 = (bf16[256,2048]{1,0:T(8,128)(2,1)}, bf16[256,2048]{1,0:T(8,128)(2,1)}, u32[]{:S(2)}, u32[]{:S(2)}) collective-permute-start(bf16[256,2048]{1,0:T(8,128)(2,1)} %add_convert_fusion.4), channel_id=1, source_target_pairs={{8,16},{16,8},{9,17},{17,9},{10,18},{18,10},{11,19},{19,11},{12,20... | collective-permute-start | bytes 3145736 | tf_op jit(solution)/shard_map/ppermute | solution.py:97
  472.5 145.8 %collective-permute-start = (bf16[8,256,384]{1,2,0:T(8,128)(2,1)}, bf16[8,256,384]{1,2,0:T(8,128)(2,1)}, u32[]{:S(2)}, u32[]{:S(2)}) collective-permute-start(bf16[8,256,384]{1,2,0:T(8,128)(2,1)} %all-to-all-done), channel_id=1, source_target_pairs={{0,8},{24,16},{1,9},{25,17},{2,10},{26,18},{3,11},{27,19},{4,12},{... | collective-permute-start | bytes 4718600 | tf_op jit(solution)/shard_map/ppermute | solution.py:93
  515.5 22.3 %copy-start.8 = (bf16[512,2048]{1,0:T(8,128)(2,1)}, bf16[512,2048]{1,0:T(8,128)(2,1)S(1)}, u32[]{:S(2)}) copy-start(bf16[512,2048]{1,0:T(8,128)(2,1)S(1)} %collective-permute-done.8.held_ref) | copy-start | bytes 6291460
  515.5 44.6 %collective-permute-start.9 = (bf16[512,2048]{1,0:T(8,128)(2,1)S(1)}, bf16[512,2048]{1,0:T(8,128)(2,1)S(1)}, u32[]{:S(2)}, u32[]{:S(2)}) collective-permute-start(bf16[512,2048]{1,0:T(8,128)(2,1)S(1)} %collective-permute-done.8.held_ref), channel_id=1, source_target_pairs={{0,1},{1,0},{2,3},{3,2},{4,5},{5,4},{6,7},{7,6},{8,9},{9,8},{10,11... | collective-permute-start | bytes 6291464 | tf_op jit(solution)/shard_map/ppermute | solution.py:926
  613.7 164.3 %all-to-all-start.2 = ((bf16[8,256,1024]{2,1,0:T(8,128)(2,1)}), bf16[8,256,1024]{2,1,0:T(8,128)(2,1)}, u32[]{:S(2)}, u32[]{:S(2)}) async-start(bf16[8,256,1024]{2,1,0:T(8,128)(2,1)} %bitcast.73), calls=%async_computation.3 | async-start | bytes 8388608 | tf_op jit(solution)/shard_map/all_to_all | solution.py:85
  618.2 5.4 copy-start.2
  618.2 5.4 copy-start.5
  618.3 246.9 %reduce-scatter.2.cloned.1.call-start = ((), (), s32[]{:S(2)}) async-start(), calls=%async_computation.4 | async-start | bytes 4718592 | tf_op jit(solution)/shard_map/reduce_scatter | solution.py:81
  621.8 121.8 %collective-permute-start.1 = (bf16[8,256,384]{1,2,0:T(8,128)(2,1)}, bf16[8,256,384]{1,2,0:T(8,128)(2,1)}, u32[]{:S(2)}, u32[]{:S(2)}) collective-permute-start(bf16[8,256,384]{1,2,0:T(8,128)(2,1)} %add_convert_fusion.2), channel_id=1, source_target_pairs={{8,16},{16,8},{9,17},{17,9},{10,18},{18,10},{11,19},{19,11},{12,20... | collective-permute-start | bytes 4718600 | tf_op jit(solution)/shard_map/ppermute | solution.py:97
  623.6 2.2 copy-start
  742.3 41.1 %collective-permute-start.5 = (bf16[256,2048]{1,0:T(8,128)(2,1)S(1)}, bf16[256,2048]{1,0:T(8,128)(2,1)S(1)}, u32[]{:S(2)}, u32[]{:S(2)}) collective-permute-start(bf16[256,2048]{1,0:T(8,128)(2,1)S(1)} %add_convert_fusion.3), channel_id=1, source_target_pairs={{8,0},{16,24},{9,1},{17,25},{10,2},{18,26},{11,3},{19,27},{12,4},{... | collective-permute-start | bytes 3145736 | tf_op jit(solution)/shard_map/ppermute | solution.py:101
  747.0 56.4 %collective-permute-start.2 = (bf16[8,256,384]{1,2,0:T(8,128)(2,1)}, bf16[8,256,384]{1,2,0:T(8,128)(2,1)}, u32[]{:S(2)}, u32[]{:S(2)}) collective-permute-start(bf16[8,256,384]{1,2,0:T(8,128)(2,1)} %add_convert_fusion.1), channel_id=1, source_target_pairs={{8,0},{16,24},{9,1},{17,25},{10,2},{18,26},{11,3},{19,27},{12,4},{... | collective-permute-start | bytes 4718600 | tf_op jit(solution)/shard_map/ppermute | solution.py:101
  777.9 79.7 %all-to-all-start.1 = ((bf16[8,256,1024]{2,1,0:T(8,128)(2,1)}), bf16[8,256,1024]{2,1,0:T(8,128)(2,1)}, u32[]{:S(2)}, u32[]{:S(2)}) async-start(bf16[8,256,1024]{2,1,0:T(8,128)(2,1)} %bitcast.74), calls=%async_computation.2 | async-start | bytes 8388608 | tf_op jit(solution)/shard_map/all_to_all | solution.py:85
  (3 other events, 4.5 us)
Sparse Core Ops, SparseCore 0:
  623.7 77.4 reduce-scatter.1

commit v4 on v3

--- a/solution.py
+++ b/solution.py
@@ -134,6 +134,7 @@
 
 
 GATHER_SEMS = 13
+BULK = (12, 2, 2)
 
 
 def gather_steps(me, out, sems):
@@ -184,9 +185,7 @@
 SCATTER_SEMS = 10
 
 
-def scatter_blocks(
-    me, partial, sib_out, sib_in, acc, x_out, x_in, y_out, y_in, sems, meanwhile=None
-):
+def scatter_steps(me, partial, sib_out, sib_in, acc, x_out, x_in, y_out, y_in, sems):
     core, px, py = (flip(me, mask) for mask in (1, 2, 4))
     half = acc.shape[1] // 2
     masks = (6, 2, 4, 0)
@@ -203,6 +202,7 @@
     for i, mask in enumerate(masks):
         sib_out[i] = partial(flip(core, mask)).astype(BF16)
         inside.append(move(sib_out.at[i], sib_in.at[i], i, core))
+    yield
     for i, mask in enumerate(masks):
         term = partial(flip(me, mask))
         inside[i].wait_recv()
@@ -218,23 +218,29 @@
         if mask == 4:
             y_out[1] = acc[i, high].astype(BF16)
             y_near = move(y_out.at[1], y_in.at[1], 7, py)
+    yield
     x_diag.wait_recv()
     y_out[2] = (acc[2, low] + x_in[0].astype(F32)).astype(BF16)
     y_last = move(y_out.at[2], y_in.at[2], 8, py)
     y_diag.wait_recv()
     x_out[2] = (acc[1, high] + y_in[0].astype(F32)).astype(BF16)
     x_last = move(x_out.at[2], x_in.at[2], 9, px)
-    if meanwhile is not None:
-        meanwhile()
+    yield
     x_near.wait_recv()
     y_near.wait_recv()
     y_last.wait_recv()
     acc[3, low] = acc[3, low] + x_in[1].astype(F32) + y_in[2].astype(F32)
     x_last.wait_recv()
     acc[3, high] = acc[3, high] + y_in[1].astype(F32) + x_in[2].astype(F32)
+    yield
     for copy in copies:
         copy.wait_send()
-    return acc[3]
+
+
+def scatter_blocks(me, partial, *buffers):
+    for unused_step in scatter_steps(me, partial, *buffers):
+        pass
+    return buffers[2][3]
 
 
 def scatter_scratch(rows, width):
@@ -264,7 +270,7 @@
 
 def front(
     tokens, attn_gain, query_weight, key_weight, value_weight, output_weight, ffn_gain,
-    gate_weight, up_weight, dealing, lengths, cotangent, freq, replicas,
+    gate_weight, up_weight, down_weight, dealing, lengths, cotangent, freq, replicas,
 ):
     local, width = tokens.shape
     total = 8 * local
@@ -276,9 +282,9 @@
 
     def kernel(
         tok_ref, gain_ref, wq_hbm, wk_ref, wv_ref, wo_ref, fgain_ref, wg_hbm, wu_hbm,
-        deal_ref, len_ref, cot_ref, freq_ref,
-        n_ref, q_ref, kv_ref, att_ref, qw_ref, kvw_ref, wg_out, wu_out, mid_ref, nf_ref, dg_out, cot_out,
-        kv_stage, c_all, dg_own,
+        wd_ref, deal_ref, len_ref, cot_ref, freq_ref,
+        n_ref, q_ref, kv_ref, att_ref, qw_ref, kvw_ref, wg_out, wu_out, mid_ref, nf_ref, dg_out, ag_out, cot_out,
+        kv_stage, c_all, dg_own, ag_stage,
         sib_out, sib_in, acc, x_out, x_in, y_out, y_in, scatter_sems,
         n_sems, c_sems, nf_sems, qkv_sems, bulk_sems, ring_sems, pair_sems, local_sems,
     ):
@@ -304,6 +310,8 @@
             kv_stage[d] = jnp.concatenate([wk_ref[:, lanes], wv_ref[:, lanes]], axis=1)
         pl.semaphore_wait(barrier, len(others) + 2)
 
+        gather_c = gather_steps(me, c_all, c_sems)
+        next(gather_c)
         gather_n = gather_steps(me, n_ref, n_sems)
         next(gather_n)
         weights = []
@@ -312,50 +320,52 @@
             columns = pl.ds(pl.multiple_of(peer * q_cols, q_cols), q_cols)
             weights.append(send(wq_hbm.at[:, columns], qw_ref.at[me], qkv_sems, 2 * mask - 2, peer))
             weights.append(send(kv_stage.at[peer], kvw_ref.at[me], qkv_sems, 2 * mask - 1, peer))
-        gather_c = gather_steps(me, c_all, c_sems)
         for copy in weights:
-            copy.start()
-        next(gather_c)
-        bulk = []
-        for i, (source, target) in enumerate(((wg_hbm, wg_out), (wu_hbm, wu_out))):
-            for mask in others:
-                peer = flip(me, mask)
-                columns = pl.ds(pl.multiple_of(peer * ff_cols, ff_cols), ff_cols)
-                bulk.append(
-                    send(source.at[:, columns], target.at[me], bulk_sems, 7 * i + mask - 1, peer)
-                )
-        for copy in bulk:
             copy.start()
         own_columns = pl.ds(pl.multiple_of(me * ff_cols, ff_cols), ff_cols)
         own_q = pl.ds(pl.multiple_of(me * q_cols, q_cols), q_cols)
+        gate_slot, up_slot = ag_stage.at[:shard_rows], ag_stage.at[pl.ds(shard_rows, shard_rows)]
         kept = [
-            pltpu.make_async_copy(wg_hbm.at[:, own_columns], wg_out.at[me], local_sems.at[0]),
-            pltpu.make_async_copy(wu_hbm.at[:, own_columns], wu_out.at[me], local_sems.at[1]),
+            pltpu.make_async_copy(wg_hbm.at[:, own_columns], gate_slot, local_sems.at[0]),
+            pltpu.make_async_copy(wu_hbm.at[:, own_columns], up_slot, local_sems.at[1]),
             pltpu.make_async_copy(wq_hbm.at[:, own_q], qw_ref.at[me], local_sems.at[2]),
         ]
         for copy in kept:
             copy.start()
         kvw_ref[me] = kv_stage[me]
-        for unused in range(5):
-            next(gather_n)
-            next(gather_c)
-        for unused in gather_n:
-            pass
+
+        bulk, waiting = [], []
+        for source, target in ((wg_hbm, wg_out), (wu_hbm, wu_out)):
+            for part in range(2):
+                rows = pl.ds(part * (shard_rows // 2), shard_rows // 2)
+                for mask in (2, 4, 6, 3, 5, 7, 1):
+                    waiting.append((source, target, rows, mask))
+
+        def more(count):
+            for unused in range(min(count, len(waiting))):
+                source, target, rows, mask = waiting.pop(0)
+                peer = flip(me, mask)
+                columns = pl.ds(pl.multiple_of(peer * ff_cols, ff_cols), ff_cols)
+                copy = send(
+                    source.at[rows, columns], target.at[me, rows], bulk_sems, len(bulk), peer
+                )
+                copy.start()
+                bulk.append(copy)
+
         for unused in gather_c:
             pass
 
-        for i in range(total // block):
-            rows = pl.ds(i * block, block)
-            packed = i * block + lax.broadcasted_iota(jnp.int32, (block, total), 0)
-            chosen = (deal_ref[...] == packed).astype(BF16)
-            dealt = mm(chosen, c_all[...].reshape(total, width))
-            dg_own[rows, :] = (RESIDUAL_SCALE * dealt).astype(BF16)
-        packed = me * local + lax.broadcasted_iota(jnp.int32, (local, total), 0)
-        chosen = (deal_ref[...] == packed).astype(BF16)
-        cot_out[...] = mm(chosen, c_all[...].reshape(total, width)).astype(BF16)
-        half = pl.ds(pl.multiple_of(core * (total // 2), total // 2), total // 2)
-        store = pltpu.make_async_copy(dg_own, dg_out.at[group], local_sems.at[3])
-        store.start()
+        def permute(first):
+            for i in range(total // 2 // block):
+                row0 = pl.multiple_of(first + i * block, block)
+                packed = row0 + lax.broadcasted_iota(jnp.int32, (block, total), 0)
+                chosen = (deal_ref[...] == packed).astype(BF16)
+                dealt = mm(chosen, c_all[...].reshape(total, width))
+                dg_own[pl.ds(row0, block), :] = (RESIDUAL_SCALE * dealt).astype(BF16)
+
+        near = pl.multiple_of(core * (total // 2), total // 2)
+        far = pl.multiple_of((1 - core) * (total // 2), total // 2)
+        half = pl.ds(near, total // 2)
 
         def ring(hop):
             held = lax.rem(group + replicas - hop, replicas)
@@ -378,12 +388,29 @@
             copy.start()
             return copy
 
+        permute(near)
         hops, shares = [ring(0)], []
-
-        for copy in kept[2:]:
+        for unused in range(4):
+            next(gather_n)
+        permute(far)
+        packed = me * local + lax.broadcasted_iota(jnp.int32, (local, total), 0)
+        chosen = (deal_ref[...] == packed).astype(BF16)
+        cot_out[...] = mm(chosen, c_all[...].reshape(total, width)).astype(BF16)
+        store = pltpu.make_async_copy(dg_own, dg_out.at[group], local_sems.at[3])
+        store.start()
+        for unused in gather_n:
+            pass
+        for copy in kept:
             copy.wait()
+        kept = [
+            pltpu.make_async_copy(gate_slot, wg_out.at[me], local_sems.at[0]),
+            pltpu.make_async_copy(up_slot, wu_out.at[me], local_sems.at[1]),
+        ]
+        for copy in kept:
+            copy.start()
         for copy in weights:
             copy.wait_recv()
+        more(BULK[0])
         for i in range(total // block):
             rows = pl.ds(i * block, block)
             x = n_ref[pl.ds(i * block // local, block // local)].reshape(block, width)
@@ -408,20 +435,51 @@
                 hops.append(ring(hop))
             shares.append(share(hop))
 
-        branch = scatter_blocks(
-            me, partial, sib_out, sib_in, acc, x_out, x_in, y_out, y_in, scatter_sems, next_hop
+        def act_grad(held, source):
+            for i in range(total // block):
+                rows = pl.ds(i * block, block)
+                ag_stage[rows, :] = mm_t(source[rows, :], wd_ref[...]).astype(BF16)
+            copy = pltpu.make_async_copy(ag_stage, ag_out.at[held], local_sems.at[3])
+            copy.start()
+            copy.wait()
+
+        next_hop()
+        scatter = scatter_steps(
+            me, partial, sib_out, sib_in, acc, x_out, x_in, y_out, y_in, scatter_sems
         )
+        next(scatter)
+        more(BULK[1])
+        for unused in scatter:
+            pass
+        branch = acc[3]
         middle = tok_ref[...].astype(F32) + RESIDUAL_SCALE * branch
         mid_ref[...] = middle
         nf_ref[me] = rms_scale(middle, fgain_ref[...]).astype(BF16)
-        gather_blocks(me, nf_ref, nf_sems)
-        while len(shares) < replicas - 1:
+        gather_nf = gather_steps(me, nf_ref, nf_sems)
+        next(gather_nf)
+        more(BULK[2])
+        for unused in gather_nf:
+            pass
+        more(len(waiting))
+        store.wait()
+        for copy in kept:
+            copy.wait()
+        act_grad(group, dg_own)
+        hops[0].wait_send()
+        if len(shares) < replicas - 1:
             next_hop()
-        for copy in kept[:2] + [store]:
-            copy.wait()
-        for copy in bulk + shares:
+        for done in range(replicas - 1):
+            if len(shares) < done + 1:
+                next_hop()
+            held = lax.rem(group + replicas - 1 - done, replicas)
+            shares[done].wait_recv()
+            load = pltpu.make_async_copy(dg_out.at[held], dg_own, local_sems.at[3])
+            load.start()
+            load.wait()
+            act_grad(held, dg_own)
+        for copy in bulk:
             copy.wait_recv()
-        for copy in weights + bulk + hops + shares:
+        for copy in weights + bulk + hops[1:] + shares:
             copy.wait_send()
 
     rows8 = jax.ShapeDtypeStruct((8, local, width), BF16)
@@ -440,14 +498,16 @@
             jax.ShapeDtypeStruct((local, width), F32),
             rows8,
             jax.ShapeDtypeStruct((replicas, total, width), BF16),
+            jax.ShapeDtypeStruct((replicas, total, ff_cols), BF16),
             jax.ShapeDtypeStruct((local, width), BF16),
         ),
-        in_specs=[VMEM, VMEM, ANY, VMEM, VMEM, VMEM, VMEM, ANY, ANY, VMEM, SMEM, VMEM, VMEM],
-        out_specs=[VMEM] * 6 + [ANY, ANY, VMEM, VMEM, ANY, VMEM],
+        in_specs=[VMEM, VMEM, ANY, VMEM, VMEM, VMEM, VMEM, ANY, ANY, VMEM, VMEM, SMEM, VMEM, VMEM],
+        out_specs=[VMEM] * 6 + [ANY, ANY, VMEM, VMEM, ANY, ANY, VMEM],
         scratch_shapes=[
             pltpu.VMEM((8, shard_rows, 2 * HEAD), BF16),
             pltpu.VMEM((8, local, width), BF16),
             pltpu.VMEM((total, width), BF16),
+            pltpu.VMEM((total, ff_cols), BF16),
         ]
         + scatter_scratch(local, width)
         + [
@@ -455,26 +515,26 @@
             half_sems((2, GATHER_SEMS)),
             half_sems((2, GATHER_SEMS)),
             half_sems((2, 14)),
-            half_sems((2, 14)),
+            half_sems((2, 28)),
             half_sems((2, replicas)),
             half_sems((2, replicas)),
             half_sems((4,)),
         ],
         compiler_params=comm_params(0, 56),
         cost_estimate=pl.CostEstimate(
-            flops=150_000_000_000, bytes_accessed=50 << 20, transcendentals=total * total
+            flops=200_000_000_000, bytes_accessed=50 << 20, transcendentals=total * total
         ),
         name="front",
     )(
         tokens, attn_gain[None, :], query_weight, key_weight, value_weight, output_weight,
-        ffn_gain[None, :], gate_weight, up_weight, dealing, lengths, cotangent, freq,
-    )
-    normed, q, kv, attention, qw, kvw, wg, wu, middle, nf, dg, cot = outs
+        ffn_gain[None, :], gate_weight, up_weight, down_weight, dealing, lengths, cotangent, freq,
+    )
+    normed, q, kv, attention, qw, kvw, wg, wu, middle, nf, dg, ag, cot = outs
     return (
         normed.reshape(total, width), q, kv, attention,
         qw.reshape(width, q_cols), kvw.reshape(width, 2 * HEAD),
         wg.reshape(width, ff_cols), wu.reshape(width, ff_cols),
-        middle, nf.reshape(total, width), dg, cot,
+        middle, nf.reshape(total, width), dg, ag, cot,
     )
 
 
@@ -520,44 +580,93 @@
         + [pltpu.SemaphoreType.DMA((2, GATHER_SEMS))],
         compiler_params=comm_params(collective_id, 44),
         cost_estimate=pl.CostEstimate(
-            flops=40 * rows * width, bytes_accessed=50 * rows * width, transcendentals=rows
+            flops=50_000_000_000, bytes_accessed=50 * rows * width, transcendentals=rows
         ),
         name="pull_gather",
     )(part, middle, gain[None, :], out_grad)
 
 
-def pull_tokens(part, hidden, gain, middle_grad, collective_id):
+def pull_tokens(part, out_part, hidden, gain, middle_grad, other_gain, replicas, collective_id):
     rows, width = middle_grad.shape
-
-    def kernel(p_ref, h_ref, gain_ref, mg_ref, out, gain_part, *scratch):
+    levels = [("shard", 1), ("shard", 2), ("shard", 4)]
+    level = 1
+    while level < replicas:
+        levels.append(("rep", level))
+        level *= 2
+
+    def kernel(
+        p_ref, o_ref, h_ref, gain_ref, mg_ref, og_ref, out, lay, gains, gain_in, gain_out, gain_sems, *scratch
+    ):
         me = lax.axis_index("shard")
-        *buffers, scatter_sems = scratch
-        greet(me, (1, 2, 4))
-        grad = scatter_blocks(
-            me,
-            lambda d: p_ref[pl.ds(pl.multiple_of(d * rows, rows), rows), :].astype(F32),
-            *buffers,
-            scatter_sems,
-        )
-        rows_part, gain_row = norm_pull(h_ref[...].astype(F32), gain_ref[...], grad)
-        gain_part[...] = gain_row
+        group = lax.axis_index("rep")
+        first, second = scratch[:8], scratch[8:]
+        barrier = pltpu.get_barrier_semaphore()
+        peers = []
+        for axis, weight in levels:
+            index = me if axis == "shard" else group
+            peers.append({axis: index + weight - 2 * weight * lax.rem(lax.div(index, weight), 2)})
+        for peer in peers:
+            pl.semaphore_signal(barrier, inc=1, device_id=peer, device_id_type=MESH)
+        pl.semaphore_wait(barrier, len(peers))
+
+        def blocks_of(ref):
+            return lambda d: ref[pl.ds(pl.multiple_of(d * rows, rows), rows), :].astype(F32)
+
+        grads = scatter_steps(me, blocks_of(p_ref), *first)
+        outputs = scatter_steps(me, blocks_of(o_ref), *second)
+        next(grads)
+        next(grads)
+        next(outputs)
+        next(grads)
+        next(outputs)
+        next(grads)
+        rows_part, gain_row = norm_pull(h_ref[...].astype(F32), gain_ref[...], first[2][3])
         out[...] = mg_ref[...] + rows_part
+        total = jnp.concatenate([gain_row, og_ref[...]], axis=0)
+        for i, peer in enumerate(peers):
+            gain_out[i] = total
+            copy = pltpu.make_async_remote_copy(
+                src_ref=gain_out.at[i],
+                dst_ref=gain_in.at[i],
+                send_sem=gain_sems.at[0, i],
+                recv_sem=gain_sems.at[1, i],
+                device_id=peer,
+                device_id_type=MESH,
+            )
+            copy.start()
+            if i == 1:
+                next(outputs)
+            copy.wait()
+            total = total + gain_in[i]
+        gains[...] = total
+        next(outputs)
+        lay[...] = second[2][3].astype(BF16)
+        for steps in (grads, outputs):
+            for unused in steps:
+                pass
 
     return pl.pallas_call(
         kernel,
         out_shape=(
             jax.ShapeDtypeStruct((rows, width), F32),
-            jax.ShapeDtypeStruct((1, width), F32),
-        ),
-        in_specs=[VMEM] * 4,
-        out_specs=[VMEM] * 2,
-        scratch_shapes=scatter_scratch(rows, width),
-        compiler_params=comm_params(collective_id, 40),
+            jax.ShapeDtypeStruct((rows, width), BF16),
+            jax.ShapeDtypeStruct((2, width), F32),
+        ),
+        in_specs=[VMEM] * 6,
+        out_specs=[VMEM] * 3,
+        scratch_shapes=[
+            pltpu.VMEM((len(levels), 2, width), F32),
+            pltpu.VMEM((len(levels), 2, width), F32),
+            pltpu.SemaphoreType.DMA((2, len(levels))),
+        ]
+        + scatter_scratch(rows, width)
+        + scatter_scratch(rows, width),
+        compiler_params=comm_params(collective_id, 52),
         cost_estimate=pl.CostEstimate(
-            flops=40 * rows * width, bytes_accessed=50 * rows * width, transcendentals=rows
+            flops=50_000_000_000, bytes_accessed=50 * rows * width, transcendentals=rows
         ),
         name="pull_tokens",
-    )(part, hidden, gain[None, :], middle_grad)
+    )(part, out_part, hidden, gain[None, :], middle_grad, other_gain)
 
 
 def softmax_block(q, k, allowed):
@@ -694,7 +803,7 @@
 
     def kernel(
         bg_ref, wo_ref, a_ref, q_ref, kv_ref, n_ref, qw_ref, kvw_ref, len_ref, freq_ref,
-        dn_ref, dqw_ref, dkvw_ref, dwo_ref, g_ref, dq_ref, dk_ref, dv_ref, pq_ref, pkv_ref,
+        dn_ref, dqkv_ref, dwo_ref, g_ref, dq_ref, dk_ref, dv_ref, pq_ref, pkv_ref,
     ):
         for i in range(total // block):
             rows = pl.ds(i * block, block)
@@ -717,20 +826,19 @@
             ).astype(BF16)
         for i in range(width // 512):
             cols = slice(i * 512, (i + 1) * 512)
-            dqw_ref[cols, :] = t_mm(n_ref[:, cols], pq_ref[...]).astype(BF16)
-            dkvw_ref[cols, :] = t_mm(n_ref[:, cols], pkv_ref[...]).astype(BF16)
+            dqkv_ref[cols, :q_cols] = t_mm(n_ref[:, cols], pq_ref[...]).astype(BF16)
+            dqkv_ref[cols, q_cols:] = t_mm(n_ref[:, cols], pkv_ref[...]).astype(BF16)
             dwo_ref[:, cols] = t_mm(a_ref[...], bg_ref[:, cols]).astype(BF16)
 
     return pl.pallas_call(
         kernel,
         out_shape=(
             jax.ShapeDtypeStruct((total, width), BF16),
-            jax.ShapeDtypeStruct((width, q_cols), BF16),
-            jax.ShapeDtypeStruct((width, 2 * HEAD), BF16),
+            jax.ShapeDtypeStruct((width, q_cols + 2 * HEAD), BF16),
             jax.ShapeDtypeStruct((q_cols, width), BF16),
         ),
         in_specs=[VMEM] * 8 + [SMEM, VMEM],
-        out_specs=[VMEM] * 4,
+        out_specs=[VMEM] * 3,
         scratch_shapes=[
             pltpu.VMEM((total, q_cols), BF16),
             pltpu.VMEM((total, q_cols), F32),
@@ -745,8 +853,9 @@
     )(branch_grad, output_weight, attention, q, kv, normed, q_weight, kv_weight, lengths, freq)
 
 
-def ffn_rows(nf, dg, wg, wu, wd):
-    gate, up, act_grad = mm(nf, wg), mm(nf, wu), mm_t(dg, wd)
+def ffn_rows(nf, act_grad, wg, wu):
+    gate, up = mm(nf, wg), mm(nf, wu)
+    act_grad = act_grad.astype(F32)
     sigmoid = 1.0 / (1.0 + jnp.exp(-gate))
     silu = gate * sigmoid
     activated = (silu * up).astype(BF16)
@@ -754,14 +863,14 @@
     return activated, gate_grad, (act_grad * silu).astype(BF16)
 
 
-def ffn_own(group, nf, dg_all, wg, wu, wd, groups):
-    total, width = nf.shape
-    cols = wg.shape[1]
+def ffn_own(group, nf, act_grads, wg, wu):
+    groups, total, cols = act_grads.shape
+    width = nf.shape[1]
     block = 256
 
-    def kernel(g_ref, nf_ref, dg_ref, wg_ref, wu_ref, wd_ref, na_ref, act_ref, gg_ref, ug_ref, dn_ref):
+    def kernel(g_ref, nf_ref, ag_ref, wg_ref, wu_ref, na_ref, act_ref, gg_ref, ug_ref, dn_ref):
         nf = nf_ref[...]
-        act, gg, ug = ffn_rows(nf, dg_ref[0], wg_ref[...], wu_ref[...], wd_ref[...])
+        act, gg, ug = ffn_rows(nf, ag_ref[0], wg_ref[...], wu_ref[...])
         na_ref[0], act_ref[0], gg_ref[0], ug_ref[0] = nf, act, gg, ug
         dn_ref[...] = (mm_t(gg, wg_ref[...]) + mm_t(ug, wu_ref[...])).astype(BF16)
 
@@ -769,7 +878,7 @@
     hid = pl.BlockSpec((1, block, cols), lambda i, g: (g[0], i, 0))
     plain = pl.BlockSpec((block, width), lambda i, g: (i, 0))
     whole = [
-        pl.BlockSpec(w.shape, lambda i, g: (0, 0), pipeline_mode=pl.Buffered(1)) for w in (wg, wu, wd)
+        pl.BlockSpec(w.shape, lambda i, g: (0, 0), pipeline_mode=pl.Buffered(1)) for w in (wg, wu)
     ]
     hidden = jax.ShapeDtypeStruct((groups, total, cols), BF16)
     return pl.pallas_call(
@@ -777,7 +886,7 @@
         grid_spec=pltpu.PrefetchScalarGridSpec(
             num_scalar_prefetch=1,
             grid=(total // block,),
-            in_specs=[plain, mine] + whole,
+            in_specs=[plain, hid] + whole,
             out_specs=[mine, hid, hid, hid, plain],
         ),
         out_shape=(
@@ -787,23 +896,21 @@
             hidden,
             jax.ShapeDtypeStruct((total, width), BF16),
         ),
-        compiler_params=pltpu.CompilerParams(vmem_limit_bytes=56 << 20),
+        compiler_params=pltpu.CompilerParams(vmem_limit_bytes=48 << 20),
         cost_estimate=pl.CostEstimate(
-            flops=10 * total * width * cols, bytes_accessed=40 << 20, transcendentals=total * cols
+            flops=12 * total * width * cols, bytes_accessed=40 << 20, transcendentals=total * cols
         ),
         name="ffn_own",
-    )(group, nf, dg_all, wg, wu, wd)
-
-
-def ffn_other(where, held, fetched, dg_all, wg, wu, wd, filled):
-    groups, total, width = dg_all.shape
-    cols = wg.shape[1]
+    )(group, nf, act_grads, wg, wu)
+
+
+def ffn_other(where, held, fetched, act_grads, wg, wu, filled):
+    groups, total, cols = act_grads.shape
+    width = held.shape[1]
     block = 256
     per_half = total // 2 // block
 
-    def kernel(
-        w_ref, held_ref, fetched_ref, dg_ref, wg_ref, wu_ref, wd_ref, *rest
-    ):
+    def kernel(w_ref, held_ref, fetched_ref, ag_ref, wg_ref, wu_ref, *rest):
         na_ref, act_ref, gg_ref, ug_ref, nf_ref = rest[4:]
         i = pl.program_id(0)
 
@@ -816,7 +923,7 @@
             nf_ref[...] = fetched_ref[...]
 
         nf = nf_ref[...]
-        act, gg, ug = ffn_rows(nf, dg_ref[0], wg_ref[...], wu_ref[...], wd_ref[...])
+        act, gg, ug = ffn_rows(nf, ag_ref[0], wg_ref[...], wu_ref[...])
         na_ref[0], act_ref[0], gg_ref[0], ug_ref[0] = nf, act, gg, ug
 
     def row(i, w):
@@ -828,7 +935,7 @@
     first = pl.BlockSpec((block, width), lambda i, w: (jnp.minimum(i, per_half - 1), 0))
     last = pl.BlockSpec((block, width), lambda i, w: (jnp.maximum(i - per_half, 0), 0))
     whole = [
-        pl.BlockSpec(w.shape, lambda i, g: (0, 0), pipeline_mode=pl.Buffered(1)) for w in (wg, wu, wd)
+        pl.BlockSpec(w.shape, lambda i, g: (0, 0), pipeline_mode=pl.Buffered(1)) for w in (wg, wu)
     ]
     hidden = jax.ShapeDtypeStruct((groups, total, cols), BF16)
     return pl.pallas_call(
@@ -836,21 +943,104 @@
         grid_spec=pltpu.PrefetchScalarGridSpec(
             num_scalar_prefetch=1,
             grid=(2 * per_half,),
-            in_specs=[first, last, mine] + whole + [pl.BlockSpec(memory_space=pl.ANY)] * 4,
+            in_specs=[first, last, hid] + whole + [pl.BlockSpec(memory_space=pl.ANY)] * 4,
             out_specs=[mine, hid, hid, hid],
             scratch_shapes=[pltpu.VMEM((block, width), BF16)],
         ),
         out_shape=(jax.ShapeDtypeStruct((groups, total, width), BF16), hidden, hidden, hidden),
-        input_output_aliases={7: 0, 8: 1, 9: 2, 10: 3},
-        compiler_params=pltpu.CompilerParams(vmem_limit_bytes=56 << 20),
+        input_output_aliases={6: 0, 7: 1, 8: 2, 9: 3},
+        compiler_params=pltpu.CompilerParams(vmem_limit_bytes=48 << 20),
         cost_estimate=pl.CostEstimate(
-            flops=6 * total * width * cols, bytes_accessed=40 << 20, transcendentals=total * cols
+            flops=8 * total * width * cols, bytes_accessed=40 << 20, transcendentals=total * cols
         ),
         name="ffn_other",
-    )(where, held, fetched, dg_all, wg, wu, wd, *filled)
-
-
-def weight_grad(left, right):
+    )(where, held, fetched, act_grads, wg, wu, *filled)
+
+
+def output_rows(where, activated, down_weight, middle, deal, total):
+    groups, total, cols = activated.shape
+    local, width = middle.shape
+    block = 256
+
+    def kernel(w_ref, act_ref, wd_ref, mid_ref, deal_ref, o_ref, rows_ref):
+        for i in range(total // block):
+            rows = pl.ds(i * block, block)
+            rows_ref[rows, :] = (RESIDUAL_SCALE * mm(act_ref[0, rows, :], wd_ref[...])).astype(BF16)
+        own = pl.ds(pl.multiple_of(w_ref[1] * local, local), local)
+        rows_ref[own, :] = (rows_ref[own, :].astype(F32) + mid_ref[...]).astype(BF16)
+        for i in range(total // block):
+            rows = pl.ds(i * block, block)
+            packed = lax.broadcasted_iota(jnp.int32, (block, total), 1)
+            chosen = (deal_ref[rows, :] == packed).astype(BF16)
+            o_ref[rows, :] = mm(chosen, rows_ref[...]).astype(BF16)
+
+    def full(shape):
+        return pl.BlockSpec(shape, lambda i, w: (0,) * len(shape), pipeline_mode=pl.Buffered(1))
+
+    return pl.pallas_call(
+        kernel,
+        grid_spec=pltpu.PrefetchScalarGridSpec(
+            num_scalar_prefetch=1,
+            grid=(1,),
+            in_specs=[
+                pl.BlockSpec((1, total, cols), lambda i, w: (w[0], 0, 0), pipeline_mode=pl.Buffered(1)),
+                full(down_weight.shape),
+                full(middle.shape),
+                full(deal.shape),
+            ],
+            out_specs=full((total, width)),
+            scratch_shapes=[pltpu.VMEM((total, width), BF16)],
+        ),
+        out_shape=jax.ShapeDtypeStruct((total, width), BF16),
+        compiler_params=pltpu.CompilerParams(vmem_limit_bytes=48 << 20),
+        cost_estimate=pl.CostEstimate(
+            flops=2 * total * width * (cols + total) * 2, bytes_accessed=12 << 20, transcendentals=0
+        ),
+        name="output_rows",
+    )(where, activated, down_weight, middle, deal)
+
+
+def join_columns(blocks):
+    n, rows, cols = blocks.shape
+
+    def kernel(b_ref, o_ref):
+        o_ref[...] = b_ref[0].astype(F32)
+
+    return pl.pallas_call(
+        kernel,
+        grid=(n,),
+        in_specs=[pl.BlockSpec((1, rows, cols), lambda i: (i, 0, 0))],
+        out_specs=pl.BlockSpec((rows, cols), lambda i: (0, i)),
+        out_shape=jax.ShapeDtypeStruct((rows, n * cols), F32),
+        cost_estimate=pl.CostEstimate(
+            flops=n * rows * cols, bytes_accessed=6 * n * rows * cols, transcendentals=0
+        ),
+        name="join_columns",
+    )(blocks)
+
+
+def join_heads(blocks, q_cols):
+    n, rows, cols = blocks.shape
+
+    def kernel(b_ref, q_ref, k_ref, v_ref):
+        for i in range(n):
+            q_ref[:, i * q_cols : (i + 1) * q_cols] = b_ref[i, :, :q_cols].astype(F32)
+        kv = [b_ref[i, :, q_cols:].astype(F32) for i in range(n)]
+        k_ref[...] = jnp.concatenate([x[:, :HEAD] for x in kv], axis=1)
+        v_ref[...] = jnp.concatenate([x[:, HEAD:] for x in kv], axis=1)
+
+    return pl.pallas_call(
+        kernel,
+        out_shape=(
+            jax.ShapeDtypeStruct((rows, n * q_cols), F32),
+            jax.ShapeDtypeStruct((rows, n * HEAD), F32),
+            jax.ShapeDtypeStruct((rows, n * HEAD), F32),
+        ),
+        name="join_heads",
+    )(blocks)
+
+
+def weight_grad(left, right, dtype):
     groups, total, m = left.shape
     n = right.shape[2]
     block = 512
@@ -880,7 +1070,7 @@
             pl.BlockSpec((block, n), lambda k: (k, 0)),
         ],
         out_specs=pl.BlockSpec((m, n), lambda k: (0, 0), pipeline_mode=pl.Buffered(1)),
-        out_shape=jax.ShapeDtypeStruct((m, n), BF16),
+        out_shape=jax.ShapeDtypeStruct((m, n), dtype),
         scratch_shapes=[pltpu.VMEM((m, n), F32)],
         compiler_params=pltpu.CompilerParams(vmem_limit_bytes=56 << 20),
         cost_estimate=pl.CostEstimate(
@@ -910,10 +1100,10 @@
 
     (
         normed, q, kv, attention, q_weight, kv_weight, gate_cols, up_cols,
-        middle, normed_ffn, down_grads, cot_own,
+        middle, normed_ffn, down_grads, act_grads, cot_own,
     ) = front(
         tokens, attn_gain, query_weight, key_weight, value_weight, output_weight, ffn_gain,
-        gate_weight, up_weight, dealing, lengths, cotangent, freq, replicas,
+        gate_weight, up_weight, down_weight, dealing, lengths, cotangent, freq, replicas,
     )
 
     held = lax.dynamic_slice_in_dim(normed_ffn, core * (total // 2), total // 2)
@@ -926,63 +1116,41 @@
         arrivals.append((where, held, lax.ppermute(held, "shard", beside)))
 
     *filled, normed_ffn_part = ffn_own(
-        group.astype(jnp.int32)[None], normed_ffn, down_grads, gate_cols, up_cols, down_weight, replicas
-    )
-    activated = lax.dynamic_index_in_dim(filled[1], group, keepdims=False)
+        group.astype(jnp.int32)[None], normed_ffn, act_grads, gate_cols, up_cols
+    )
     middle_grad, ffn_gain_part, branch_grad = pull_gather(
         normed_ffn_part, middle, ffn_gain, cot_own, 2
     )
     branch_grad = branch_grad.reshape(total, width)
+    output_part = output_rows(
+        jnp.stack([group, here]).astype(jnp.int32), filled[1], down_weight, middle,
+        dealing.reshape(total, 1), total,
+    )
+    normed_part, qkv_grad, output_grad = attention_backward(
+        branch_grad, output_weight, attention, q, kv, normed, q_weight, kv_weight, lengths, freq
+    )
+    tokens_grad, layer_output, gains = pull_tokens(
+        normed_part, output_part, tokens, attn_gain, middle_grad, ffn_gain_part, replicas, 3
+    )
     for where, from_ring, from_core in arrivals:
-        filled = ffn_other(
-            where, from_ring, from_core, down_grads, gate_cols, up_cols, down_weight, filled
-        )
+        filled = ffn_other(where, from_ring, from_core, act_grads, gate_cols, up_cols, filled)
     all_normed, all_activated, all_gate_grad, all_up_grad = filled
 
-    normed_part, q_grad, kv_grad, output_grad = attention_backward(
-        branch_grad, output_weight, attention, q, kv, normed, q_weight, kv_weight, lengths, freq
-    )
-    tokens_grad, attn_gain_part = pull_tokens(normed_part, tokens, attn_gain, middle_grad, 3)
-
-    packed = jnp.arange(total, dtype=jnp.int32)
-    dealt = (dealing[0][:, None] == packed[None, :]).astype(BF16)
-    own_rows = (packed[:, None] - here * local == jnp.arange(local, dtype=jnp.int32)[None, :]).astype(BF16)
-    layer_output = scatter_rows(
-        mm(
-            dealt,
-            (
-                RESIDUAL_SCALE * mm(activated, down_weight)
-                + mm(own_rows, middle.astype(BF16))
-            ).astype(BF16),
-        ).astype(BF16)
-    )
-
-    gate_part = exchange(weight_grad(all_normed, all_gate_grad).reshape(n, rows, ff_cols))
-    up_part = exchange(weight_grad(all_normed, all_up_grad).reshape(n, rows, ff_cols))
-    down_part = weight_grad(all_activated, down_grads)
-    output_part = rep_sum(output_grad)
-    qkv_part = rep_sum(
-        exchange(jnp.concatenate([q_grad, kv_grad], axis=1).reshape(n, rows, q_cols + 2 * HEAD))
-    )
-
-    def join(blocks):
-        return blocks.transpose(1, 0, 2).reshape(rows, -1).astype(F32)
-
-    gains = lax.all_gather(
-        jnp.concatenate([attn_gain_part, ffn_gain_part]), ("rep", "shard"), axis=0
-    ).sum(axis=0)
+    gate_part = exchange(weight_grad(all_normed, all_gate_grad, BF16).reshape(n, rows, ff_cols))
+    up_part = exchange(weight_grad(all_normed, all_up_grad, BF16).reshape(n, rows, ff_cols))
+    down_grad = weight_grad(all_activated, down_grads, F32)
+    output_grad = rep_sum(output_grad)
+    qkv_part = rep_sum(exchange(qkv_grad.reshape(n, rows, q_cols + 2 * HEAD)))
     return (
         layer_output,
         tokens_grad,
         gains[0],
-        join(qkv_part[:, :, :q_cols]),
-        join(qkv_part[:, :, q_cols : q_cols + HEAD]),
-        join(qkv_part[:, :, q_cols + HEAD :]),
-        output_part.astype(F32),
+        *join_heads(qkv_part, q_cols),
+        output_grad.astype(F32),
         gains[1],
-        join(gate_part),
-        join(up_part),
-        down_part.astype(F32),
+        join_columns(gate_part),
+        join_columns(up_part),
+        down_grad,
     )
 
 

time: 883 us -> 746 us (0.84)
  blocking collectives: 38.9 us -> 0 us
  Pallas kernels: 642 us -> 613 us
  other arithmetic: 35.3 us -> 12.8 us
  matrix products: 21.1 us -> 0 us
  between operations: 14.8 us -> 1.11 us
  local copies, waits for them, and re-layouts: 28 us -> 14.6 us
    pallas_call x1, Pallas kernels: 307 us -> 233 us  [front(): pl.pallas_call(kernel, out_shape=(rows8, jax.ShapeDtypeStruct((total, q_c...]
    all_gather x1 -> x0, blocking collectives: 38.9 us -> none  [per_device_plane(): lax.all_gather(jnp.concatenate([attn_gain_part, ffn_gain_part]), ('rep',...]
    pallas_call x1, Pallas kernels: 75.4 us -> 111 us  [pull_tokens(): pl.pallas_call(kernel, out_shape=(jax.ShapeDtypeStruct((rows, width), F32...]
    pallas_call x0 -> x4, Pallas kernels: none -> 30.5 us  [the longest x2 14.6 us: join_columns(): pl.pallas_call(kernel, grid=(n,), in_specs=[pl.BlockSpec((1, rows, cols),...]
    dot_general x2 -> x0, matrix products: 21.1 us -> none  [mm(): return jnp.dot(a, b, preferred_element_type=F32)]
    ppermute x2, waiting for transfers between devices: 18.6 us -> 0.01 us  [rep_sum(): moved = lax.ppermute(x, 'rep', [(near, near - 1), (far, far + 1)])]
    pallas_call x3, Pallas kernels: 66.9 us -> 51.2 us  [ffn_other(): pl.pallas_call(kernel, grid_spec=pltpu.PrefetchScalarGridSpec(num_scalar_...]
    all_to_all x3, waiting for transfers between devices: 0.01 us -> 10.5 us  [exchange(): lax.all_to_all(blocks, 'shard', split_axis=0, concat_axis=0, tiled=True)]
  transfers between devices with their start and end apart: 16 -> 15, of which waited for: 4 -> 4; matrix products, arithmetic and copies ran while one was open for 8% -> 2% of each run, Pallas kernels for 38% -> 51%
where the time goes in v4:
time: 746 us; the launch traced here: 736 us
  Pallas kernels  613 us (82%)
  waiting for transfers between devices  61.5 us (8%)
  starting transfers between devices  33.5 us (4%)
  local copies, waits for them, and re-layouts  14.6 us (2%)
  other arithmetic  12.8 us (2%)
    pallas_call x1, Pallas kernels, front(): pl.pallas_call(kernel, out_shape=(rows8, jax.ShapeDtypeStruct((total, q_c...  233 us
    pallas_call x1, Pallas kernels, pull_tokens(): pl.pallas_call(kernel, out_shape=(jax.ShapeDtypeStruct((rows, width), F32...  111 us
    pallas_call x3, Pallas kernels, weight_grad(): pl.pallas_call(kernel, grid=(steps,), in_specs=[pl.BlockSpec((block, m),...  90.5 us
    pallas_call x3, Pallas kernels, ffn_other(): pl.pallas_call(kernel, grid_spec=pltpu.PrefetchScalarGridSpec(num_scalar_...  51.2 us
    ppermute x3, waiting for transfers between devices, per_device_plane(): held = lax.ppermute(held, 'rep', onward)  49.2 us
    pallas_call x1, Pallas kernels, pull_gather(): pl.pallas_call(kernel, out_shape=(jax.ShapeDtypeStruct((rows, width), F32...  45.8 us
    pallas_call x1, Pallas kernels, attention_backward(): pl.pallas_call(kernel, out_shape=(jax.ShapeDtypeStruct((total, width), BF...  27.5 us
    pallas_call x1, Pallas kernels, ffn_own(): pl.pallas_call(kernel, grid_spec=pltpu.PrefetchScalarGridSpec(num_scalar_...  23.7 us
  transfers between devices with their start and end apart: 15, of which 4 were waited for; matrix products, arithmetic and copies ran while one was open for 2% of the time, Pallas kernels for 51%

profile of v4, /device:TPU:0, one launch (start us, length us, event | category | flops | bytes accessed | tf_op | source)
XLA Modules:
  0.0 736.0 jit_solution(4350437390904254457)
XLA Ops:
  1.3 232.7 %front.1 = (bf16[8,128,2048]{2,1,0:T(8,128)(2,1)}, bf16[1024,256]{1,0:T(8,128)(2,1)}, bf16[1024,128]{1,0:T(8,128)(2,1)}, bf16[1024,256]{1,0:T(8,128)(2,1)}, bf16...) custom-call(bf16[128,2048]{1,0:T(8,128)(2,1)} %h_ref.1, ...), custom_call_target="tpu_custom_call" | custom-call | flops 199999995904 | bytes 52428800 | tf_op jit(solution)/shard_map/front/pallas_call | solution.py:487
  234.0 3.2 constant_dynamic-slice_fusion
  237.3 23.7 %ffn_own.1 = (bf16[4,1024,2048]{2,1,0:T(8,128)(2,1)}, bf16[4,1024,1024]{2,1,0:T(8,128)(2,1)}, bf16[4,1024,1024]{2,1,0:T(8,128)(2,1)}, bf16[4,1024,1024]{2,1,0:T(8,128)(2,1)}, bf16[1024,2048]{1,0:T(8,128)(2,1)S(1)}) custom-call(s32[1]{0:T(128)} %bitcast.g_ref, bf16[1024,2048]{1,0:T(8,128)(2,1)} %bitcast.35, bf16[4,1024,1024]{2,1,0:T(8,128)(2,1)} %get-tuple-element.54.ag_ref, ...), custom_call_target="tpu_custom_call" | custom-call | flops 25769803776 | bytes 41943040 | tf_op jit(solution)/shard_map/ffn_own/pallas_call | solution.py:884
  263.0 45.8 %pull_gather.1 = (f32[128,2048]{1,0:T(8,128)S(1)}, f32[1,2048]{1,0:T(1,128)S(1)}, bf16[8,128,2048]{2,1,0:T(8,128)(2,1)S(1)}) custom-call(bf16[1024,2048]{1,0:T(8,128)(2,1)} %copy-done.5, f32[128,2048]{1,0:T(8,128)S(1)} %copy-done.6, f32[1,2048]{1,0:T(1,128)S(1)} %bitcast.27, bf16[128,2048]{1,0:T(8,128)(2,1)S(1)} %copy-done.9), custom_call_target="tpu_custom_call" | custom-call | flops 49999998976 | bytes 13107200 | tf_op jit(solution)/shard_map/pull_gather/pallas_call | solution.py:570
  312.4 27.5 %attention_backward.1 = (bf16[1024,2048]{1,0:T(8,128)(2,1)}, bf16[2048,384]{1,0:T(8,128)(2,1)}, bf16[256,2048]{1,0:T(8,128)(2,1)}) custom-call(bf16[1024,2048]{1,0:T(8,128)(2,1)} %bitcast.30, bf16[256,2048]{1,0:T(8,128)(2,1)} %wo_ref.3, bf16[1024,256]{1,0:T(8,128)(2,1)} %get-tuple-element.61.a_ref, bf16[1024,256]{1,0:T(8,128)(2,1)} %get-tuple-element.62.q_ref, ...), custom_call_target="tpu_custom_call" | custom-call | flops 30000001024 | bytes 31457280 | tf_op jit(solution)/shard_map/attention_backward/pallas_call | solution.py:833
  339.9 4.4 all-to-all-start
  344.3 4.5 collective-permute-start.3
  349.2 13.6 %collective-permute-done.7.held_ref = bf16[512,2048]{1,0:T(8,128)(2,1)} collective-permute-done((bf16[512,2048]{1,0:T(8,128)(2,1)S(1)}, bf16[512,2048]{1,0:T(8,128)(2,1)}, u32[]{:S(2)}, u32[]{:S(2)}) %collective-permute-start.7) | collective-permute-done | bytes 2097184 | tf_op jit(solution)/shard_map/ppermute | solution.py:1114
  364.3 12.7 %output_rows.1.o_ref = bf16[1024,2048]{1,0:T(8,128)(2,1)S(1)} custom-call(s32[2]{0:T(128)S(1)} %pad_add_fusion.w_ref, bf16[4,1024,1024]{2,1,0:T(8,128)(2,1)} %get-tuple-element.68.act_ref.rest_1_, bf16[1024,2048]{1,0:T(8,128)(2,1)} %wd_ref.3, f32[128,2048]{1,0:T(8,128)S(1)} %copy-done.7, s32[1024,1]{1,0:T(8,128)S(1)} %copy.36.deal_ref), custom_call_target="tpu_custom_call" | custom-call | flops 17179869184 | bytes 12582912 | tf_op jit(solution)/shard_map/output_rows/pallas_call | solution.py:980
  384.5 10.2 %collective-permute-start = (bf16[8,256,384]{2,1,0:T(8,128)(2,1)}, bf16[8,256,384]{2,1,0:T(8,128)(2,1)}, u32[]{:S(2)}, u32[]{:S(2)}) collective-permute-start(bf16[8,256,384]{2,1,0:T(8,128)(2,1)} %all-to-all-done), channel_id=1, source_target_pairs={{0,8},{24,16},{1,9},{25,17},{2,10},{26,18},{3,11},{27,19},{4,12},{... | collective-permute-start | bytes 4718600 | tf_op jit(solution)/shard_map/ppermute | solution.py:93
  394.7 35.6 %collective-permute-done.8.held_ref = bf16[512,2048]{1,0:T(8,128)(2,1)} collective-permute-done((bf16[512,2048]{1,0:T(8,128)(2,1)}, bf16[512,2048]{1,0:T(8,128)(2,1)}, u32[]{:S(2)}, u32[]{:S(2)}) %collective-permute-start.8) | collective-permute-done | bytes 2097184 | tf_op jit(solution)/shard_map/ppermute | solution.py:1114
  430.3 16.9 %ffn_other.3 = (bf16[4,1024,2048]{2,1,0:T(8,128)(2,1)}, bf16[4,1024,1024]{2,1,0:T(8,128)(2,1)}, bf16[4,1024,1024]{2,1,0:T(8,128)(2,1)}, bf16[4,1024,1024]{2,1,0:T(8,128)(2,1)}) custom-call(s32[2]{0:T(128)S(1)} %pad_add_fusion.3.w_ref, ...), custom_call_target="tpu_custom_call", output_to_operand_aliasing={{0}: (6, {}), {1}: (7, {}), {2}: (8, {}), {3}: (9, {})} | custom-call | flops 17179869184 | bytes 41943040 | tf_op jit(solution)/shard_map/ffn_other/pallas_call | solution.py:941
  447.2 17.3 %ffn_other.4 = (bf16[4,1024,2048]{2,1,0:T(8,128)(2,1)}, bf16[4,1024,1024]{2,1,0:T(8,128)(2,1)}, bf16[4,1024,1024]{2,1,0:T(8,128)(2,1)}, bf16[4,1024,1024]{2,1,0:T(8,128)(2,1)}) custom-call(s32[2]{0:T(128)S(1)} %pad_add_fusion.2.w_ref, ...), custom_call_target="tpu_custom_call", output_to_operand_aliasing={{0}: (6, {}), {1}: (7, {}), {2}: (8, {}), {3}: (9, {})} | custom-call | flops 17179869184 | bytes 41943040 | tf_op jit(solution)/shard_map/ffn_other/pallas_call | solution.py:941
  464.5 17.0 %ffn_other.5 = (bf16[4,1024,2048]{2,1,0:T(8,128)(2,1)}, bf16[4,1024,1024]{2,1,0:T(8,128)(2,1)}, bf16[4,1024,1024]{2,1,0:T(8,128)(2,1)}, bf16[4,1024,1024]{2,1,0:T(8,128)(2,1)}) custom-call(s32[2]{0:T(128)S(1)} %pad_add_fusion.1.w_ref, ...), custom_call_target="tpu_custom_call", output_to_operand_aliasing={{0}: (6, {}), {1}: (7, {}), {2}: (8, {}), {3}: (9, {})} | custom-call | flops 17179869184 | bytes 41943040 | tf_op jit(solution)/shard_map/ffn_other/pallas_call | solution.py:941
  481.5 29.6 %weight_grad.4 = bf16[2048,1024]{1,0:T(8,128)(2,1)} custom-call(bf16[4096,2048]{1,0:T(8,128)(2,1)} %bitcast.40, bf16[4096,1024]{1,0:T(8,128)(2,1)} %bitcast.44), custom_call_target="tpu_custom_call" | custom-call | flops 17179869184 | bytes 25165824 | tf_op jit(solution)/shard_map/weight_grad/pallas_call | solution.py:1065
  511.1 4.5 all-to-all-start.2
  524.6 29.7 %weight_grad.3 = bf16[2048,1024]{1,0:T(8,128)(2,1)} custom-call(bf16[4096,2048]{1,0:T(8,128)(2,1)} %bitcast.41, bf16[4096,1024]{1,0:T(8,128)(2,1)} %bitcast.43), custom_call_target="tpu_custom_call" | custom-call | flops 17179869184 | bytes 25165824 | tf_op jit(solution)/shard_map/weight_grad/pallas_call | solution.py:1065
  554.2 10.5 %all-to-all-done.2.b_ref = bf16[8,256,1024]{2,1,0:T(8,128)(2,1)} async-done(((bf16[8,256,1024]{2,1,0:T(8,128)(2,1)}), bf16[8,256,1024]{2,1,0:T(8,128)(2,1)}, u32[]{:S(2)}, u32[]{:S(2)}) %all-to-all-start.2) | async-done | bytes 4194336 | tf_op jit(solution)/shard_map/all_to_all | solution.py:85
  564.8 4.7 all-to-all-start.1
  569.5 110.7 %pull_tokens.1 = (f32[128,2048]{1,0:T(8,128)}, bf16[128,2048]{1,0:T(8,128)(2,1)S(1)}, f32[2,2048]{1,0:T(2,128)S(1)}) custom-call(bf16[1024,2048]{1,0:T(8,128)(2,1)} %get-tuple-element.67.p_ref, bf16[1024,2048]{1,0:T(8,128)(2,1)} %copy-done.4, bf16[128,2048]{1,0:T(8,128)(2,1)S(1)} %copy-done, f32[1,2048]{1,0:T(1,128)S(1)} %bitcast.29, f32[128,2048]{1,0:T(8,128)} %copy-done.8, ...), custom_call_target="tpu_custom_call" | custom-call | flops 49999998976 | bytes 13107200 | tf_op jit(solution)/shard_map/pull_tokens/pallas_call | solution.py:648
  685.0 3.2 join_heads.1
  688.2 31.2 %weight_grad.5 = f32[1024,2048]{1,0:T(8,128)} custom-call(bf16[4096,1024]{1,0:T(8,128)(2,1)} %bitcast.42, bf16[4096,2048]{1,0:T(8,128)(2,1)} %bitcast.39), custom_call_target="tpu_custom_call" | custom-call | flops 17179869184 | bytes 25165824 | tf_op jit(solution)/shard_map/weight_grad/pallas_call | solution.py:1065
  719.4 7.3 join_columns.3
  726.7 7.3 join_columns.2
  (63 shorter events, 31.1 us)
Async XLA Ops:
  237.1 74.7 %collective-permute-start.6 = (bf16[512,2048]{1,0:T(8,128)(2,1)}, bf16[512,2048]{1,0:T(8,128)(2,1)S(1)}, u32[]{:S(2)}, u32[]{:S(2)}) collective-permute-start(bf16[512,2048]{1,0:T(8,128)(2,1)} %constant_dynamic-slice_fusion), channel_id=1, source_target_pairs={{0,8},{8,16},{16,24},{24,0},{1,9},{9,17},{17,25},{25,1},{2,10},{10... | collective-permute-start | bytes 6291464 | tf_op jit(solution)/shard_map/ppermute | solution.py:1114
  237.3 25.7 %copy-start.1 = (f32[2048]{0:T(1024)S(1)}, f32[2048]{0:T(1024)}, u32[]{:S(2)}) copy-start(f32[2048]{0:T(1024)} %param.19) | copy-start | bytes 24580
  237.3 25.7 %copy-start.6 = (f32[128,2048]{1,0:T(8,128)S(1)}, f32[128,2048]{1,0:T(8,128)}, u32[]{:S(2)}) copy-start(f32[128,2048]{1,0:T(8,128)} %get-tuple-element.58.m_ref.mid_ref) | copy-start | bytes 3145732
  237.3 25.7 %copy-start.9 = (bf16[128,2048]{1,0:T(8,128)(2,1)S(1)}, bf16[128,2048]{1,0:T(8,128)(2,1)}, u32[]{:S(2)}) copy-start(bf16[128,2048]{1,0:T(8,128)(2,1)} %get-tuple-element.59.g_ref) | copy-start | bytes 1572868
  261.0 2.0 copy-start.5
  308.8 2.0 copy-start.3
  311.8 51.0 %collective-permute-start.7 = (bf16[512,2048]{1,0:T(8,128)(2,1)S(1)}, bf16[512,2048]{1,0:T(8,128)(2,1)}, u32[]{:S(2)}, u32[]{:S(2)}) collective-permute-start(bf16[512,2048]{1,0:T(8,128)(2,1)S(1)} %collective-permute-done.6.held_ref), channel_id=1, source_target_pairs={{0,8},{8,16},{16,24},{24,0},{1,9},{9,17},{17,25},{25,1},{2,10},{10... | collective-permute-start | bytes 6291464 | tf_op jit(solution)/shard_map/ppermute | solution.py:1114
  339.9 8.9 %copy-start.11 = (s32[1,1024]{1,0:T(1,128)S(1)}, s32[1,1024]{1,0:T(1,128)}, u32[]{:S(2)}) copy-start(s32[1,1024]{1,0:T(1,128)} %deal_ref.1) | copy-start | bytes 12292
  339.9 44.6 %all-to-all-start = ((bf16[8,256,384]{2,1,0:T(8,128)(2,1)}), bf16[8,256,384]{2,1,0:T(8,128)(2,1)}, u32[]{:S(2)}, u32[]{:S(2)}) async-start(bf16[8,256,384]{2,1,0:T(8,128)(2,1)} %bitcast.33), calls=%async_computation | async-start | bytes 3145728 | tf_op jit(solution)/shard_map/all_to_all | solution.py:85
  344.3 36.6 %collective-permute-start.3 = (bf16[256,2048]{1,0:T(8,128)(2,1)}, bf16[256,2048]{1,0:T(8,128)(2,1)}, u32[]{:S(2)}, u32[]{:S(2)}) collective-permute-start(bf16[256,2048]{1,0:T(8,128)(2,1)} %get-tuple-element.78), channel_id=1, source_target_pairs={{0,8},{24,16},{1,9},{25,17},{2,10},{26,18},{3,11},{27,19},{4,12},{... | collective-permute-start | bytes 3145736 | tf_op jit(solution)/shard_map/ppermute | solution.py:93
  349.1 81.2 %collective-permute-start.11 = (bf16[512,2048]{1,0:T(8,128)(2,1)S(1)}, bf16[512,2048]{1,0:T(8,128)(2,1)}, u32[]{:S(2)}, u32[]{:S(2)}) collective-permute-start(bf16[512,2048]{1,0:T(8,128)(2,1)S(1)} %collective-permute-done.6.held_ref), channel_id=1, source_target_pairs={{0,1},{1,0},{2,3},{3,2},{4,5},{5,4},{6,7},{7,6},{8,9},{9,8},{10,11... | collective-permute-start | bytes 6291464 | tf_op jit(solution)/shard_map/ppermute | solution.py:1116
  362.8 67.5 %collective-permute-start.8 = (bf16[512,2048]{1,0:T(8,128)(2,1)}, bf16[512,2048]{1,0:T(8,128)(2,1)}, u32[]{:S(2)}, u32[]{:S(2)}) collective-permute-start(bf16[512,2048]{1,0:T(8,128)(2,1)} %collective-permute-done.7.held_ref), channel_id=1, source_target_pairs={{0,8},{8,16},{16,24},{24,0},{1,9},{9,17},{17,25},{25,1},{2,10},{10... | collective-permute-start | bytes 6291464 | tf_op jit(solution)/shard_map/ppermute | solution.py:1114
  379.1 68.1 %collective-permute-start.10 = (bf16[512,2048]{1,0:T(8,128)(2,1)}, bf16[512,2048]{1,0:T(8,128)(2,1)}, u32[]{:S(2)}, u32[]{:S(2)}) collective-permute-start(bf16[512,2048]{1,0:T(8,128)(2,1)} %collective-permute-done.7.held_ref), channel_id=1, source_target_pairs={{0,1},{1,0},{2,3},{3,2},{4,5},{5,4},{6,7},{7,6},{8,9},{9,8},{10,11... | collective-permute-start | bytes 6291464 | tf_op jit(solution)/shard_map/ppermute | solution.py:1116
  383.8 135.1 %collective-permute-start.4 = (bf16[256,2048]{1,0:T(8,128)(2,1)}, bf16[256,2048]{1,0:T(8,128)(2,1)S(1)}, u32[]{:S(2)}, u32[]{:S(2)}) collective-permute-start(bf16[256,2048]{1,0:T(8,128)(2,1)} %add_convert_fusion.3), channel_id=1, source_target_pairs={{8,16},{16,8},{9,17},{17,9},{10,18},{18,10},{11,19},{19,11},{12,20... | collective-permute-start | bytes 3145736 | tf_op jit(solution)/shard_map/ppermute | solution.py:97
  384.5 131.1 %collective-permute-start = (bf16[8,256,384]{2,1,0:T(8,128)(2,1)}, bf16[8,256,384]{2,1,0:T(8,128)(2,1)}, u32[]{:S(2)}, u32[]{:S(2)}) collective-permute-start(bf16[8,256,384]{2,1,0:T(8,128)(2,1)} %all-to-all-done), channel_id=1, source_target_pairs={{0,8},{24,16},{1,9},{25,17},{2,10},{26,18},{3,11},{27,19},{4,12},{... | collective-permute-start | bytes 4718600 | tf_op jit(solution)/shard_map/ppermute | solution.py:93
  430.3 34.2 %collective-permute-start.9 = (bf16[512,2048]{1,0:T(8,128)(2,1)}, bf16[512,2048]{1,0:T(8,128)(2,1)S(1)}, u32[]{:S(2)}, u32[]{:S(2)}) collective-permute-start(bf16[512,2048]{1,0:T(8,128)(2,1)} %collective-permute-done.8.held_ref), channel_id=1, source_target_pairs={{0,1},{1,0},{2,3},{3,2},{4,5},{5,4},{6,7},{7,6},{8,9},{9,8},{10,11... | collective-permute-start | bytes 6291464 | tf_op jit(solution)/shard_map/ppermute | solution.py:1116
  511.1 53.7 %all-to-all-start.2 = ((bf16[8,256,1024]{2,1,0:T(8,128)(2,1)}), bf16[8,256,1024]{2,1,0:T(8,128)(2,1)}, u32[]{:S(2)}, u32[]{:S(2)}) async-start(bf16[8,256,1024]{2,1,0:T(8,128)(2,1)} %bitcast.32), calls=%async_computation.2 | async-start | bytes 8388608 | tf_op jit(solution)/shard_map/all_to_all | solution.py:85
  517.9 3.8 collective-permute-start.1
  520.4 160.4 %collective-permute-start.5 = (bf16[256,2048]{1,0:T(8,128)(2,1)S(1)}, bf16[256,2048]{1,0:T(8,128)(2,1)S(1)}, u32[]{:S(2)}, u32[]{:S(2)}) collective-permute-start(bf16[256,2048]{1,0:T(8,128)(2,1)S(1)} %add_convert_fusion.2), channel_id=1, source_target_pairs={{8,0},{16,24},{9,1},{17,25},{10,2},{18,26},{11,3},{19,27},{12,4},{... | collective-permute-start | bytes 3145736 | tf_op jit(solution)/shard_map/ppermute | solution.py:101
  523.3 159.0 %collective-permute-start.2 = (bf16[8,256,384]{2,1,0:T(8,128)(2,1)}, bf16[8,256,384]{2,1,0:T(8,128)(2,1)}, u32[]{:S(2)}, u32[]{:S(2)}) collective-permute-start(bf16[8,256,384]{2,1,0:T(8,128)(2,1)} %add_convert_fusion), channel_id=1, source_target_pairs={{8,0},{16,24},{9,1},{17,25},{10,2},{18,26},{11,3},{19,27},{12,4},{... | collective-permute-start | bytes 4718600 | tf_op jit(solution)/shard_map/ppermute | solution.py:101
  564.8 4.7 copy-start
  564.8 4.7 copy-start.2
  564.8 161.9 %all-to-all-start.1 = ((bf16[8,256,1024]{2,1,0:T(8,128)(2,1)}), bf16[8,256,1024]{2,1,0:T(8,128)(2,1)}, u32[]{:S(2)}, u32[]{:S(2)}) async-start(bf16[8,256,1024]{2,1,0:T(8,128)(2,1)} %bitcast.31), calls=%async_computation.1 | async-start | bytes 8388608 | tf_op jit(solution)/shard_map/all_to_all | solution.py:85
  726.7 8.1 %copy-start.10 = (f32[128,2048]{1,0:T(8,128)S(1)}, f32[128,2048]{1,0:T(8,128)}, u32[]{:S(2)}) copy-start(f32[128,2048]{1,0:T(8,128)} %get-tuple-element.109) | copy-start | bytes 3145732
  (3 other events, 4.2 us)

commit v5 on v4

--- a/solution.py
+++ b/solution.py
@@ -101,6 +101,23 @@
         moved = lax.ppermute(x, "rep", [(near, near - 1), (far, far + 1)])
         x = jnp.where((where == near - 1) | (where == far + 1), moved, x)
     return x
+
+
+def sum_over_replicas(arrays):
+    count = lax.axis_size("rep")
+    where = lax.axis_index("rep")
+    half = count // 2
+    for hop in range(half):
+        inward = [(hop, hop + 1), (count - 1 - hop, count - 2 - hop)]
+        moved = [lax.ppermute(x, "rep", inward) for x in arrays]
+        yield moved
+        arrays = [(x.astype(F32) + y.astype(F32)).astype(BF16) for x, y in zip(arrays, moved)]
+    for hop in range(half - 1):
+        near, far = half - 1 - hop, half + hop
+        moved = [lax.ppermute(x, "rep", [(near, near - 1), (far, far + 1)]) for x in arrays]
+        outside = (where == near - 1) | (where == far + 1)
+        arrays = [jnp.where(outside, y, x) for x, y in zip(arrays, moved)]
+    yield arrays
 
 
 MESH = pl.DeviceIdType.MESH
@@ -1121,7 +1138,9 @@
     middle_grad, ffn_gain_part, branch_grad = pull_gather(
         normed_ffn_part, middle, ffn_gain, cot_own, 2
     )
-    branch_grad = branch_grad.reshape(total, width)
+    branch_grad, unused_hop = lax.optimization_barrier(
+        (branch_grad.reshape(total, width), arrivals[0][1])
+    )
     output_part = output_rows(
         jnp.stack([group, here]).astype(jnp.int32), filled[1], down_weight, middle,
         dealing.reshape(total, 1), total,
@@ -1129,18 +1148,31 @@
     normed_part, qkv_grad, output_grad = attention_backward(
         branch_grad, output_weight, attention, q, kv, normed, q_weight, kv_weight, lengths, freq
     )
+    normed_part, unused_hop = lax.optimization_barrier((normed_part, arrivals[1][1]))
     tokens_grad, layer_output, gains = pull_tokens(
         normed_part, output_part, tokens, attn_gain, middle_grad, ffn_gain_part, replicas, 3
     )
-    for where, from_ring, from_core in arrivals:
+    act_grads, tokens_grad = lax.optimization_barrier((act_grads, tokens_grad))
+    qkv_part = exchange(qkv_grad.reshape(n, rows, q_cols + 2 * HEAD))
+    for hop, (where, from_ring, from_core) in enumerate(arrivals):
+        if hop == len(arrivals) - 1:
+            act_grads, qkv_part = lax.optimization_barrier((act_grads, qkv_part))
         filled = ffn_other(where, from_ring, from_core, act_grads, gate_cols, up_cols, filled)
     all_normed, all_activated, all_gate_grad, all_up_grad = filled
 
+    output_grad, qkv_part, unused_hop = lax.optimization_barrier(
+        (output_grad, qkv_part, arrivals[-1][1])
+    )
+    summed = sum_over_replicas([output_grad, qkv_part])
+    output_moved = next(summed)
     gate_part = exchange(weight_grad(all_normed, all_gate_grad, BF16).reshape(n, rows, ff_cols))
+    all_up_grad, unused_move = lax.optimization_barrier((all_up_grad, output_moved))
+    output_moved = next(summed)
     up_part = exchange(weight_grad(all_normed, all_up_grad, BF16).reshape(n, rows, ff_cols))
+    all_activated, unused_move = lax.optimization_barrier((all_activated, output_moved))
     down_grad = weight_grad(all_activated, down_grads, F32)
-    output_grad = rep_sum(output_grad)
-    qkv_part = rep_sum(exchange(qkv_grad.reshape(n, rows, q_cols + 2 * HEAD)))
+    for output_grad, qkv_part in summed:
+        pass
     return (
         layer_output,
         tokens_grad,

time: 746 us -> 684 us (0.917)
  Pallas kernels: 613 us -> 557 us
  starting transfers between devices: 33.5 us -> 24 us
    pallas_call x1, Pallas kernels: 111 us -> 54.4 us  [pull_tokens(): pl.pallas_call(kernel, out_shape=(jax.ShapeDtypeStruct((rows, width), F32...]
    ppermute x6, waiting for transfers between devices: 1.75 us -> 38.5 us  [the longest x4 20.8 us: sum_over_replicas(): moved = [lax.ppermute(x, 'rep', inward) for x in arrays]]
    ppermute x3, waiting for transfers between devices: 49.2 us -> 17.8 us  [per_device_plane(): held = lax.ppermute(held, 'rep', onward)]
    ppermute x6, starting transfers between devices: 18.9 us -> 9.07 us  [the longest x4 6.23 us: sum_over_replicas(): moved = [lax.ppermute(x, 'rep', inward) for x in arrays]]
  transfers between devices with their start and end apart: 15 -> 15, of which waited for: 4 -> 5; matrix products, arithmetic and copies ran while one was open for 2% -> 1% of each run, Pallas kernels for 51% -> 43%
where the time goes in v5:
time: 684 us; the launch traced here: 675 us
  Pallas kernels  557 us (81%)
  waiting for transfers between devices  68.8 us (10%)
  starting transfers between devices  24 us (4%)
  local copies, waits for them, and re-layouts  14.7 us (2%)
  other arithmetic  8.69 us (1%)
    pallas_call x1, Pallas kernels, front(): pl.pallas_call(kernel, out_shape=(rows8, jax.ShapeDtypeStruct((total, q_c...  233 us
    pallas_call x3, Pallas kernels, weight_grad(): pl.pallas_call(kernel, grid=(steps,), in_specs=[pl.BlockSpec((block, m),...  91.1 us
    pallas_call x1, Pallas kernels, pull_tokens(): pl.pallas_call(kernel, out_shape=(jax.ShapeDtypeStruct((rows, width), F32...  54.4 us
    pallas_call x3, Pallas kernels, ffn_other(): pl.pallas_call(kernel, grid_spec=pltpu.PrefetchScalarGridSpec(num_scalar_...  51.2 us
    pallas_call x1, Pallas kernels, pull_gather(): pl.pallas_call(kernel, out_shape=(jax.ShapeDtypeStruct((rows, width), F32...  45.8 us
    pallas_call x1, Pallas kernels, attention_backward(): pl.pallas_call(kernel, out_shape=(jax.ShapeDtypeStruct((total, width), BF...  27.5 us
    pallas_call x1, Pallas kernels, ffn_own(): pl.pallas_call(kernel, grid_spec=pltpu.PrefetchScalarGridSpec(num_scalar_...  23.9 us
    ppermute x4, waiting for transfers between devices, sum_over_replicas(): moved = [lax.ppermute(x, 'rep', inward) for x in arrays]  20.8 us
  transfers between devices with their start and end apart: 15, of which 5 were waited for; matrix products, arithmetic and copies ran while one was open for 1% of the time, Pallas kernels for 43%

profile of v5, /device:TPU:0, one launch (start us, length us, event | category | flops | bytes accessed | tf_op | source)
XLA Modules:
  0.0 674.6 jit_solution(5139899976204430339)
XLA Ops:
  1.3 232.7 %front.1 = (bf16[8,128,2048]{2,1,0:T(8,128)(2,1)}, bf16[1024,256]{1,0:T(8,128)(2,1)}, bf16[1024,128]{1,0:T(8,128)(2,1)}, bf16[1024,256]{1,0:T(8,128)(2,1)}, bf16...) custom-call(bf16[128,2048]{1,0:T(8,128)(2,1)} %h_ref.1, ...), custom_call_target="tpu_custom_call" | custom-call | flops 199999995904 | bytes 52428800 | tf_op jit(solution)/shard_map/front/pallas_call | solution.py:504
  234.0 3.2 constant_dynamic-slice_fusion
  237.3 23.9 %ffn_own.1 = (bf16[4,1024,2048]{2,1,0:T(8,128)(2,1)}, bf16[4,1024,1024]{2,1,0:T(8,128)(2,1)}, bf16[4,1024,1024]{2,1,0:T(8,128)(2,1)}, bf16[4,1024,1024]{2,1,0:T(8,128)(2,1)}, bf16[1024,2048]{1,0:T(8,128)(2,1)S(1)}) custom-call(s32[1]{0:T(128)} %bitcast.g_ref, bf16[1024,2048]{1,0:T(8,128)(2,1)} %bitcast.35, bf16[4,1024,1024]{2,1,0:T(8,128)(2,1)} %get-tuple-element.96.ag_ref, ...), custom_call_target="tpu_custom_call" | custom-call | flops 25769803776 | bytes 41943040 | tf_op jit(solution)/shard_map/ffn_own/pallas_call | solution.py:901
  263.2 45.8 %pull_gather.1 = (f32[128,2048]{1,0:T(8,128)S(1)}, f32[1,2048]{1,0:T(1,128)S(1)}, bf16[8,128,2048]{2,1,0:T(8,128)(2,1)S(1)}) custom-call(bf16[1024,2048]{1,0:T(8,128)(2,1)} %copy-done.5, f32[128,2048]{1,0:T(8,128)S(1)} %copy-done.6, f32[1,2048]{1,0:T(1,128)S(1)} %bitcast.27, bf16[128,2048]{1,0:T(8,128)(2,1)S(1)} %copy-done.9), custom_call_target="tpu_custom_call" | custom-call | flops 49999998976 | bytes 13107200 | tf_op jit(solution)/shard_map/pull_gather/pallas_call | solution.py:587
  313.7 12.6 %output_rows.1.o_ref = bf16[1024,2048]{1,0:T(8,128)(2,1)S(1)} custom-call(s32[2]{0:T(128)S(1)} %pad_add_fusion.w_ref, bf16[4,1024,1024]{2,1,0:T(8,128)(2,1)} %get-tuple-element.80.act_ref.rest_1_, bf16[1024,2048]{1,0:T(8,128)(2,1)} %wd_ref.3, f32[128,2048]{1,0:T(8,128)S(1)} %copy-done.7, s32[1024,1]{1,0:T(8,128)S(1)} %copy.36.deal_ref), custom_call_target="tpu_custom_call" | custom-call | flops 17179869184 | bytes 12582912 | tf_op jit(solution)/shard_map/output_rows/pallas_call | solution.py:997
  329.0 27.5 %attention_backward.1 = (bf16[1024,2048]{1,0:T(8,128)(2,1)}, bf16[2048,384]{1,0:T(8,128)(2,1)}, bf16[256,2048]{1,0:T(8,128)(2,1)}) custom-call(bf16[1024,2048]{1,0:T(8,128)(2,1)} %bitcast.30, bf16[256,2048]{1,0:T(8,128)(2,1)} %wo_ref.3, bf16[1024,256]{1,0:T(8,128)(2,1)} %get-tuple-element.72.a_ref, bf16[1024,256]{1,0:T(8,128)(2,1)} %get-tuple-element.73.q_ref, ...), custom_call_target="tpu_custom_call" | custom-call | flops 30000001024 | bytes 31457280 | tf_op jit(solution)/shard_map/attention_backward/pallas_call | solution.py:850
  356.5 4.4 all-to-all-start
  361.3 17.8 %collective-permute-done.1.held_ref = bf16[512,2048]{1,0:T(8,128)(2,1)} collective-permute-done((bf16[512,2048]{1,0:T(8,128)(2,1)S(1)}, bf16[512,2048]{1,0:T(8,128)(2,1)}, u32[]{:S(2)}, u32[]{:S(2)}) %collective-permute-start.1) | collective-permute-done | bytes 2097184 | tf_op jit(solution)/shard_map/ppermute | solution.py:1131
  379.2 54.4 %pull_tokens.1 = (f32[128,2048]{1,0:T(8,128)}, bf16[128,2048]{1,0:T(8,128)(2,1)S(1)}, f32[2,2048]{1,0:T(2,128)S(1)}) custom-call(bf16[1024,2048]{1,0:T(8,128)(2,1)} %get-tuple-element.79.p_ref, bf16[1024,2048]{1,0:T(8,128)(2,1)} %copy-done.4, bf16[128,2048]{1,0:T(8,128)(2,1)S(1)} %copy-done, f32[1,2048]{1,0:T(1,128)S(1)} %bitcast.29, f32[128,2048]{1,0:T(8,128)} %copy-done.8, ...), custom_call_target="tpu_custom_call" | custom-call | flops 49999998976 | bytes 13107200 | tf_op jit(solution)/shard_map/pull_tokens/pallas_call | solution.py:665
  433.7 16.6 %ffn_other.3 = (bf16[4,1024,2048]{2,1,0:T(8,128)(2,1)}, bf16[4,1024,1024]{2,1,0:T(8,128)(2,1)}, bf16[4,1024,1024]{2,1,0:T(8,128)(2,1)}, bf16[4,1024,1024]{2,1,0:T(8,128)(2,1)}) custom-call(s32[2]{0:T(128)S(1)} %pad_add_fusion.3.w_ref, ...), custom_call_target="tpu_custom_call", output_to_operand_aliasing={{0}: (6, {}), {1}: (7, {}), {2}: (8, {}), {3}: (9, {})} | custom-call | flops 17179869184 | bytes 41943040 | tf_op jit(solution)/shard_map/ffn_other/pallas_call | solution.py:958
  453.9 17.3 %ffn_other.4 = (bf16[4,1024,2048]{2,1,0:T(8,128)(2,1)}, bf16[4,1024,1024]{2,1,0:T(8,128)(2,1)}, bf16[4,1024,1024]{2,1,0:T(8,128)(2,1)}, bf16[4,1024,1024]{2,1,0:T(8,128)(2,1)}) custom-call(s32[2]{0:T(128)S(1)} %pad_add_fusion.2.w_ref, ...), custom_call_target="tpu_custom_call", output_to_operand_aliasing={{0}: (6, {}), {1}: (7, {}), {2}: (8, {}), {3}: (9, {})} | custom-call | flops 17179869184 | bytes 41943040 | tf_op jit(solution)/shard_map/ffn_other/pallas_call | solution.py:958
  471.1 17.3 %ffn_other.5 = (bf16[4,1024,2048]{2,1,0:T(8,128)(2,1)}, bf16[4,1024,1024]{2,1,0:T(8,128)(2,1)}, bf16[4,1024,1024]{2,1,0:T(8,128)(2,1)}, bf16[4,1024,1024]{2,1,0:T(8,128)(2,1)}) custom-call(s32[2]{0:T(128)S(1)} %pad_add_fusion.1.w_ref, ...), custom_call_target="tpu_custom_call", output_to_operand_aliasing={{0}: (6, {}), {1}: (7, {}), {2}: (8, {}), {3}: (9, {})} | custom-call | flops 17179869184 | bytes 41943040 | tf_op jit(solution)/shard_map/ffn_other/pallas_call | solution.py:958
  488.4 20.8 %collective-permute-done.3 = bf16[8,256,384]{2,1,0:T(8,128)(2,1)S(1)} collective-permute-done((bf16[8,256,384]{2,1,0:T(8,128)(2,1)}, bf16[8,256,384]{2,1,0:T(8,128)(2,1)S(1)}, u32[]{:S(2)}, u32[]{:S(2)}) %collective-permute-start.3) | collective-permute-done | bytes 1572896 | tf_op jit(solution)/shard_map/ppermute | solution.py:112
  509.2 30.2 %weight_grad.4 = bf16[2048,1024]{1,0:T(8,128)(2,1)} custom-call(bf16[4096,2048]{1,0:T(8,128)(2,1)} %bitcast.40, bf16[4096,1024]{1,0:T(8,128)(2,1)} %bitcast.44), custom_call_target="tpu_custom_call" | custom-call | flops 17179869184 | bytes 25165824 | tf_op jit(solution)/shard_map/weight_grad/pallas_call | solution.py:1082
  539.5 4.7 all-to-all-start.2
  551.2 29.7 %weight_grad.3 = bf16[2048,1024]{1,0:T(8,128)(2,1)} custom-call(bf16[4096,2048]{1,0:T(8,128)(2,1)} %bitcast.41, bf16[4096,1024]{1,0:T(8,128)(2,1)} %bitcast.43), custom_call_target="tpu_custom_call" | custom-call | flops 17179869184 | bytes 25165824 | tf_op jit(solution)/shard_map/weight_grad/pallas_call | solution.py:1082
  580.9 12.4 %all-to-all-done.2.b_ref = bf16[8,256,1024]{2,1,0:T(8,128)(2,1)} async-done(((bf16[8,256,1024]{2,1,0:T(8,128)(2,1)}), bf16[8,256,1024]{2,1,0:T(8,128)(2,1)}, u32[]{:S(2)}, u32[]{:S(2)}) %all-to-all-start.2) | async-done | bytes 4194336 | tf_op jit(solution)/shard_map/all_to_all | solution.py:85
  593.3 4.5 all-to-all-start.1
  600.7 2.7 select_convert_fusion
  606.5 31.2 %weight_grad.5 = f32[1024,2048]{1,0:T(8,128)} custom-call(bf16[4096,1024]{1,0:T(8,128)(2,1)} %bitcast.42, bf16[4096,2048]{1,0:T(8,128)(2,1)} %bitcast.39), custom_call_target="tpu_custom_call" | custom-call | flops 17179869184 | bytes 25165824 | tf_op jit(solution)/shard_map/weight_grad/pallas_call | solution.py:1082
  637.7 15.5 %collective-permute-done.5 = bf16[8,256,384]{2,1,0:T(8,128)(2,1)S(1)} collective-permute-done((bf16[8,256,384]{2,1,0:T(8,128)(2,1)S(1)}, bf16[8,256,384]{2,1,0:T(8,128)(2,1)S(1)}, u32[]{:S(2)}, u32[]{:S(2)}) %collective-permute-start.5) | collective-permute-done | bytes 1572896 | tf_op jit(solution)/shard_map/ppermute | solution.py:117
  654.6 3.2 join_heads.1
  657.8 7.3 %join_columns.3 = f32[256,8192]{1,0:T(8,128)} custom-call(bf16[8,256,1024]{2,1,0:T(8,128)(2,1)} %all-to-all-done.2.b_ref), custom_call_target="tpu_custom_call" | custom-call | flops 2097152 | bytes 12582912 | tf_op jit(solution)/shard_map/join_columns/pallas_call | solution.py:1026
  665.0 7.3 %join_columns.2 = f32[256,8192]{1,0:T(8,128)} custom-call(bf16[8,256,1024]{2,1,0:T(8,128)(2,1)} %all-to-all-done.1.b_ref), custom_call_target="tpu_custom_call" | custom-call | flops 2097152 | bytes 12582912 | tf_op jit(solution)/shard_map/join_columns/pallas_call | solution.py:1026
  (69 shorter events, 30.1 us)
Async XLA Ops:
  237.1 91.3 %collective-permute-start = (bf16[512,2048]{1,0:T(8,128)(2,1)}, bf16[512,2048]{1,0:T(8,128)(2,1)S(1)}, u32[]{:S(2)}, u32[]{:S(2)}) collective-permute-start(bf16[512,2048]{1,0:T(8,128)(2,1)} %constant_dynamic-slice_fusion), channel_id=1, source_target_pairs={{0,8},{8,16},{16,24},{24,0},{1,9},{9,17},{17,25},{25,1},{2,10},{10... | collective-permute-start | bytes 6291464 | tf_op jit(solution)/shard_map/ppermute | solution.py:1131
  237.3 25.9 %copy-start.1 = (f32[2048]{0:T(1024)S(1)}, f32[2048]{0:T(1024)}, u32[]{:S(2)}) copy-start(f32[2048]{0:T(1024)} %param.19) | copy-start | bytes 24580
  237.3 25.9 %copy-start.6 = (f32[128,2048]{1,0:T(8,128)S(1)}, f32[128,2048]{1,0:T(8,128)}, u32[]{:S(2)}) copy-start(f32[128,2048]{1,0:T(8,128)} %get-tuple-element.68.m_ref.mid_ref) | copy-start | bytes 3145732
  237.3 25.9 %copy-start.9 = (bf16[128,2048]{1,0:T(8,128)(2,1)S(1)}, bf16[128,2048]{1,0:T(8,128)(2,1)}, u32[]{:S(2)}) copy-start(bf16[128,2048]{1,0:T(8,128)(2,1)} %get-tuple-element.69.g_ref) | copy-start | bytes 1572868
  263.2 48.8 %copy-start.14 = (s32[1,1024]{1,0:T(1,128)S(1)}, s32[1,1024]{1,0:T(1,128)}, u32[]{:S(2)}) copy-start(s32[1,1024]{1,0:T(1,128)} %deal_ref.1) | copy-start | bytes 12292
  328.4 50.8 %collective-permute-start.1 = (bf16[512,2048]{1,0:T(8,128)(2,1)S(1)}, bf16[512,2048]{1,0:T(8,128)(2,1)}, u32[]{:S(2)}, u32[]{:S(2)}) collective-permute-start(bf16[512,2048]{1,0:T(8,128)(2,1)S(1)} %collective-permute-done.held_ref), channel_id=1, source_target_pairs={{0,8},{8,16},{16,24},{24,0},{1,9},{9,17},{17,25},{25,1},{2,10},{10... | collective-permute-start | bytes 6291464 | tf_op jit(solution)/shard_map/ppermute | solution.py:1131
  356.5 22.7 %copy-start = (bf16[128,2048]{1,0:T(8,128)(2,1)S(1)}, bf16[128,2048]{1,0:T(8,128)(2,1)}, u32[]{:S(2)}) copy-start(bf16[128,2048]{1,0:T(8,128)(2,1)} %h_ref.1) | copy-start | bytes 1572868
  356.5 22.7 %copy-start.2 = (f32[2048]{0:T(1024)S(1)}, f32[2048]{0:T(1024)}, u32[]{:S(2)}) copy-start(f32[2048]{0:T(1024)} %param.14) | copy-start | bytes 24580
  356.5 93.8 %all-to-all-start = ((bf16[8,256,384]{2,1,0:T(8,128)(2,1)}), bf16[8,256,384]{2,1,0:T(8,128)(2,1)}, u32[]{:S(2)}, u32[]{:S(2)}) async-start(bf16[8,256,384]{2,1,0:T(8,128)(2,1)} %bitcast.33), calls=%async_computation | async-start | bytes 3145728 | tf_op jit(solution)/shard_map/all_to_all | solution.py:85
  361.0 72.7 %collective-permute-start.11 = (bf16[512,2048]{1,0:T(8,128)(2,1)S(1)}, bf16[512,2048]{1,0:T(8,128)(2,1)S(1)}, u32[]{:S(2)}, u32[]{:S(2)}) collective-permute-start(bf16[512,2048]{1,0:T(8,128)(2,1)S(1)} %collective-permute-done.held_ref), channel_id=1, source_target_pairs={{0,1},{1,0},{2,3},{3,2},{4,5},{5,4},{6,7},{7,6},{8,9},{9,8},{10,11... | collective-permute-start | bytes 6291464 | tf_op jit(solution)/shard_map/ppermute | solution.py:1133
  379.2 74.7 %collective-permute-start.10 = (bf16[512,2048]{1,0:T(8,128)(2,1)}, bf16[512,2048]{1,0:T(8,128)(2,1)}, u32[]{:S(2)}, u32[]{:S(2)}) collective-permute-start(bf16[512,2048]{1,0:T(8,128)(2,1)} %collective-permute-done.1.held_ref), channel_id=1, source_target_pairs={{0,1},{1,0},{2,3},{3,2},{4,5},{5,4},{6,7},{7,6},{8,9},{9,8},{10,11... | collective-permute-start | bytes 6291464 | tf_op jit(solution)/shard_map/ppermute | solution.py:1133
  379.2 54.4 %collective-permute-start.2 = (bf16[512,2048]{1,0:T(8,128)(2,1)}, bf16[512,2048]{1,0:T(8,128)(2,1)}, u32[]{:S(2)}, u32[]{:S(2)}) collective-permute-start(bf16[512,2048]{1,0:T(8,128)(2,1)} %collective-permute-done.1.held_ref), channel_id=1, source_target_pairs={{0,8},{8,16},{16,24},{24,0},{1,9},{9,17},{17,25},{25,1},{2,10},{10... | collective-permute-start | bytes 6291464 | tf_op jit(solution)/shard_map/ppermute | solution.py:1131
  433.6 37.5 %collective-permute-start.9 = (bf16[512,2048]{1,0:T(8,128)(2,1)}, bf16[512,2048]{1,0:T(8,128)(2,1)}, u32[]{:S(2)}, u32[]{:S(2)}) collective-permute-start(bf16[512,2048]{1,0:T(8,128)(2,1)} %collective-permute-done.2.held_ref), channel_id=1, source_target_pairs={{0,1},{1,0},{2,3},{3,2},{4,5},{5,4},{6,7},{7,6},{8,9},{9,8},{10,11... | collective-permute-start | bytes 6291464 | tf_op jit(solution)/shard_map/ppermute | solution.py:1133
  450.3 38.1 %collective-permute-start.6 = (bf16[256,2048]{1,0:T(8,128)(2,1)}, bf16[256,2048]{1,0:T(8,128)(2,1)S(1)}, u32[]{:S(2)}, u32[]{:S(2)}) collective-permute-start(bf16[256,2048]{1,0:T(8,128)(2,1)} %get-tuple-element.95), channel_id=1, source_target_pairs={{0,8},{24,16},{1,9},{25,17},{2,10},{26,18},{3,11},{27,19},{4,12},{... | collective-permute-start | bytes 3145736 | tf_op jit(solution)/shard_map/ppermute | solution.py:112
  452.2 57.0 %collective-permute-start.3 = (bf16[8,256,384]{2,1,0:T(8,128)(2,1)}, bf16[8,256,384]{2,1,0:T(8,128)(2,1)S(1)}, u32[]{:S(2)}, u32[]{:S(2)}) collective-permute-start(bf16[8,256,384]{2,1,0:T(8,128)(2,1)} %all-to-all-done), channel_id=1, source_target_pairs={{0,8},{24,16},{1,9},{25,17},{2,10},{26,18},{3,11},{27,19},{4,12},{... | collective-permute-start | bytes 4718600 | tf_op jit(solution)/shard_map/ppermute | solution.py:112
  509.2 30.2 %copy-start.10 = (bf16[8,256,384]{2,1,0:T(8,128)(2,1)}, bf16[8,256,384]{2,1,0:T(8,128)(2,1)S(1)}, u32[]{:S(2)}) copy-start(bf16[8,256,384]{2,1,0:T(8,128)(2,1)S(1)} %collective-permute-done.3) | copy-start | bytes 4718596
  539.5 4.7 copy-start.12
  539.5 53.8 %all-to-all-start.2 = ((bf16[8,256,1024]{2,1,0:T(8,128)(2,1)}), bf16[8,256,1024]{2,1,0:T(8,128)(2,1)}, u32[]{:S(2)}, u32[]{:S(2)}) async-start(bf16[8,256,1024]{2,1,0:T(8,128)(2,1)} %bitcast.32), calls=%async_computation.2 | async-start | bytes 8388608 | tf_op jit(solution)/shard_map/all_to_all | solution.py:85
  544.6 4.7 collective-permute-start.7
  547.4 56.0 %collective-permute-start.4 = (bf16[8,256,384]{2,1,0:T(8,128)(2,1)S(1)}, bf16[8,256,384]{2,1,0:T(8,128)(2,1)}, u32[]{:S(2)}, u32[]{:S(2)}) collective-permute-start(bf16[8,256,384]{2,1,0:T(8,128)(2,1)S(1)} %add_convert_fusion.1), channel_id=1, source_target_pairs={{8,16},{16,8},{9,17},{17,9},{10,18},{18,10},{11,19},{19,11},{12,20... | collective-permute-start | bytes 4718600 | tf_op jit(solution)/shard_map/ppermute | solution.py:112
  549.7 51.0 %collective-permute-start.8 = (bf16[256,2048]{1,0:T(8,128)(2,1)S(1)}, bf16[256,2048]{1,0:T(8,128)(2,1)}, u32[]{:S(2)}, u32[]{:S(2)}) collective-permute-start(bf16[256,2048]{1,0:T(8,128)(2,1)S(1)} %add_convert_fusion.2), channel_id=1, source_target_pairs={{8,0},{16,24},{9,1},{17,25},{10,2},{18,26},{11,3},{19,27},{12,4},{... | collective-permute-start | bytes 3145736 | tf_op jit(solution)/shard_map/ppermute | solution.py:117
  593.3 71.7 %all-to-all-start.1 = ((bf16[8,256,1024]{2,1,0:T(8,128)(2,1)}), bf16[8,256,1024]{2,1,0:T(8,128)(2,1)}, u32[]{:S(2)}, u32[]{:S(2)}) async-start(bf16[8,256,1024]{2,1,0:T(8,128)(2,1)} %bitcast.31), calls=%async_computation.1 | async-start | bytes 8388608 | tf_op jit(solution)/shard_map/all_to_all | solution.py:85
  605.2 48.1 %collective-permute-start.5 = (bf16[8,256,384]{2,1,0:T(8,128)(2,1)S(1)}, bf16[8,256,384]{2,1,0:T(8,128)(2,1)S(1)}, u32[]{:S(2)}, u32[]{:S(2)}) collective-permute-start(bf16[8,256,384]{2,1,0:T(8,128)(2,1)S(1)} %add_convert_fusion), channel_id=1, source_target_pairs={{8,0},{16,24},{9,1},{17,25},{10,2},{18,26},{11,3},{19,27},{12,4},{... | collective-permute-start | bytes 4718600 | tf_op jit(solution)/shard_map/ppermute | solution.py:117
  665.0 8.1 %copy-start.13 = (f32[128,2048]{1,0:T(8,128)S(1)}, f32[128,2048]{1,0:T(8,128)}, u32[]{:S(2)}) copy-start(f32[128,2048]{1,0:T(8,128)} %get-tuple-element.129) | copy-start | bytes 3145732
  (6 other events, 9.6 us)

commit v6 on v4

--- a/solution.py
+++ b/solution.py
@@ -1000,23 +1000,317 @@
     )(where, activated, down_weight, middle, deal)
 
 
-def join_columns(blocks):
+def join_heads(blocks, q_cols):
     n, rows, cols = blocks.shape
 
-    def kernel(b_ref, o_ref):
-        o_ref[...] = b_ref[0].astype(F32)
+    def kernel(b_ref, q_ref, k_ref, v_ref):
+        for i in range(n):
+            q_ref[:, i * q_cols : (i + 1) * q_cols] = b_ref[i, :, :q_cols].astype(F32)
+        kv = [b_ref[i, :, q_cols:].astype(F32) for i in range(n)]
+        k_ref[...] = jnp.concatenate([x[:, :HEAD] for x in kv], axis=1)
+        v_ref[...] = jnp.concatenate([x[:, HEAD:] for x in kv], axis=1)
 
     return pl.pallas_call(
         kernel,
-        grid=(n,),
-        in_specs=[pl.BlockSpec((1, rows, cols), lambda i: (i, 0, 0))],
-        out_specs=pl.BlockSpec((rows, cols), lambda i: (0, i)),
-        out_shape=jax.ShapeDtypeStruct((rows, n * cols), F32),
+        out_shape=(
+            jax.ShapeDtypeStruct((rows, n * q_cols), F32),
+            jax.ShapeDtypeStruct((rows, n * HEAD), F32),
+            jax.ShapeDtypeStruct((rows, n * HEAD), F32),
+        ),
+        name="join_heads",
+    )(blocks)
+
+
+def finish(normed, gate_grad, up_grad, activated, down_grad, output_part, qkv_part, collective_id):
+    depth, width = normed.shape
+    cols = gate_grad.shape[1]
+    rows = width // 8
+    tall = cols // rows
+    steps = 8 + tall
+    chunks = 4
+    sums = (output_part, qkv_part)
+
+    def kernel(
+        nf_hbm, gg_hbm, ug_hbm, act_hbm, dg_hbm, o_in, qkv_in,
+        gate_out, up_out, down_out, o_out, qkv_out,
+        gg, ug, dg, left, stage, tall_stage, o_mid, qkv_mid, o_last, qkv_last,
+        load_sems, left_sems, own_sems, tall_sems, push_sems, relay_sems,
+    ):
+        me = lax.axis_index("shard")
+        group = lax.axis_index("rep")
+        inner = (group == 1) | (group == 2)
+        outer = (group == 0) | (group == 3)
+        beside = group + 1 - 2 * lax.rem(group, 2)
+        across = 3 - group
+
+        def peer_of(i):
+            mask = 7 - i
+            index = 0
+            for weight in (1, 2, 4):
+                bits = lax.rem(lax.div(me, weight), 2) + lax.rem(lax.div(mask, weight), 2)
+                index = index + weight * lax.rem(bits, 2)
+            return index
+
+        def start_left(i, slot):
+            @pl.when(i < 8)
+            def _():
+                first = pl.multiple_of(peer_of(i) * rows, rows)
+                pltpu.make_async_copy(
+                    nf_hbm.at[:, pl.ds(first, rows)], left.at[slot], left_sems.at[slot]
+                ).start()
+
+            @pl.when((i >= 8) & (i < steps))
+            def _():
+                first = pl.multiple_of((i - 8) * rows, rows)
+                pltpu.make_async_copy(
+                    act_hbm.at[:, pl.ds(first, rows)], left.at[slot], left_sems.at[slot]
+                ).start()
+
+        def wait_left(slot):
+            pltpu.make_async_copy(
+                nf_hbm.at[:, pl.ds(0, rows)], left.at[slot], left_sems.at[slot]
+            ).wait()
+
+        loads = [
+            pltpu.make_async_copy(source, target, load_sems.at[k])
+            for k, (source, target) in enumerate(((gg_hbm, gg), (ug_hbm, ug), (dg_hbm, dg)))
+        ]
+        start_left(0, 0)
+        for load in loads:
+            load.start()
+        barrier = pltpu.get_barrier_semaphore()
+        for mask in range(1, 8):
+            pl.semaphore_signal(
+                barrier, inc=1, device_id={"shard": flip(me, mask)}, device_id_type=MESH
+            )
+        for neighbour in (beside, across):
+            pl.semaphore_signal(
+                barrier, inc=1, device_id={"rep": neighbour}, device_id_type=MESH
+            )
+        pl.semaphore_wait(barrier, 9)
+
+        arrays = ((o_in, o_mid, o_last, o_out), (qkv_in, qkv_mid, qkv_last, qkv_out))
+
+        def relay_copy(stage_index, k, c, target):
+            start, mid, last, out = arrays[k]
+            size = start.shape[0] // chunks
+            part = pl.ds(pl.multiple_of(c * size, size), size)
+            source, arrived = ((start, mid), (mid, last), (out, out))[stage_index]
+            return pltpu.make_async_remote_copy(
+                src_ref=source.at[part],
+                dst_ref=arrived.at[part],
+                send_sem=relay_sems.at[0, stage_index, k * chunks + c],
+                recv_sem=relay_sems.at[1, stage_index, k * chunks + c],
+                device_id={"rep": target},
+                device_id_type=MESH,
+            )
+
+        @pl.when(outer)
+        def _():
+            for c in range(chunks):
+                for k in range(2):
+                    relay_copy(0, k, c, beside).start()
+
+        def relay(t):
+            def part_of(k, c):
+                size = arrays[k][0].shape[0] // chunks
+                return pl.ds(pl.multiple_of(c * size, size), size)
+
+            @pl.when(inner & (t < chunks))
+            def _():
+                for k in range(2):
+                    start, mid, last, out = arrays[k]
+                    part = part_of(k, t)
+                    relay_copy(0, k, t, beside).wait_recv()
+                    mid[part, :] = (start[part, :].astype(F32) + mid[part, :].astype(F32)).astype(BF16)
+                    relay_copy(1, k, t, across).start()
+
+            @pl.when(inner & (t >= 1) & (t <= chunks))
+            def _():
+                for k in range(2):
+                    start, mid, last, out = arrays[k]
+                    part = part_of(k, t - 1)
+                    relay_copy(1, k, t - 1, across).wait_recv()
+                    out[part, :] = (mid[part, :].astype(F32) + last[part, :].astype(F32)).astype(BF16)
+                    relay_copy(2, k, t - 1, beside).start()
+
+            @pl.when(outer & (t >= 2) & (t <= chunks + 1))
+            def _():
+                for k in range(2):
+                    relay_copy(2, k, t - 2, beside).wait_recv()
+
+        outputs = (gate_out, up_out)
+        own_columns = pl.ds(pl.multiple_of(me * cols, cols), cols)
+
+        def push(i, j, target):
+            return send(
+                stage.at[i, j], outputs[j].at[:, own_columns], push_sems, 2 * i + j, target
+            )
+
+        def wide(i, carry):
+            slot = lax.rem(i, 2)
+            start_left(i + 1, 1 - slot)
+            wait_left(slot)
+            for j, right in enumerate((gg, ug)):
+
+                @pl.when(i == 0)
+                def _():
+                    loads[j].wait()
+
+                stage[i, j] = t_mm(left[slot], right[...]).astype(BF16)
+
+                @pl.when(i < 7)
+                def _():
+                    push(i, j, peer_of(i)).start()
+
+                @pl.when(i == 7)
+                def _():
+                    pltpu.make_async_copy(
+                        stage.at[7, j], outputs[j].at[:, own_columns], own_sems.at[j]
+                    ).start()
+
+            @pl.when(lax.rem(i, 2) == 1)
+            def _():
+                relay(lax.div(i, 2))
+
+            return carry
+
+        lax.fori_loop(0, 8, wide, 0)
+        loads[2].wait()
+
+        def tall_copy(i):
+            slot = lax.rem(i, 2)
+            first = pl.multiple_of((i - 8) * rows, rows)
+            return pltpu.make_async_copy(
+                tall_stage.at[slot], down_out.at[pl.ds(first, rows), :], tall_sems.at[slot]
+            )
+
+        def high(i, carry):
+            slot = lax.rem(i, 2)
+            start_left(i + 1, 1 - slot)
+            wait_left(slot)
+
+            @pl.when(i >= 10)
+            def _():
+                tall_copy(i - 2).wait()
+
+            tall_stage[slot] = t_mm(left[slot], dg[...]).astype(BF16)
+            tall_copy(i).start()
+
+            @pl.when(lax.rem(i, 2) == 1)
+            def _():
+                relay(lax.div(i, 2))
+
+            return carry
+
+        lax.fori_loop(8, steps, high, 0)
+        for i in (steps - 2, steps - 1):
+            tall_copy(i).wait()
+        for j in range(2):
+            pltpu.make_async_copy(
+                stage.at[7, j], outputs[j].at[:, own_columns], own_sems.at[j]
+            ).wait()
+        for t in range(steps // 2, chunks + 2):
+            relay(t)
+
+        def drain(i, carry):
+            for j in range(2):
+                push(i, j, peer_of(i)).wait()
+            return carry
+
+        lax.fori_loop(0, 7, drain, 0)
+
+        @pl.when(outer)
+        def _():
+            for c in range(chunks):
+                for k in range(2):
+                    relay_copy(0, k, c, beside).wait_send()
+
+        @pl.when(inner)
+        def _():
+            for c in range(chunks):
+                for k in range(2):
+                    relay_copy(1, k, c, across).wait_send()
+                    relay_copy(2, k, c, beside).wait_send()
+
+    exchanged = jax.ShapeDtypeStruct((rows, 8 * cols), BF16)
+    return pl.pallas_call(
+        kernel,
+        out_shape=(
+            exchanged,
+            exchanged,
+            jax.ShapeDtypeStruct((cols, width), BF16),
+            jax.ShapeDtypeStruct(output_part.shape, BF16),
+            jax.ShapeDtypeStruct(qkv_part.shape, BF16),
+        ),
+        in_specs=[ANY] * 5 + [VMEM] * 2,
+        out_specs=[ANY] * 3 + [VMEM] * 2,
+        scratch_shapes=[
+            pltpu.VMEM((depth, cols), BF16),
+            pltpu.VMEM((depth, cols), BF16),
+            pltpu.VMEM((depth, width), BF16),
+            pltpu.VMEM((2, depth, rows), BF16),
+            pltpu.VMEM((8, 2, rows, cols), BF16),
+            pltpu.VMEM((2, rows, width), BF16),
+        ]
+        + [pltpu.VMEM(x.shape, BF16) for unused in range(2) for x in sums]
+        + [
+            pltpu.SemaphoreType.DMA((3,)),
+            pltpu.SemaphoreType.DMA((2,)),
+            pltpu.SemaphoreType.DMA((2,)),
+            pltpu.SemaphoreType.DMA((2,)),
+            pltpu.SemaphoreType.DMA((2, 14)),
+            pltpu.SemaphoreType.DMA((2, 3, 2 * chunks)),
+        ],
+        compiler_params=comm_params(collective_id, 62),
         cost_estimate=pl.CostEstimate(
-            flops=n * rows * cols, bytes_accessed=6 * n * rows * cols, transcendentals=0
-        ),
-        name="join_columns",
-    )(blocks)
+            flops=120_000_000_000, bytes_accessed=80 << 20, transcendentals=0
+        ),
+        name="finish",
+    )(normed, gate_grad, up_grad, activated, down_grad, output_part, qkv_part)
+
+
+def output_rows(where, activated, down_weight, middle, deal, total):
+    groups, total, cols = activated.shape
+    local, width = middle.shape
+    block = 256
+
+    def kernel(w_ref, act_ref, wd_ref, mid_ref, deal_ref, o_ref, rows_ref):
+        for i in range(total // block):
+            rows = pl.ds(i * block, block)
+            rows_ref[rows, :] = (RESIDUAL_SCALE * mm(act_ref[0, rows, :], wd_ref[...])).astype(BF16)
+        own = pl.ds(pl.multiple_of(w_ref[1] * local, local), local)
+        rows_ref[own, :] = (rows_ref[own, :].astype(F32) + mid_ref[...]).astype(BF16)
+        for i in range(total // block):
+            rows = pl.ds(i * block, block)
+            packed = lax.broadcasted_iota(jnp.int32, (block, total), 1)
+            chosen = (deal_ref[rows, :] == packed).astype(BF16)
+            o_ref[rows, :] = mm(chosen, rows_ref[...]).astype(BF16)
+
+    def full(shape):
+        return pl.BlockSpec(shape, lambda i, w: (0,) * len(shape), pipeline_mode=pl.Buffered(1))
+
+    return pl.pallas_call(
+        kernel,
+        grid_spec=pltpu.PrefetchScalarGridSpec(
+            num_scalar_prefetch=1,
+            grid=(1,),
+            in_specs=[
+                pl.BlockSpec((1, total, cols), lambda i, w: (w[0], 0, 0), pipeline_mode=pl.Buffered(1)),
+                full(down_weight.shape),
+                full(middle.shape),
+                full(deal.shape),
+            ],
+            out_specs=full((total, width)),
+            scratch_shapes=[pltpu.VMEM((total, width), BF16)],
+        ),
+        out_shape=jax.ShapeDtypeStruct((total, width), BF16),
+        compiler_params=pltpu.CompilerParams(vmem_limit_bytes=48 << 20),
+        cost_estimate=pl.CostEstimate(
+            flops=2 * total * width * (cols + total) * 2, bytes_accessed=12 << 20, transcendentals=0
+        ),
+        name="output_rows",
+    )(where, activated, down_weight, middle, deal)
 
 
 def join_heads(blocks, q_cols):
@@ -1121,7 +1415,9 @@
     middle_grad, ffn_gain_part, branch_grad = pull_gather(
         normed_ffn_part, middle, ffn_gain, cot_own, 2
     )
-    branch_grad = branch_grad.reshape(total, width)
+    branch_grad, unused_hop = lax.optimization_barrier(
+        (branch_grad.reshape(total, width), arrivals[0][1])
+    )
     output_part = output_rows(
         jnp.stack([group, here]).astype(jnp.int32), filled[1], down_weight, middle,
         dealing.reshape(total, 1), total,
@@ -1129,28 +1425,29 @@
     normed_part, qkv_grad, output_grad = attention_backward(
         branch_grad, output_weight, attention, q, kv, normed, q_weight, kv_weight, lengths, freq
     )
+    normed_part, unused_hop = lax.optimization_barrier((normed_part, arrivals[1][1]))
     tokens_grad, layer_output, gains = pull_tokens(
         normed_part, output_part, tokens, attn_gain, middle_grad, ffn_gain_part, replicas, 3
     )
+    act_grads, tokens_grad = lax.optimization_barrier((act_grads, tokens_grad))
+    qkv_part = exchange(qkv_grad.reshape(n, rows, q_cols + 2 * HEAD))
     for where, from_ring, from_core in arrivals:
         filled = ffn_other(where, from_ring, from_core, act_grads, gate_cols, up_cols, filled)
-    all_normed, all_activated, all_gate_grad, all_up_grad = filled
-
-    gate_part = exchange(weight_grad(all_normed, all_gate_grad, BF16).reshape(n, rows, ff_cols))
-    up_part = exchange(weight_grad(all_normed, all_up_grad, BF16).reshape(n, rows, ff_cols))
-    down_grad = weight_grad(all_activated, down_grads, F32)
-    output_grad = rep_sum(output_grad)
-    qkv_part = rep_sum(exchange(qkv_grad.reshape(n, rows, q_cols + 2 * HEAD)))
+    left, *rights = [x.reshape(replicas * total, -1) for x in (filled[0], filled[2], filled[3])]
+    gate_grad, up_grad, down_grad, output_grad, qkv_grad = finish(
+        left, *rights, filled[1].reshape(replicas * total, -1), down_grads.reshape(replicas * total, -1),
+        output_grad, qkv_part.reshape(width, -1), 4,
+    )
     return (
         layer_output,
         tokens_grad,
         gains[0],
-        *join_heads(qkv_part, q_cols),
+        *join_heads(qkv_grad.reshape(n, rows, -1), q_cols),
         output_grad.astype(F32),
         gains[1],
-        join_columns(gate_part),
-        join_columns(up_part),
-        down_grad,
+        gate_grad.astype(F32),
+        up_grad.astype(F32),
+        down_grad.astype(F32),
     )
 
 
@@ -1307,7 +1604,7 @@
     both = P(("rep", "shard"), None)
     rowed = P("shard", None)
     return jax.shard_map(
-        per_device_plane if mesh.shape["shard"] == 8 else per_device,
+        per_device_plane if (mesh.shape["rep"], mesh.shape["shard"]) == (4, 8) else per_device,
         mesh=mesh,
         in_specs=(
             both, P(), rowed, rowed, rowed, rowed, P(), rowed, rowed, rowed,

time: 746 us -> 621 us (0.83)
  Pallas kernels: 613 us -> 557 us
  waiting for transfers between devices: 61.5 us -> 18.1 us
  starting transfers between devices: 33.5 us -> 5.32 us
    pallas_call x1, Pallas kernels: 111 us -> 54.4 us  [pull_tokens(): pl.pallas_call(kernel, out_shape=(jax.ShapeDtypeStruct((rows, width), F32...]
    ppermute x3, waiting for transfers between devices: 49.2 us -> 18.1 us  [per_device_plane(): held = lax.ppermute(held, 'rep', onward)]
    ppermute x6 -> x0, starting transfers between devices: 18.9 us -> none  [the longest x2 14.7 us: rep_sum(): lax.ppermute(x, 'rep', [(hop, hop + 1), (count - 1 - hop, count - 2 - hop)])]
    all_to_all x3 -> x1, waiting for transfers between devices: 10.5 us -> 0.01 us  [exchange(): lax.all_to_all(blocks, 'shard', split_axis=0, concat_axis=0, tiled=True)]
    all_to_all x3 -> x1, starting transfers between devices: 13.6 us -> 4.29 us  [exchange(): lax.all_to_all(blocks, 'shard', split_axis=0, concat_axis=0, tiled=True)]
    convert_element_type x4 -> x3, other arithmetic: 8.24 us -> 15.6 us  [the longest x1 6.73 us: per_device_plane(): gate_grad.astype(F32)]
    pallas_call x5 -> x1, Pallas kernels: 105 us -> 106 us  [finish(): pl.pallas_call(kernel, out_shape=(exchanged, exchanged, jax.ShapeDtypeStr...]
  transfers between devices with their start and end apart: 15 -> 7, of which waited for: 4 -> 1; matrix products, arithmetic and copies ran while one was open for 2% -> 0% of each run, Pallas kernels for 51% -> 35%
where the time goes in v6:
time: 621 us; the launch traced here: 612 us
  Pallas kernels  557 us (90%)
  waiting for transfers between devices  18.1 us (3%)
  other arithmetic  17.4 us (3%)
  local copies, waits for them, and re-layouts  13.3 us (2%)
    pallas_call x1, Pallas kernels, front(): pl.pallas_call(kernel, out_shape=(rows8, jax.ShapeDtypeStruct((total, q_c...  233 us
    pallas_call x1, Pallas kernels, finish(): pl.pallas_call(kernel, out_shape=(exchanged, exchanged, jax.ShapeDtypeStr...  106 us
    pallas_call x1, Pallas kernels, pull_tokens(): pl.pallas_call(kernel, out_shape=(jax.ShapeDtypeStruct((rows, width), F32...  54.4 us
    pallas_call x3, Pallas kernels, ffn_other(): pl.pallas_call(kernel, grid_spec=pltpu.PrefetchScalarGridSpec(num_scalar_...  50.7 us
    pallas_call x1, Pallas kernels, pull_gather(): pl.pallas_call(kernel, out_shape=(jax.ShapeDtypeStruct((rows, width), F32...  45.9 us
    pallas_call x1, Pallas kernels, attention_backward(): pl.pallas_call(kernel, out_shape=(jax.ShapeDtypeStruct((total, width), BF...  27.6 us
    pallas_call x1, Pallas kernels, ffn_own(): pl.pallas_call(kernel, grid_spec=pltpu.PrefetchScalarGridSpec(num_scalar_...  23.9 us
    ppermute x3, waiting for transfers between devices, per_device_plane(): held = lax.ppermute(held, 'rep', onward)  18.1 us
  transfers between devices with their start and end apart: 7, of which 1 were waited for; matrix products, arithmetic and copies ran while one was open for 0% of the time, Pallas kernels for 35%

profile of v6, /device:TPU:0, one launch (start us, length us, event | category | flops | bytes accessed | tf_op | source)
XLA Modules:
  0.0 612.2 jit_solution(1690468252222130310)
XLA Ops:
  1.3 232.7 %front.1 = (bf16[8,128,2048]{2,1,0:T(8,128)(2,1)}, bf16[1024,256]{1,0:T(8,128)(2,1)}, bf16[1024,128]{1,0:T(8,128)(2,1)}, bf16[1024,256]{1,0:T(8,128)(2,1)}, bf16...) custom-call(bf16[128,2048]{1,0:T(8,128)(2,1)} %h_ref.1, ...), custom_call_target="tpu_custom_call" | custom-call | flops 199999995904 | bytes 52428800 | tf_op jit(solution)/shard_map/front/pallas_call | solution.py:487
  234.0 3.2 constant_dynamic-slice_fusion
  237.3 23.9 %ffn_own.1 = (bf16[4,1024,2048]{2,1,0:T(8,128)(2,1)}, bf16[4,1024,1024]{2,1,0:T(8,128)(2,1)}, bf16[4,1024,1024]{2,1,0:T(8,128)(2,1)}, bf16[4,1024,1024]{2,1,0:T(8,128)(2,1)}, bf16[1024,2048]{1,0:T(8,128)(2,1)S(1)}) custom-call(s32[1]{0:T(128)} %bitcast.g_ref, bf16[1024,2048]{1,0:T(8,128)(2,1)} %bitcast.34, bf16[4,1024,1024]{2,1,0:T(8,128)(2,1)} %get-tuple-element.86.ag_ref, ...), custom_call_target="tpu_custom_call" | custom-call | flops 25769803776 | bytes 41943040 | tf_op jit(solution)/shard_map/ffn_own/pallas_call | solution.py:884
  261.2 2.0 copy-done.5
  263.2 45.9 %pull_gather.1 = (f32[128,2048]{1,0:T(8,128)S(1)}, f32[1,2048]{1,0:T(1,128)S(1)}, bf16[8,128,2048]{2,1,0:T(8,128)(2,1)S(1)}) custom-call(bf16[1024,2048]{1,0:T(8,128)(2,1)} %copy-done.5, f32[128,2048]{1,0:T(8,128)S(1)} %copy-done.6, f32[1,2048]{1,0:T(1,128)S(1)} %bitcast.27, bf16[128,2048]{1,0:T(8,128)(2,1)S(1)} %copy-done.8), custom_call_target="tpu_custom_call" | custom-call | flops 49999998976 | bytes 13107200 | tf_op jit(solution)/shard_map/pull_gather/pallas_call | solution.py:570
  309.1 2.0 copy-done.3
  311.1 1.0 copy-done.7
  312.6 12.7 %output_rows.1.o_ref = bf16[1024,2048]{1,0:T(8,128)(2,1)S(1)} custom-call(s32[2]{0:T(128)S(1)} %pad_add_fusion.w_ref, bf16[4,1024,1024]{2,1,0:T(8,128)(2,1)} %get-tuple-element.79.act_ref.rest_1_, bf16[1024,2048]{1,0:T(8,128)(2,1)} %wd_ref.3, f32[128,2048]{1,0:T(8,128)S(1)} %copy-done.6, s32[1024,1]{1,0:T(8,128)S(1)} %copy.36.deal_ref), custom_call_target="tpu_custom_call" | custom-call | flops 17179869184 | bytes 12582912 | tf_op jit(solution)/shard_map/output_rows/pallas_call | solution.py:1293
  325.3 2.0 copy-done.4
  327.7 27.6 %attention_backward.1 = (bf16[1024,2048]{1,0:T(8,128)(2,1)}, bf16[2048,384]{1,0:T(8,128)(2,1)}, bf16[256,2048]{1,0:T(8,128)(2,1)}) custom-call(bf16[1024,2048]{1,0:T(8,128)(2,1)} %bitcast.30, bf16[256,2048]{1,0:T(8,128)(2,1)} %wo_ref.3, bf16[1024,256]{1,0:T(8,128)(2,1)} %get-tuple-element.71.a_ref, bf16[1024,256]{1,0:T(8,128)(2,1)} %get-tuple-element.72.q_ref, ...), custom_call_target="tpu_custom_call" | custom-call | flops 30000001024 | bytes 31457280 | tf_op jit(solution)/shard_map/attention_backward/pallas_call | solution.py:833
  355.3 4.3 all-to-all-start
  360.0 18.1 %collective-permute-done.1.held_ref = bf16[512,2048]{1,0:T(8,128)(2,1)} collective-permute-done((bf16[512,2048]{1,0:T(8,128)(2,1)}, bf16[512,2048]{1,0:T(8,128)(2,1)}, u32[]{:S(2)}, u32[]{:S(2)}) %collective-permute-start.1) | collective-permute-done | bytes 2097184 | tf_op jit(solution)/shard_map/ppermute | solution.py:1408
  378.1 54.4 %pull_tokens.1 = (f32[128,2048]{1,0:T(8,128)}, bf16[128,2048]{1,0:T(8,128)(2,1)S(1)}, f32[2,2048]{1,0:T(2,128)S(1)}) custom-call(bf16[1024,2048]{1,0:T(8,128)(2,1)} %get-tuple-element.78.p_ref, bf16[1024,2048]{1,0:T(8,128)(2,1)} %copy-done.4, bf16[128,2048]{1,0:T(8,128)(2,1)S(1)} %copy-done, f32[1,2048]{1,0:T(1,128)S(1)} %bitcast.29, f32[128,2048]{1,0:T(8,128)} %copy-done.7, ...), custom_call_target="tpu_custom_call" | custom-call | flops 49999998976 | bytes 13107200 | tf_op jit(solution)/shard_map/pull_tokens/pallas_call | solution.py:648
  432.6 17.2 %ffn_other.3 = (bf16[4,1024,2048]{2,1,0:T(8,128)(2,1)}, bf16[4,1024,1024]{2,1,0:T(8,128)(2,1)}, bf16[4,1024,1024]{2,1,0:T(8,128)(2,1)}, bf16[4,1024,1024]{2,1,0:T(8,128)(2,1)}) custom-call(s32[2]{0:T(128)S(1)} %pad_add_fusion.3.w_ref, ...), custom_call_target="tpu_custom_call", output_to_operand_aliasing={{0}: (6, {}), {1}: (7, {}), {2}: (8, {}), {3}: (9, {})} | custom-call | flops 17179869184 | bytes 41943040 | tf_op jit(solution)/shard_map/ffn_other/pallas_call | solution.py:941
  450.4 17.0 %ffn_other.4 = (bf16[4,1024,2048]{2,1,0:T(8,128)(2,1)}, bf16[4,1024,1024]{2,1,0:T(8,128)(2,1)}, bf16[4,1024,1024]{2,1,0:T(8,128)(2,1)}, bf16[4,1024,1024]{2,1,0:T(8,128)(2,1)}) custom-call(s32[2]{0:T(128)S(1)} %pad_add_fusion.2.w_ref, ...), custom_call_target="tpu_custom_call", output_to_operand_aliasing={{0}: (6, {}), {1}: (7, {}), {2}: (8, {}), {3}: (9, {})} | custom-call | flops 17179869184 | bytes 41943040 | tf_op jit(solution)/shard_map/ffn_other/pallas_call | solution.py:941
  467.4 16.6 %ffn_other.5 = (bf16[4,1024,2048]{2,1,0:T(8,128)(2,1)}, bf16[4,1024,1024]{2,1,0:T(8,128)(2,1)}, bf16[4,1024,1024]{2,1,0:T(8,128)(2,1)}, bf16[4,1024,1024]{2,1,0:T(8,128)(2,1)}) custom-call(s32[2]{0:T(128)S(1)} %pad_add_fusion.1.w_ref, ...), custom_call_target="tpu_custom_call", output_to_operand_aliasing={{0}: (6, {}), {1}: (7, {}), {2}: (8, {}), {3}: (9, {})} | custom-call | flops 17179869184 | bytes 41943040 | tf_op jit(solution)/shard_map/ffn_other/pallas_call | solution.py:941
  484.0 105.6 %finish.1 = (bf16[256,8192]{1,0:T(8,128)(2,1)}, bf16[256,8192]{1,0:T(8,128)(2,1)}, bf16[1024,2048]{1,0:T(8,128)(2,1)}, bf16[256,2048]{1,0:T(8,128)(2,1)}, bf16[2048,384]{1,0:T(8,128)(2,1)}) custom-call(bf16[4096,2048]{1,0:T(8,128)(2,1)} %bitcast.39, bf16[4096,1024]{1,0:T(8,128)(2,1)} %bitcast.41, bf16[4096,1024]{1,0:T(8,128)(2,1)} %bitcast.42, ...), custom_call_target="tpu_custom_call" | custom-call | flops 120000004096 | bytes 83886080 | tf_op jit(solution)/shard_map/finish/pallas_call | solution.py:1237
  589.6 6.7 %convert_element_type.13 = f32[256,8192]{1,0:T(8,128)} convert(bf16[256,8192]{1,0:T(8,128)(2,1)} %get-tuple-element.110) | non-fusion elementwise | flops 2097152 | bytes 12582912 | tf_op jit(solution)/shard_map/convert_element_type | solution.py:1448
  596.3 4.4 convert_element_type.14
  600.7 4.4 convert_element_type.15
  605.1 3.3 join_heads.1
  608.5 1.6 convert_element_type.12
  610.0 0.8 copy.51
  610.8 1.0 copy.52
  (45 shorter events, 2.8 us)
Async XLA Ops:
  237.2 90.1 %collective-permute-start = (bf16[512,2048]{1,0:T(8,128)(2,1)}, bf16[512,2048]{1,0:T(8,128)(2,1)}, u32[]{:S(2)}, u32[]{:S(2)}) collective-permute-start(bf16[512,2048]{1,0:T(8,128)(2,1)} %constant_dynamic-slice_fusion), channel_id=1, source_target_pairs={{0,8},{8,16},{16,24},{24,0},{1,9},{9,17},{17,25},{25,1},{2,10},{10... | collective-permute-start | bytes 6291464 | tf_op jit(solution)/shard_map/ppermute | solution.py:1408
  237.3 25.9 %copy-start.1 = (f32[2048]{0:T(1024)S(1)}, f32[2048]{0:T(1024)}, u32[]{:S(2)}) copy-start(f32[2048]{0:T(1024)} %param.19) | copy-start | bytes 24580
  237.3 25.9 %copy-start.6 = (f32[128,2048]{1,0:T(8,128)S(1)}, f32[128,2048]{1,0:T(8,128)}, u32[]{:S(2)}) copy-start(f32[128,2048]{1,0:T(8,128)} %get-tuple-element.67.m_ref.mid_ref) | copy-start | bytes 3145732
  237.3 25.9 %copy-start.8 = (bf16[128,2048]{1,0:T(8,128)(2,1)S(1)}, bf16[128,2048]{1,0:T(8,128)(2,1)}, u32[]{:S(2)}) copy-start(bf16[128,2048]{1,0:T(8,128)(2,1)} %get-tuple-element.68.g_ref) | copy-start | bytes 1572868
  261.2 2.0 copy-start.5
  263.2 48.9 %copy-start.13 = (s32[1,1024]{1,0:T(1,128)S(1)}, s32[1,1024]{1,0:T(1,128)}, u32[]{:S(2)}) copy-start(s32[1,1024]{1,0:T(1,128)} %deal_ref.1) | copy-start | bytes 12292
  309.1 2.0 copy-start.3
  311.1 1.0 copy-start.7
  325.3 2.0 copy-start.4
  327.2 50.8 %collective-permute-start.1 = (bf16[512,2048]{1,0:T(8,128)(2,1)}, bf16[512,2048]{1,0:T(8,128)(2,1)}, u32[]{:S(2)}, u32[]{:S(2)}) collective-permute-start(bf16[512,2048]{1,0:T(8,128)(2,1)} %collective-permute-done.held_ref), channel_id=1, source_target_pairs={{0,8},{8,16},{16,24},{24,0},{1,9},{9,17},{17,25},{25,1},{2,10},{10... | collective-permute-start | bytes 6291464 | tf_op jit(solution)/shard_map/ppermute | solution.py:1408
  327.7 50.4 %copy-start = (bf16[128,2048]{1,0:T(8,128)(2,1)S(1)}, bf16[128,2048]{1,0:T(8,128)(2,1)}, u32[]{:S(2)}) copy-start(bf16[128,2048]{1,0:T(8,128)(2,1)} %h_ref.1) | copy-start | bytes 1572868
  327.7 50.4 %copy-start.2 = (f32[2048]{0:T(1024)S(1)}, f32[2048]{0:T(1024)}, u32[]{:S(2)}) copy-start(f32[2048]{0:T(1024)} %param.14) | copy-start | bytes 24580
  355.3 128.7 %all-to-all-start = ((bf16[8,256,384]{2,1,0:T(8,128)(2,1)}), bf16[8,256,384]{2,1,0:T(8,128)(2,1)}, u32[]{:S(2)}, u32[]{:S(2)}) async-start(bf16[8,256,384]{2,1,0:T(8,128)(2,1)} %bitcast.31), calls=%async_computation | async-start | bytes 3145728 | tf_op jit(solution)/shard_map/all_to_all | solution.py:85
  359.6 73.0 %collective-permute-start.5 = (bf16[512,2048]{1,0:T(8,128)(2,1)}, bf16[512,2048]{1,0:T(8,128)(2,1)S(1)}, u32[]{:S(2)}, u32[]{:S(2)}) collective-permute-start(bf16[512,2048]{1,0:T(8,128)(2,1)} %collective-permute-done.held_ref), channel_id=1, source_target_pairs={{0,1},{1,0},{2,3},{3,2},{4,5},{5,4},{6,7},{7,6},{8,9},{9,8},{10,11... | collective-permute-start | bytes 6291464 | tf_op jit(solution)/shard_map/ppermute | solution.py:1410
  378.1 72.3 %collective-permute-start.4 = (bf16[512,2048]{1,0:T(8,128)(2,1)}, bf16[512,2048]{1,0:T(8,128)(2,1)S(1)}, u32[]{:S(2)}, u32[]{:S(2)}) collective-permute-start(bf16[512,2048]{1,0:T(8,128)(2,1)} %collective-permute-done.1.held_ref), channel_id=1, source_target_pairs={{0,1},{1,0},{2,3},{3,2},{4,5},{5,4},{6,7},{7,6},{8,9},{9,8},{10,11... | collective-permute-start | bytes 6291464 | tf_op jit(solution)/shard_map/ppermute | solution.py:1410
  378.1 54.4 %collective-permute-start.2 = (bf16[512,2048]{1,0:T(8,128)(2,1)}, bf16[512,2048]{1,0:T(8,128)(2,1)S(1)}, u32[]{:S(2)}, u32[]{:S(2)}) collective-permute-start(bf16[512,2048]{1,0:T(8,128)(2,1)} %collective-permute-done.1.held_ref), channel_id=1, source_target_pairs={{0,8},{8,16},{16,24},{24,0},{1,9},{9,17},{17,25},{25,1},{2,10},{10... | collective-permute-start | bytes 6291464 | tf_op jit(solution)/shard_map/ppermute | solution.py:1408
  432.5 34.8 %collective-permute-start.3 = (bf16[512,2048]{1,0:T(8,128)(2,1)S(1)}, bf16[512,2048]{1,0:T(8,128)(2,1)S(1)}, u32[]{:S(2)}, u32[]{:S(2)}) collective-permute-start(bf16[512,2048]{1,0:T(8,128)(2,1)S(1)} %collective-permute-done.2.held_ref), channel_id=1, source_target_pairs={{0,1},{1,0},{2,3},{3,2},{4,5},{5,4},{6,7},{7,6},{8,9},{9,8},{10,11... | collective-permute-start | bytes 6291464 | tf_op jit(solution)/shard_map/ppermute | solution.py:1410
  589.6 6.7 %copy-start.10 = (bf16[256,8192]{1,0:T(8,128)(2,1)S(1)}, bf16[256,8192]{1,0:T(8,128)(2,1)}, u32[]{:S(2)}) copy-start(bf16[256,8192]{1,0:T(8,128)(2,1)} %get-tuple-element.111) | copy-start | bytes 12582916
  596.3 4.4 copy-start.9
  600.7 7.8 %copy-start.11 = (bf16[256,2048]{1,0:T(8,128)(2,1)S(1)}, bf16[256,2048]{1,0:T(8,128)(2,1)}, u32[]{:S(2)}) copy-start(bf16[256,2048]{1,0:T(8,128)(2,1)} %get-tuple-element.109) | copy-start | bytes 3145732
  605.1 5.7 copy-start.12

commit v7 on v6

--- a/solution.py
+++ b/solution.py
@@ -283,7 +283,7 @@
     def kernel(
         tok_ref, gain_ref, wq_hbm, wk_ref, wv_ref, wo_ref, fgain_ref, wg_hbm, wu_hbm,
         wd_ref, deal_ref, len_ref, cot_ref, freq_ref,
-        n_ref, q_ref, kv_ref, att_ref, qw_ref, kvw_ref, wg_out, wu_out, mid_ref, nf_ref, dg_out, ag_out, cot_out,
+        n_ref, q_ref, kv_ref, att_ref, qw_ref, kvw_ref, wg_out, wu_out, mid_ref, nf_ref, dg_out, ag_out, cot_out, half_out,
         kv_stage, c_all, dg_own, ag_stage,
         sib_out, sib_in, acc, x_out, x_in, y_out, y_in, scatter_sems,
         n_sems, c_sems, nf_sems, qkv_sems, bulk_sems, ring_sems, pair_sems, local_sems,
@@ -461,6 +461,8 @@
         for unused in gather_nf:
             pass
         more(len(waiting))
+        give = pltpu.make_async_copy(nf_ref.at[pl.ds(4 * core, 4)], half_out, local_sems.at[4])
+        give.start()
         store.wait()
         for copy in kept:
             copy.wait()
@@ -477,6 +479,7 @@
             load.start()
             load.wait()
             act_grad(held, dg_own)
+        give.wait()
         for copy in bulk:
             copy.wait_recv()
         for copy in weights + bulk + hops[1:] + shares:
@@ -500,9 +503,10 @@
             jax.ShapeDtypeStruct((replicas, total, width), BF16),
             jax.ShapeDtypeStruct((replicas, total, ff_cols), BF16),
             jax.ShapeDtypeStruct((local, width), BF16),
+            jax.ShapeDtypeStruct((4, local, width), BF16),
         ),
         in_specs=[VMEM, VMEM, ANY, VMEM, VMEM, VMEM, VMEM, ANY, ANY, VMEM, VMEM, SMEM, VMEM, VMEM],
-        out_specs=[VMEM] * 6 + [ANY, ANY, VMEM, VMEM, ANY, ANY, VMEM],
+        out_specs=[VMEM] * 6 + [ANY, ANY, VMEM, VMEM, ANY, ANY, VMEM, ANY],
         scratch_shapes=[
             pltpu.VMEM((8, shard_rows, 2 * HEAD), BF16),
             pltpu.VMEM((8, local, width), BF16),
@@ -518,7 +522,7 @@
             half_sems((2, 28)),
             half_sems((2, replicas)),
             half_sems((2, replicas)),
-            half_sems((4,)),
+            half_sems((5,)),
         ],
         compiler_params=comm_params(0, 56),
         cost_estimate=pl.CostEstimate(
@@ -529,12 +533,13 @@
         tokens, attn_gain[None, :], query_weight, key_weight, value_weight, output_weight,
         ffn_gain[None, :], gate_weight, up_weight, down_weight, dealing, lengths, cotangent, freq,
     )
-    normed, q, kv, attention, qw, kvw, wg, wu, middle, nf, dg, ag, cot = outs
+    normed, q, kv, attention, qw, kvw, wg, wu, middle, nf, dg, ag, cot, held = outs
     return (
         normed.reshape(total, width), q, kv, attention,
         qw.reshape(width, q_cols), kvw.reshape(width, 2 * HEAD),
         wg.reshape(width, ff_cols), wu.reshape(width, ff_cols),
         middle, nf.reshape(total, width), dg, ag, cot,
+        held.reshape(total // 2, width),
     )
 
 
@@ -547,25 +552,63 @@
     return rows_part, jnp.sum(grad * x * scale, axis=0, keepdims=True)
 
 
-def pull_gather(part, middle, gain, out_grad, collective_id):
+def pull_gather(part, middle, gain, out_grad, activated, down_weight, deal, collective_id):
     rows, width = middle.shape
-
-    def kernel(p_ref, m_ref, gain_ref, g_ref, mg_ref, gain_part, out, *scratch):
+    groups, total, cols = activated.shape
+    block = 256
+
+    def kernel(
+        p_ref, m_ref, gain_ref, g_ref, act_hbm, wd_ref, deal_ref,
+        mg_ref, gain_part, out, dealt_ref, act_ref, packed_ref, act_sem, *scratch,
+    ):
         me = lax.axis_index("shard")
         *buffers, scatter_sems, sems = scratch
+        load = pltpu.make_async_copy(act_hbm.at[lax.axis_index("rep")], act_ref, act_sem.at[0])
+        load.start()
         greet(me, (1, 2, 4))
-        grad = scatter_blocks(
+
+        def down(i, carry):
+            chunk = pl.ds(pl.multiple_of(i * block, block), block)
+            packed_ref[chunk, :] = (RESIDUAL_SCALE * mm(act_ref[chunk, :], wd_ref[...])).astype(BF16)
+            return carry
+
+        def deal_out(i, carry):
+            chunk = pl.ds(pl.multiple_of(i * block, block), block)
+            packed = lax.broadcasted_iota(jnp.int32, (block, total), 1)
+            chosen = (deal_ref[chunk, :] == packed).astype(BF16)
+            dealt_ref[chunk, :] = mm(chosen, packed_ref[...]).astype(BF16)
+            return carry
+
+        half = total // block // 2
+        scatter = scatter_steps(
             me,
             lambda d: p_ref[pl.ds(pl.multiple_of(d * rows, rows), rows), :].astype(F32),
             *buffers,
             scatter_sems,
         )
-        rows_part, gain_row = norm_pull(m_ref[...], gain_ref[...], grad)
+        next(scatter)
+        load.wait()
+        lax.fori_loop(0, half, down, 0)
+        next(scatter)
+        lax.fori_loop(half, 2 * half, down, 0)
+        own = pl.ds(pl.multiple_of(me * rows, rows), rows)
+        packed_ref[own, :] = (packed_ref[own, :].astype(F32) + m_ref[...]).astype(BF16)
+        next(scatter)
+        for unused in scatter:
+            pass
+        rows_part, gain_row = norm_pull(m_ref[...], gain_ref[...], buffers[2][3])
         gain_part[...] = gain_row
         middle_grad = g_ref[...].astype(F32) + rows_part
         mg_ref[...] = middle_grad
         out[me] = (RESIDUAL_SCALE * middle_grad).astype(BF16)
-        gather_blocks(me, out, sems)
+        gather = gather_steps(me, out, sems)
+        next(gather)
+        lax.fori_loop(0, half, deal_out, 0)
+        for unused in range(2):
+            next(gather)
+        lax.fori_loop(half, 2 * half, deal_out, 0)
+        for unused in gather:
+            pass
 
     return pl.pallas_call(
         kernel,
@@ -573,33 +616,113 @@
             jax.ShapeDtypeStruct((rows, width), F32),
             jax.ShapeDtypeStruct((1, width), F32),
             jax.ShapeDtypeStruct((8, rows, width), BF16),
-        ),
-        in_specs=[VMEM] * 4,
-        out_specs=[VMEM] * 3,
-        scratch_shapes=scatter_scratch(rows, width)
+            jax.ShapeDtypeStruct((total, width), BF16),
+        ),
+        in_specs=[VMEM] * 4 + [ANY] + [VMEM] * 2,
+        out_specs=[VMEM] * 4,
+        scratch_shapes=[
+            pltpu.VMEM((total, cols), BF16),
+            pltpu.VMEM((total, width), BF16),
+            pltpu.SemaphoreType.DMA((1,)),
+        ]
+        + scatter_scratch(rows, width)
         + [pltpu.SemaphoreType.DMA((2, GATHER_SEMS))],
-        compiler_params=comm_params(collective_id, 44),
+        compiler_params=comm_params(collective_id, 56),
         cost_estimate=pl.CostEstimate(
-            flops=50_000_000_000, bytes_accessed=50 * rows * width, transcendentals=rows
+            flops=60_000_000_000, bytes_accessed=50 * rows * width, transcendentals=rows
         ),
         name="pull_gather",
-    )(part, middle, gain[None, :], out_grad)
-
-
-def pull_tokens(part, out_part, hidden, gain, middle_grad, other_gain, replicas, collective_id):
+    )(part, middle, gain[None, :], out_grad, activated, down_weight, deal)
+
+
+def pull_tokens(
+    part, out_part, hidden, gain, middle_grad, other_gain, near, act_grads, wg, wu, filled, replicas, collective_id
+):
     rows, width = middle_grad.shape
+    groups, total, cols = act_grads.shape
+    block = 256
     levels = [("shard", 1), ("shard", 2), ("shard", 4)]
     level = 1
     while level < replicas:
         levels.append(("rep", level))
         level *= 2
+    per_half = total // 2 // block
 
     def kernel(
-        p_ref, o_ref, h_ref, gain_ref, mg_ref, og_ref, out, lay, gains, gain_in, gain_out, gain_sems, *scratch
+        p_ref, o_ref, h_ref, gain_ref, mg_ref, og_ref, wg_ref, wu_ref, ag_hbm,
+        before_held, before_fetched, after_held, after_fetched, unused_na, unused_act, unused_gg, unused_ug,
+        out, lay, gains, na_hbm, act_hbm, gg_hbm, ug_hbm,
+        nf_buf, ag_buf, done_buf, in_sems, out_sems, gain_in, gain_out, gain_sems, *scratch,
     ):
         me = lax.axis_index("shard")
         group = lax.axis_index("rep")
+        core = lax.rem(me, 2)
+        before = lax.rem(group + replicas - 1, replicas)
+        after = lax.rem(group + 1, replicas)
         first, second = scratch[:8], scratch[8:]
+        parts = (
+            (before, before_held, core),
+            (before, before_fetched, 1 - core),
+            (after, after_held, core),
+            (after, after_fetched, 1 - core),
+        )
+
+        def rows_of(p, r):
+            return pl.ds(pl.multiple_of((parts[p][2] * per_half + r) * block, block), block)
+
+        def loads(p, r):
+            held, source, unused = parts[p]
+            slot = (p % 2) * per_half + r
+            return [
+                pltpu.make_async_copy(
+                    source.at[pl.ds(pl.multiple_of(r * block, block), block)],
+                    nf_buf.at[slot],
+                    in_sems.at[0, slot],
+                ),
+                pltpu.make_async_copy(ag_hbm.at[held, rows_of(p, r)], ag_buf.at[slot], in_sems.at[1, slot]),
+            ]
+
+        def stores(p, r):
+            held = parts[p][0]
+            slot = (p % 2) * per_half + r
+            where = rows_of(p, r)
+            return [
+                pltpu.make_async_copy(nf_buf.at[slot], na_hbm.at[held, where], out_sems.at[0, slot])
+            ] + [
+                pltpu.make_async_copy(done_buf.at[k, slot], target.at[held, where], out_sems.at[k + 1, slot])
+                for k, target in enumerate((act_hbm, gg_hbm, ug_hbm))
+            ]
+
+        def start_loads(p):
+            for r in range(per_half):
+                for copy in loads(p, r):
+                    copy.start()
+
+        def wait_stores(p):
+            for r in range(per_half):
+                for copy in stores(p, r):
+                    copy.wait()
+
+        def fill(p):
+            if p > 0:
+                wait_stores(p - 1)
+            if p + 1 < len(parts):
+                start_loads(p + 1)
+
+            def step(r, carry):
+                slot = (p % 2) * per_half + r
+                for copy in loads(p, r):
+                    copy.wait()
+                results = ffn_rows(nf_buf[slot], ag_buf[slot], wg_ref[...], wu_ref[...])
+                for k, result in enumerate(results):
+                    done_buf[k, slot] = result
+                for copy in stores(p, r):
+                    copy.start()
+                return carry
+
+            lax.fori_loop(0, per_half, step, 0)
+
+        start_loads(0)
         barrier = pltpu.get_barrier_semaphore()
         peers = []
         for axis, weight in levels:
@@ -615,16 +738,20 @@
         grads = scatter_steps(me, blocks_of(p_ref), *first)
         outputs = scatter_steps(me, blocks_of(o_ref), *second)
         next(grads)
+        next(outputs)
+        fill(0)
+        next(grads)
+        fill(1)
         next(grads)
         next(outputs)
+        fill(2)
         next(grads)
         next(outputs)
-        next(grads)
         rows_part, gain_row = norm_pull(h_ref[...].astype(F32), gain_ref[...], first[2][3])
         out[...] = mg_ref[...] + rows_part
-        total = jnp.concatenate([gain_row, og_ref[...]], axis=0)
+        sums = jnp.concatenate([gain_row, og_ref[...]], axis=0)
         for i, peer in enumerate(peers):
-            gain_out[i] = total
+            gain_out[i] = sums
             copy = pltpu.make_async_remote_copy(
                 src_ref=gain_out.at[i],
                 dst_ref=gain_in.at[i],
@@ -634,39 +761,53 @@
                 device_id_type=MESH,
             )
             copy.start()
-            if i == 1:
-                next(outputs)
+            if i == 0:
+                fill(3)
             copy.wait()
-            total = total + gain_in[i]
-        gains[...] = total
+            sums = sums + gain_in[i]
+        gains[...] = sums
         next(outputs)
         lay[...] = second[2][3].astype(BF16)
         for steps in (grads, outputs):
             for unused in steps:
                 pass
-
+        wait_stores(3)
+
+    hidden_shape = jax.ShapeDtypeStruct((groups, total, cols), BF16)
     return pl.pallas_call(
         kernel,
         out_shape=(
             jax.ShapeDtypeStruct((rows, width), F32),
             jax.ShapeDtypeStruct((rows, width), BF16),
             jax.ShapeDtypeStruct((2, width), F32),
-        ),
-        in_specs=[VMEM] * 6,
-        out_specs=[VMEM] * 3,
+            jax.ShapeDtypeStruct((groups, total, width), BF16),
+            hidden_shape,
+            hidden_shape,
+            hidden_shape,
+        ),
+        in_specs=[VMEM] * 8 + [ANY] * 9,
+        out_specs=[VMEM] * 3 + [ANY] * 4,
+        input_output_aliases={13: 3, 14: 4, 15: 5, 16: 6},
         scratch_shapes=[
+            pltpu.VMEM((2 * per_half, block, width), BF16),
+            pltpu.VMEM((2 * per_half, block, cols), BF16),
+            pltpu.VMEM((3, 2 * per_half, block, cols), BF16),
+            pltpu.SemaphoreType.DMA((2, 2 * per_half)),
+            pltpu.SemaphoreType.DMA((4, 2 * per_half)),
             pltpu.VMEM((len(levels), 2, width), F32),
             pltpu.VMEM((len(levels), 2, width), F32),
             pltpu.SemaphoreType.DMA((2, len(levels))),
         ]
         + scatter_scratch(rows, width)
         + scatter_scratch(rows, width),
-        compiler_params=comm_params(collective_id, 52),
+        compiler_params=comm_params(collective_id, 62),
         cost_estimate=pl.CostEstimate(
-            flops=50_000_000_000, bytes_accessed=50 * rows * width, transcendentals=rows
+            flops=60_000_000_000, bytes_accessed=50 * rows * width, transcendentals=rows
         ),
         name="pull_tokens",
-    )(part, out_part, hidden, gain[None, :], middle_grad, other_gain)
+    )(
+        part, out_part, hidden, gain[None, :], middle_grad, other_gain, wg, wu, act_grads, *near, *filled
+    )
 
 
 def softmax_block(q, k, allowed):
@@ -957,49 +1098,6 @@
     )(where, held, fetched, act_grads, wg, wu, *filled)
 
 
-def output_rows(where, activated, down_weight, middle, deal, total):
-    groups, total, cols = activated.shape
-    local, width = middle.shape
-    block = 256
-
-    def kernel(w_ref, act_ref, wd_ref, mid_ref, deal_ref, o_ref, rows_ref):
-        for i in range(total // block):
-            rows = pl.ds(i * block, block)
-            rows_ref[rows, :] = (RESIDUAL_SCALE * mm(act_ref[0, rows, :], wd_ref[...])).astype(BF16)
-        own = pl.ds(pl.multiple_of(w_ref[1] * local, local), local)
-        rows_ref[own, :] = (rows_ref[own, :].astype(F32) + mid_ref[...]).astype(BF16)
-        for i in range(total // block):
-            rows = pl.ds(i * block, block)
-            packed = lax.broadcasted_iota(jnp.int32, (block, total), 1)
-            chosen = (deal_ref[rows, :] == packed).astype(BF16)
-            o_ref[rows, :] = mm(chosen, rows_ref[...]).astype(BF16)
-
-    def full(shape):
-        return pl.BlockSpec(shape, lambda i, w: (0,) * len(shape), pipeline_mode=pl.Buffered(1))
-
-    return pl.pallas_call(
-        kernel,
-        grid_spec=pltpu.PrefetchScalarGridSpec(
-            num_scalar_prefetch=1,
-            grid=(1,),
-            in_specs=[
-                pl.BlockSpec((1, total, cols), lambda i, w: (w[0], 0, 0), pipeline_mode=pl.Buffered(1)),
-                full(down_weight.shape),
-                full(middle.shape),
-                full(deal.shape),
-            ],
-            out_specs=full((total, width)),
-            scratch_shapes=[pltpu.VMEM((total, width), BF16)],
-        ),
-        out_shape=jax.ShapeDtypeStruct((total, width), BF16),
-        compiler_params=pltpu.CompilerParams(vmem_limit_bytes=48 << 20),
-        cost_estimate=pl.CostEstimate(
-            flops=2 * total * width * (cols + total) * 2, bytes_accessed=12 << 20, transcendentals=0
-        ),
-        name="output_rows",
-    )(where, activated, down_weight, middle, deal)
-
-
 def join_heads(blocks, q_cols):
     n, rows, cols = blocks.shape
 
@@ -1394,45 +1492,39 @@
 
     (
         normed, q, kv, attention, q_weight, kv_weight, gate_cols, up_cols,
-        middle, normed_ffn, down_grads, act_grads, cot_own,
+        middle, normed_ffn, down_grads, act_grads, cot_own, held,
     ) = front(
         tokens, attn_gain, query_weight, key_weight, value_weight, output_weight, ffn_gain,
         gate_weight, up_weight, down_weight, dealing, lengths, cotangent, freq, replicas,
     )
 
-    held = lax.dynamic_slice_in_dim(normed_ffn, core * (total // 2), total // 2)
-    onward = [(i, (i + 1) % replicas) for i in range(replicas)]
-    beside = [(i, i ^ 1) for i in range(n)]
-    arrivals = []
-    for hop in range(1, replicas):
-        held = lax.ppermute(held, "rep", onward)
-        where = jnp.stack([lax.rem(group + replicas - hop, replicas), core]).astype(jnp.int32)
-        arrivals.append((where, held, lax.ppermute(held, "shard", beside)))
-
+    def shift(x, by):
+        return lax.ppermute(x, "rep", [(i, (i + by) % replicas) for i in range(replicas)])
+
+    def fetch(x):
+        return lax.ppermute(x, "shard", [(i, i ^ 1) for i in range(n)])
+
+    before, after = shift(held, 1), shift(held, replicas - 1)
     *filled, normed_ffn_part = ffn_own(
         group.astype(jnp.int32)[None], normed_ffn, act_grads, gate_cols, up_cols
     )
-    middle_grad, ffn_gain_part, branch_grad = pull_gather(
-        normed_ffn_part, middle, ffn_gain, cot_own, 2
-    )
-    branch_grad, unused_hop = lax.optimization_barrier(
-        (branch_grad.reshape(total, width), arrivals[0][1])
-    )
-    output_part = output_rows(
-        jnp.stack([group, here]).astype(jnp.int32), filled[1], down_weight, middle,
-        dealing.reshape(total, 1), total,
+    middle_grad, ffn_gain_part, branch_grad, output_part = pull_gather(
+        normed_ffn_part, middle, ffn_gain, cot_own, filled[1], down_weight, dealing.reshape(total, 1), 2
     )
     normed_part, qkv_grad, output_grad = attention_backward(
-        branch_grad, output_weight, attention, q, kv, normed, q_weight, kv_weight, lengths, freq
-    )
-    normed_part, unused_hop = lax.optimization_barrier((normed_part, arrivals[1][1]))
-    tokens_grad, layer_output, gains = pull_tokens(
-        normed_part, output_part, tokens, attn_gain, middle_grad, ffn_gain_part, replicas, 3
-    )
-    act_grads, tokens_grad = lax.optimization_barrier((act_grads, tokens_grad))
+        branch_grad.reshape(total, width), output_weight, attention, q, kv, normed, q_weight, kv_weight,
+        lengths, freq,
+    )
+    before, after, unused_part = lax.optimization_barrier((before, after, normed_part))
+    opposite = shift(before, 1)
     qkv_part = exchange(qkv_grad.reshape(n, rows, q_cols + 2 * HEAD))
-    for where, from_ring, from_core in arrivals:
-        filled = ffn_other(where, from_ring, from_core, act_grads, gate_cols, up_cols, filled)
+    tokens_grad, layer_output, gains, *filled = pull_tokens(
+        normed_part, output_part, tokens, attn_gain, middle_grad, ffn_gain_part,
+        (before, fetch(before), after, fetch(after)), act_grads, gate_cols, up_cols, filled, replicas, 3,
+    )
+    opposite, unused_rows = lax.optimization_barrier((opposite, tokens_grad))
+    where = jnp.stack([lax.rem(group + replicas - 2, replicas), core]).astype(jnp.int32)
+    filled = ffn_other(where, opposite, fetch(opposite), act_grads, gate_cols, up_cols, filled)
     left, *rights = [x.reshape(replicas * total, -1) for x in (filled[0], filled[2], filled[3])]
     gate_grad, up_grad, down_grad, output_grad, qkv_grad = finish(
         left, *rights, filled[1].reshape(replicas * total, -1), down_grads.reshape(replicas * total, -1),

time: 621 us -> 574 us (0.924)
  Pallas kernels: 557 us -> 520 us
  waiting for transfers between devices: 18.1 us -> 8.14 us
    pallas_call x3 -> x1, Pallas kernels: 50.7 us -> 17 us  [ffn_other(): pl.pallas_call(kernel, grid_spec=pltpu.PrefetchScalarGridSpec(num_scalar_...]
    pallas_call x1 -> x0, Pallas kernels: 12.7 us -> none  [output_rows(): pl.pallas_call(kernel, grid_spec=pltpu.PrefetchScalarGridSpec(num_scalar_...]
    ppermute x6, waiting for transfers between devices: 18.1 us -> 5.55 us  [the longest x3 5.54 us: fetch(): return lax.ppermute(x, 'shard', [(i, i ^ 1) for i in range(n)])]
  transfers between devices with their start and end apart: 7 -> 7, of which waited for: 1 -> 3; matrix products, arithmetic and copies ran while one was open for 0% -> 0% of each run, Pallas kernels for 35% -> 32%
where the time goes in v7:
time: 574 us; the launch traced here: 565 us
  Pallas kernels  520 us (91%)
  other arithmetic  17.2 us (3%)
  starting transfers between devices  9.51 us (2%)
  local copies, waits for them, and re-layouts  9 us (2%)
  waiting for transfers between devices  8.14 us (1%)
    pallas_call x1, Pallas kernels, front(): pl.pallas_call(kernel, out_shape=(rows8, jax.ShapeDtypeStruct((total, q_c...  233 us
    pallas_call x1, Pallas kernels, finish(): pl.pallas_call(kernel, out_shape=(exchanged, exchanged, jax.ShapeDtypeStr...  104 us
    pallas_call x1, Pallas kernels, pull_tokens(): pl.pallas_call(kernel, out_shape=(jax.ShapeDtypeStruct((rows, width), F32...  59.3 us
    pallas_call x1, Pallas kernels, pull_gather(): pl.pallas_call(kernel, out_shape=(jax.ShapeDtypeStruct((rows, width), F32...  51.8 us
    pallas_call x1, Pallas kernels, attention_backward(): pl.pallas_call(kernel, out_shape=(jax.ShapeDtypeStruct((total, width), BF...  27.8 us
    pallas_call x1, Pallas kernels, ffn_own(): pl.pallas_call(kernel, grid_spec=pltpu.PrefetchScalarGridSpec(num_scalar_...  23.5 us
    pallas_call x1, Pallas kernels, ffn_other(): pl.pallas_call(kernel, grid_spec=pltpu.PrefetchScalarGridSpec(num_scalar_...  17 us
  transfers between devices with their start and end apart: 7, of which 3 were waited for; matrix products, arithmetic and copies ran while one was open for 0% of the time, Pallas kernels for 32%

profile of v7, /device:TPU:0, one launch (start us, length us, event | category | flops | bytes accessed | tf_op | source)
XLA Modules:
  0.0 565.1 jit_solution(14064341781307628439)
XLA Ops:
  1.3 232.9 %front.1 = (bf16[8,128,2048]{2,1,0:T(8,128)(2,1)}, bf16[1024,256]{1,0:T(8,128)(2,1)}, bf16[1024,128]{1,0:T(8,128)(2,1)}, bf16[1024,256]{1,0:T(8,128)(2,1)}, bf16...) custom-call(bf16[128,2048]{1,0:T(8,128)(2,1)} %h_ref.1, ...), custom_call_target="tpu_custom_call" | custom-call | flops 199999995904 | bytes 52428800 | tf_op jit(solution)/shard_map/front/pallas_call | solution.py:490
  234.3 3.9 collective-permute-start.1
  238.2 1.0 copy.32.deal_ref
  239.3 23.5 %ffn_own.1 = (bf16[4,1024,2048]{2,1,0:T(8,128)(2,1)}, bf16[4,1024,1024]{2,1,0:T(8,128)(2,1)}, bf16[4,1024,1024]{2,1,0:T(8,128)(2,1)}, bf16[4,1024,1024]{2,1,0:T(8,128)(2,1)}, bf16[1024,2048]{1,0:T(8,128)(2,1)S(1)}) custom-call(s32[1]{0:T(128)} %bitcast.g_ref, bf16[1024,2048]{1,0:T(8,128)(2,1)} %bitcast.47, ...), custom_call_target="tpu_custom_call" | custom-call | flops 25769803776 | bytes 41943040 | tf_op jit(solution)/shard_map/ffn_own/pallas_call | solution.py:1025
  262.8 2.0 copy-done
  264.8 51.8 %pull_gather.1 = (f32[128,2048]{1,0:T(8,128)}, f32[1,2048]{1,0:T(1,128)}, bf16[8,128,2048]{2,1,0:T(8,128)(2,1)}, bf16[1024,2048]{1,0:T(8,128)(2,1)}) custom-call(bf16[1024,2048]{1,0:T(8,128)(2,1)} %copy-done, f32[128,2048]{1,0:T(8,128)} %get-tuple-element.64.m_ref, f32[1,2048]{1,0:T(1,128)} %bitcast.32, bf16[128,2048]{1,0:T(8,128)(2,1)} %get-tuple-element.65.g_ref, ...), custom_call_target="tpu_custom_call" | custom-call | flops 60000002048 | bytes 13107200 | tf_op jit(solution)/shard_map/pull_gather/pallas_call | solution.py:613
  316.6 27.8 %attention_backward.1 = (bf16[1024,2048]{1,0:T(8,128)(2,1)}, bf16[2048,384]{1,0:T(8,128)(2,1)}, bf16[256,2048]{1,0:T(8,128)(2,1)}) custom-call(bf16[1024,2048]{1,0:T(8,128)(2,1)} %bitcast.48, bf16[256,2048]{1,0:T(8,128)(2,1)} %wo_ref.3, bf16[1024,256]{1,0:T(8,128)(2,1)} %get-tuple-element.68.a_ref, bf16[1024,256]{1,0:T(8,128)(2,1)} %get-tuple-element.69.q_ref, ...), custom_call_target="tpu_custom_call" | custom-call | flops 30000001024 | bytes 31457280 | tf_op jit(solution)/shard_map/attention_backward/pallas_call | solution.py:974
  344.9 0.9 copy-done.7
  346.1 2.7 collective-permute-done.2.before_fetched
  348.9 2.8 collective-permute-done.3.after_fetched
  351.6 1.3 copy-done.9
  353.0 59.3 %pull_tokens.1 = (f32[128,2048]{1,0:T(8,128)}, bf16[128,2048]{1,0:T(8,128)(2,1)}, f32[2,2048]{1,0:T(2,128)}, bf16[4,1024,2048]{2,1,0:T(8,128)(2,1)}, bf16[4,1024...) custom-call(bf16[1024,2048]{1,0:T(8,128)(2,1)} %get-tuple-element.74, ...), custom_call_target="tpu_custom_call", output_to_operand_aliasing={{3}: (13, {}), {4}: (14, {}), {5}: (15, {}), {6}: (16, {})} | custom-call | flops 60000002048 | bytes 13107200 | tf_op jit(solution)/shard_map/pull_tokens/pallas_call | solution.py:777
  412.3 4.5 all-to-all-start
  417.0 1.4 fusion
  418.4 17.0 %ffn_other.1 = (bf16[4,1024,2048]{2,1,0:T(8,128)(2,1)}, bf16[4,1024,1024]{2,1,0:T(8,128)(2,1)}, bf16[4,1024,1024]{2,1,0:T(8,128)(2,1)}, bf16[4,1024,1024]{2,1,0:T(8,128)(2,1)}) custom-call(s32[2]{0:T(128)S(1)} %pad_add_fusion.w_ref, ...), custom_call_target="tpu_custom_call", output_to_operand_aliasing={{0}: (6, {}), {1}: (7, {}), {2}: (8, {}), {3}: (9, {})} | custom-call | flops 17179869184 | bytes 41943040 | tf_op jit(solution)/shard_map/ffn_other/pallas_call | solution.py:1082
  435.3 2.6 all-to-all-done
  437.9 104.5 %finish.1 = (bf16[256,8192]{1,0:T(8,128)(2,1)}, bf16[256,8192]{1,0:T(8,128)(2,1)}, bf16[1024,2048]{1,0:T(8,128)(2,1)}, bf16[256,2048]{1,0:T(8,128)(2,1)}, bf16[2048,384]{1,0:T(8,128)(2,1)}) custom-call(bf16[4096,2048]{1,0:T(8,128)(2,1)} %bitcast.36, bf16[4096,1024]{1,0:T(8,128)(2,1)} %bitcast.38, bf16[4096,1024]{1,0:T(8,128)(2,1)} %bitcast.39, ...), custom_call_target="tpu_custom_call" | custom-call | flops 120000004096 | bytes 83886080 | tf_op jit(solution)/shard_map/finish/pallas_call | solution.py:1335
  542.4 6.7 %convert_element_type.13 = f32[256,8192]{1,0:T(8,128)} convert(bf16[256,8192]{1,0:T(8,128)(2,1)} %get-tuple-element.104) | non-fusion elementwise | flops 2097152 | bytes 12582912 | tf_op jit(solution)/shard_map/convert_element_type | solution.py:1540
  549.1 4.4 convert_element_type.14
  553.5 4.4 convert_element_type.15
  558.0 3.3 join_heads.1
  561.3 1.6 convert_element_type.12
  562.9 0.8 copy.43
  563.7 1.0 copy.44
  (30 shorter events, 1.8 us)
Async XLA Ops:
  1.3 237.0 %copy-start.6 = (s32[1,1024]{1,0:T(1,128)S(1)}, s32[1,1024]{1,0:T(1,128)}, u32[]{:S(2)}) copy-start(s32[1,1024]{1,0:T(1,128)} %deal_ref.1) | copy-start | bytes 12292
  234.2 110.2 %collective-permute-start = (bf16[512,2048]{1,0:T(8,128)(2,1)}, bf16[512,2048]{1,0:T(8,128)(2,1)}, u32[]{:S(2)}, u32[]{:S(2)}) collective-permute-start(bf16[512,2048]{1,0:T(8,128)(2,1)} %bitcast.29), channel_id=1, source_target_pairs={{0,8},{8,16},{16,24},{24,0},{1,9},{9,17},{17,25},{25,1},{2,10},{10... | collective-permute-start | bytes 6291464 | tf_op jit(solution)/shard_map/ppermute | solution.py:1502
  234.3 110.0 %collective-permute-start.1 = (bf16[512,2048]{1,0:T(8,128)(2,1)}, bf16[512,2048]{1,0:T(8,128)(2,1)S(1)}, u32[]{:S(2)}, u32[]{:S(2)}) collective-permute-start(bf16[512,2048]{1,0:T(8,128)(2,1)} %bitcast.30), channel_id=1, source_target_pairs={{0,24},{8,0},{16,8},{24,16},{1,25},{9,1},{17,9},{25,17},{2,26},{10... | collective-permute-start | bytes 6291464 | tf_op jit(solution)/shard_map/ppermute | solution.py:1502
  262.8 2.0 copy-start
  344.4 1.3 copy-start.7
  344.4 4.5 collective-permute-start.2
  345.7 5.9 %collective-permute-start.3 = (bf16[512,2048]{1,0:T(8,128)(2,1)S(1)}, bf16[512,2048]{1,0:T(8,128)(2,1)S(1)}, u32[]{:S(2)}, u32[]{:S(2)}) collective-permute-start(bf16[512,2048]{1,0:T(8,128)(2,1)S(1)} %collective-permute-done.1.after_held), channel_id=1, source_target_pairs={{0,1},{1,0},{2,3},{3,2},{4,5},{5,4},{6,7},{7,6},{8,9},{9,8},{10,11... | collective-permute-start | bytes 6291464 | tf_op jit(solution)/shard_map/ppermute | solution.py:1505
  346.1 66.2 %collective-permute-start.4 = (bf16[512,2048]{1,0:T(8,128)(2,1)}, bf16[512,2048]{1,0:T(8,128)(2,1)}, u32[]{:S(2)}, u32[]{:S(2)}) collective-permute-start(bf16[512,2048]{1,0:T(8,128)(2,1)} %collective-permute-done.before_held), channel_id=1, source_target_pairs={{0,8},{8,16},{16,24},{24,0},{1,9},{9,17},{17,25},{25,1},{2,10},{10... | collective-permute-start | bytes 6291464 | tf_op jit(solution)/shard_map/ppermute | solution.py:1502
  348.9 2.8 copy-start.8
  351.6 1.3 copy-start.9
  412.3 6.1 %collective-permute-start.5 = (bf16[512,2048]{1,0:T(8,128)(2,1)}, bf16[512,2048]{1,0:T(8,128)(2,1)S(1)}, u32[]{:S(2)}, u32[]{:S(2)}) collective-permute-start(bf16[512,2048]{1,0:T(8,128)(2,1)} %collective-permute-done.4.held_ref), channel_id=1, source_target_pairs={{0,1},{1,0},{2,3},{3,2},{4,5},{5,4},{6,7},{7,6},{8,9},{9,8},{10,11... | collective-permute-start | bytes 6291464 | tf_op jit(solution)/shard_map/ppermute | solution.py:1505
  412.3 25.6 %all-to-all-start = ((bf16[8,256,384]{2,1,0:T(8,128)(2,1)}), bf16[8,256,384]{2,1,0:T(8,128)(2,1)}, u32[]{:S(2)}, u32[]{:S(2)}) async-start(bf16[8,256,384]{2,1,0:T(8,128)(2,1)} %bitcast.24), calls=%async_computation | async-start | bytes 3145728 | tf_op jit(solution)/shard_map/all_to_all | solution.py:85
  542.4 6.7 %copy-start.2 = (bf16[256,8192]{1,0:T(8,128)(2,1)S(1)}, bf16[256,8192]{1,0:T(8,128)(2,1)}, u32[]{:S(2)}) copy-start(bf16[256,8192]{1,0:T(8,128)(2,1)} %get-tuple-element.105) | copy-start | bytes 12582916
  549.1 4.4 copy-start.1
  553.5 7.8 %copy-start.3 = (bf16[256,2048]{1,0:T(8,128)(2,1)S(1)}, bf16[256,2048]{1,0:T(8,128)(2,1)}, u32[]{:S(2)}) copy-start(bf16[256,2048]{1,0:T(8,128)(2,1)} %get-tuple-element.103) | copy-start | bytes 3145732
  558.0 4.9 copy-start.5
  558.0 5.7 %copy-start.4 = (f32[128,2048]{1,0:T(8,128)S(1)}, f32[128,2048]{1,0:T(8,128)}, u32[]{:S(2)}) copy-start(f32[128,2048]{1,0:T(8,128)} %get-tuple-element.121) | copy-start | bytes 3145732

commit v8 on v7

--- a/solution.py
+++ b/solution.py
@@ -303,7 +303,6 @@
             pl.semaphore_signal(
                 barrier, inc=1, device_id={"rep": neighbour}, device_id_type=MESH
             )
-        n_ref[me] = rms_scale(tok_ref[...].astype(F32), gain_ref[...]).astype(BF16)
         c_all[me] = cot_ref[...]
         for d in range(8):
             lanes = slice(d * HEAD, (d + 1) * HEAD)
@@ -312,16 +311,13 @@
 
         gather_c = gather_steps(me, c_all, c_sems)
         next(gather_c)
-        gather_n = gather_steps(me, n_ref, n_sems)
-        next(gather_n)
+        n_ref[me] = rms_scale(tok_ref[...].astype(F32), gain_ref[...]).astype(BF16)
         weights = []
         for mask in others:
             peer = flip(me, mask)
             columns = pl.ds(pl.multiple_of(peer * q_cols, q_cols), q_cols)
             weights.append(send(wq_hbm.at[:, columns], qw_ref.at[me], qkv_sems, 2 * mask - 2, peer))
             weights.append(send(kv_stage.at[peer], kvw_ref.at[me], qkv_sems, 2 * mask - 1, peer))
-        for copy in weights:
-            copy.start()
         own_columns = pl.ds(pl.multiple_of(me * ff_cols, ff_cols), ff_cols)
         own_q = pl.ds(pl.multiple_of(me * q_cols, q_cols), q_cols)
         gate_slot, up_slot = ag_stage.at[:shard_rows], ag_stage.at[pl.ds(shard_rows, shard_rows)]
@@ -354,6 +350,10 @@
 
         for unused in gather_c:
             pass
+        gather_n = gather_steps(me, n_ref, n_sems)
+        next(gather_n)
+        for copy in weights:
+            copy.start()
 
         def permute(first):
             for i in range(total // 2 // block):
@@ -367,29 +367,30 @@
         far = pl.multiple_of((1 - core) * (total // 2), total // 2)
         half = pl.ds(near, total // 2)
 
-        def ring(hop):
-            held = lax.rem(group + replicas - hop, replicas)
-            ref = dg_out.at[held, half]
+        opposite = lax.rem(group + 2, replicas)
+        held_groups = (before, after, opposite)
+
+        def pass_on(k):
+            ref = dg_out.at[before if k == 2 else group, half]
             copy = pltpu.make_async_remote_copy(
-                src_ref=dg_own.at[half] if hop == 0 else ref,
+                src_ref=ref if k == 2 else dg_own.at[half],
                 dst_ref=ref,
-                send_sem=ring_sems.at[0, hop],
-                recv_sem=ring_sems.at[1, hop],
-                device_id={"rep": after},
+                send_sem=ring_sems.at[0, k],
+                recv_sem=ring_sems.at[1, k],
+                device_id={"rep": before if k == 1 else after},
                 device_id_type=MESH,
             )
             copy.start()
             return copy
 
-        def share(hop):
-            held = lax.rem(group + replicas - hop, replicas)
-            ref = dg_out.at[held, half]
-            copy = send(ref, ref, pair_sems, hop - 1, flip(me, 1))
+        def share(k):
+            ref = dg_out.at[held_groups[k], half]
+            copy = send(ref, ref, pair_sems, k, flip(me, 1))
             copy.start()
             return copy
 
         permute(near)
-        hops, shares = [ring(0)], []
+        hops = [pass_on(0)]
         for unused in range(4):
             next(gather_n)
         permute(far)
@@ -423,27 +424,36 @@
             cosine, sine = keys_only(cosine, sine)
             y = mm(x, kvw_ref[...].reshape(width, 2 * HEAD))
             kv_ref[rows, :] = (y * cosine + lane_swap(y) * sine).astype(BF16)
+        hops.append(pass_on(1))
         attend(q_cols // HEAD, block, q_ref, kv_ref, len_ref, att_ref)
 
         def partial(d):
             return mm(att_ref[pl.ds(pl.multiple_of(d * local, local), local), :], wo_ref[...])
 
-        def next_hop():
-            hop = len(hops)
-            hops[-1].wait_recv()
-            if hop < replicas - 1:
-                hops.append(ring(hop))
-            shares.append(share(hop))
-
-        def act_grad(held, source):
-            for i in range(total // block):
-                rows = pl.ds(i * block, block)
-                ag_stage[rows, :] = mm_t(source[rows, :], wd_ref[...]).astype(BF16)
-            copy = pltpu.make_async_copy(ag_stage, ag_out.at[held], local_sems.at[3])
-            copy.start()
-            copy.wait()
-
-        next_hop()
+        pending = {}
+
+        def act_grad(held, first, loaded):
+            rows = pl.ds(first, total // 2)
+            if not loaded:
+                load = pltpu.make_async_copy(
+                    dg_out.at[held, rows], dg_own.at[rows], local_sems.at[3]
+                )
+                load.start()
+                load.wait()
+            slot = 0 if first is near else 1
+            if slot in pending:
+                pending[slot].wait()
+            for i in range(total // 2 // block):
+                part = pl.ds(pl.multiple_of(first + i * block, block), block)
+                ag_stage[part, :] = mm_t(dg_own[part, :], wd_ref[...]).astype(BF16)
+            pending[slot] = pltpu.make_async_copy(
+                ag_stage.at[rows], ag_out.at[held, rows], local_sems.at[5 + slot]
+            )
+            pending[slot].start()
+
+        hops[0].wait_recv()
+        hops.append(pass_on(2))
+        shares = [share(0)]
         scatter = scatter_steps(
             me, partial, sib_out, sib_in, acc, x_out, x_in, y_out, y_in, scatter_sems
         )
@@ -466,23 +476,23 @@
         store.wait()
         for copy in kept:
             copy.wait()
-        act_grad(group, dg_own)
+        act_grad(group, near, True)
+        act_grad(group, far, True)
         hops[0].wait_send()
-        if len(shares) < replicas - 1:
-            next_hop()
-        for done in range(replicas - 1):
-            if len(shares) < done + 1:
-                next_hop()
-            held = lax.rem(group + replicas - 1 - done, replicas)
-            shares[done].wait_recv()
-            load = pltpu.make_async_copy(dg_out.at[held], dg_own, local_sems.at[3])
-            load.start()
-            load.wait()
-            act_grad(held, dg_own)
+        hops[1].wait_send()
+        for k in range(3):
+            if k > 0:
+                hops[k].wait_recv()
+                shares.append(share(k))
+            act_grad(held_groups[k], near, False)
+            shares[k].wait_recv()
+            act_grad(held_groups[k], far, False)
+        for copy in pending.values():
+            copy.wait()
         give.wait()
         for copy in bulk:
             copy.wait_recv()
-        for copy in weights + bulk + hops[1:] + shares:
+        for copy in weights + bulk + hops[2:] + shares:
             copy.wait_send()
 
     rows8 = jax.ShapeDtypeStruct((8, local, width), BF16)
@@ -522,7 +532,7 @@
             half_sems((2, 28)),
             half_sems((2, replicas)),
             half_sems((2, replicas)),
-            half_sems((5,)),
+            half_sems((7,)),
         ],
         compiler_params=comm_params(0, 56),
         cost_estimate=pl.CostEstimate(

time: 574 us -> 546 us (0.951)
  Pallas kernels: 520 us -> 492 us
    pallas_call x1, Pallas kernels: 233 us -> 206 us  [front(): pl.pallas_call(kernel, out_shape=(rows8, jax.ShapeDtypeStruct((total, q_c...]
  transfers between devices with their start and end apart: 7 -> 7, of which waited for: 3 -> 3; matrix products, arithmetic and copies ran while one was open for 0% -> 0% of each run, Pallas kernels for 32% -> 33%
where the time goes in v8:
time: 546 us; the launch traced here: 537 us
  Pallas kernels  492 us (90%)
  other arithmetic  17.2 us (3%)
  starting transfers between devices  9.49 us (2%)
  local copies, waits for them, and re-layouts  9 us (2%)
  waiting for transfers between devices  8.15 us (1%)
    pallas_call x1, Pallas kernels, front(): pl.pallas_call(kernel, out_shape=(rows8, jax.ShapeDtypeStruct((total, q_c...  206 us
    pallas_call x1, Pallas kernels, finish(): pl.pallas_call(kernel, out_shape=(exchanged, exchanged, jax.ShapeDtypeStr...  104 us
    pallas_call x1, Pallas kernels, pull_tokens(): pl.pallas_call(kernel, out_shape=(jax.ShapeDtypeStruct((rows, width), F32...  59.3 us
    pallas_call x1, Pallas kernels, pull_gather(): pl.pallas_call(kernel, out_shape=(jax.ShapeDtypeStruct((rows, width), F32...  50.7 us
    pallas_call x1, Pallas kernels, attention_backward(): pl.pallas_call(kernel, out_shape=(jax.ShapeDtypeStruct((total, width), BF...  27.8 us
    pallas_call x1, Pallas kernels, ffn_own(): pl.pallas_call(kernel, grid_spec=pltpu.PrefetchScalarGridSpec(num_scalar_...  23.5 us
    pallas_call x1, Pallas kernels, ffn_other(): pl.pallas_call(kernel, grid_spec=pltpu.PrefetchScalarGridSpec(num_scalar_...  16.9 us
  transfers between devices with their start and end apart: 7, of which 3 were waited for; matrix products, arithmetic and copies ran while one was open for 0% of the time, Pallas kernels for 33%

profile of v8, /device:TPU:0, one launch (start us, length us, event | category | flops | bytes accessed | tf_op | source)
XLA Modules:
  0.0 537.0 jit_solution(16921450713359596908)
XLA Ops:
  1.3 205.9 %front.1 = (bf16[8,128,2048]{2,1,0:T(8,128)(2,1)}, bf16[1024,256]{1,0:T(8,128)(2,1)}, bf16[1024,128]{1,0:T(8,128)(2,1)}, bf16[1024,256]{1,0:T(8,128)(2,1)}, bf16...) custom-call(bf16[128,2048]{1,0:T(8,128)(2,1)} %h_ref.1, ...), custom_call_target="tpu_custom_call" | custom-call | flops 199999995904 | bytes 52428800 | tf_op jit(solution)/shard_map/front/pallas_call | solution.py:500
  207.2 3.9 collective-permute-start.1
  211.2 1.0 copy.32.deal_ref
  212.2 23.5 %ffn_own.1 = (bf16[4,1024,2048]{2,1,0:T(8,128)(2,1)}, bf16[4,1024,1024]{2,1,0:T(8,128)(2,1)}, bf16[4,1024,1024]{2,1,0:T(8,128)(2,1)}, bf16[4,1024,1024]{2,1,0:T(8,128)(2,1)}, bf16[1024,2048]{1,0:T(8,128)(2,1)S(1)}) custom-call(s32[1]{0:T(128)} %bitcast.g_ref, bf16[1024,2048]{1,0:T(8,128)(2,1)} %bitcast.47, ...), custom_call_target="tpu_custom_call" | custom-call | flops 25769803776 | bytes 41943040 | tf_op jit(solution)/shard_map/ffn_own/pallas_call | solution.py:1035
  235.7 2.0 copy-done
  237.8 50.7 %pull_gather.1 = (f32[128,2048]{1,0:T(8,128)}, f32[1,2048]{1,0:T(1,128)}, bf16[8,128,2048]{2,1,0:T(8,128)(2,1)}, bf16[1024,2048]{1,0:T(8,128)(2,1)}) custom-call(bf16[1024,2048]{1,0:T(8,128)(2,1)} %copy-done, f32[128,2048]{1,0:T(8,128)} %get-tuple-element.64.m_ref, f32[1,2048]{1,0:T(1,128)} %bitcast.32, bf16[128,2048]{1,0:T(8,128)(2,1)} %get-tuple-element.65.g_ref, ...), custom_call_target="tpu_custom_call" | custom-call | flops 60000002048 | bytes 13107200 | tf_op jit(solution)/shard_map/pull_gather/pallas_call | solution.py:623
  288.5 27.8 %attention_backward.1 = (bf16[1024,2048]{1,0:T(8,128)(2,1)}, bf16[2048,384]{1,0:T(8,128)(2,1)}, bf16[256,2048]{1,0:T(8,128)(2,1)}) custom-call(bf16[1024,2048]{1,0:T(8,128)(2,1)} %bitcast.48, bf16[256,2048]{1,0:T(8,128)(2,1)} %wo_ref.3, bf16[1024,256]{1,0:T(8,128)(2,1)} %get-tuple-element.68.a_ref, bf16[1024,256]{1,0:T(8,128)(2,1)} %get-tuple-element.69.q_ref, ...), custom_call_target="tpu_custom_call" | custom-call | flops 30000001024 | bytes 31457280 | tf_op jit(solution)/shard_map/attention_backward/pallas_call | solution.py:984
  316.7 0.9 copy-done.7
  318.0 2.7 collective-permute-done.2.before_fetched
  320.7 2.8 collective-permute-done.3.after_fetched
  323.5 1.3 copy-done.9
  324.8 59.3 %pull_tokens.1 = (f32[128,2048]{1,0:T(8,128)}, bf16[128,2048]{1,0:T(8,128)(2,1)}, f32[2,2048]{1,0:T(2,128)}, bf16[4,1024,2048]{2,1,0:T(8,128)(2,1)}, bf16[4,1024...) custom-call(bf16[1024,2048]{1,0:T(8,128)(2,1)} %get-tuple-element.74, ...), custom_call_target="tpu_custom_call", output_to_operand_aliasing={{3}: (13, {}), {4}: (14, {}), {5}: (15, {}), {6}: (16, {})} | custom-call | flops 60000002048 | bytes 13107200 | tf_op jit(solution)/shard_map/pull_tokens/pallas_call | solution.py:787
  384.3 4.5 all-to-all-start
  388.9 1.4 fusion
  390.3 16.9 %ffn_other.1 = (bf16[4,1024,2048]{2,1,0:T(8,128)(2,1)}, bf16[4,1024,1024]{2,1,0:T(8,128)(2,1)}, bf16[4,1024,1024]{2,1,0:T(8,128)(2,1)}, bf16[4,1024,1024]{2,1,0:T(8,128)(2,1)}) custom-call(s32[2]{0:T(128)S(1)} %pad_add_fusion.w_ref, ...), custom_call_target="tpu_custom_call", output_to_operand_aliasing={{0}: (6, {}), {1}: (7, {}), {2}: (8, {}), {3}: (9, {})} | custom-call | flops 17179869184 | bytes 41943040 | tf_op jit(solution)/shard_map/ffn_other/pallas_call | solution.py:1092
  407.3 2.6 all-to-all-done
  409.9 104.5 %finish.1 = (bf16[256,8192]{1,0:T(8,128)(2,1)}, bf16[256,8192]{1,0:T(8,128)(2,1)}, bf16[1024,2048]{1,0:T(8,128)(2,1)}, bf16[256,2048]{1,0:T(8,128)(2,1)}, bf16[2048,384]{1,0:T(8,128)(2,1)}) custom-call(bf16[4096,2048]{1,0:T(8,128)(2,1)} %bitcast.36, bf16[4096,1024]{1,0:T(8,128)(2,1)} %bitcast.38, bf16[4096,1024]{1,0:T(8,128)(2,1)} %bitcast.39, ...), custom_call_target="tpu_custom_call" | custom-call | flops 120000004096 | bytes 83886080 | tf_op jit(solution)/shard_map/finish/pallas_call | solution.py:1345
  514.3 6.7 %convert_element_type.13 = f32[256,8192]{1,0:T(8,128)} convert(bf16[256,8192]{1,0:T(8,128)(2,1)} %get-tuple-element.104) | non-fusion elementwise | flops 2097152 | bytes 12582912 | tf_op jit(solution)/shard_map/convert_element_type | solution.py:1550
  521.1 4.4 convert_element_type.14
  525.4 4.4 convert_element_type.15
  529.9 3.3 join_heads.1
  533.2 1.6 convert_element_type.12
  534.8 0.8 copy.43
  535.6 1.0 copy.44
  (30 shorter events, 1.7 us)
Async XLA Ops:
  1.3 209.9 %copy-start.6 = (s32[1,1024]{1,0:T(1,128)S(1)}, s32[1,1024]{1,0:T(1,128)}, u32[]{:S(2)}) copy-start(s32[1,1024]{1,0:T(1,128)} %deal_ref.1) | copy-start | bytes 12292
  207.1 109.1 %collective-permute-start = (bf16[512,2048]{1,0:T(8,128)(2,1)}, bf16[512,2048]{1,0:T(8,128)(2,1)}, u32[]{:S(2)}, u32[]{:S(2)}) collective-permute-start(bf16[512,2048]{1,0:T(8,128)(2,1)} %bitcast.29), channel_id=1, source_target_pairs={{0,8},{8,16},{16,24},{24,0},{1,9},{9,17},{17,25},{25,1},{2,10},{10... | collective-permute-start | bytes 6291464 | tf_op jit(solution)/shard_map/ppermute | solution.py:1512
  207.2 109.0 %collective-permute-start.1 = (bf16[512,2048]{1,0:T(8,128)(2,1)}, bf16[512,2048]{1,0:T(8,128)(2,1)S(1)}, u32[]{:S(2)}, u32[]{:S(2)}) collective-permute-start(bf16[512,2048]{1,0:T(8,128)(2,1)} %bitcast.30), channel_id=1, source_target_pairs={{0,24},{8,0},{16,8},{24,16},{1,25},{9,1},{17,9},{25,17},{2,26},{10... | collective-permute-start | bytes 6291464 | tf_op jit(solution)/shard_map/ppermute | solution.py:1512
  235.7 2.0 copy-start
  316.2 1.3 copy-start.7
  316.3 4.5 collective-permute-start.2
  317.6 5.9 %collective-permute-start.3 = (bf16[512,2048]{1,0:T(8,128)(2,1)S(1)}, bf16[512,2048]{1,0:T(8,128)(2,1)S(1)}, u32[]{:S(2)}, u32[]{:S(2)}) collective-permute-start(bf16[512,2048]{1,0:T(8,128)(2,1)S(1)} %collective-permute-done.1.after_held), channel_id=1, source_target_pairs={{0,1},{1,0},{2,3},{3,2},{4,5},{5,4},{6,7},{7,6},{8,9},{9,8},{10,11... | collective-permute-start | bytes 6291464 | tf_op jit(solution)/shard_map/ppermute | solution.py:1515
  318.0 66.2 %collective-permute-start.4 = (bf16[512,2048]{1,0:T(8,128)(2,1)}, bf16[512,2048]{1,0:T(8,128)(2,1)}, u32[]{:S(2)}, u32[]{:S(2)}) collective-permute-start(bf16[512,2048]{1,0:T(8,128)(2,1)} %collective-permute-done.before_held), channel_id=1, source_target_pairs={{0,8},{8,16},{16,24},{24,0},{1,9},{9,17},{17,25},{25,1},{2,10},{10... | collective-permute-start | bytes 6291464 | tf_op jit(solution)/shard_map/ppermute | solution.py:1512
  320.7 2.8 copy-start.8
  323.5 1.3 copy-start.9
  384.2 6.1 %collective-permute-start.5 = (bf16[512,2048]{1,0:T(8,128)(2,1)}, bf16[512,2048]{1,0:T(8,128)(2,1)S(1)}, u32[]{:S(2)}, u32[]{:S(2)}) collective-permute-start(bf16[512,2048]{1,0:T(8,128)(2,1)} %collective-permute-done.4.held_ref), channel_id=1, source_target_pairs={{0,1},{1,0},{2,3},{3,2},{4,5},{5,4},{6,7},{7,6},{8,9},{9,8},{10,11... | collective-permute-start | bytes 6291464 | tf_op jit(solution)/shard_map/ppermute | solution.py:1515
  384.3 25.6 %all-to-all-start = ((bf16[8,256,384]{2,1,0:T(8,128)(2,1)}), bf16[8,256,384]{2,1,0:T(8,128)(2,1)}, u32[]{:S(2)}, u32[]{:S(2)}) async-start(bf16[8,256,384]{2,1,0:T(8,128)(2,1)} %bitcast.24), calls=%async_computation | async-start | bytes 3145728 | tf_op jit(solution)/shard_map/all_to_all | solution.py:85
  514.3 6.7 %copy-start.2 = (bf16[256,8192]{1,0:T(8,128)(2,1)S(1)}, bf16[256,8192]{1,0:T(8,128)(2,1)}, u32[]{:S(2)}) copy-start(bf16[256,8192]{1,0:T(8,128)(2,1)} %get-tuple-element.105) | copy-start | bytes 12582916
  521.1 4.4 copy-start.1
  525.4 7.8 %copy-start.3 = (bf16[256,2048]{1,0:T(8,128)(2,1)S(1)}, bf16[256,2048]{1,0:T(8,128)(2,1)}, u32[]{:S(2)}) copy-start(bf16[256,2048]{1,0:T(8,128)(2,1)} %get-tuple-element.103) | copy-start | bytes 3145732
  529.9 4.9 copy-start.5
  529.9 5.7 %copy-start.4 = (f32[128,2048]{1,0:T(8,128)S(1)}, f32[128,2048]{1,0:T(8,128)}, u32[]{:S(2)}) copy-start(f32[128,2048]{1,0:T(8,128)} %get-tuple-element.121) | copy-start | bytes 3145732

commit v9 on v8

--- a/solution.py
+++ b/solution.py
@@ -356,12 +356,15 @@
             copy.start()
 
         def permute(first):
-            for i in range(total // 2 // block):
+            def step(i, carry):
                 row0 = pl.multiple_of(first + i * block, block)
                 packed = row0 + lax.broadcasted_iota(jnp.int32, (block, total), 0)
                 chosen = (deal_ref[...] == packed).astype(BF16)
                 dealt = mm(chosen, c_all[...].reshape(total, width))
                 dg_own[pl.ds(row0, block), :] = (RESIDUAL_SCALE * dealt).astype(BF16)
+                return carry
+
+            lax.fori_loop(0, total // 2 // block, step, 0)
 
         near = pl.multiple_of(core * (total // 2), total // 2)
         far = pl.multiple_of((1 - core) * (total // 2), total // 2)
@@ -412,10 +415,11 @@
         for copy in weights:
             copy.wait_recv()
         more(BULK[0])
-        for i in range(total // block):
-            rows = pl.ds(i * block, block)
-            x = n_ref[pl.ds(i * block // local, block // local)].reshape(block, width)
-            cosine, sine = lane_rope(i * block, block, freq_ref[...], len_ref)
+        def project(i, carry):
+            row0 = pl.multiple_of(i * block, block)
+            rows = pl.ds(row0, block)
+            x = n_ref[pl.ds(i * (block // local), block // local)].reshape(block, width)
+            cosine, sine = lane_rope(row0, block, freq_ref[...], len_ref)
             pre = mm(x, qw_ref[...].reshape(width, q_cols))
             for j in range(q_cols // (2 * HEAD)):
                 lanes = slice(j * 2 * HEAD, (j + 1) * 2 * HEAD)
@@ -424,6 +428,9 @@
             cosine, sine = keys_only(cosine, sine)
             y = mm(x, kvw_ref[...].reshape(width, 2 * HEAD))
             kv_ref[rows, :] = (y * cosine + lane_swap(y) * sine).astype(BF16)
+            return carry
+
+        lax.fori_loop(0, total // block, project, 0)
         hops.append(pass_on(1))
         attend(q_cols // HEAD, block, q_ref, kv_ref, len_ref, att_ref)
 
@@ -443,9 +450,13 @@
             slot = 0 if first is near else 1
             if slot in pending:
                 pending[slot].wait()
-            for i in range(total // 2 // block):
+
+            def step(i, carry):
                 part = pl.ds(pl.multiple_of(first + i * block, block), block)
                 ag_stage[part, :] = mm_t(dg_own[part, :], wd_ref[...]).astype(BF16)
+                return carry
+
+            lax.fori_loop(0, total // 2 // block, step, 0)
             pending[slot] = pltpu.make_async_copy(
                 ag_stage.at[rows], ag_out.at[held, rows], local_sems.at[5 + slot]
             )
@@ -660,8 +671,8 @@
 
     def kernel(
         p_ref, o_ref, h_ref, gain_ref, mg_ref, og_ref, wg_ref, wu_ref, ag_hbm,
-        before_held, before_fetched, after_held, after_fetched, unused_na, unused_act, unused_gg, unused_ug,
-        out, lay, gains, na_hbm, act_hbm, gg_hbm, ug_hbm,
+        before_held, after_held, unused_na, unused_act, unused_gg, unused_ug,
+        out, lay, gains, na_hbm, act_hbm, gg_hbm, ug_hbm, fetched, share_sems,
         nf_buf, ag_buf, done_buf, in_sems, out_sems, gain_in, gain_out, gain_sems, *scratch,
     ):
         me = lax.axis_index("shard")
@@ -672,9 +683,9 @@
         first, second = scratch[:8], scratch[8:]
         parts = (
             (before, before_held, core),
-            (before, before_fetched, 1 - core),
             (after, after_held, core),
-            (after, after_fetched, 1 - core),
+            (before, fetched.at[0], 1 - core),
+            (after, fetched.at[1], 1 - core),
         )
 
         def rows_of(p, r):
@@ -716,6 +727,8 @@
         def fill(p):
             if p > 0:
                 wait_stores(p - 1)
+            if p in (1, 2):
+                shares[p - 1].wait_recv()
             if p + 1 < len(parts):
                 start_loads(p + 1)
 
@@ -749,6 +762,12 @@
         outputs = scatter_steps(me, blocks_of(o_ref), *second)
         next(grads)
         next(outputs)
+        shares = [
+            send(source, fetched.at[k], share_sems, k, flip(me, 1))
+            for k, source in enumerate((before_held, after_held))
+        ]
+        for copy in shares:
+            copy.start()
         fill(0)
         next(grads)
         fill(1)
@@ -782,6 +801,8 @@
             for unused in steps:
                 pass
         wait_stores(3)
+        for copy in shares:
+            copy.wait_send()
 
     hidden_shape = jax.ShapeDtypeStruct((groups, total, cols), BF16)
     return pl.pallas_call(
@@ -794,11 +815,13 @@
             hidden_shape,
             hidden_shape,
             hidden_shape,
+            jax.ShapeDtypeStruct((2, total // 2, width), BF16),
         ),
-        in_specs=[VMEM] * 8 + [ANY] * 9,
-        out_specs=[VMEM] * 3 + [ANY] * 4,
-        input_output_aliases={13: 3, 14: 4, 15: 5, 16: 6},
+        in_specs=[VMEM] * 8 + [ANY] * 7,
+        out_specs=[VMEM] * 3 + [ANY] * 5,
+        input_output_aliases={11: 3, 12: 4, 13: 5, 14: 6},
         scratch_shapes=[
+            pltpu.SemaphoreType.DMA((2, 2)),
             pltpu.VMEM((2 * per_half, block, width), BF16),
             pltpu.VMEM((2 * per_half, block, cols), BF16),
             pltpu.VMEM((3, 2 * per_half, block, cols), BF16),
@@ -956,15 +979,19 @@
         bg_ref, wo_ref, a_ref, q_ref, kv_ref, n_ref, qw_ref, kvw_ref, len_ref, freq_ref,
         dn_ref, dqkv_ref, dwo_ref, g_ref, dq_ref, dk_ref, dv_ref, pq_ref, pkv_ref,
     ):
-        for i in range(total // block):
-            rows = pl.ds(i * block, block)
+        def open_up(i, carry):
+            rows = pl.ds(pl.multiple_of(i * block, block), block)
             g_ref[rows, :] = mm_t(bg_ref[rows, :], wo_ref[...]).astype(BF16)
+            return carry
+
+        lax.fori_loop(0, total // block, open_up, 0)
         attend_back(
             q_cols // HEAD, block, q_ref, kv_ref, g_ref, len_ref, dq_ref, dk_ref, dv_ref
         )
-        for i in range(total // block):
-            rows = pl.ds(i * block, block)
-            cosine, sine = lane_rope(i * block, block, freq_ref[...], len_ref)
+        def close_up(i, carry):
+            row0 = pl.multiple_of(i * block, block)
+            rows = pl.ds(row0, block)
+            cosine, sine = lane_rope(row0, block, freq_ref[...], len_ref)
             for j in range(q_cols // (2 * HEAD)):
                 lanes = slice(j * 2 * HEAD, (j + 1) * 2 * HEAD)
                 x = dq_ref[rows, lanes]
@@ -975,11 +1002,18 @@
             dn_ref[rows, :] = (
                 mm_t(pq_ref[rows, :], qw_ref[...]) + mm_t(pkv_ref[rows, :], kvw_ref[...])
             ).astype(BF16)
-        for i in range(width // 512):
-            cols = slice(i * 512, (i + 1) * 512)
+            return carry
+
+        lax.fori_loop(0, total // block, close_up, 0)
+
+        def weigh(i, carry):
+            cols = pl.ds(pl.multiple_of(i * 512, 512), 512)
             dqkv_ref[cols, :q_cols] = t_mm(n_ref[:, cols], pq_ref[...]).astype(BF16)
             dqkv_ref[cols, q_cols:] = t_mm(n_ref[:, cols], pkv_ref[...]).astype(BF16)
             dwo_ref[:, cols] = t_mm(a_ref[...], bg_ref[:, cols]).astype(BF16)
+            return carry
+
+        lax.fori_loop(0, width // 512, weigh, 0)
 
     return pl.pallas_call(
         kernel,
@@ -1106,27 +1140,6 @@
         ),
         name="ffn_other",
     )(where, held, fetched, act_grads, wg, wu, *filled)
-
-
-def join_heads(blocks, q_cols):
-    n, rows, cols = blocks.shape
-
-    def kernel(b_ref, q_ref, k_ref, v_ref):
-        for i in range(n):
-            q_ref[:, i * q_cols : (i + 1) * q_cols] = b_ref[i, :, :q_cols].astype(F32)
-        kv = [b_ref[i, :, q_cols:].astype(F32) for i in range(n)]
-        k_ref[...] = jnp.concatenate([x[:, :HEAD] for x in kv], axis=1)
-        v_ref[...] = jnp.concatenate([x[:, HEAD:] for x in kv], axis=1)
-
-    return pl.pallas_call(
-        kernel,
-        out_shape=(
-            jax.ShapeDtypeStruct((rows, n * q_cols), F32),
-            jax.ShapeDtypeStruct((rows, n * HEAD), F32),
-            jax.ShapeDtypeStruct((rows, n * HEAD), F32),
-        ),
-        name="join_heads",
-    )(blocks)
 
 
 def finish(normed, gate_grad, up_grad, activated, down_grad, output_part, qkv_part, collective_id):
@@ -1378,108 +1391,43 @@
     )(normed, gate_grad, up_grad, activated, down_grad, output_part, qkv_part)
 
 
-def output_rows(where, activated, down_weight, middle, deal, total):
-    groups, total, cols = activated.shape
-    local, width = middle.shape
-    block = 256
-
-    def kernel(w_ref, act_ref, wd_ref, mid_ref, deal_ref, o_ref, rows_ref):
-        for i in range(total // block):
-            rows = pl.ds(i * block, block)
-            rows_ref[rows, :] = (RESIDUAL_SCALE * mm(act_ref[0, rows, :], wd_ref[...])).astype(BF16)
-        own = pl.ds(pl.multiple_of(w_ref[1] * local, local), local)
-        rows_ref[own, :] = (rows_ref[own, :].astype(F32) + mid_ref[...]).astype(BF16)
-        for i in range(total // block):
-            rows = pl.ds(i * block, block)
-            packed = lax.broadcasted_iota(jnp.int32, (block, total), 1)
-            chosen = (deal_ref[rows, :] == packed).astype(BF16)
-            o_ref[rows, :] = mm(chosen, rows_ref[...]).astype(BF16)
-
-    def full(shape):
-        return pl.BlockSpec(shape, lambda i, w: (0,) * len(shape), pipeline_mode=pl.Buffered(1))
-
-    return pl.pallas_call(
-        kernel,
-        grid_spec=pltpu.PrefetchScalarGridSpec(
-            num_scalar_prefetch=1,
-            grid=(1,),
-            in_specs=[
-                pl.BlockSpec((1, total, cols), lambda i, w: (w[0], 0, 0), pipeline_mode=pl.Buffered(1)),
-                full(down_weight.shape),
-                full(middle.shape),
-                full(deal.shape),
-            ],
-            out_specs=full((total, width)),
-            scratch_shapes=[pltpu.VMEM((total, width), BF16)],
-        ),
-        out_shape=jax.ShapeDtypeStruct((total, width), BF16),
-        compiler_params=pltpu.CompilerParams(vmem_limit_bytes=48 << 20),
-        cost_estimate=pl.CostEstimate(
-            flops=2 * total * width * (cols + total) * 2, bytes_accessed=12 << 20, transcendentals=0
-        ),
-        name="output_rows",
-    )(where, activated, down_weight, middle, deal)
-
-
-def join_heads(blocks, q_cols):
-    n, rows, cols = blocks.shape
-
-    def kernel(b_ref, q_ref, k_ref, v_ref):
+def widen(gate, up, down, out, heads, q_cols):
+    rows, wide = gate.shape
+    tall, width = down.shape
+    n = heads.shape[0]
+    steps = 16
+    block, high = rows // steps, tall // steps
+
+    def kernel(g_ref, u_ref, d_ref, o_ref, h_ref, g_out, u_out, d_out, o_out, q_out, k_out, v_out):
+        g_out[...] = g_ref[...].astype(F32)
+        u_out[...] = u_ref[...].astype(F32)
+        d_out[...] = d_ref[...].astype(F32)
+        o_out[...] = o_ref[...].astype(F32)
         for i in range(n):
-            q_ref[:, i * q_cols : (i + 1) * q_cols] = b_ref[i, :, :q_cols].astype(F32)
-        kv = [b_ref[i, :, q_cols:].astype(F32) for i in range(n)]
-        k_ref[...] = jnp.concatenate([x[:, :HEAD] for x in kv], axis=1)
-        v_ref[...] = jnp.concatenate([x[:, HEAD:] for x in kv], axis=1)
-
-    return pl.pallas_call(
-        kernel,
-        out_shape=(
-            jax.ShapeDtypeStruct((rows, n * q_cols), F32),
-            jax.ShapeDtypeStruct((rows, n * HEAD), F32),
-            jax.ShapeDtypeStruct((rows, n * HEAD), F32),
-        ),
-        name="join_heads",
-    )(blocks)
-
-
-def weight_grad(left, right, dtype):
-    groups, total, m = left.shape
-    n = right.shape[2]
-    block = 512
-    steps = groups * total // block
-
-    def kernel(l_ref, r_ref, o_ref, acc):
-        k = pl.program_id(0)
-        term = t_mm(l_ref[...], r_ref[...])
-
-        @pl.when(k == 0)
-        def _():
-            acc[...] = term
-
-        @pl.when(k > 0)
-        def _():
-            acc[...] += term
-
-        @pl.when(k == steps - 1)
-        def _():
-            o_ref[...] = acc[...].astype(o_ref.dtype)
-
+            q_out[:, i * q_cols : (i + 1) * q_cols] = h_ref[i, :, :q_cols].astype(F32)
+        kv = [h_ref[i, :, q_cols:].astype(F32) for i in range(n)]
+        k_out[...] = jnp.concatenate([x[:, :HEAD] for x in kv], axis=1)
+        v_out[...] = jnp.concatenate([x[:, HEAD:] for x in kv], axis=1)
+
+    def spec(height, across):
+        return pl.BlockSpec((height, across), lambda i: (i, 0))
+
+    shapes = [(rows, wide), (rows, wide), (tall, width), (rows, width)]
+    blocks = [spec(block, wide), spec(block, wide), spec(high, width), spec(block, width)]
+    narrow = [n * q_cols, n * HEAD, n * HEAD]
     return pl.pallas_call(
         kernel,
         grid=(steps,),
-        in_specs=[
-            pl.BlockSpec((block, m), lambda k: (k, 0)),
-            pl.BlockSpec((block, n), lambda k: (k, 0)),
-        ],
-        out_specs=pl.BlockSpec((m, n), lambda k: (0, 0), pipeline_mode=pl.Buffered(1)),
-        out_shape=jax.ShapeDtypeStruct((m, n), dtype),
-        scratch_shapes=[pltpu.VMEM((m, n), F32)],
-        compiler_params=pltpu.CompilerParams(vmem_limit_bytes=56 << 20),
+        in_specs=blocks + [pl.BlockSpec((n, block, heads.shape[2]), lambda i: (0, i, 0))],
+        out_specs=blocks + [spec(block, across) for across in narrow],
+        out_shape=[jax.ShapeDtypeStruct(shape, F32) for shape in shapes]
+        + [jax.ShapeDtypeStruct((rows, across), F32) for across in narrow],
+        compiler_params=pltpu.CompilerParams(vmem_limit_bytes=24 << 20),
         cost_estimate=pl.CostEstimate(
-            flops=2 * groups * total * m * n, bytes_accessed=2 * groups * total * (m + n), transcendentals=0
+            flops=4 * rows * wide, bytes_accessed=20 * rows * wide, transcendentals=0
         ),
-        name="weight_grad",
-    )(left.reshape(groups * total, m), right.reshape(groups * total, n))
+        name="widen",
+    )(gate, up, down, out, heads)
 
 
 def per_device_plane(
@@ -1528,9 +1476,9 @@
     before, after, unused_part = lax.optimization_barrier((before, after, normed_part))
     opposite = shift(before, 1)
     qkv_part = exchange(qkv_grad.reshape(n, rows, q_cols + 2 * HEAD))
-    tokens_grad, layer_output, gains, *filled = pull_tokens(
+    tokens_grad, layer_output, gains, *filled, unused_half = pull_tokens(
         normed_part, output_part, tokens, attn_gain, middle_grad, ffn_gain_part,
-        (before, fetch(before), after, fetch(after)), act_grads, gate_cols, up_cols, filled, replicas, 3,
+        (before, after), act_grads, gate_cols, up_cols, filled, replicas, 3,
     )
     opposite, unused_rows = lax.optimization_barrier((opposite, tokens_grad))
     where = jnp.stack([lax.rem(group + replicas - 2, replicas), core]).astype(jnp.int32)
@@ -1540,16 +1488,12 @@
         left, *rights, filled[1].reshape(replicas * total, -1), down_grads.reshape(replicas * total, -1),
         output_grad, qkv_part.reshape(width, -1), 4,
     )
+    gate_grad, up_grad, down_grad, output_grad, q_grad, k_grad, v_grad = widen(
+        gate_grad, up_grad, down_grad, output_grad, qkv_grad.reshape(n, rows, -1), q_cols
+    )
     return (
-        layer_output,
-        tokens_grad,
-        gains[0],
-        *join_heads(qkv_grad.reshape(n, rows, -1), q_cols),
-        output_grad.astype(F32),
-        gains[1],
-        gate_grad.astype(F32),
-        up_grad.astype(F32),
-        down_grad.astype(F32),
+        layer_output, tokens_grad, gains[0], q_grad, k_grad, v_grad, output_grad, gains[1],
+        gate_grad, up_grad, down_grad,
     )
 
 

time: 546 us -> 537 us (0.984)
  other arithmetic: 17.2 us -> 0.09 us
  Pallas kernels: 492 us -> 506 us
  local copies, waits for them, and re-layouts: 9 us -> 16 us
  waiting for transfers between devices: 8.15 us -> 2.61 us
    convert_element_type x4 -> x0, other arithmetic: 17.1 us -> none  [the longest x1 6.73 us: per_device_plane(): gate_grad.astype(F32)]
    pallas_call x1, Pallas kernels: 3.34 us -> 10.5 us  [widen(): pl.pallas_call(kernel, grid=(steps,), in_specs=blocks + [pl.BlockSpec((n,...]
    unnamed x22 -> x20, local copies, waits for them, and re-layouts: 5.97 us -> 13 us
    ppermute x3 -> x1, waiting for transfers between devices: 5.54 us -> 0.01 us  [fetch(): return lax.ppermute(x, 'shard', [(i, i ^ 1) for i in range(n)])]
  transfers between devices with their start and end apart: 7 -> 5, of which waited for: 3 -> 1; matrix products, arithmetic and copies ran while one was open for 0% -> 0% of each run, Pallas kernels for 33% -> 35%
where the time goes in v9:
time: 537 us; the launch traced here: 533 us
  Pallas kernels  506 us (94%)
  local copies, waits for them, and re-layouts  16 us (3%)
  starting transfers between devices  6.74 us (1%)
    pallas_call x1, Pallas kernels, front(): pl.pallas_call(kernel, out_shape=(rows8, jax.ShapeDtypeStruct((total, q_c...  206 us
    pallas_call x1, Pallas kernels, finish(): pl.pallas_call(kernel, out_shape=(exchanged, exchanged, jax.ShapeDtypeStr...  104 us
    pallas_call x1, Pallas kernels, pull_tokens(): pl.pallas_call(kernel, out_shape=(jax.ShapeDtypeStruct((rows, width), F32...  62.1 us
    pallas_call x1, Pallas kernels, pull_gather(): pl.pallas_call(kernel, out_shape=(jax.ShapeDtypeStruct((rows, width), F32...  51.4 us
    pallas_call x1, Pallas kernels, attention_backward(): pl.pallas_call(kernel, out_shape=(jax.ShapeDtypeStruct((total, width), BF...  31.1 us
    pallas_call x1, Pallas kernels, ffn_own(): pl.pallas_call(kernel, grid_spec=pltpu.PrefetchScalarGridSpec(num_scalar_...  24 us
    pallas_call x1, Pallas kernels, ffn_other(): pl.pallas_call(kernel, grid_spec=pltpu.PrefetchScalarGridSpec(num_scalar_...  16.9 us
    unnamed x20, local copies, waits for them, and re-layouts  13 us
  transfers between devices with their start and end apart: 5, of which 1 were waited for; matrix products, arithmetic and copies ran while one was open for 0% of the time, Pallas kernels for 35%

profile of v9, /device:TPU:0, one launch (start us, length us, event | category | flops | bytes accessed | tf_op | source)
XLA Modules:
  0.0 532.7 jit_solution(14797042239309743436)
XLA Ops:
  0.7 0.6 broadcast_in_dim_tile.5.freq_ref
  1.3 206.0 %front.1 = (bf16[8,128,2048]{2,1,0:T(8,128)(2,1)}, bf16[1024,256]{1,0:T(8,128)(2,1)}, bf16[1024,128]{1,0:T(8,128)(2,1)}, bf16[1024,256]{1,0:T(8,128)(2,1)}, bf16...) custom-call(bf16[128,2048]{1,0:T(8,128)(2,1)} %h_ref.1, ...), custom_call_target="tpu_custom_call" | custom-call | flops 199999995904 | bytes 52428800 | tf_op jit(solution)/shard_map/front/pallas_call | solution.py:511
  207.3 2.1 collective-permute-start.1
  209.4 1.0 copy.32.deal_ref
  210.4 24.0 %ffn_own.1 = (bf16[4,1024,2048]{2,1,0:T(8,128)(2,1)}, bf16[4,1024,1024]{2,1,0:T(8,128)(2,1)}, bf16[4,1024,1024]{2,1,0:T(8,128)(2,1)}, bf16[4,1024,1024]{2,1,0:T(8,128)(2,1)}, bf16[1024,2048]{1,0:T(8,128)(2,1)S(1)}) custom-call(s32[1]{0:T(128)} %bitcast.g_ref, bf16[1024,2048]{1,0:T(8,128)(2,1)} %bitcast.47, ...), custom_call_target="tpu_custom_call" | custom-call | flops 25769803776 | bytes 41943040 | tf_op jit(solution)/shard_map/ffn_own/pallas_call | solution.py:1069
  234.4 2.0 copy-done.5
  236.4 51.4 %pull_gather.1 = (f32[128,2048]{1,0:T(8,128)}, f32[1,2048]{1,0:T(1,128)}, bf16[8,128,2048]{2,1,0:T(8,128)(2,1)}, bf16[1024,2048]{1,0:T(8,128)(2,1)}) custom-call(bf16[1024,2048]{1,0:T(8,128)(2,1)} %copy-done.5, f32[128,2048]{1,0:T(8,128)} %get-tuple-element.68.m_ref, f32[1,2048]{1,0:T(1,128)} %bitcast.32, bf16[128,2048]{1,0:T(8,128)(2,1)} %get-tuple-element.69.g_ref, ...), custom_call_target="tpu_custom_call" | custom-call | flops 60000002048 | bytes 13107200 | tf_op jit(solution)/shard_map/pull_gather/pallas_call | solution.py:634
  287.9 31.1 %attention_backward.1 = (bf16[1024,2048]{1,0:T(8,128)(2,1)}, bf16[2048,384]{1,0:T(8,128)(2,1)}, bf16[256,2048]{1,0:T(8,128)(2,1)}) custom-call(bf16[1024,2048]{1,0:T(8,128)(2,1)} %bitcast.48, bf16[256,2048]{1,0:T(8,128)(2,1)} %wo_ref.3, bf16[1024,256]{1,0:T(8,128)(2,1)} %get-tuple-element.72.a_ref, bf16[1024,256]{1,0:T(8,128)(2,1)} %get-tuple-element.73.q_ref, ...), custom_call_target="tpu_custom_call" | custom-call | flops 30000001024 | bytes 31457280 | tf_op jit(solution)/shard_map/attention_backward/pallas_call | solution.py:1018
  319.1 62.1 %pull_tokens.1 = (f32[128,2048]{1,0:T(8,128)}, bf16[128,2048]{1,0:T(8,128)(2,1)}, f32[2,2048]{1,0:T(2,128)}, bf16[4,1024,2048]{2,1,0:T(8,128)(2,1)}, bf16[4,1024...) custom-call(bf16[1024,2048]{1,0:T(8,128)(2,1)} %get-tuple-element.78, ...), custom_call_target="tpu_custom_call", output_to_operand_aliasing={{3}: (11, {}), {4}: (12, {}), {5}: (13, {}), {6}: (14, {})} | custom-call | flops 60000002048 | bytes 13107200 | tf_op jit(solution)/shard_map/pull_tokens/pallas_call | solution.py:808
  381.2 0.1 collective-permute-start.3
  381.2 4.5 all-to-all-start
  385.8 0.1 pad_add_fusion.w_ref
  385.8 1.4 fusion
  387.2 16.9 %ffn_other.1 = (bf16[4,1024,2048]{2,1,0:T(8,128)(2,1)}, bf16[4,1024,1024]{2,1,0:T(8,128)(2,1)}, bf16[4,1024,1024]{2,1,0:T(8,128)(2,1)}, bf16[4,1024,1024]{2,1,0:T(8,128)(2,1)}) custom-call(s32[2]{0:T(128)S(1)} %pad_add_fusion.w_ref, ...), custom_call_target="tpu_custom_call", output_to_operand_aliasing={{0}: (6, {}), {1}: (7, {}), {2}: (8, {}), {3}: (9, {})} | custom-call | flops 17179869184 | bytes 41943040 | tf_op jit(solution)/shard_map/ffn_other/pallas_call | solution.py:1126
  404.2 2.6 all-to-all-done
  406.8 104.2 %finish.1 = (bf16[256,8192]{1,0:T(8,128)(2,1)}, bf16[256,8192]{1,0:T(8,128)(2,1)}, bf16[1024,2048]{1,0:T(8,128)(2,1)}, bf16[256,2048]{1,0:T(8,128)(2,1)}, bf16[2048,384]{1,0:T(8,128)(2,1)}) custom-call(bf16[4096,2048]{1,0:T(8,128)(2,1)} %bitcast.36, bf16[4096,1024]{1,0:T(8,128)(2,1)} %bitcast.38, bf16[4096,1024]{1,0:T(8,128)(2,1)} %bitcast.39, ...), custom_call_target="tpu_custom_call" | custom-call | flops 120000004096 | bytes 83886080 | tf_op jit(solution)/shard_map/finish/pallas_call | solution.py:1358
  511.0 2.2 copy-done
  513.2 2.2 copy-done.1
  515.4 2.2 copy-done.2
  517.6 1.4 copy-done.3
  519.0 1.2 copy-done.4
  520.2 10.5 %widen.1 = (f32[256,8192]{1,0:T(8,128)}, f32[256,8192]{1,0:T(8,128)}, f32[1024,2048]{1,0:T(8,128)}, f32[256,2048]{1,0:T(8,128)}, f32[256,2048]{1,0:T(8,128)}, /*index=5*/f32[256,512]{1,0:T(8,128)}, f32[256,512]{1,0:T(8,128)}) custom-call(bf16[256,8192]{1,0:T(8,128)(2,1)S(1)} %copy-done, bf16[256,8192]{1,0:T(8,128)(2,1)S(1)} %copy-done.1, ...), custom_call_target="tpu_custom_call" | custom-call | flops 8388608 | bytes 41943040 | tf_op jit(solution)/shard_map/widen/pallas_call | solution.py:1418
  530.7 0.8 copy.43
  531.5 1.0 copy.44
  (20 shorter events, 0.1 us)
Async XLA Ops:
  1.3 208.2 %copy-start.8 = (s32[1,1024]{1,0:T(1,128)S(1)}, s32[1,1024]{1,0:T(1,128)}, u32[]{:S(2)}) copy-start(s32[1,1024]{1,0:T(1,128)} %deal_ref.1) | copy-start | bytes 12292
  207.3 111.7 %collective-permute-start.1 = (bf16[512,2048]{1,0:T(8,128)(2,1)}, bf16[512,2048]{1,0:T(8,128)(2,1)}, u32[]{:S(2)}, u32[]{:S(2)}) collective-permute-start(bf16[512,2048]{1,0:T(8,128)(2,1)} %bitcast.29), channel_id=1, source_target_pairs={{0,24},{8,0},{16,8},{24,16},{1,25},{9,1},{17,9},{25,17},{2,26},{10... | collective-permute-start | bytes 6291464 | tf_op jit(solution)/shard_map/ppermute | solution.py:1460
  209.4 109.6 %collective-permute-start = (bf16[512,2048]{1,0:T(8,128)(2,1)}, bf16[512,2048]{1,0:T(8,128)(2,1)}, u32[]{:S(2)}, u32[]{:S(2)}) collective-permute-start(bf16[512,2048]{1,0:T(8,128)(2,1)} %bitcast.30), channel_id=1, source_target_pairs={{0,8},{8,16},{16,24},{24,0},{1,9},{9,17},{17,25},{25,1},{2,10},{10... | collective-permute-start | bytes 6291464 | tf_op jit(solution)/shard_map/ppermute | solution.py:1460
  234.4 2.0 copy-start.5
  319.0 62.1 %collective-permute-start.2 = (bf16[512,2048]{1,0:T(8,128)(2,1)}, bf16[512,2048]{1,0:T(8,128)(2,1)}, u32[]{:S(2)}, u32[]{:S(2)}) collective-permute-start(bf16[512,2048]{1,0:T(8,128)(2,1)} %collective-permute-done.before_held), channel_id=1, source_target_pairs={{0,8},{8,16},{16,24},{24,0},{1,9},{9,17},{17,25},{25,1},{2,10},{10... | collective-permute-start | bytes 6291464 | tf_op jit(solution)/shard_map/ppermute | solution.py:1460
  381.2 6.1 %collective-permute-start.3 = (bf16[512,2048]{1,0:T(8,128)(2,1)}, bf16[512,2048]{1,0:T(8,128)(2,1)S(1)}, u32[]{:S(2)}, u32[]{:S(2)}) collective-permute-start(bf16[512,2048]{1,0:T(8,128)(2,1)} %collective-permute-done.2.held_ref), channel_id=1, source_target_pairs={{0,1},{1,0},{2,3},{3,2},{4,5},{5,4},{6,7},{7,6},{8,9},{9,8},{10,11... | collective-permute-start | bytes 6291464 | tf_op jit(solution)/shard_map/ppermute | solution.py:1463
  381.2 25.5 %all-to-all-start = ((bf16[8,256,384]{2,1,0:T(8,128)(2,1)}), bf16[8,256,384]{2,1,0:T(8,128)(2,1)}, u32[]{:S(2)}, u32[]{:S(2)}) async-start(bf16[8,256,384]{2,1,0:T(8,128)(2,1)} %bitcast.25), calls=%async_computation | async-start | bytes 3145728 | tf_op jit(solution)/shard_map/all_to_all | solution.py:85
  511.0 2.2 copy-start
  513.2 2.2 copy-start.1
  515.4 2.2 copy-start.2
  517.6 1.4 copy-start.3
  519.0 1.2 copy-start.4
  520.2 10.5 %copy-start.7 = (bf16[128,2048]{1,0:T(8,128)(2,1)S(1)}, bf16[128,2048]{1,0:T(8,128)(2,1)}, u32[]{:S(2)}) copy-start(bf16[128,2048]{1,0:T(8,128)(2,1)} %get-tuple-element.128) | copy-start | bytes 1572868
  520.2 11.3 %copy-start.6 = (f32[128,2048]{1,0:T(8,128)S(1)}, f32[128,2048]{1,0:T(8,128)}, u32[]{:S(2)}) copy-start(f32[128,2048]{1,0:T(8,128)} %get-tuple-element.129) | copy-start | bytes 3145732

commit v10 on v9

--- a/solution.py
+++ b/solution.py
@@ -657,7 +657,8 @@
 
 
 def pull_tokens(
-    part, out_part, hidden, gain, middle_grad, other_gain, near, act_grads, wg, wu, filled, replicas, collective_id
+    part, out_part, qkv, hidden, gain, middle_grad, other_gain, near, act_grads, wg, wu, filled, replicas,
+    collective_id,
 ):
     rows, width = middle_grad.shape
     groups, total, cols = act_grads.shape
@@ -671,8 +672,8 @@
 
     def kernel(
         p_ref, o_ref, h_ref, gain_ref, mg_ref, og_ref, wg_ref, wu_ref, ag_hbm,
-        before_held, after_held, unused_na, unused_act, unused_gg, unused_ug,
-        out, lay, gains, na_hbm, act_hbm, gg_hbm, ug_hbm, fetched, share_sems,
+        before_held, after_held, qkv_hbm, unused_na, unused_act, unused_gg, unused_ug,
+        out, lay, gains, na_hbm, act_hbm, gg_hbm, ug_hbm, fetched, qkv_out, share_sems, qkv_sems, own_sem,
         nf_buf, ag_buf, done_buf, in_sems, out_sems, gain_in, gain_out, gain_sems, *scratch,
     ):
         me = lax.axis_index("shard")
@@ -751,9 +752,10 @@
         for axis, weight in levels:
             index = me if axis == "shard" else group
             peers.append({axis: index + weight - 2 * weight * lax.rem(lax.div(index, weight), 2)})
-        for peer in peers:
+        far = [{"shard": flip(me, mask)} for mask in (3, 5, 6, 7)]
+        for peer in peers + far:
             pl.semaphore_signal(barrier, inc=1, device_id=peer, device_id_type=MESH)
-        pl.semaphore_wait(barrier, len(peers))
+        pl.semaphore_wait(barrier, len(peers) + len(far))
 
         def blocks_of(ref):
             return lambda d: ref[pl.ds(pl.multiple_of(d * rows, rows), rows), :].astype(F32)
@@ -768,8 +770,15 @@
         ]
         for copy in shares:
             copy.start()
+        exchange_qkv = []
+        for mask in range(1, 8):
+            peer = flip(me, mask)
+            exchange_qkv.append(send(qkv_hbm.at[peer], qkv_out.at[me], qkv_sems, mask - 1, peer))
+        own_qkv = pltpu.make_async_copy(qkv_hbm.at[me], qkv_out.at[me], own_sem.at[0])
         fill(0)
         next(grads)
+        for copy in exchange_qkv + [own_qkv]:
+            copy.start()
         fill(1)
         next(grads)
         next(outputs)
@@ -801,7 +810,10 @@
             for unused in steps:
                 pass
         wait_stores(3)
-        for copy in shares:
+        own_qkv.wait()
+        for copy in exchange_qkv:
+            copy.wait_recv()
+        for copy in shares + exchange_qkv:
             copy.wait_send()
 
     hidden_shape = jax.ShapeDtypeStruct((groups, total, cols), BF16)
@@ -816,12 +828,15 @@
             hidden_shape,
             hidden_shape,
             jax.ShapeDtypeStruct((2, total // 2, width), BF16),
+            jax.ShapeDtypeStruct(qkv.shape, BF16),
         ),
-        in_specs=[VMEM] * 8 + [ANY] * 7,
-        out_specs=[VMEM] * 3 + [ANY] * 5,
-        input_output_aliases={11: 3, 12: 4, 13: 5, 14: 6},
+        in_specs=[VMEM] * 8 + [ANY] * 8,
+        out_specs=[VMEM] * 3 + [ANY] * 6,
+        input_output_aliases={12: 3, 13: 4, 14: 5, 15: 6},
         scratch_shapes=[
             pltpu.SemaphoreType.DMA((2, 2)),
+            pltpu.SemaphoreType.DMA((2, 7)),
+            pltpu.SemaphoreType.DMA((1,)),
             pltpu.VMEM((2 * per_half, block, width), BF16),
             pltpu.VMEM((2 * per_half, block, cols), BF16),
             pltpu.VMEM((3, 2 * per_half, block, cols), BF16),
@@ -839,7 +854,7 @@
         ),
         name="pull_tokens",
     )(
-        part, out_part, hidden, gain[None, :], middle_grad, other_gain, wg, wu, act_grads, *near, *filled
+        part, out_part, hidden, gain[None, :], middle_grad, other_gain, wg, wu, act_grads, *near, qkv, *filled
     )
 
 
@@ -1006,14 +1021,11 @@
 
         lax.fori_loop(0, total // block, close_up, 0)
 
-        def weigh(i, carry):
-            cols = pl.ds(pl.multiple_of(i * 512, 512), 512)
+        for i in range(width // 512):
+            cols = slice(i * 512, (i + 1) * 512)
             dqkv_ref[cols, :q_cols] = t_mm(n_ref[:, cols], pq_ref[...]).astype(BF16)
             dqkv_ref[cols, q_cols:] = t_mm(n_ref[:, cols], pkv_ref[...]).astype(BF16)
             dwo_ref[:, cols] = t_mm(a_ref[...], bg_ref[:, cols]).astype(BF16)
-            return carry
-
-        lax.fori_loop(0, width // 512, weigh, 0)
 
     return pl.pallas_call(
         kernel,
@@ -1081,7 +1093,7 @@
             hidden,
             jax.ShapeDtypeStruct((total, width), BF16),
         ),
-        compiler_params=pltpu.CompilerParams(vmem_limit_bytes=48 << 20),
+        compiler_params=pltpu.CompilerParams(vmem_limit_bytes=62 << 20),
         cost_estimate=pl.CostEstimate(
             flops=12 * total * width * cols, bytes_accessed=40 << 20, transcendentals=total * cols
         ),
@@ -1134,7 +1146,7 @@
         ),
         out_shape=(jax.ShapeDtypeStruct((groups, total, width), BF16), hidden, hidden, hidden),
         input_output_aliases={6: 0, 7: 1, 8: 2, 9: 3},
-        compiler_params=pltpu.CompilerParams(vmem_limit_bytes=48 << 20),
+        compiler_params=pltpu.CompilerParams(vmem_limit_bytes=62 << 20),
         cost_estimate=pl.CostEstimate(
             flops=8 * total * width * cols, bytes_accessed=40 << 20, transcendentals=total * cols
         ),
@@ -1422,7 +1434,7 @@
         out_specs=blocks + [spec(block, across) for across in narrow],
         out_shape=[jax.ShapeDtypeStruct(shape, F32) for shape in shapes]
         + [jax.ShapeDtypeStruct((rows, across), F32) for across in narrow],
-        compiler_params=pltpu.CompilerParams(vmem_limit_bytes=24 << 20),
+        compiler_params=pltpu.CompilerParams(vmem_limit_bytes=62 << 20),
         cost_estimate=pl.CostEstimate(
             flops=4 * rows * wide, bytes_accessed=20 * rows * wide, transcendentals=0
         ),
@@ -1475,9 +1487,8 @@
     )
     before, after, unused_part = lax.optimization_barrier((before, after, normed_part))
     opposite = shift(before, 1)
-    qkv_part = exchange(qkv_grad.reshape(n, rows, q_cols + 2 * HEAD))
-    tokens_grad, layer_output, gains, *filled, unused_half = pull_tokens(
-        normed_part, output_part, tokens, attn_gain, middle_grad, ffn_gain_part,
+    tokens_grad, layer_output, gains, *filled, unused_half, qkv_part = pull_tokens(
+        normed_part, output_part, qkv_grad.reshape(n, rows, q_cols + 2 * HEAD), tokens, attn_gain, middle_grad, ffn_gain_part,
         (before, after), act_grads, gate_cols, up_cols, filled, replicas, 3,
     )
     opposite, unused_rows = lax.optimization_barrier((opposite, tokens_grad))

time: 537 us -> 548 us (1.020)
  Pallas kernels: 506 us -> 533 us
  local copies, waits for them, and re-layouts: 16 us -> 4.81 us
    pallas_call x1, Pallas kernels: 62.1 us -> 79.6 us  [pull_tokens(): pl.pallas_call(kernel, out_shape=(jax.ShapeDtypeStruct((rows, width), F32...]
    unnamed x20 -> x8, local copies, waits for them, and re-layouts: 13 us -> 1.78 us
    pallas_call x1, Pallas kernels: 10.5 us -> 18 us  [widen(): pl.pallas_call(kernel, grid=(steps,), in_specs=blocks + [pl.BlockSpec((n,...]
  transfers between devices with their start and end apart: 5 -> 4, of which waited for: 1 -> 1; matrix products, arithmetic and copies ran while one was open for 0% -> 1% of each run, Pallas kernels for 35% -> 34%
where the time goes in v10:
time: 548 us; the launch traced here: 544 us
  Pallas kernels  533 us (97%)
    pallas_call x1, Pallas kernels, front(): pl.pallas_call(kernel, out_shape=(rows8, jax.ShapeDtypeStruct((total, q_c...  206 us
    pallas_call x1, Pallas kernels, finish(): pl.pallas_call(kernel, out_shape=(exchanged, exchanged, jax.ShapeDtypeStr...  105 us
    pallas_call x1, Pallas kernels, pull_tokens(): pl.pallas_call(kernel, out_shape=(jax.ShapeDtypeStruct((rows, width), F32...  79.6 us
    pallas_call x1, Pallas kernels, pull_gather(): pl.pallas_call(kernel, out_shape=(jax.ShapeDtypeStruct((rows, width), F32...  51.5 us
    pallas_call x1, Pallas kernels, attention_backward(): pl.pallas_call(kernel, out_shape=(jax.ShapeDtypeStruct((total, width), BF...  29.9 us
    pallas_call x1, Pallas kernels, ffn_own(): pl.pallas_call(kernel, grid_spec=pltpu.PrefetchScalarGridSpec(num_scalar_...  24.8 us
    pallas_call x1, Pallas kernels, widen(): pl.pallas_call(kernel, grid=(steps,), in_specs=blocks + [pl.BlockSpec((n,...  18 us
    pallas_call x1, Pallas kernels, ffn_other(): pl.pallas_call(kernel, grid_spec=pltpu.PrefetchScalarGridSpec(num_scalar_...  17.5 us
  transfers between devices with their start and end apart: 4, of which 1 were waited for; matrix products, arithmetic and copies ran while one was open for 1% of the time, Pallas kernels for 34%

profile of v10, /device:TPU:0, one launch (start us, length us, event | category | flops | bytes accessed | tf_op | source)
XLA Modules:
  0.0 543.7 jit_solution(17761687828298294576)
XLA Ops:
  0.7 0.6 broadcast_in_dim_tile.5.freq_ref
  1.3 206.1 %front.1 = (bf16[8,128,2048]{2,1,0:T(8,128)(2,1)}, bf16[1024,256]{1,0:T(8,128)(2,1)}, bf16[1024,128]{1,0:T(8,128)(2,1)}, bf16[1024,256]{1,0:T(8,128)(2,1)}, bf16...) custom-call(bf16[128,2048]{1,0:T(8,128)(2,1)} %h_ref.1, ...), custom_call_target="tpu_custom_call" | custom-call | flops 199999995904 | bytes 52428800 | tf_op jit(solution)/shard_map/front/pallas_call | solution.py:511
  207.4 2.1 collective-permute-start.1
  209.5 0.0 collective-permute-start
  209.5 1.0 copy.32.deal_ref
  210.5 24.8 %ffn_own.1 = (bf16[4,1024,2048]{2,1,0:T(8,128)(2,1)}, bf16[4,1024,1024]{2,1,0:T(8,128)(2,1)}, bf16[4,1024,1024]{2,1,0:T(8,128)(2,1)}, bf16[4,1024,1024]{2,1,0:T(8,128)(2,1)}, bf16[1024,2048]{1,0:T(8,128)(2,1)}) custom-call(s32[1]{0:T(128)} %bitcast.g_ref, bf16[1024,2048]{1,0:T(8,128)(2,1)} %bitcast.46, ...), custom_call_target="tpu_custom_call" | custom-call | flops 25769803776 | bytes 41943040 | tf_op jit(solution)/shard_map/ffn_own/pallas_call | solution.py:1081
  235.3 51.5 %pull_gather.1 = (f32[128,2048]{1,0:T(8,128)}, f32[1,2048]{1,0:T(1,128)}, bf16[8,128,2048]{2,1,0:T(8,128)(2,1)}, bf16[1024,2048]{1,0:T(8,128)(2,1)}) custom-call(bf16[1024,2048]{1,0:T(8,128)(2,1)} %get-tuple-element.68.p_ref, f32[128,2048]{1,0:T(8,128)} %get-tuple-element.69.m_ref, f32[1,2048]{1,0:T(1,128)} %bitcast.31, ...), custom_call_target="tpu_custom_call" | custom-call | flops 60000002048 | bytes 13107200 | tf_op jit(solution)/shard_map/pull_gather/pallas_call | solution.py:634
  286.8 29.9 %attention_backward.1 = (bf16[1024,2048]{1,0:T(8,128)(2,1)}, bf16[2048,384]{1,0:T(8,128)(2,1)}, bf16[256,2048]{1,0:T(8,128)(2,1)}) custom-call(bf16[1024,2048]{1,0:T(8,128)(2,1)} %bitcast.47, bf16[256,2048]{1,0:T(8,128)(2,1)} %wo_ref.3, bf16[1024,256]{1,0:T(8,128)(2,1)} %get-tuple-element.73.a_ref, bf16[1024,256]{1,0:T(8,128)(2,1)} %get-tuple-element.74.q_ref, ...), custom_call_target="tpu_custom_call" | custom-call | flops 30000001024 | bytes 31457280 | tf_op jit(solution)/shard_map/attention_backward/pallas_call | solution.py:1030
  316.7 0.0 collective-permute-done.1.after_held
  316.7 0.0 collective-permute-done.before_held
  316.7 0.1 collective-permute-start.2
  316.8 79.6 %pull_tokens.1 = (f32[128,2048]{1,0:T(8,128)}, bf16[128,2048]{1,0:T(8,128)(2,1)}, f32[2,2048]{1,0:T(2,128)}, bf16[4,1024,2048]{2,1,0:T(8,128)(2,1)}, bf16[4,1024...) custom-call(bf16[1024,2048]{1,0:T(8,128)(2,1)} %get-tuple-element.79, ...), custom_call_target="tpu_custom_call", output_to_operand_aliasing={{3}: (12, {}), {4}: (13, {}), {5}: (14, {}), {6}: (15, {})} | custom-call | flops 60000002048 | bytes 13107200 | tf_op jit(solution)/shard_map/pull_tokens/pallas_call | solution.py:820
  396.3 0.0 collective-permute-done.2.held_ref
  396.4 0.1 collective-permute-start.3
  396.4 0.6 pad_add_fusion.w_ref
  397.0 1.4 fusion
  398.4 2.5 collective-permute-done.3.fetched_ref
  400.9 17.5 %ffn_other.1 = (bf16[4,1024,2048]{2,1,0:T(8,128)(2,1)}, bf16[4,1024,1024]{2,1,0:T(8,128)(2,1)}, bf16[4,1024,1024]{2,1,0:T(8,128)(2,1)}, bf16[4,1024,1024]{2,1,0:T(8,128)(2,1)}) custom-call(s32[2]{0:T(128)} %pad_add_fusion.w_ref, ...), custom_call_target="tpu_custom_call", output_to_operand_aliasing={{0}: (6, {}), {1}: (7, {}), {2}: (8, {}), {3}: (9, {})} | custom-call | flops 17179869184 | bytes 41943040 | tf_op jit(solution)/shard_map/ffn_other/pallas_call | solution.py:1138
  418.5 105.2 %finish.1 = (bf16[256,8192]{1,0:T(8,128)(2,1)}, bf16[256,8192]{1,0:T(8,128)(2,1)}, bf16[1024,2048]{1,0:T(8,128)(2,1)}, bf16[256,2048]{1,0:T(8,128)(2,1)}, bf16[2048,384]{1,0:T(8,128)(2,1)}) custom-call(bf16[4096,2048]{1,0:T(8,128)(2,1)} %bitcast.35, bf16[4096,1024]{1,0:T(8,128)(2,1)} %bitcast.37, bf16[4096,1024]{1,0:T(8,128)(2,1)} %bitcast.38, ...), custom_call_target="tpu_custom_call" | custom-call | flops 120000004096 | bytes 83886080 | tf_op jit(solution)/shard_map/finish/pallas_call | solution.py:1370
  523.7 0.0 copy-start.1
  523.7 0.0 copy-start
  523.7 18.0 %widen.1 = (f32[256,8192]{1,0:T(8,128)}, f32[256,8192]{1,0:T(8,128)}, f32[1024,2048]{1,0:T(8,128)}, f32[256,2048]{1,0:T(8,128)}, f32[256,2048]{1,0:T(8,128)}, /*index=5*/f32[256,512]{1,0:T(8,128)}, f32[256,512]{1,0:T(8,128)}) custom-call(bf16[256,8192]{1,0:T(8,128)(2,1)} %get-tuple-element.105.g_ref, bf16[256,8192]{1,0:T(8,128)(2,1)} %get-tuple-element.106.u_ref, ...), custom_call_target="tpu_custom_call" | custom-call | flops 8388608 | bytes 41943040 | tf_op jit(solution)/shard_map/widen/pallas_call | solution.py:1430
  541.7 0.8 copy.43
  542.5 1.0 copy.44
  (6 shorter events, 0.0 us)
Async XLA Ops:
  1.3 208.2 %copy-start.2 = (s32[1,1024]{1,0:T(1,128)S(1)}, s32[1,1024]{1,0:T(1,128)}, u32[]{:S(2)}) copy-start(s32[1,1024]{1,0:T(1,128)} %deal_ref.1) | copy-start | bytes 12292
  207.4 109.3 %collective-permute-start.1 = (bf16[512,2048]{1,0:T(8,128)(2,1)}, bf16[512,2048]{1,0:T(8,128)(2,1)}, u32[]{:S(2)}, u32[]{:S(2)}) collective-permute-start(bf16[512,2048]{1,0:T(8,128)(2,1)} %bitcast.28), channel_id=1, source_target_pairs={{0,24},{8,0},{16,8},{24,16},{1,25},{9,1},{17,9},{25,17},{2,26},{10... | collective-permute-start | bytes 6291464 | tf_op jit(solution)/shard_map/ppermute | solution.py:1472
  209.5 107.2 %collective-permute-start = (bf16[512,2048]{1,0:T(8,128)(2,1)}, bf16[512,2048]{1,0:T(8,128)(2,1)}, u32[]{:S(2)}, u32[]{:S(2)}) collective-permute-start(bf16[512,2048]{1,0:T(8,128)(2,1)} %bitcast.29), channel_id=1, source_target_pairs={{0,8},{8,16},{16,24},{24,0},{1,9},{9,17},{17,25},{25,1},{2,10},{10... | collective-permute-start | bytes 6291464 | tf_op jit(solution)/shard_map/ppermute | solution.py:1472
  316.7 79.6 %collective-permute-start.2 = (bf16[512,2048]{1,0:T(8,128)(2,1)}, bf16[512,2048]{1,0:T(8,128)(2,1)}, u32[]{:S(2)}, u32[]{:S(2)}) collective-permute-start(bf16[512,2048]{1,0:T(8,128)(2,1)} %collective-permute-done.before_held), channel_id=1, source_target_pairs={{0,8},{8,16},{16,24},{24,0},{1,9},{9,17},{17,25},{25,1},{2,10},{10... | collective-permute-start | bytes 6291464 | tf_op jit(solution)/shard_map/ppermute | solution.py:1472
  396.4 4.6 collective-permute-start.3
  523.7 18.0 %copy-start.1 = (bf16[128,2048]{1,0:T(8,128)(2,1)S(1)}, bf16[128,2048]{1,0:T(8,128)(2,1)}, u32[]{:S(2)}) copy-start(bf16[128,2048]{1,0:T(8,128)(2,1)} %get-tuple-element.130) | copy-start | bytes 1572868
  523.7 18.8 %copy-start = (f32[128,2048]{1,0:T(8,128)S(1)}, f32[128,2048]{1,0:T(8,128)}, u32[]{:S(2)}) copy-start(f32[128,2048]{1,0:T(8,128)} %get-tuple-element.131) | copy-start | bytes 3145732

commit v11 on v10

--- a/solution.py
+++ b/solution.py
@@ -673,7 +673,7 @@
     def kernel(
         p_ref, o_ref, h_ref, gain_ref, mg_ref, og_ref, wg_ref, wu_ref, ag_hbm,
         before_held, after_held, qkv_hbm, unused_na, unused_act, unused_gg, unused_ug,
-        out, lay, gains, na_hbm, act_hbm, gg_hbm, ug_hbm, fetched, qkv_out, share_sems, qkv_sems, own_sem,
+        out, lay, gains, na_hbm, act_hbm, gg_hbm, ug_hbm, fetched, qkv_out, share_sems, qkv_sems, own_sem, own_block,
         nf_buf, ag_buf, done_buf, in_sems, out_sems, gain_in, gain_out, gain_sems, *scratch,
     ):
         me = lax.axis_index("shard")
@@ -774,14 +774,17 @@
         for mask in range(1, 8):
             peer = flip(me, mask)
             exchange_qkv.append(send(qkv_hbm.at[peer], qkv_out.at[me], qkv_sems, mask - 1, peer))
-        own_qkv = pltpu.make_async_copy(qkv_hbm.at[me], qkv_out.at[me], own_sem.at[0])
+        own_in = pltpu.make_async_copy(qkv_hbm.at[me], own_block, own_sem.at[0])
+        own_in.start()
+        own_qkv = pltpu.make_async_copy(own_block, qkv_out.at[me], own_sem.at[1])
         fill(0)
         next(grads)
-        for copy in exchange_qkv + [own_qkv]:
-            copy.start()
         fill(1)
         next(grads)
         next(outputs)
+        own_in.wait()
+        for copy in exchange_qkv + [own_qkv]:
+            copy.start()
         fill(2)
         next(grads)
         next(outputs)
@@ -836,7 +839,8 @@
         scratch_shapes=[
             pltpu.SemaphoreType.DMA((2, 2)),
             pltpu.SemaphoreType.DMA((2, 7)),
-            pltpu.SemaphoreType.DMA((1,)),
+            pltpu.SemaphoreType.DMA((2,)),
+            pltpu.VMEM(qkv.shape[1:], BF16),
             pltpu.VMEM((2 * per_half, block, width), BF16),
             pltpu.VMEM((2 * per_half, block, cols), BF16),
             pltpu.VMEM((3, 2 * per_half, block, cols), BF16),

time: 548 us -> 548 us (level)
  no operation moved by 1% of the time
where the time goes in v11:
time: 548 us; the launch traced here: 544 us
  Pallas kernels  533 us (97%)
    pallas_call x1, Pallas kernels, front(): pl.pallas_call(kernel, out_shape=(rows8, jax.ShapeDtypeStruct((total, q_c...  206 us
    pallas_call x1, Pallas kernels, finish(): pl.pallas_call(kernel, out_shape=(exchanged, exchanged, jax.ShapeDtypeStr...  105 us
    pallas_call x1, Pallas kernels, pull_tokens(): pl.pallas_call(kernel, out_shape=(jax.ShapeDtypeStruct((rows, width), F32...  79.5 us
    pallas_call x1, Pallas kernels, pull_gather(): pl.pallas_call(kernel, out_shape=(jax.ShapeDtypeStruct((rows, width), F32...  51.5 us
    pallas_call x1, Pallas kernels, attention_backward(): pl.pallas_call(kernel, out_shape=(jax.ShapeDtypeStruct((total, width), BF...  29.9 us
    pallas_call x1, Pallas kernels, ffn_own(): pl.pallas_call(kernel, grid_spec=pltpu.PrefetchScalarGridSpec(num_scalar_...  24.8 us
    pallas_call x1, Pallas kernels, widen(): pl.pallas_call(kernel, grid=(steps,), in_specs=blocks + [pl.BlockSpec((n,...  18 us
    pallas_call x1, Pallas kernels, ffn_other(): pl.pallas_call(kernel, grid_spec=pltpu.PrefetchScalarGridSpec(num_scalar_...  17.6 us
  transfers between devices with their start and end apart: 4, of which 1 were waited for; matrix products, arithmetic and copies ran while one was open for 1% of the time, Pallas kernels for 34%

profile of v11, /device:TPU:0, one launch (start us, length us, event | category | flops | bytes accessed | tf_op | source)
XLA Modules:
  0.0 543.7 jit_solution(5776269366866651823)
XLA Ops:
  0.7 0.6 broadcast_in_dim_tile.5.freq_ref
  1.3 206.1 %front.1 = (bf16[8,128,2048]{2,1,0:T(8,128)(2,1)}, bf16[1024,256]{1,0:T(8,128)(2,1)}, bf16[1024,128]{1,0:T(8,128)(2,1)}, bf16[1024,256]{1,0:T(8,128)(2,1)}, bf16...) custom-call(bf16[128,2048]{1,0:T(8,128)(2,1)} %h_ref.1, ...), custom_call_target="tpu_custom_call" | custom-call | flops 199999995904 | bytes 52428800 | tf_op jit(solution)/shard_map/front/pallas_call | solution.py:511
  207.4 2.1 collective-permute-start.1
  209.5 0.0 collective-permute-start
  209.5 0.0 copy-done.2
  209.5 1.0 copy.32.deal_ref
  210.5 24.8 %ffn_own.1 = (bf16[4,1024,2048]{2,1,0:T(8,128)(2,1)}, bf16[4,1024,1024]{2,1,0:T(8,128)(2,1)}, bf16[4,1024,1024]{2,1,0:T(8,128)(2,1)}, bf16[4,1024,1024]{2,1,0:T(8,128)(2,1)}, bf16[1024,2048]{1,0:T(8,128)(2,1)}) custom-call(s32[1]{0:T(128)} %bitcast.g_ref, bf16[1024,2048]{1,0:T(8,128)(2,1)} %bitcast.46, ...), custom_call_target="tpu_custom_call" | custom-call | flops 25769803776 | bytes 41943040 | tf_op jit(solution)/shard_map/ffn_own/pallas_call | solution.py:1085
  235.3 51.5 %pull_gather.1 = (f32[128,2048]{1,0:T(8,128)}, f32[1,2048]{1,0:T(1,128)}, bf16[8,128,2048]{2,1,0:T(8,128)(2,1)}, bf16[1024,2048]{1,0:T(8,128)(2,1)}) custom-call(bf16[1024,2048]{1,0:T(8,128)(2,1)} %get-tuple-element.68.p_ref, f32[128,2048]{1,0:T(8,128)} %get-tuple-element.69.m_ref, f32[1,2048]{1,0:T(1,128)} %bitcast.31, ...), custom_call_target="tpu_custom_call" | custom-call | flops 60000002048 | bytes 13107200 | tf_op jit(solution)/shard_map/pull_gather/pallas_call | solution.py:634
  286.8 29.9 %attention_backward.1 = (bf16[1024,2048]{1,0:T(8,128)(2,1)}, bf16[2048,384]{1,0:T(8,128)(2,1)}, bf16[256,2048]{1,0:T(8,128)(2,1)}) custom-call(bf16[1024,2048]{1,0:T(8,128)(2,1)} %bitcast.47, bf16[256,2048]{1,0:T(8,128)(2,1)} %wo_ref.3, bf16[1024,256]{1,0:T(8,128)(2,1)} %get-tuple-element.73.a_ref, bf16[1024,256]{1,0:T(8,128)(2,1)} %get-tuple-element.74.q_ref, ...), custom_call_target="tpu_custom_call" | custom-call | flops 30000001024 | bytes 31457280 | tf_op jit(solution)/shard_map/attention_backward/pallas_call | solution.py:1034
  316.7 0.0 collective-permute-done.1.after_held
  316.7 0.0 collective-permute-done.before_held
  316.7 0.1 collective-permute-start.2
  316.8 79.5 %pull_tokens.1 = (f32[128,2048]{1,0:T(8,128)}, bf16[128,2048]{1,0:T(8,128)(2,1)}, f32[2,2048]{1,0:T(2,128)}, bf16[4,1024,2048]{2,1,0:T(8,128)(2,1)}, bf16[4,1024...) custom-call(bf16[1024,2048]{1,0:T(8,128)(2,1)} %get-tuple-element.79, ...), custom_call_target="tpu_custom_call", output_to_operand_aliasing={{3}: (12, {}), {4}: (13, {}), {5}: (14, {}), {6}: (15, {})} | custom-call | flops 60000002048 | bytes 13107200 | tf_op jit(solution)/shard_map/pull_tokens/pallas_call | solution.py:823
  396.3 0.0 collective-permute-done.2.held_ref
  396.3 0.1 collective-permute-start.3
  396.4 0.6 pad_add_fusion.w_ref
  397.0 1.4 fusion
  398.4 2.5 collective-permute-done.3.fetched_ref
  400.9 17.6 %ffn_other.1 = (bf16[4,1024,2048]{2,1,0:T(8,128)(2,1)}, bf16[4,1024,1024]{2,1,0:T(8,128)(2,1)}, bf16[4,1024,1024]{2,1,0:T(8,128)(2,1)}, bf16[4,1024,1024]{2,1,0:T(8,128)(2,1)}) custom-call(s32[2]{0:T(128)} %pad_add_fusion.w_ref, ...), custom_call_target="tpu_custom_call", output_to_operand_aliasing={{0}: (6, {}), {1}: (7, {}), {2}: (8, {}), {3}: (9, {})} | custom-call | flops 17179869184 | bytes 41943040 | tf_op jit(solution)/shard_map/ffn_other/pallas_call | solution.py:1142
  418.5 105.3 %finish.1 = (bf16[256,8192]{1,0:T(8,128)(2,1)}, bf16[256,8192]{1,0:T(8,128)(2,1)}, bf16[1024,2048]{1,0:T(8,128)(2,1)}, bf16[256,2048]{1,0:T(8,128)(2,1)}, bf16[2048,384]{1,0:T(8,128)(2,1)}) custom-call(bf16[4096,2048]{1,0:T(8,128)(2,1)} %bitcast.35, bf16[4096,1024]{1,0:T(8,128)(2,1)} %bitcast.37, bf16[4096,1024]{1,0:T(8,128)(2,1)} %bitcast.38, ...), custom_call_target="tpu_custom_call" | custom-call | flops 120000004096 | bytes 83886080 | tf_op jit(solution)/shard_map/finish/pallas_call | solution.py:1374
  523.7 0.0 copy-start.1
  523.8 18.0 %widen.1 = (f32[256,8192]{1,0:T(8,128)}, f32[256,8192]{1,0:T(8,128)}, f32[1024,2048]{1,0:T(8,128)}, f32[256,2048]{1,0:T(8,128)}, f32[256,2048]{1,0:T(8,128)}, /*index=5*/f32[256,512]{1,0:T(8,128)}, f32[256,512]{1,0:T(8,128)}) custom-call(bf16[256,8192]{1,0:T(8,128)(2,1)} %get-tuple-element.105.g_ref, bf16[256,8192]{1,0:T(8,128)(2,1)} %get-tuple-element.106.u_ref, ...), custom_call_target="tpu_custom_call" | custom-call | flops 8388608 | bytes 41943040 | tf_op jit(solution)/shard_map/widen/pallas_call | solution.py:1434
  541.8 0.8 copy.43
  542.6 1.0 copy.44
  (6 shorter events, 0.0 us)
Async XLA Ops:
  1.3 208.2 %copy-start.2 = (s32[1,1024]{1,0:T(1,128)S(1)}, s32[1,1024]{1,0:T(1,128)}, u32[]{:S(2)}) copy-start(s32[1,1024]{1,0:T(1,128)} %deal_ref.1) | copy-start | bytes 12292
  207.4 109.3 %collective-permute-start.1 = (bf16[512,2048]{1,0:T(8,128)(2,1)}, bf16[512,2048]{1,0:T(8,128)(2,1)}, u32[]{:S(2)}, u32[]{:S(2)}) collective-permute-start(bf16[512,2048]{1,0:T(8,128)(2,1)} %bitcast.28), channel_id=1, source_target_pairs={{0,24},{8,0},{16,8},{24,16},{1,25},{9,1},{17,9},{25,17},{2,26},{10... | collective-permute-start | bytes 6291464 | tf_op jit(solution)/shard_map/ppermute | solution.py:1476
  209.5 107.2 %collective-permute-start = (bf16[512,2048]{1,0:T(8,128)(2,1)}, bf16[512,2048]{1,0:T(8,128)(2,1)}, u32[]{:S(2)}, u32[]{:S(2)}) collective-permute-start(bf16[512,2048]{1,0:T(8,128)(2,1)} %bitcast.29), channel_id=1, source_target_pairs={{0,8},{8,16},{16,24},{24,0},{1,9},{9,17},{17,25},{25,1},{2,10},{10... | collective-permute-start | bytes 6291464 | tf_op jit(solution)/shard_map/ppermute | solution.py:1476
  316.7 79.6 %collective-permute-start.2 = (bf16[512,2048]{1,0:T(8,128)(2,1)}, bf16[512,2048]{1,0:T(8,128)(2,1)}, u32[]{:S(2)}, u32[]{:S(2)}) collective-permute-start(bf16[512,2048]{1,0:T(8,128)(2,1)} %collective-permute-done.before_held), channel_id=1, source_target_pairs={{0,8},{8,16},{16,24},{24,0},{1,9},{9,17},{17,25},{25,1},{2,10},{10... | collective-permute-start | bytes 6291464 | tf_op jit(solution)/shard_map/ppermute | solution.py:1476
  396.3 4.6 collective-permute-start.3
  523.7 18.0 %copy-start.1 = (bf16[128,2048]{1,0:T(8,128)(2,1)S(1)}, bf16[128,2048]{1,0:T(8,128)(2,1)}, u32[]{:S(2)}) copy-start(bf16[128,2048]{1,0:T(8,128)(2,1)} %get-tuple-element.130) | copy-start | bytes 1572868
  523.8 18.8 %copy-start = (f32[128,2048]{1,0:T(8,128)S(1)}, f32[128,2048]{1,0:T(8,128)}, u32[]{:S(2)}) copy-start(f32[128,2048]{1,0:T(8,128)} %get-tuple-element.131) | copy-start | bytes 3145732

commit v12 on v9

--- a/solution.py
+++ b/solution.py
@@ -1006,14 +1006,11 @@
 
         lax.fori_loop(0, total // block, close_up, 0)
 
-        def weigh(i, carry):
-            cols = pl.ds(pl.multiple_of(i * 512, 512), 512)
+        for i in range(width // 512):
+            cols = slice(i * 512, (i + 1) * 512)
             dqkv_ref[cols, :q_cols] = t_mm(n_ref[:, cols], pq_ref[...]).astype(BF16)
             dqkv_ref[cols, q_cols:] = t_mm(n_ref[:, cols], pkv_ref[...]).astype(BF16)
             dwo_ref[:, cols] = t_mm(a_ref[...], bg_ref[:, cols]).astype(BF16)
-            return carry
-
-        lax.fori_loop(0, width // 512, weigh, 0)
 
     return pl.pallas_call(
         kernel,
@@ -1081,7 +1078,7 @@
             hidden,
             jax.ShapeDtypeStruct((total, width), BF16),
         ),
-        compiler_params=pltpu.CompilerParams(vmem_limit_bytes=48 << 20),
+        compiler_params=pltpu.CompilerParams(vmem_limit_bytes=62 << 20),
         cost_estimate=pl.CostEstimate(
             flops=12 * total * width * cols, bytes_accessed=40 << 20, transcendentals=total * cols
         ),
@@ -1134,7 +1131,7 @@
         ),
         out_shape=(jax.ShapeDtypeStruct((groups, total, width), BF16), hidden, hidden, hidden),
         input_output_aliases={6: 0, 7: 1, 8: 2, 9: 3},
-        compiler_params=pltpu.CompilerParams(vmem_limit_bytes=48 << 20),
+        compiler_params=pltpu.CompilerParams(vmem_limit_bytes=62 << 20),
         cost_estimate=pl.CostEstimate(
             flops=8 * total * width * cols, bytes_accessed=40 << 20, transcendentals=total * cols
         ),
@@ -1422,7 +1419,7 @@
         out_specs=blocks + [spec(block, across) for across in narrow],
         out_shape=[jax.ShapeDtypeStruct(shape, F32) for shape in shapes]
         + [jax.ShapeDtypeStruct((rows, across), F32) for across in narrow],
-        compiler_params=pltpu.CompilerParams(vmem_limit_bytes=24 << 20),
+        compiler_params=pltpu.CompilerParams(vmem_limit_bytes=62 << 20),
         cost_estimate=pl.CostEstimate(
             flops=4 * rows * wide, bytes_accessed=20 * rows * wide, transcendentals=0
         ),

time: 537 us -> 534 us (level)
  local copies, waits for them, and re-layouts: 16 us -> 5.95 us
  Pallas kernels: 506 us -> 515 us
    unnamed x20 -> x10, local copies, waits for them, and re-layouts: 13 us -> 2.92 us
    pallas_call x1, Pallas kernels: 10.5 us -> 18 us  [widen(): pl.pallas_call(kernel, grid=(steps,), in_specs=blocks + [pl.BlockSpec((n,...]
  transfers between devices with their start and end apart: 5 -> 5, of which waited for: 1 -> 1; matrix products, arithmetic and copies ran while one was open for 0% -> 1% of each run, Pallas kernels for 35% -> 35%
where the time goes in v12:
time: 534 us; the launch traced here: 530 us
  Pallas kernels  515 us (96%)
  starting transfers between devices  6.02 us (1%)
  local copies, waits for them, and re-layouts  5.95 us (1%)
    pallas_call x1, Pallas kernels, front(): pl.pallas_call(kernel, out_shape=(rows8, jax.ShapeDtypeStruct((total, q_c...  206 us
    pallas_call x1, Pallas kernels, finish(): pl.pallas_call(kernel, out_shape=(exchanged, exchanged, jax.ShapeDtypeStr...  105 us
    pallas_call x1, Pallas kernels, pull_tokens(): pl.pallas_call(kernel, out_shape=(jax.ShapeDtypeStruct((rows, width), F32...  62 us
    pallas_call x1, Pallas kernels, pull_gather(): pl.pallas_call(kernel, out_shape=(jax.ShapeDtypeStruct((rows, width), F32...  51.5 us
    pallas_call x1, Pallas kernels, attention_backward(): pl.pallas_call(kernel, out_shape=(jax.ShapeDtypeStruct((total, width), BF...  29.9 us
    pallas_call x1, Pallas kernels, ffn_own(): pl.pallas_call(kernel, grid_spec=pltpu.PrefetchScalarGridSpec(num_scalar_...  24.8 us
    pallas_call x1, Pallas kernels, widen(): pl.pallas_call(kernel, grid=(steps,), in_specs=blocks + [pl.BlockSpec((n,...  18 us
    pallas_call x1, Pallas kernels, ffn_other(): pl.pallas_call(kernel, grid_spec=pltpu.PrefetchScalarGridSpec(num_scalar_...  17.4 us
  transfers between devices with their start and end apart: 5, of which 1 were waited for; matrix products, arithmetic and copies ran while one was open for 1% of the time, Pallas kernels for 35%

profile of v12, /device:TPU:0, one launch (start us, length us, event | category | flops | bytes accessed | tf_op | source)
XLA Modules:
  0.0 529.9 jit_solution(5510407571579064751)
XLA Ops:
  0.7 0.6 broadcast_in_dim_tile.5.freq_ref
  1.3 206.1 %front.1 = (bf16[8,128,2048]{2,1,0:T(8,128)(2,1)}, bf16[1024,256]{1,0:T(8,128)(2,1)}, bf16[1024,128]{1,0:T(8,128)(2,1)}, bf16[1024,256]{1,0:T(8,128)(2,1)}, bf16...) custom-call(bf16[128,2048]{1,0:T(8,128)(2,1)} %h_ref.1, ...), custom_call_target="tpu_custom_call" | custom-call | flops 199999995904 | bytes 52428800 | tf_op jit(solution)/shard_map/front/pallas_call | solution.py:511
  207.3 2.1 collective-permute-start.1
  209.5 0.0 collective-permute-start
  209.5 1.0 copy.32.deal_ref
  210.5 24.8 %ffn_own.1 = (bf16[4,1024,2048]{2,1,0:T(8,128)(2,1)}, bf16[4,1024,1024]{2,1,0:T(8,128)(2,1)}, bf16[4,1024,1024]{2,1,0:T(8,128)(2,1)}, bf16[4,1024,1024]{2,1,0:T(8,128)(2,1)}, bf16[1024,2048]{1,0:T(8,128)(2,1)}) custom-call(s32[1]{0:T(128)} %bitcast.g_ref, bf16[1024,2048]{1,0:T(8,128)(2,1)} %bitcast.47, ...), custom_call_target="tpu_custom_call" | custom-call | flops 25769803776 | bytes 41943040 | tf_op jit(solution)/shard_map/ffn_own/pallas_call | solution.py:1066
  235.3 51.5 %pull_gather.1 = (f32[128,2048]{1,0:T(8,128)}, f32[1,2048]{1,0:T(1,128)}, bf16[8,128,2048]{2,1,0:T(8,128)(2,1)}, bf16[1024,2048]{1,0:T(8,128)(2,1)}) custom-call(bf16[1024,2048]{1,0:T(8,128)(2,1)} %get-tuple-element.67.p_ref, f32[128,2048]{1,0:T(8,128)} %get-tuple-element.68.m_ref, f32[1,2048]{1,0:T(1,128)} %bitcast.32, ...), custom_call_target="tpu_custom_call" | custom-call | flops 60000002048 | bytes 13107200 | tf_op jit(solution)/shard_map/pull_gather/pallas_call | solution.py:634
  286.8 29.9 %attention_backward.1 = (bf16[1024,2048]{1,0:T(8,128)(2,1)}, bf16[2048,384]{1,0:T(8,128)(2,1)}, bf16[256,2048]{1,0:T(8,128)(2,1)}) custom-call(bf16[1024,2048]{1,0:T(8,128)(2,1)} %bitcast.48, bf16[256,2048]{1,0:T(8,128)(2,1)} %wo_ref.3, bf16[1024,256]{1,0:T(8,128)(2,1)} %get-tuple-element.72.a_ref, bf16[1024,256]{1,0:T(8,128)(2,1)} %get-tuple-element.73.q_ref, ...), custom_call_target="tpu_custom_call" | custom-call | flops 30000001024 | bytes 31457280 | tf_op jit(solution)/shard_map/attention_backward/pallas_call | solution.py:1015
  316.7 0.0 collective-permute-done.1.after_held
  316.7 0.0 collective-permute-done.before_held
  316.7 0.1 collective-permute-start.2
  316.8 62.0 %pull_tokens.1 = (f32[128,2048]{1,0:T(8,128)}, bf16[128,2048]{1,0:T(8,128)(2,1)}, f32[2,2048]{1,0:T(2,128)}, bf16[4,1024,2048]{2,1,0:T(8,128)(2,1)}, bf16[4,1024...) custom-call(bf16[1024,2048]{1,0:T(8,128)(2,1)} %get-tuple-element.78, ...), custom_call_target="tpu_custom_call", output_to_operand_aliasing={{3}: (11, {}), {4}: (12, {}), {5}: (13, {}), {6}: (14, {})} | custom-call | flops 60000002048 | bytes 13107200 | tf_op jit(solution)/shard_map/pull_tokens/pallas_call | solution.py:808
  378.8 0.1 collective-permute-start.3
  378.9 3.8 all-to-all-start
  382.7 0.6 pad_add_fusion.w_ref
  383.3 1.4 fusion
  384.7 0.0 collective-permute-done.3.fetched_ref
  384.7 17.4 %ffn_other.1 = (bf16[4,1024,2048]{2,1,0:T(8,128)(2,1)}, bf16[4,1024,1024]{2,1,0:T(8,128)(2,1)}, bf16[4,1024,1024]{2,1,0:T(8,128)(2,1)}, bf16[4,1024,1024]{2,1,0:T(8,128)(2,1)}) custom-call(s32[2]{0:T(128)} %pad_add_fusion.w_ref, ...), custom_call_target="tpu_custom_call", output_to_operand_aliasing={{0}: (6, {}), {1}: (7, {}), {2}: (8, {}), {3}: (9, {})} | custom-call | flops 17179869184 | bytes 41943040 | tf_op jit(solution)/shard_map/ffn_other/pallas_call | solution.py:1123
  402.0 1.6 all-to-all-done
  403.6 1.1 copy-done
  404.8 105.1 %finish.1 = (bf16[256,8192]{1,0:T(8,128)(2,1)}, bf16[256,8192]{1,0:T(8,128)(2,1)}, bf16[1024,2048]{1,0:T(8,128)(2,1)}, bf16[256,2048]{1,0:T(8,128)(2,1)}, bf16[2048,384]{1,0:T(8,128)(2,1)}) custom-call(bf16[4096,2048]{1,0:T(8,128)(2,1)} %bitcast.36, bf16[4096,1024]{1,0:T(8,128)(2,1)} %bitcast.38, bf16[4096,1024]{1,0:T(8,128)(2,1)} %bitcast.39, ...), custom_call_target="tpu_custom_call" | custom-call | flops 120000004096 | bytes 83886080 | tf_op jit(solution)/shard_map/finish/pallas_call | solution.py:1355
  509.9 18.0 %widen.1 = (f32[256,8192]{1,0:T(8,128)}, f32[256,8192]{1,0:T(8,128)}, f32[1024,2048]{1,0:T(8,128)}, f32[256,2048]{1,0:T(8,128)}, f32[256,2048]{1,0:T(8,128)}, /*index=5*/f32[256,512]{1,0:T(8,128)}, f32[256,512]{1,0:T(8,128)}) custom-call(bf16[256,8192]{1,0:T(8,128)(2,1)} %get-tuple-element.103.g_ref, bf16[256,8192]{1,0:T(8,128)(2,1)} %get-tuple-element.104.u_ref, ...), custom_call_target="tpu_custom_call" | custom-call | flops 8388608 | bytes 41943040 | tf_op jit(solution)/shard_map/widen/pallas_call | solution.py:1415
  527.9 0.8 copy.43
  528.7 1.0 copy.44
  (10 shorter events, 0.0 us)
Async XLA Ops:
  1.3 208.2 %copy-start.3 = (s32[1,1024]{1,0:T(1,128)S(1)}, s32[1,1024]{1,0:T(1,128)}, u32[]{:S(2)}) copy-start(s32[1,1024]{1,0:T(1,128)} %deal_ref.1) | copy-start | bytes 12292
  207.3 109.4 %collective-permute-start.1 = (bf16[512,2048]{1,0:T(8,128)(2,1)}, bf16[512,2048]{1,0:T(8,128)(2,1)}, u32[]{:S(2)}, u32[]{:S(2)}) collective-permute-start(bf16[512,2048]{1,0:T(8,128)(2,1)} %bitcast.29), channel_id=1, source_target_pairs={{0,24},{8,0},{16,8},{24,16},{1,25},{9,1},{17,9},{25,17},{2,26},{10... | collective-permute-start | bytes 6291464 | tf_op jit(solution)/shard_map/ppermute | solution.py:1457
  209.5 107.2 %collective-permute-start = (bf16[512,2048]{1,0:T(8,128)(2,1)}, bf16[512,2048]{1,0:T(8,128)(2,1)}, u32[]{:S(2)}, u32[]{:S(2)}) collective-permute-start(bf16[512,2048]{1,0:T(8,128)(2,1)} %bitcast.30), channel_id=1, source_target_pairs={{0,8},{8,16},{16,24},{24,0},{1,9},{9,17},{17,25},{25,1},{2,10},{10... | collective-permute-start | bytes 6291464 | tf_op jit(solution)/shard_map/ppermute | solution.py:1457
  316.7 62.1 %collective-permute-start.2 = (bf16[512,2048]{1,0:T(8,128)(2,1)}, bf16[512,2048]{1,0:T(8,128)(2,1)}, u32[]{:S(2)}, u32[]{:S(2)}) collective-permute-start(bf16[512,2048]{1,0:T(8,128)(2,1)} %collective-permute-done.before_held), channel_id=1, source_target_pairs={{0,8},{8,16},{16,24},{24,0},{1,9},{9,17},{17,25},{25,1},{2,10},{10... | collective-permute-start | bytes 6291464 | tf_op jit(solution)/shard_map/ppermute | solution.py:1457
  378.8 5.9 %collective-permute-start.3 = (bf16[512,2048]{1,0:T(8,128)(2,1)}, bf16[512,2048]{1,0:T(8,128)(2,1)}, u32[]{:S(2)}, u32[]{:S(2)}) collective-permute-start(bf16[512,2048]{1,0:T(8,128)(2,1)} %collective-permute-done.2.held_ref), channel_id=1, source_target_pairs={{0,1},{1,0},{2,3},{3,2},{4,5},{5,4},{6,7},{7,6},{8,9},{9,8},{10,11... | collective-permute-start | bytes 6291464 | tf_op jit(solution)/shard_map/ppermute | solution.py:1460
  378.9 24.7 %all-to-all-start = ((bf16[8,256,384]{2,1,0:T(8,128)(2,1)}), bf16[8,256,384]{2,1,0:T(8,128)(2,1)S(1)}, u32[]{:S(2)}, u32[]{:S(2)}) async-start(bf16[8,256,384]{2,1,0:T(8,128)(2,1)} %bitcast.20), calls=%async_computation | async-start | bytes 3145728 | tf_op jit(solution)/shard_map/all_to_all | solution.py:85
  403.6 1.1 copy-start
  509.9 18.0 %copy-start.2 = (bf16[128,2048]{1,0:T(8,128)(2,1)S(1)}, bf16[128,2048]{1,0:T(8,128)(2,1)}, u32[]{:S(2)}) copy-start(bf16[128,2048]{1,0:T(8,128)(2,1)} %get-tuple-element.128) | copy-start | bytes 1572868
  509.9 18.8 %copy-start.1 = (f32[128,2048]{1,0:T(8,128)S(1)}, f32[128,2048]{1,0:T(8,128)}, u32[]{:S(2)}) copy-start(f32[128,2048]{1,0:T(8,128)} %get-tuple-element.129) | copy-start | bytes 3145732
